TPU v7x, 32 devices: a whole 2x2x4 slice. The times are simulated.
32 devices in a mesh: section: 2 (over core), group: 4 (over y, x), dp: 4 (over z).
Axes of the slice: x: 2, y: 2, z: 4, core: 2. Of those that a mesh axis runs over, the one named last changes fastest.
Arguments:
- tokens: int32 [4096], P(('group', 'dp')), may hold values from 0 to 16383
- lengths: int32 [32], P(('group', 'dp')), may hold values from 16 to 128, as said below
- levels: int32 [32], P(('group', 'dp')), may hold values from 0 to 63
- noise_rows: bfloat16 [4096, 256], P(('group', 'dp')), may hold values from -6 to 6
- embed_table: bfloat16 [16384, 256], P('dp'), may hold values from -0.75 to 0.75
- w_in: bfloat16 [256, 1024], P('dp'), may hold values from -0.375 to 0.375
- ln_attn: bfloat16 [2, 1024], P('section', 'dp'), may hold values from 0.5 to 1.5
- w_qkv: bfloat16 [2, 1024, 3072], P('section', 'dp'), may hold values from -0.1875 to 0.1875
- w_proj: bfloat16 [2, 1024, 1024], P('section', 'dp'), may hold values from -0.75 to 0.75
- ln_mlp: bfloat16 [2, 1024], P('section', 'dp'), may hold values from 0.5 to 1.5
- w_up: bfloat16 [2, 1024, 4096], P('section', 'dp'), may hold values from -0.1875 to 0.1875
- w_down: bfloat16 [2, 4096, 1024], P('section', 'dp'), may hold values from -0.09375 to 0.09375
- ln_final: bfloat16 [1024], P('dp'), may hold values from 0.5 to 1.5
- w_out: bfloat16 [1024, 256], P('dp'), may hold values from -0.1875 to 0.1875
Outputs:
- token_loss: bfloat16 [4096], P(('group', 'dp'))
- grad_table: float32 [16384, 256], P('dp')
- grad_w_in: float32 [256, 1024], P('dp')
- grad_ln_attn: float32 [2, 1024], P('section', 'dp')
- grad_w_qkv: float32 [2, 1024, 3072], P('section', 'dp')
- grad_w_proj: float32 [2, 1024, 1024], P('section', 'dp')
- grad_ln_mlp: float32 [2, 1024], P('section', 'dp')
- grad_w_up: float32 [2, 1024, 4096], P('section', 'dp')
- grad_w_down: float32 [2, 4096, 1024], P('section', 'dp')
- grad_ln_final: float32 [1024], P('dp')
- grad_w_out: float32 [1024, 256], P('dp')
Inputs may be any that keep to these rules, and one draw needn't show every extreme that they name: Sequence lengths; the longest has exactly 128 tokens.
All inputs are finite; a program needn't handle non-finite values.
Results may differ from a plain program's by a relative error of at most 0.015.
Values may be sent and summed in bfloat16 or wider, within the bound.
A program may use at most 320 MiB of HBM per device.

v0:
```python
import math

import jax
import jax.numpy as jnp
from jax import lax
from jax.sharding import PartitionSpec as P

HEAD = 64
LEVELS = 64
LEN = 128
MB = 2


EPS = 1e-05
LOG_LOW = -2.995732273553991
LOG_SPAN = 2.995732273553991
EMB_VAR = 0.015625
MASKED = -1e30
LOSS_GAIN = 16.0


def passed_along(x, axis, by):
    count = lax.axis_size(axis)
    pairs = [(i, i + by) for i in range(count) if 0 <= i + by < count]
    return lax.ppermute(x, axis, pairs)


def product(left_side, right_side):
    return jnp.dot(left_side, right_side, preferred_element_type=jnp.float32)


def product_tn(left_side, right_side):
    return lax.dot_general(
        left_side, right_side, (((0,), (0,)), ((), ())), preferred_element_type=jnp.float32
    )


def product_nt(left_side, right_side):
    return lax.dot_general(
        left_side, right_side, (((1,), (1,)), ((), ())), preferred_element_type=jnp.float32
    )


def normed(inputs, gain_vec):
    center = inputs - jnp.mean(inputs, -1, keepdims=True)
    return center * lax.rsqrt(jnp.mean(center * center, -1, keepdims=True) + EPS) * gain_vec


def norm_back(inputs, gain_vec, upstream):
    output, pullback = jax.vjp(normed, inputs, gain_vec)
    return pullback(upstream)


def gelu_exact(values_in):
    return jax.nn.gelu(values_in, approximate=False)


def attn_scores(split_rows, key_valid):
    scores = (
        jnp.einsum(
            "qhd,khd->hqk", split_rows[:, 0], split_rows[:, 1], preferred_element_type=jnp.float32
        )
        * 0.125
    )
    return jnp.where(key_valid[None, None, :], scores, MASKED)


def attend(qkv_rows, key_valid):
    length = qkv_rows.shape[0]
    model_width = qkv_rows.shape[1] // 3
    split_rows = qkv_rows.reshape(length, 3, model_width // HEAD, HEAD)
    scores = attn_scores(split_rows, key_valid)
    row_max = jnp.max(scores, -1, keepdims=True)
    log_total = row_max + jnp.log(jnp.sum(jnp.exp(scores - row_max), -1, keepdims=True))
    probs_low = jnp.exp(scores - log_total).astype(jnp.bfloat16)
    mixed_rows = jnp.einsum(
        "hqk,khd->qhd", probs_low, split_rows[:, 2], preferred_element_type=jnp.float32
    )
    return (mixed_rows.reshape(length, model_width).astype(jnp.bfloat16), log_total)


def attend_back(qkv_rows, key_valid, log_total, grad_mixed):
    length = qkv_rows.shape[0]
    model_width = qkv_rows.shape[1] // 3
    head_count = model_width // HEAD
    split_rows = qkv_rows.reshape(length, 3, head_count, HEAD)
    grad_heads = grad_mixed.reshape(length, head_count, HEAD)
    probs_full = jnp.exp(attn_scores(split_rows, key_valid) - log_total)
    grad_values = jnp.einsum(
        "hqk,qhd->khd",
        probs_full.astype(jnp.bfloat16),
        grad_heads,
        preferred_element_type=jnp.float32,
    )
    grad_probs = jnp.einsum(
        "qhd,khd->hqk", grad_heads, split_rows[:, 2], preferred_element_type=jnp.float32
    )
    grad_scores = (
        probs_full * (grad_probs - jnp.sum(grad_probs * probs_full, -1, keepdims=True))
    ).astype(jnp.bfloat16)
    grad_query = (
        jnp.einsum(
            "hqk,khd->qhd", grad_scores, split_rows[:, 1], preferred_element_type=jnp.float32
        )
        * 0.125
    )
    grad_key = (
        jnp.einsum(
            "hqk,qhd->khd", grad_scores, split_rows[:, 0], preferred_element_type=jnp.float32
        )
        * 0.125
    )
    stacked = jnp.stack([grad_query, grad_key, grad_values], 1).reshape(length, 3 * model_width)
    return stacked.astype(jnp.bfloat16)


def layer_forward(hidden, key_valid, weights):
    gain_attn, qkv_weight, proj_weight, gain_mlp, up_weight, down_weight = weights
    normed_in = normed(hidden, gain_attn).astype(jnp.bfloat16)
    qkv_rows = product(normed_in, qkv_weight).astype(jnp.bfloat16)
    mixed_rows, log_total = attend(qkv_rows, key_valid)
    hidden_mid = hidden + product(mixed_rows, proj_weight)
    mlp_in = normed(hidden_mid, gain_mlp).astype(jnp.bfloat16)
    pre_act = product(mlp_in, up_weight)
    activated = gelu_exact(pre_act).astype(jnp.bfloat16)
    hidden_out = hidden_mid + product(activated, down_weight)
    return (
        hidden_out,
        (
            hidden,
            normed_in,
            qkv_rows,
            log_total,
            mixed_rows,
            hidden_mid,
            mlp_in,
            pre_act,
            activated,
        ),
    )


def empty_kept(length, model_width, hidden_units, head_count):
    return (
        jnp.zeros((length, model_width), jnp.float32),
        jnp.zeros((length, model_width), jnp.bfloat16),
        jnp.zeros((length, 3 * model_width), jnp.bfloat16),
        jnp.zeros((head_count, length, 1), jnp.float32),
        jnp.zeros((length, model_width), jnp.bfloat16),
        jnp.zeros((length, model_width), jnp.float32),
        jnp.zeros((length, model_width), jnp.bfloat16),
        jnp.zeros((length, hidden_units), jnp.float32),
        jnp.zeros((length, hidden_units), jnp.bfloat16),
    )


def layer_backward(kept_vals, grad_out, key_valid, weights):
    hidden, normed_in, qkv_rows, log_total, mixed_rows, hidden_mid, mlp_in, pre_act, activated = (
        kept_vals
    )
    gain_attn, qkv_weight, proj_weight, gain_mlp, up_weight, down_weight = weights
    grad_low = grad_out.astype(jnp.bfloat16)
    grad_activated = product_nt(grad_low, down_weight)
    grad_pre = jax.vjp(gelu_exact, pre_act)[1](grad_activated)[0].astype(jnp.bfloat16)
    grad_mlp_in = product_nt(grad_pre, up_weight)
    grad_mid_norm, grad_gain_mlp = norm_back(hidden_mid, gain_mlp, grad_mlp_in)
    grad_mid = grad_out + grad_mid_norm
    grad_mid_low = grad_mid.astype(jnp.bfloat16)
    grad_mixed = product_nt(grad_mid_low, proj_weight).astype(jnp.bfloat16)
    grad_qkv = attend_back(qkv_rows, key_valid, log_total, grad_mixed)
    grad_normed = product_nt(grad_qkv, qkv_weight)
    grad_in_norm, grad_gain_attn = norm_back(hidden, gain_attn, grad_normed)
    records = (activated, grad_low, mlp_in, grad_pre, mixed_rows, grad_mid_low, normed_in, grad_qkv)
    return (grad_mid + grad_in_norm, (grad_gain_attn, grad_gain_mlp), records)


def layer_zero(length, model_width, hidden_units):
    records = (
        jnp.zeros((length, hidden_units), jnp.bfloat16),
        jnp.zeros((length, model_width), jnp.bfloat16),
        jnp.zeros((length, model_width), jnp.bfloat16),
        jnp.zeros((length, hidden_units), jnp.bfloat16),
        jnp.zeros((length, model_width), jnp.bfloat16),
        jnp.zeros((length, model_width), jnp.bfloat16),
        jnp.zeros((length, model_width), jnp.bfloat16),
        jnp.zeros((length, 3 * model_width), jnp.bfloat16),
    )
    gains = (jnp.zeros((model_width,), jnp.float32), jnp.zeros((model_width,), jnp.float32))
    return (jnp.zeros((length, model_width), jnp.float32), gains, records)


def layer_grads(records):
    activated, grad_low, mlp_in, grad_pre, mixed_rows, grad_mid_low, normed_in, grad_qkv = records
    return (
        product_tn(normed_in, grad_qkv),
        product_tn(mixed_rows, grad_mid_low),
        product_tn(mlp_in, grad_pre),
        product_tn(activated, grad_low),
    )


def embed_inputs(token_ids, noise_block, level_id, table_full):
    noise_level = jnp.exp(LOG_LOW + level_id.astype(jnp.float32) * (LOG_SPAN / (LEVELS - 1)))
    scale_in = lax.rsqrt(EMB_VAR + noise_level * noise_level)
    looked = jnp.take(table_full, token_ids, axis=0).astype(jnp.float32)
    mixed_in = ((looked + noise_level * noise_block.astype(jnp.float32)) * scale_in).astype(
        jnp.bfloat16
    )
    return (mixed_in, scale_in)


def embed_backward(token_ids, noise_block, level_id, grad_start, table_full, in_weight):
    mixed_in, scale_in = embed_inputs(token_ids, noise_block, level_id, table_full)
    grad_low = grad_start.astype(jnp.bfloat16)
    grad_looked = product_nt(grad_low, in_weight) * scale_in
    return (mixed_in, grad_low, grad_looked)


def embed_zero(length, model_width, emb_width):
    return (
        jnp.zeros((length, emb_width), jnp.bfloat16),
        jnp.zeros((length, model_width), jnp.bfloat16),
        jnp.zeros((length, emb_width), jnp.float32),
    )


def tail_pass(hidden, token_ids, key_valid, final_gain, out_weight, table_full, loss_scale):
    final_in = normed(hidden, final_gain).astype(jnp.bfloat16)
    projected = product(final_in, out_weight).astype(jnp.bfloat16)
    logits = product_nt(projected, table_full)
    row_max = jnp.max(logits, -1, keepdims=True)
    log_total = row_max + jnp.log(jnp.sum(jnp.exp(logits - row_max), -1, keepdims=True))
    vocab_ids = lax.broadcasted_iota(jnp.int32, logits.shape, 1)
    target_hit = vocab_ids == token_ids[:, None]
    picked = jnp.sum(jnp.where(target_hit, logits, 0.0), -1)
    entropy = jnp.where(key_valid, log_total[:, 0] - picked, 0.0)
    row_scale = jnp.where(key_valid, loss_scale, 0.0)[:, None]
    grad_logits = (
        (jnp.exp(logits - log_total) - target_hit.astype(jnp.float32)) * row_scale
    ).astype(jnp.bfloat16)
    grad_proj = product(grad_logits, table_full).astype(jnp.bfloat16)
    grad_final = product_nt(grad_proj, out_weight)
    grad_hidden, grad_gain = norm_back(hidden, final_gain, grad_final)
    return (grad_hidden, entropy, grad_gain, (grad_logits, projected, final_in, grad_proj))


def tail_zero(length, model_width, emb_width, vocab_rows):
    records = (
        jnp.zeros((length, vocab_rows), jnp.bfloat16),
        jnp.zeros((length, emb_width), jnp.bfloat16),
        jnp.zeros((length, model_width), jnp.bfloat16),
        jnp.zeros((length, emb_width), jnp.bfloat16),
    )
    return (
        jnp.zeros((length, model_width), jnp.float32),
        jnp.zeros((length,), jnp.float32),
        jnp.zeros((model_width,), jnp.float32),
        records,
    )


def edge_grads(tail_records, embed_records, token_ids):
    grad_logits, projected, final_in, grad_proj = tail_records
    mixed_in, grad_low, grad_looked = embed_records
    table_grad = product_tn(grad_logits, projected).at[token_ids].add(grad_looked)
    return (table_grad, product_tn(mixed_in, grad_low), product_tn(final_in, grad_proj))


def joined_rows(record_list):
    return jax.tree.map(lambda *pieces: jnp.concatenate(pieces, 0), *record_list)


def assemble(gain_attn_sum, gain_mlp_sum, layer_set, edge_set, gain_final_sum):
    return (
        gain_attn_sum[None],
        layer_set[0][None],
        layer_set[1][None],
        gain_mlp_sum[None],
        layer_set[2][None],
        layer_set[3][None],
        edge_set[0],
        edge_set[1],
        gain_final_sum,
        edge_set[2],
    )


def per_device(
    tokens,
    lengths,
    levels,
    noise_rows,
    embed_table,
    w_in,
    ln_attn,
    w_qkv,
    w_proj,
    ln_mlp,
    w_up,
    w_down,
    ln_final,
    w_out,
):
    gathered = (
        lax.all_gather(embed_table, "dp", axis=0, tiled=True),
        lax.all_gather(w_in, "dp", axis=0, tiled=True),
        lax.all_gather(ln_attn, "dp", axis=1, tiled=True),
        lax.all_gather(w_qkv, "dp", axis=1, tiled=True),
        lax.all_gather(w_proj, "dp", axis=1, tiled=True),
        lax.all_gather(ln_mlp, "dp", axis=1, tiled=True),
        lax.all_gather(w_up, "dp", axis=1, tiled=True),
        lax.all_gather(w_down, "dp", axis=1, tiled=True),
        lax.all_gather(ln_final, "dp", axis=0, tiled=True),
        lax.all_gather(w_out, "dp", axis=0, tiled=True),
    )
    table_full = gathered[0]
    in_weight = gathered[1]
    layer_weights = (
        gathered[2][0].astype(jnp.float32),
        gathered[3][0],
        gathered[4][0],
        gathered[5][0].astype(jnp.float32),
        gathered[6][0],
        gathered[7][0],
    )
    final_gain = gathered[8].astype(jnp.float32)
    out_weight = gathered[9]
    model_width = out_weight.shape[0]
    emb_width = out_weight.shape[1]
    vocab_rows = table_full.shape[0]
    hidden_units = layer_weights[4].shape[1]
    head_count = model_width // HEAD
    section_index = lax.axis_index("section")
    first_section = section_index == 0
    token_grid = tokens.reshape(MB, LEN)
    noise_grid = noise_rows.reshape(MB, LEN, noise_rows.shape[1])
    positions = jnp.arange(LEN, dtype=jnp.int32)
    valid_grid = positions[None, :] < lengths[:, None]
    loss_scale = LOSS_GAIN / math.sqrt(tokens.shape[0] * lax.axis_size(("group", "dp")))
    gain_attn_sum = jnp.zeros((model_width,), jnp.float32)
    gain_mlp_sum = jnp.zeros((model_width,), jnp.float32)
    gain_final_sum = jnp.zeros((model_width,), jnp.float32)
    recv_act = jnp.zeros((LEN, model_width), jnp.bfloat16)
    recv_grad = jnp.zeros((LEN, model_width), jnp.bfloat16)
    zero_rows = jnp.zeros((LEN, model_width), jnp.float32)
    kept_ticks = {}
    layer_recs = {}
    tail_recs = {}
    embed_recs = {}
    losses = []
    for moment in range(MB + 2):
        offset = moment - section_index
        fwd_valid = (offset >= 0) & (offset < MB)
        fwd_index = jnp.clip(offset, 0, MB - 1)
        ids_now = lax.dynamic_index_in_dim(token_grid, fwd_index, 0, False)
        noise_now = lax.dynamic_index_in_dim(noise_grid, fwd_index, 0, False)
        level_now = lax.dynamic_index_in_dim(levels, fwd_index, 0, False)
        valid_now = lax.dynamic_index_in_dim(valid_grid, fwd_index, 0, False)

        def first_input():
            mixed_in, scale_in = embed_inputs(ids_now, noise_now, level_now, table_full)
            return product(mixed_in, in_weight)

        layer_input = lax.cond(first_section, first_input, lambda: recv_act.astype(jnp.float32))
        hidden_out, kept_now = lax.cond(
            fwd_valid,
            lambda: layer_forward(layer_input, valid_now, layer_weights),
            lambda: (zero_rows, empty_kept(LEN, model_width, hidden_units, head_count)),
        )
        kept_ticks[moment] = kept_now
        tail_live = jnp.logical_not(first_section) & fwd_valid
        tail_grad, entropy, final_step, tail_now = lax.cond(
            tail_live,
            lambda: tail_pass(
                hidden_out, ids_now, valid_now, final_gain, out_weight, table_full, loss_scale
            ),
            lambda: tail_zero(LEN, model_width, emb_width, vocab_rows),
        )
        tail_recs[moment] = tail_now
        gain_final_sum = gain_final_sum + final_step
        back_tick = moment - 2
        late_live = 0 <= back_tick < MB
        late_index = min(max(back_tick, 0), MB - 1)
        kept_late = kept_ticks[back_tick] if back_tick >= 0 else kept_now
        kept_back = lax.cond(first_section, lambda: kept_late, lambda: kept_now)
        grad_top = jnp.where(first_section, recv_grad.astype(jnp.float32), tail_grad)
        valid_back = jnp.where(first_section, valid_grid[late_index], valid_now)
        back_live = jnp.where(first_section, late_live, fwd_valid)
        grad_start, gain_pair, layer_now = lax.cond(
            back_live,
            lambda: layer_backward(kept_back, grad_top, valid_back, layer_weights),
            lambda: layer_zero(LEN, model_width, hidden_units),
        )
        layer_recs[moment] = layer_now
        gain_attn_sum = gain_attn_sum + gain_pair[0]
        gain_mlp_sum = gain_mlp_sum + gain_pair[1]
        if late_live:
            embed_now = lax.cond(
                first_section,
                lambda: embed_backward(
                    token_grid[late_index],
                    noise_grid[late_index],
                    levels[late_index],
                    grad_start,
                    table_full,
                    in_weight,
                ),
                lambda: embed_zero(LEN, model_width, emb_width),
            )
        else:
            embed_now = embed_zero(LEN, model_width, emb_width)
        embed_recs[moment] = embed_now
        if moment < MB:
            recv_act = passed_along(hidden_out.astype(jnp.bfloat16), "section", 1)
        if 1 <= moment <= MB:
            entropy_low = entropy.astype(jnp.bfloat16)
            recv_grad, loss_back = passed_along(
                (grad_start.astype(jnp.bfloat16), entropy_low), "section", -1
            )
            losses.append(jnp.where(first_section, loss_back, entropy_low))
    chosen = [
        jax.tree.map(
            lambda early, late: jnp.where(first_section, early, late),
            layer_recs[micro + 2],
            layer_recs[micro + 1],
        )
        for micro in range(MB)
    ]
    all_layer = layer_grads(joined_rows(chosen))
    all_tail = joined_rows([tail_recs[micro + 1] for micro in range(MB)])
    all_embed = joined_rows([embed_recs[micro + 2] for micro in range(MB)])
    all_edge = edge_grads(all_tail, all_embed, tokens)
    grad_pack = assemble(gain_attn_sum, gain_mlp_sum, all_layer, all_edge, gain_final_sum)
    parted = (
        lax.psum_scatter(
            grad_pack[0].astype(jnp.bfloat16), "dp", scatter_dimension=1, tiled=True
        ).astype(jnp.float32),
        lax.psum_scatter(
            grad_pack[1].astype(jnp.bfloat16), "dp", scatter_dimension=1, tiled=True
        ).astype(jnp.float32),
        lax.psum_scatter(
            grad_pack[2].astype(jnp.bfloat16), "dp", scatter_dimension=1, tiled=True
        ).astype(jnp.float32),
        lax.psum_scatter(
            grad_pack[3].astype(jnp.bfloat16), "dp", scatter_dimension=1, tiled=True
        ).astype(jnp.float32),
        lax.psum_scatter(
            grad_pack[4].astype(jnp.bfloat16), "dp", scatter_dimension=1, tiled=True
        ).astype(jnp.float32),
        lax.psum_scatter(
            grad_pack[5].astype(jnp.bfloat16), "dp", scatter_dimension=1, tiled=True
        ).astype(jnp.float32),
        lax.psum_scatter(
            grad_pack[6].astype(jnp.bfloat16), "dp", scatter_dimension=0, tiled=True
        ).astype(jnp.float32),
        lax.psum_scatter(
            grad_pack[7].astype(jnp.bfloat16), "dp", scatter_dimension=0, tiled=True
        ).astype(jnp.float32),
        lax.psum_scatter(
            grad_pack[8].astype(jnp.bfloat16), "dp", scatter_dimension=0, tiled=True
        ).astype(jnp.float32),
        lax.psum_scatter(
            grad_pack[9].astype(jnp.bfloat16), "dp", scatter_dimension=0, tiled=True
        ).astype(jnp.float32),
    )
    layer_total = (
        lax.psum(parted[0].astype(jnp.bfloat16), "group").astype(jnp.float32),
        lax.psum(parted[1].astype(jnp.bfloat16), "group").astype(jnp.float32),
        lax.psum(parted[2].astype(jnp.bfloat16), "group").astype(jnp.float32),
        lax.psum(parted[3].astype(jnp.bfloat16), "group").astype(jnp.float32),
        lax.psum(parted[4].astype(jnp.bfloat16), "group").astype(jnp.float32),
        lax.psum(parted[5].astype(jnp.bfloat16), "group").astype(jnp.float32),
    )
    edge_total = (
        lax.psum(parted[6].astype(jnp.bfloat16), ("section", "group")).astype(jnp.float32),
        lax.psum(parted[7].astype(jnp.bfloat16), ("section", "group")).astype(jnp.float32),
        lax.psum(parted[8].astype(jnp.bfloat16), ("section", "group")).astype(jnp.float32),
        lax.psum(parted[9].astype(jnp.bfloat16), ("section", "group")).astype(jnp.float32),
    )
    token_loss = jnp.concatenate(losses)
    return (
        token_loss,
        edge_total[0],
        edge_total[1],
        layer_total[0],
        layer_total[1],
        layer_total[2],
        layer_total[3],
        layer_total[4],
        layer_total[5],
        edge_total[2],
        edge_total[3],
    )


def solution(mesh):
    placed = (
        P(("group", "dp")),
        P(("group", "dp")),
        P(("group", "dp")),
        P(("group", "dp"), None),
        P("dp", None),
        P("dp", None),
        P("section", "dp"),
        P("section", "dp", None),
        P("section", "dp", None),
        P("section", "dp"),
        P("section", "dp", None),
        P("section", "dp", None),
        P("dp"),
        P("dp", None),
    )
    return jax.shard_map(
        per_device,
        mesh=mesh,
        in_specs=placed,
        out_specs=(
            P(("group", "dp")),
            P("dp", None),
            P("dp", None),
            P("section", "dp"),
            P("section", "dp", None),
            P("section", "dp", None),
            P("section", "dp"),
            P("section", "dp", None),
            P("section", "dp", None),
            P("dp"),
            P("dp", None),
        ),
        check_vma=False,
    )
```

profile of v0, /device:TPU:0, one launch (start us, length us, event | category | flops | bytes accessed | tf_op | source)
XLA Modules:
  0.0 1910.5 jit_solution(9120408552318256409)
XLA Ops:
  10.7 12.6 all_gather.32
  23.3 7.7 all_gather.35
  31.7 26.6 %all_gather.31 = bf16[256,1024]{1,0:T(8,128)(2,1)} all-gather(bf16[64,1024]{1,0:T(8,128)(2,1)S(1)} %copy-done.63), channel_id=1, replica_groups=mesh['section'=2,'group'=4,'dp'=4] {'dp'}, dimensions={0}, use_global_device_ids=true | all-gather | bytes 655360 | tf_op jit(solution)/shard_map/all_gather | solution.py:306
  59.5 110.8 %all-gather.7.cloned.1.call-done = bf16[16384,256]{1,0:T(8,128)(2,1)} async-done(((bf16[4096,256]{1,0:T(8,128)(2,1)}), bf16[16384,256]{1,0:T(8,128)(2,1)}) %all-gather.7.cloned.1.call-update) | async-done | bytes 8388624 | tf_op jit(solution)/shard_map/all_gather | solution.py:305
  170.3 9.1 conditional.20
  172.9 5.2 gather_fusion
  179.5 36.7 %all-gather.11.cloned.1.call-done = bf16[1,1024,1024]{2,1,0:T(8,128)(2,1)} async-done(((bf16[1,256,1024]{2,1,0:T(8,128)(2,1)}), bf16[1,1024,1024]{2,1,0:T(8,128)(2,1)}) %all-gather.11.cloned.1.call-update) | async-done | bytes 2097168 | tf_op jit(solution)/shard_map/all_gather | solution.py:309
  216.1 115.7 %all-gather.9.cloned.1.call-done = bf16[1,1024,3072]{2,1,0:T(8,128)(2,1)} async-done(((bf16[1,256,3072]{2,1,0:T(8,128)(2,1)}), bf16[1,1024,3072]{2,1,0:T(8,128)(2,1)}) %all-gather.9.cloned.1.call-update) | async-done | bytes 6291472 | tf_op jit(solution)/shard_map/all_gather | solution.py:308
  331.8 149.3 %all-gather.13.cloned.1.call-done = bf16[1,1024,4096]{2,1,0:T(8,128)(2,1)} async-done(((bf16[1,256,4096]{2,1,0:T(8,128)(2,1)}), bf16[1,1024,4096]{2,1,0:T(8,128)(2,1)}) %all-gather.13.cloned.1.call-update) | async-done | bytes 8388624 | tf_op jit(solution)/shard_map/all_gather | solution.py:311
  481.1 149.3 %all-gather.15.cloned.1.call-done = bf16[1,4096,1024]{2,1,0:T(8,128)(2,1)} async-done(((bf16[1,1024,1024]{2,1,0:T(8,128)(2,1)}), bf16[1,4096,1024]{2,1,0:T(8,128)(2,1)}) %all-gather.15.cloned.1.call-update) | async-done | bytes 8388624 | tf_op jit(solution)/shard_map/all_gather | solution.py:312
  630.5 28.0 %conditional.21 = (f32[128,1024]{1,0:T(8,128)S(1)}, f32[128,1024]{1,0:T(8,128)S(1)}, bf16[128,1024]{1,0:T(8,128)(2,1)}, bf16[128,3072]{1,0:T(8,128)(2,1)}, f32[1...) conditional(s32[]{:T(128)} %convert_element_type.572, ...), branch_computations={%region_2.4_spmd, %region_3.0_spmd} | conditional | flops 3327129856 | bytes 77702520 | solution.py:365
  631.0 4.8 convolution_convert_fusion
  646.6 9.1 fusion.2
  662.0 8.7 conditional.22
  664.0 5.2 gather_fusion.1
  670.7 29.4 %conditional.23 = (f32[128,1024]{1,0:T(8,128)}, f32[128,1024]{1,0:T(8,128)S(1)}, bf16[128,1024]{1,0:T(8,128)(2,1)S(1)}, bf16[128,3072]{1,0:T(8,128)(2,1)}, f32[1...) conditional(s32[]{:T(128)} %convert_element_type.570, ...), branch_computations={%region_12.14_spmd, %region_13.0_spmd} | conditional | flops 3327129856 | bytes 69313880 | solution.py:365
  671.3 4.8 convolution_convert_fusion.2
  687.4 9.1 fusion.14
  696.6 3.6 convolution_add_fusion.3
  704.5 7.9 all-gather
  712.4 15.7 all_gather.39
  728.1 6.0 conditional.24
  734.1 12.6 conditional.25
  738.7 6.0 gather_fusion.2
  746.8 9.2 conditional.26
  756.0 5.9 conditional.27
  765.1 8.3 conditional.28
  774.8 15.4 conditional.29
  786.7 3.1 copy.306
  790.2 71.8 %collective-permute-done.4 = bf16[128,1024]{1,0:T(8,128)(2,1)S(1)} collective-permute-done((bf16[128,1024]{1,0:T(8,128)(2,1)}, bf16[128,1024]{1,0:T(8,128)(2,1)S(1)}, u32[]{:S(2)}, u32[]{:S(2)}) %collective-permute-start.4) | collective-permute-done | bytes 262176 | tf_op jit(solution)/shard_map/ppermute | solution.py:25
  862.0 42.2 %conditional.30 = (bf16[128,1024]{1,0:T(8,128)(2,1)}, f32[1024]{0:T(1024)}, f32[1024]{0:T(1024)S(1)}, bf16[128,4096]{1,0:T(8,128)(2,1)}, bf16[128,1024]{1,0:T(8,...) conditional(s32[]{:T(128)} %convert_element_type.582, ...), branch_computations={%region_65.67_spmd, %region_66.79_spmd} | conditional | flops 3436705536 | bytes 129978432 | solution.py:389
  871.8 9.8 fusion.67
  881.7 4.4 multiply_reduce_fusion.20
  899.0 4.1 multiply_reduce_fusion.21
  905.6 11.3 conditional.32
  909.6 5.8 gather_fusion.4
  916.9 13.1 conditional.31
  919.4 6.0 gather_fusion.3
  930.7 8.2 conditional.33
  938.9 14.9 conditional.35
  955.7 39.5 %conditional.36 = (bf16[128,1024]{1,0:T(8,128)(2,1)}, f32[1024]{0:T(1024)}, f32[1024]{0:T(1024)}, bf16[128,4096]{1,0:T(8,128)(2,1)}, bf16[128,1024]{1,0:T(8,128)...) conditional(s32[]{:T(128)} %convert_element_type.586, ...), branch_computations={%region_101.103_spmd, %region_102.115_spmd} | conditional | flops 3436705536 | bytes 127877040 | solution.py:389
  964.4 10.7 fusion.118
  975.1 5.0 multiply_reduce_fusion.32
  990.0 4.1 multiply_reduce_fusion.33
  995.2 10.7 conditional.37
  998.3 5.2 gather_fusion.5
  1008.8 11.6 fusion.300
  1020.5 13.7 scatter_custom_fusion
  1034.2 8.9 convert_element_type.591
  1050.3 4.5 convert_bitcast_fusion.2
  1059.9 5.6 convert_bitcast_fusion
  1066.5 5.6 convert_bitcast_fusion.1
  1079.8 107.7 %reduce-scatter.14.cloned.1.call-done = bf16[4096,256]{1,0:T(8,128)(2,1)} async-done(((bf16[16384,256]{1,0:T(8,128)(2,1)}), bf16[4096,256]{1,0:T(8,128)(2,1)}) %reduce-scatter.14.cloned.1.call-update) | async-done | bytes 2097168 | tf_op jit(solution)/shard_map/reduce_scatter | solution.py:453
  1187.6 47.4 %reduce-scatter.20.cloned.1.call-done = bf16[1,256,1024]{2,1,0:T(8,128)(2,1)} async-done(((bf16[1,1024,1024]{2,1,0:T(8,128)(2,1)}), bf16[1,256,1024]{2,1,0:T(8,128)(2,1)}) %reduce-scatter.20.cloned.1.call-update) | async-done | bytes 524304 | tf_op jit(solution)/shard_map/reduce_scatter | solution.py:441
  1235.0 112.4 %reduce-scatter.18.cloned.1.call-done = bf16[1,256,3072]{2,1,0:T(8,128)(2,1)} async-done(((bf16[1,1024,3072]{2,1,0:T(8,128)(2,1)}), bf16[1,256,3072]{2,1,0:T(8,128)(2,1)}) %reduce-scatter.18.cloned.1.call-update) | async-done | bytes 1572880 | tf_op jit(solution)/shard_map/reduce_scatter | solution.py:438
  1347.4 147.5 %reduce-scatter.24.cloned.1.call-done = bf16[1,1024,1024]{2,1,0:T(8,128)(2,1)} async-done(((bf16[1,4096,1024]{2,1,0:T(8,128)(2,1)}), bf16[1,1024,1024]{2,1,0:T(8,128)(2,1)}) %reduce-scatter.24.cloned.1.call-update) | async-done | bytes 2097168 | tf_op jit(solution)/shard_map/reduce_scatter | solution.py:450
  1494.9 147.6 %reduce-scatter.22.cloned.1.call-done = bf16[1,256,4096]{2,1,0:T(8,128)(2,1)} async-done(((bf16[1,1024,4096]{2,1,0:T(8,128)(2,1)}), bf16[1,256,4096]{2,1,0:T(8,128)(2,1)}) %reduce-scatter.22.cloned.1.call-update) | async-done | bytes 2097168 | tf_op jit(solution)/shard_map/reduce_scatter | solution.py:447
  1647.4 11.2 all-reduce
  1658.7 14.5 psum.78
  1675.2 11.2 reduce-scatter.30.cloned.1.call-done
  1687.3 10.0 all-reduce.2
  1698.4 53.2 %all-reduce.7.cloned.1.call-done = (bf16[4096,256]{1,0:T(8,128)(2,1)}, bf16[64,1024]{1,0:T(8,128)(2,1)}, bf16[256,256]{1,0:T(8,128)(2,1)}) async-done(((bf16[4096,256]{1,0:T(8,128)(2,1)}, bf16[64,1024]{1,0:T(8,128)(2,1)}, bf16[256,256]{1,0:T(8,128)(2,1)}), (bf16[4096,256]{1,0:T(8,128)(2,1)}, bf16[64,1024]{1,0:T(8,128)(2,1)}, bf16[256,256]{1,0:T(8,128)(2,1)})) %all-reduce.7.cloned.1.call-update) | async-done | bytes 2359312 | tf_op jit(solution)/shard_map/psum | solution.py:475
  1754.9 3.9 convert_element_type.592
  1758.8 135.4 %all-reduce.9.cloned.1.call-done = (bf16[1,256,3072]{2,1,0:T(8,128)(2,1)}, bf16[1,256,1024]{2,1,0:T(8,128)(2,1)}, bf16[1,256,4096]{2,1,0:T(8,128)(2,1)}, bf16[1,1024,1024]{2,1,0:T(8,128)(2,1)}) async-done(((bf16[1,256,3072]{2,1,0:T(8,128)(2,1)}, bf16[1,256,1024]{2,1,0:T(8,128)(2,1)}, bf16[1,256,4096]{2,1,0:T(8,128)(2,1)}, bf16[1,1024,1024]{2,1,0:T(8,128)(2,1)}), (bf16[1,256,3072]{2,1,0:T(8,128)(2,1)}, ...) | async-done | bytes 6291472 | tf_op jit(solution)/shard_map/psum | solution.py:468
  (479 shorter events, 227.5 us)
Async XLA Ops:
  7.2 163.1 %all-gather.7.cloned.1.call-start = ((), (), s32[]{:S(2)}) async-start(), calls=%async_computation.9 | async-start | bytes 10485760 | tf_op jit(solution)/shard_map/all_gather | solution.py:305
  7.9 208.2 %all-gather.11.cloned.1.call-start = ((), (), s32[]{:S(2)}) async-start(), calls=%async_computation.11 | async-start | bytes 2621440 | tf_op jit(solution)/shard_map/all_gather | solution.py:309
  8.7 323.2 %all-gather.9.cloned.1.call-start = ((), (), s32[]{:S(2)}) async-start(), calls=%async_computation.10 | async-start | bytes 7864320 | tf_op jit(solution)/shard_map/all_gather | solution.py:308
  9.4 13.9 copy-start.113
  9.4 21.6 %copy-start.80 = (s32[256]{0:T(256)S(1)}, s32[256]{0:T(256)}, u32[]{:S(2)}) copy-start(s32[256]{0:T(256)} %param.56) | copy-start | bytes 3076
  9.4 22.2 %copy-start.63 = (bf16[64,1024]{1,0:T(8,128)(2,1)S(1)}, bf16[64,1024]{1,0:T(8,128)(2,1)}, u32[]{:S(2)}) copy-start(bf16[64,1024]{1,0:T(8,128)(2,1)} %param.61) | copy-start | bytes 393220
  9.4 48.9 %copy-start.128 = (s32[2]{0:T(128)S(1)}, s32[2]{0:T(128)}, u32[]{:S(2)}) copy-start(s32[2]{0:T(128)} %param.57) | copy-start | bytes 28
  9.4 160.9 %copy-start.46 = (bf16[256,256]{1,0:T(8,128)(2,1)S(1)}, bf16[256,256]{1,0:T(8,128)(2,1)}, u32[]{:S(2)}) copy-start(bf16[256,256]{1,0:T(8,128)(2,1)} %param.59) | copy-start | bytes 393220
  9.5 160.9 %copy-start.129 = (s32[2]{0:T(128)S(1)}, s32[2]{0:T(128)}, u32[]{:S(2)}) copy-start(s32[2]{0:T(128)} %param.58) | copy-start | bytes 28
  9.5 471.7 %all-gather.13.cloned.1.call-start = ((), (), s32[]{:S(2)}) async-start(), calls=%async_computation.12 | async-start | bytes 10485760 | tf_op jit(solution)/shard_map/all_gather | solution.py:311
  10.0 620.4 %all-gather.15.cloned.1.call-start = ((), (), s32[]{:S(2)}) async-start(), calls=%async_computation.13 | async-start | bytes 10485760 | tf_op jit(solution)/shard_map/all_gather | solution.py:312
  10.6 1069.2 %reduce-scatter.26.cloned.1.call-start = ((), (), s32[]{:S(2)}) async-start(), calls=%async_computation.20 | async-start | bytes 655360 | tf_op jit(solution)/shard_map/reduce_scatter | solution.py:462
  31.7 630.3 %copy-start.90 = (s32[128]{0:T(128)}, s32[128]{0:T(128)S(1)}, u32[]{:S(2)}) copy-start(s32[128]{0:T(128)S(1)} %get-tuple-element.1613) | copy-start | bytes 1540
  59.5 571.0 %copy-start.92 = (pred[128]{0:T(512)(128)(4,1)}, pred[128]{0:T(512)(128)(4,1)S(1)}, u32[]{:S(2)}) copy-start(pred[128]{0:T(512)(128)(4,1)S(1)} %get-tuple-element.1619) | copy-start | bytes 388
  644.0 11.7 slice-start.12
  646.6 9.1 copy-start.47
  646.6 9.1 slice-start.13
  658.4 116.3 %copy-start.9 = (f32[128,1024]{1,0:T(8,128)}, f32[128,1024]{1,0:T(8,128)S(1)}, u32[]{:S(2)}) copy-start(f32[128,1024]{1,0:T(8,128)S(1)} %get-tuple-element.907) | copy-start | bytes 1572868
  658.4 12.3 copy-start
  658.5 12.3 copy-start.99
  659.2 2.8 collective-permute-start
  684.1 12.4 slice-start.14
  687.4 9.1 slice-start.15
  701.9 32.2 %collective-permute-start.2 = (bf16[128,1024]{1,0:T(8,128)(2,1)}, bf16[128,1024]{1,0:T(8,128)(2,1)}, u32[]{:S(2)}, u32[]{:S(2)}) collective-permute-start(bf16[128,1024]{1,0:T(8,128)(2,1)} %convert_element_type.581), channel_id=1, source_target_pairs={{0,16},{1,17},{2,18},{3,19},{4,20},{5,21},{6,22},{7,23},{8,24},{9,... | collective-permute-start | bytes 786440 | tf_op jit(solution)/shard_map/ppermute | solution.py:25
  734.1 12.7 copy-start.74
  746.8 9.2 copy-start.89
  764.1 315.8 %reduce-scatter.16.cloned.1.call-start = ((), (), s32[]{:S(2)}) async-start(), calls=%async_computation.15 | async-start | bytes 655360 | tf_op jit(solution)/shard_map/reduce_scatter | solution.py:456
  773.4 88.5 %collective-permute-start.4 = (bf16[128,1024]{1,0:T(8,128)(2,1)}, bf16[128,1024]{1,0:T(8,128)(2,1)S(1)}, u32[]{:S(2)}, u32[]{:S(2)}) collective-permute-start(bf16[128,1024]{1,0:T(8,128)(2,1)} %get-tuple-element.896), channel_id=1, source_target_pairs={{16,0},{17,1},{18,2},{19,3},{20,4},{21,5},{22,6},{23,7},{24,8},{25... | collective-permute-start | bytes 786440 | tf_op jit(solution)/shard_map/ppermute | solution.py:25
  774.7 87.3 %copy-start.81 = (pred[128]{0:T(512)(128)(4,1)S(1)}, pred[128]{0:T(512)(128)(4,1)}, u32[]{:S(2)}) copy-start(pred[128]{0:T(512)(128)(4,1)} %get-tuple-element.1616) | copy-start | bytes 388
  774.7 87.3 %copy-start.96 = (pred[128]{0:T(512)(128)(4,1)S(1)}, pred[128]{0:T(512)(128)(4,1)}, u32[]{:S(2)}) copy-start(pred[128]{0:T(512)(128)(4,1)} %get-tuple-element.1617) | copy-start | bytes 388
  774.8 4.9 copy-start.48
  790.2 71.8 %copy-start.55 = (bf16[128,1024]{1,0:T(8,128)(2,1)}, bf16[128,1024]{1,0:T(8,128)(2,1)S(1)}, u32[]{:S(2)}) copy-start(bf16[128,1024]{1,0:T(8,128)(2,1)S(1)} %get-tuple-element.923) | copy-start | bytes 786436
  863.7 7.4 copy-start.85
  869.8 11.8 slice-start.22
  871.1 16.5 copy-start.28
  871.8 9.8 slice-start.23
  881.6 7.4 copy-start.18
  887.6 5.9 copy-start.24
  889.0 9.7 slice-start.2
  904.3 12.6 copy-start.70
  904.3 50.4 %collective-permute-start.5 = (bf16[128,1024]{1,0:T(8,128)(2,1)}, bf16[128,1024]{1,0:T(8,128)(2,1)}, u32[]{:S(2)}, u32[]{:S(2)}) collective-permute-start(bf16[128,1024]{1,0:T(8,128)(2,1)} %get-tuple-element.925), channel_id=1, source_target_pairs={{16,0},{17,1},{18,2},{19,3},{20,4},{21,5},{22,6},{23,7},{24,8},{25... | collective-permute-start | bytes 786440 | tf_op jit(solution)/shard_map/ppermute | solution.py:25
  905.6 11.3 copy-start.1
  955.7 8.6 copy-start.7
  962.4 12.7 slice-start.24
  964.4 17.2 copy-start.30
  964.4 10.7 slice-start.25
  983.0 7.0 slice-start.4
  995.2 10.7 copy-start.62
  995.2 13.6 copy-start.58
  995.2 13.6 copy-start.60
  1008.1 179.4 %reduce-scatter.14.cloned.1.call-start = ((), (), s32[]{:S(2)}) async-start(), calls=%async_computation.14 | async-start | bytes 10485760 | tf_op jit(solution)/shard_map/reduce_scatter | solution.py:453
  1043.1 191.9 %reduce-scatter.20.cloned.1.call-start = ((), (), s32[]{:S(2)}) async-start(), calls=%async_computation.17 | async-start | bytes 2621440 | tf_op jit(solution)/shard_map/reduce_scatter | solution.py:441
  1047.2 300.2 %reduce-scatter.18.cloned.1.call-start = ((), (), s32[]{:S(2)}) async-start(), calls=%async_computation.16 | async-start | bytes 7864320 | tf_op jit(solution)/shard_map/reduce_scatter | solution.py:438
  1054.8 440.0 %reduce-scatter.24.cloned.1.call-start = ((), (), s32[]{:S(2)}) async-start(), calls=%async_computation.19 | async-start | bytes 10485760 | tf_op jit(solution)/shard_map/reduce_scatter | solution.py:450
  1065.5 576.9 %reduce-scatter.22.cloned.1.call-start = ((), (), s32[]{:S(2)}) async-start(), calls=%async_computation.18 | async-start | bytes 10485760 | tf_op jit(solution)/shard_map/reduce_scatter | solution.py:447
  1072.1 602.2 %reduce-scatter.28.cloned.1.call-start = ((), (), s32[]{:S(2)}) async-start(), calls=%async_computation.21 | async-start | bytes 327680
  1078.0 608.4 %reduce-scatter.30.cloned.1.call-start = ((), (), s32[]{:S(2)}) async-start(), calls=%async_computation.22 | async-start | bytes 327680
  1079.7 671.9 %all-reduce.7.cloned.1.call-start = ((), (), s32[]{:S(2)}) async-start(), calls=%async_computation.23 | async-start | bytes 4718592 | tf_op jit(solution)/shard_map/psum | solution.py:475
  1187.5 706.7 %all-reduce.9.cloned.1.call-start = ((), (), s32[]{:S(2)}) async-start(), calls=%async_computation.24 | async-start | bytes 12582912 | tf_op jit(solution)/shard_map/psum | solution.py:468
  1642.4 5.0 copy-start.75
  1642.4 5.0 copy-start.77
  1642.4 5.0 copy-start.79
  1643.1 3.0 collective-permute-start.1
  1646.1 27.7 %collective-permute-start.3 = (bf16[128]{0:T(256)(128)(2,1)S(1)}, bf16[128]{0:T(256)(128)(2,1)S(1)}, u32[]{:S(2)}, u32[]{:S(2)}) collective-permute-start(bf16[128]{0:T(256)(128)(2,1)S(1)} %copy-done.127), channel_id=1, source_target_pairs={{16,0},{17,1},{18,2},{19,3},{20,4},{21,5},{22,6},{23,7},{24,8},{25... | collective-permute-start | bytes 776 | tf_op jit(solution)/shard_map/ppermute | solution.py:25
  (57 other events, 133.7 us)
Sparse Core Ops, SparseCore 0:
  9.6 160.6 all-gather.6
  171.9 44.2 all-gather.10
  217.7 114.0 all-gather.8
  333.2 147.8 all-gather.12
  482.6 147.8 all-gather.14
  764.2 62.0 reduce-scatter.25
  1008.2 21.4 reduce-scatter.15
  1043.2 144.2 reduce-scatter.13
  1190.4 44.5 reduce-scatter.19
  1237.3 110.0 reduce-scatter.17
  1349.9 144.9 reduce-scatter.23
  1497.2 145.1 reduce-scatter.21
  1645.3 20.3 reduce-scatter.27
  1668.4 17.9 reduce-scatter.29
  1690.2 61.4 all-reduce.6
  1755.3 138.9 all-reduce.8
where the time goes:
time: 1920 us; the launch traced here: 1910 us
  waiting for transfers between devices  1400 us (73%)
  local copies, waits for them, and re-layouts  138 us (7%)
  matrix products  138 us (7%)
  blocking collectives  106 us (6%)
  other arithmetic  93.2 us (5%)
    all_gather x1, waiting for transfers between devices, per_device(): lax.all_gather(w_up, 'dp', axis=1, tiled=True)  149 us
    all_gather x1, waiting for transfers between devices, per_device(): lax.all_gather(w_down, 'dp', axis=1, tiled=True)  149 us
    reduce_scatter x1, waiting for transfers between devices, per_device(): lax.psum_scatter(grad_pack[4].astype(jnp.bfloat16), 'dp', scatter_dimensi...  148 us
    reduce_scatter x1, waiting for transfers between devices, per_device(): lax.psum_scatter(grad_pack[5].astype(jnp.bfloat16), 'dp', scatter_dimensi...  147 us
    psum x1, waiting for transfers between devices, per_device(): lax.psum(parted[1].astype(jnp.bfloat16), 'group').astype(jnp.float32)  135 us
    all_gather x1, waiting for transfers between devices, per_device(): lax.all_gather(w_qkv, 'dp', axis=1, tiled=True)  116 us
    reduce_scatter x1, waiting for transfers between devices, per_device(): lax.psum_scatter(grad_pack[1].astype(jnp.bfloat16), 'dp', scatter_dimensi...  112 us
    all_gather x1, waiting for transfers between devices, per_device(): lax.all_gather(embed_table, 'dp', axis=0, tiled=True)  111 us
  transfers between devices with their start and end apart: 22, of which 16 were waited for; matrix products, arithmetic and copies ran while one was open for 13% of the time, Pallas kernels for 0%

commit v1 on v0

--- a/solution.py
+++ b/solution.py
@@ -1,8 +1,11 @@
+import functools
 import math
 
 import jax
 import jax.numpy as jnp
 from jax import lax
+from jax.experimental import pallas as pl
+from jax.experimental.pallas import tpu as pltpu
 from jax.sharding import PartitionSpec as P
 
 HEAD = 64
@@ -285,7 +288,7 @@
     )
 
 
-def per_device(
+def per_device_general(
     tokens,
     lengths,
     levels,
@@ -493,6 +496,418 @@
     )
 
 
+MESH = pl.DeviceIdType.MESH
+LAYER_ARRAYS = 4
+
+
+def gather_kernel(count_z, *refs):
+    shards = refs[:8]
+    wholes = refs[8:16]
+    own_sem, zsend, zrecv, psend, precv, gate = refs[16:]
+    sec = lax.axis_index("section")
+    grp = lax.axis_index("group")
+    pos = lax.axis_index("dp")
+    beside_x = (sec, grp ^ 1, pos)
+    beside_y = (sec, grp ^ 2, pos)
+
+    def along(step):
+        return (sec, grp, lax.rem(pos + step, count_z))
+
+    barrier = pltpu.get_barrier_semaphore()
+    partners = [beside_x, beside_y, (1 - sec, grp, pos)] + [along(k) for k in range(1, count_z)]
+    for partner in partners:
+        pl.semaphore_signal(barrier, inc=1, device_id=partner, device_id_type=MESH)
+    pl.semaphore_wait(barrier, len(partners))
+
+    def remote(src, dst, send_sem, recv_sem, device):
+        return pltpu.make_async_remote_copy(
+            src_ref=src,
+            dst_ref=dst,
+            send_sem=send_sem,
+            recv_sem=recv_sem,
+            device_id=device,
+            device_id_type=MESH,
+        )
+
+    def run(order, gains, before, middle):
+        own = []
+        for slot, idx in enumerate(order):
+            rows = shards[idx].shape[0]
+            own.append(
+                pltpu.make_async_copy(
+                    shards[idx], wholes[idx].at[pl.ds(pos * rows, rows)], own_sem.at[slot]
+                )
+            )
+        if before is not None:
+            before()
+        sends = []
+        zin = {}
+        rows_g = shards[gains].shape[0]
+        own.append(
+            pltpu.make_async_copy(
+                shards[gains], wholes[gains].at[pl.ds(pos * rows_g, rows_g)], own_sem.at[len(order)]
+            )
+        )
+        for k in range(1, count_z):
+            copy = remote(
+                shards[gains],
+                wholes[gains].at[pl.ds(pos * rows_g, rows_g)],
+                zsend.at[len(order), k],
+                zrecv.at[len(order), k],
+                along(k),
+            )
+            copy.start()
+            zin[len(order), k] = copy
+            sends.append(copy)
+        for slot, idx in enumerate(order):
+            rows = shards[idx].shape[0]
+            part = rows // 4
+            for k in range(1, count_z):
+                copy = remote(
+                    shards[idx].at[pl.ds(grp * part, part)],
+                    wholes[idx].at[pl.ds(pos * rows + grp * part, part)],
+                    zsend.at[slot, k],
+                    zrecv.at[slot, k],
+                    along(k),
+                )
+                copy.start()
+                zin[slot, k] = copy
+                sends.append(copy)
+        for copy in own:
+            copy.start()
+        items = [(slot, idx, k) for slot, idx in enumerate(order) for k in range(1, count_z)]
+        crossing = {}
+
+        def block(idx, k, who):
+            rows = shards[idx].shape[0]
+            part = rows // 4
+            origin = lax.rem(pos - k + count_z, count_z)
+            return pl.ds(origin * rows + who * part, part)
+
+        def first(slot, idx, k):
+            zin[slot, k].wait_recv()
+            here = block(idx, k, grp)
+            for way, device in ((0, beside_x), (1, beside_y)):
+                copy = remote(
+                    wholes[idx].at[here],
+                    wholes[idx].at[here],
+                    psend.at[slot, k, way],
+                    precv.at[slot, k, way],
+                    device,
+                )
+                copy.start()
+                crossing[slot, k, way] = copy
+                sends.append(copy)
+
+        def second(slot, idx, k):
+            half = shards[idx].shape[1] // 2
+            for way, who, lo, device in ((0, grp ^ 1, 0, beside_y), (1, grp ^ 2, half, beside_x)):
+                crossing[slot, k, way].wait_recv()
+                there = block(idx, k, who)
+                copy = remote(
+                    wholes[idx].at[there, pl.ds(lo, half)],
+                    wholes[idx].at[there, pl.ds(lo, half)],
+                    psend.at[slot, k, 2 + way],
+                    precv.at[slot, k, 2 + way],
+                    device,
+                )
+                copy.start()
+                crossing[slot, k, 2 + way] = copy
+                sends.append(copy)
+
+        lag = 2
+        for at in range(len(items) + lag):
+            if at < len(items):
+                first(*items[at])
+            if at == len(items) - 1 and middle is not None:
+                middle()
+            if at >= lag:
+                second(*items[at - lag])
+        for slot, idx, k in items:
+            crossing[slot, k, 2].wait_recv()
+            crossing[slot, k, 3].wait_recv()
+        for k in range(1, count_z):
+            zin[len(order), k].wait_recv()
+        for copy in sends:
+            copy.wait_send()
+        for copy in own:
+            copy.wait()
+
+    def let_go():
+        pl.semaphore_signal(gate, inc=1, device_id=(1 - sec, grp, pos), device_id_type=MESH)
+
+    def hold():
+        pl.semaphore_wait(gate, 1)
+
+    @pl.when(sec == 0)
+    def _():
+        run((4, 0, 1, 2, 3), 7, None, let_go)
+
+    @pl.when(sec == 1)
+    def _():
+        run((0, 1, 2, 3, 5, 6), 7, hold, None)
+
+
+def gather_all(shards, count_z):
+    wholes = tuple(
+        jax.ShapeDtypeStruct((s.shape[0] * count_z, s.shape[1]), s.dtype) for s in shards
+    )
+    return pl.pallas_call(
+        functools.partial(gather_kernel, count_z),
+        out_shape=wholes,
+        in_specs=[pl.BlockSpec(memory_space=pl.ANY)] * len(shards),
+        out_specs=[pl.BlockSpec(memory_space=pl.ANY)] * len(shards),
+        scratch_shapes=[
+            pltpu.SemaphoreType.DMA((8,)),
+            pltpu.SemaphoreType.DMA((8, 4)),
+            pltpu.SemaphoreType.DMA((8, 4)),
+            pltpu.SemaphoreType.DMA((8, 4, 4)),
+            pltpu.SemaphoreType.DMA((8, 4, 4)),
+            pltpu.SemaphoreType.REGULAR,
+        ],
+        compiler_params=pltpu.CompilerParams(collective_id=0, has_side_effects=True),
+    )(*shards)
+
+
+def swap_kernel(count_z, rows_ref, out_ref, own_sem, send_sem, recv_sem):
+    sec = lax.axis_index("section")
+    grp = lax.axis_index("group")
+    pos = lax.axis_index("dp")
+
+    @pl.when(sec == 0)
+    def _():
+        barrier = pltpu.get_barrier_semaphore()
+        for k in range(1, count_z):
+            pl.semaphore_signal(
+                barrier,
+                inc=1,
+                device_id=(sec, grp, lax.rem(pos + k, count_z)),
+                device_id_type=MESH,
+            )
+        pl.semaphore_wait(barrier, count_z - 1)
+        copies = []
+        for k in range(1, count_z):
+            to = lax.rem(pos + k, count_z)
+            copy = pltpu.make_async_remote_copy(
+                src_ref=rows_ref.at[to],
+                dst_ref=out_ref.at[pos],
+                send_sem=send_sem.at[k],
+                recv_sem=recv_sem.at[k],
+                device_id=(sec, grp, to),
+                device_id_type=MESH,
+            )
+            copy.start()
+            copies.append(copy)
+        own = pltpu.make_async_copy(rows_ref.at[pos], out_ref.at[pos], own_sem)
+        own.start()
+        own.wait()
+        for copy in copies:
+            copy.wait()
+
+
+def swap_rows(rows, count_z):
+    return pl.pallas_call(
+        functools.partial(swap_kernel, count_z),
+        out_shape=jax.ShapeDtypeStruct(rows.shape, rows.dtype),
+        in_specs=[pl.BlockSpec(memory_space=pl.ANY)],
+        out_specs=pl.BlockSpec(memory_space=pl.ANY),
+        scratch_shapes=[
+            pltpu.SemaphoreType.DMA,
+            pltpu.SemaphoreType.DMA((4,)),
+            pltpu.SemaphoreType.DMA((4,)),
+        ],
+        compiler_params=pltpu.CompilerParams(collective_id=1, has_side_effects=True),
+    )(rows)
+
+
+def attend2(qkv_rows, key_valid):
+    return jax.vmap(attend)(qkv_rows, key_valid)
+
+
+def block_forward(hidden, key_valid, weights):
+    gain_attn, qkv_weight, proj_weight, gain_mlp, up_weight, down_weight = weights
+    seqs, length = key_valid.shape
+    normed_in = normed(hidden, gain_attn).astype(jnp.bfloat16)
+    qkv_rows = product(normed_in, qkv_weight).astype(jnp.bfloat16)
+    mixed_rows, log_total = jax.vmap(attend)(qkv_rows.reshape(seqs, length, -1), key_valid)
+    mixed_rows = mixed_rows.reshape(seqs * length, -1)
+    hidden_mid = hidden + product(mixed_rows, proj_weight)
+    mlp_in = normed(hidden_mid, gain_mlp).astype(jnp.bfloat16)
+    pre_act = product(mlp_in, up_weight)
+    activated = gelu_exact(pre_act).astype(jnp.bfloat16)
+    hidden_out = hidden_mid + product(activated, down_weight)
+    kept = (hidden, normed_in, qkv_rows, log_total, mixed_rows, hidden_mid, mlp_in, pre_act, activated)
+    return hidden_out, kept
+
+
+def block_backward(kept, grad_out, key_valid, weights):
+    hidden, normed_in, qkv_rows, log_total, mixed_rows, hidden_mid, mlp_in, pre_act, activated = kept
+    gain_attn, qkv_weight, proj_weight, gain_mlp, up_weight, down_weight = weights
+    seqs, length = key_valid.shape
+    grad_low = grad_out.astype(jnp.bfloat16)
+    grad_activated = product_nt(grad_low, down_weight)
+    grad_pre = jax.vjp(gelu_exact, pre_act)[1](grad_activated)[0].astype(jnp.bfloat16)
+    grad_mlp_in = product_nt(grad_pre, up_weight)
+    grad_mid_norm, grad_gain_mlp = norm_back(hidden_mid, gain_mlp, grad_mlp_in)
+    grad_mid = grad_out + grad_mid_norm
+    grad_mid_low = grad_mid.astype(jnp.bfloat16)
+    grad_mixed = product_nt(grad_mid_low, proj_weight).astype(jnp.bfloat16)
+    grad_qkv = jax.vmap(attend_back)(
+        qkv_rows.reshape(seqs, length, -1),
+        key_valid,
+        log_total,
+        grad_mixed.reshape(seqs, length, -1),
+    ).reshape(seqs * length, -1)
+    grad_normed = product_nt(grad_qkv, qkv_weight)
+    grad_in_norm, grad_gain_attn = norm_back(hidden, gain_attn, grad_normed)
+    grads = (
+        product_tn(normed_in, grad_qkv).astype(jnp.bfloat16),
+        product_tn(mixed_rows, grad_mid_low).astype(jnp.bfloat16),
+        product_tn(mlp_in, grad_pre).astype(jnp.bfloat16),
+        product_tn(activated, grad_low).astype(jnp.bfloat16),
+    )
+    return grad_mid + grad_in_norm, (grad_gain_attn, grad_gain_mlp), grads
+
+
+def nothing_like(run):
+    return jax.tree.map(lambda a: jnp.zeros(a.shape, a.dtype), jax.eval_shape(run))
+
+
+def only_on(live, run):
+    return lax.cond(live, run, lambda: nothing_like(run))
+
+
+def per_device(
+    tokens,
+    lengths,
+    levels,
+    noise_rows,
+    embed_table,
+    w_in,
+    ln_attn,
+    w_qkv,
+    w_proj,
+    ln_mlp,
+    w_up,
+    w_down,
+    ln_final,
+    w_out,
+):
+    count_z = lax.axis_size("dp")
+    sec = lax.axis_index("section")
+    pos = lax.axis_index("dp")
+    first_section = sec == 0
+    last_section = sec == 1
+    rows = tokens.shape[0]
+    seqs = lengths.shape[0]
+    length = rows // seqs
+    width = w_out.shape[0] * count_z
+    emb = w_out.shape[1]
+    vocab_part = embed_table.shape[0]
+    gains = jnp.concatenate(
+        [ln_attn, ln_mlp, ln_final[None], jnp.zeros((13, ln_final.shape[0]), jnp.bfloat16)], 0
+    )
+    shards = (w_qkv[0], w_proj[0], w_up[0], w_down[0], w_in, w_out, embed_table, gains)
+    line_tokens = lax.all_gather(tokens, "dp", axis=0, tiled=True)
+    wholes = gather_all(shards, count_z)
+    qkv_weight, proj_weight, up_weight, down_weight, in_weight, out_weight, table_full, gain_all = wholes
+    gain_all = gain_all.reshape(count_z, 16, -1).astype(jnp.float32)
+    gain_attn = gain_all[:, 0].reshape(-1)
+    gain_mlp = gain_all[:, 1].reshape(-1)
+    final_gain = gain_all[:, 2].reshape(-1)
+    weights = (gain_attn, qkv_weight, proj_weight, gain_mlp, up_weight, down_weight)
+    key_valid = jnp.arange(length, dtype=jnp.int32)[None, :] < lengths[:, None]
+    loss_scale = LOSS_GAIN / math.sqrt(rows * lax.axis_size(("group", "dp")))
+
+    def look_up():
+        local = line_tokens - pos * vocab_part
+        hit = local[:, None] == lax.broadcasted_iota(jnp.int32, (1, vocab_part), 1)
+        return product(hit.astype(jnp.bfloat16), embed_table).astype(jnp.bfloat16)
+
+    looked_parts = only_on(first_section, look_up).reshape(count_z, rows, emb)
+    looked_parts = swap_rows(looked_parts, count_z)
+    noise_level = jnp.exp(LOG_LOW + levels.astype(jnp.float32) * (LOG_SPAN / (LEVELS - 1)))
+    scale_in = lax.rsqrt(EMB_VAR + noise_level * noise_level)
+    row_level = jnp.repeat(noise_level, length)[:, None]
+    row_scale = jnp.repeat(scale_in, length)[:, None]
+
+    def front():
+        looked = jnp.sum(looked_parts.astype(jnp.float32), 0)
+        mixed_in = ((looked + row_level * noise_rows.astype(jnp.float32)) * row_scale).astype(
+            jnp.bfloat16
+        )
+        out, kept = block_forward(product(mixed_in, in_weight), key_valid, weights)
+        return out.astype(jnp.bfloat16), kept, mixed_in
+
+    out_first, kept_first, mixed_in = only_on(first_section, front)
+    x_second = passed_along(out_first, "section", 1)
+
+    def back():
+        hidden_out, kept = block_forward(x_second.astype(jnp.float32), key_valid, weights)
+        grad_top, entropy, gain_step, tail_now = tail_pass(
+            hidden_out,
+            tokens,
+            key_valid.reshape(-1),
+            final_gain,
+            out_weight,
+            table_full,
+            loss_scale,
+        )
+        grad_logits, projected, final_in, grad_proj = tail_now
+        grad_start, gain_pair, grads = block_backward(kept, grad_top, key_valid, weights)
+        return (
+            grad_start.astype(jnp.bfloat16),
+            entropy.astype(jnp.bfloat16),
+            gain_pair,
+            grads,
+            product_tn(grad_logits, projected).astype(jnp.bfloat16),
+            product_tn(final_in, grad_proj).astype(jnp.bfloat16),
+            gain_step,
+        )
+
+    grad_second, loss_low, gain_pair_b, grads_b, table_b, out_b, gain_final = only_on(last_section, back)
+    grad_first, loss_first = passed_along((grad_second, loss_low), "section", -1)
+    token_loss = jnp.where(first_section, loss_first, loss_low)
+
+    def front_back():
+        grad_start, gain_pair, grads = block_backward(
+            kept_first, grad_first.astype(jnp.float32), key_valid, weights
+        )
+        grad_low = grad_start.astype(jnp.bfloat16)
+        looked_grad = product_nt(grad_low, in_weight) * row_scale
+        table_grad = jnp.zeros(table_full.shape, jnp.float32).at[tokens].add(looked_grad)
+        return (gain_pair, grads, table_grad.astype(jnp.bfloat16), product_tn(mixed_in, grad_low).astype(jnp.bfloat16))
+
+    gain_pair, grads, table_g, in_g = lax.cond(
+        first_section,
+        front_back,
+        lambda: (gain_pair_b, grads_b, table_b, jnp.zeros(in_weight.shape, jnp.bfloat16)),
+    )
+
+    def scatter(x):
+        return lax.psum_scatter(x, "dp", scatter_dimension=0, tiled=True)
+
+    layer = [lax.psum(scatter(x), "group").astype(jnp.float32) for x in grads]
+    gain_out = [lax.psum(scatter(x.astype(jnp.bfloat16)), "group").astype(jnp.float32) for x in gain_pair]
+    edge = [
+        lax.psum(scatter(x), ("section", "group")).astype(jnp.float32)
+        for x in (table_g, in_g, gain_final.astype(jnp.bfloat16), out_b)
+    ]
+    return (
+        token_loss,
+        edge[0],
+        edge[1],
+        gain_out[0][None],
+        layer[0][None],
+        layer[1][None],
+        gain_out[1][None],
+        layer[2][None],
+        layer[3][None],
+        edge[2],
+        edge[3],
+    )
+
+
 def solution(mesh):
     placed = (
         P(("group", "dp")),
@@ -510,8 +925,9 @@
         P("dp"),
         P("dp", None),
     )
+    fits = mesh.shape["dp"] == 4 and mesh.shape["group"] == 4 and mesh.shape["section"] == 2
     return jax.shard_map(
-        per_device,
+        per_device if fits else per_device_general,
         mesh=mesh,
         in_specs=placed,
         out_specs=(

time: 1920 us -> 1480 us (0.77)
  waiting for transfers between devices: 1400 us -> 896 us
  Pallas kernels: 0 us -> 197 us
  starting transfers between devices: 9.36 us -> 83.7 us
  blocking collectives: 106 us -> 43 us
  local copies, waits for them, and re-layouts: 138 us -> 89.9 us
  matrix products: 138 us -> 91.1 us
  other arithmetic: 93.2 us -> 50.4 us
    all_gather x5 -> x0, waiting for transfers between devices: 562 us -> none  [the longest x1 149 us: per_device(): lax.all_gather(w_up, 'dp', axis=1, tiled=True)]
    pallas_call x0 -> x2, Pallas kernels: none -> 197 us  [the longest x1 188 us: gather_all(): pl.pallas_call(functools.partial(gather_kernel, count_z), out_shape=whole...]
    ppermute x6 -> x3, starting transfers between devices: 8.55 us -> 83.3 us  [passed_along(): return lax.ppermute(x, axis, pairs)]
    all_gather x5 -> x1, blocking collectives: 70.5 us -> 9.08 us  [per_device(): line_tokens = lax.all_gather(tokens, 'dp', axis=0, tiled=True)]
    reduce_scatter x7, waiting for transfers between devices: 563 us -> 616 us  [scatter(): return lax.psum_scatter(x, 'dp', scatter_dimension=0, tiled=True)]
    ppermute x6 -> x3, waiting for transfers between devices: 73.6 us -> 111 us  [passed_along(): return lax.ppermute(x, axis, pairs)]
    gather x6 -> x0, local copies, waits for them, and re-layouts: 33.4 us -> none  [embed_inputs(): looked = jnp.take(table_full, token_ids, axis=0).astype(jnp.float32)]
    another operation x56 -> x12, local copies, waits for them, and re-layouts: 47 us -> 21 us
  transfers between devices with their start and end apart: 22 -> 12, of which waited for: 16 -> 11; matrix products, arithmetic and copies ran while one was open for 13% -> 9% of each run, Pallas kernels for 0% -> 0%
where the time goes in v1:
time: 1480 us; the launch traced here: 1470 us
  waiting for transfers between devices  896 us (61%)
  Pallas kernels  197 us (13%)
  matrix products  91.1 us (6%)
  local copies, waits for them, and re-layouts  89.9 us (6%)
  starting transfers between devices  83.7 us (6%)
  other arithmetic  50.4 us (3%)
  blocking collectives  43 us (3%)
  between operations  14.9 us (1%)
    reduce_scatter x7, waiting for transfers between devices, scatter(): return lax.psum_scatter(x, 'dp', scatter_dimension=0, tiled=True)  616 us
    pallas_call x1, Pallas kernels, gather_all(): pl.pallas_call(functools.partial(gather_kernel, count_z), out_shape=whole...  188 us
    psum x1, waiting for transfers between devices, per_device(): layer = [lax.psum(scatter(x), 'group').astype(jnp.float32) for x in grads]  137 us
    ppermute x3, waiting for transfers between devices, passed_along(): return lax.ppermute(x, axis, pairs)  111 us
    ppermute x3, starting transfers between devices, passed_along(): return lax.ppermute(x, axis, pairs)  83.3 us
    dot_general x6, matrix products, product(): return jnp.dot(left_side, right_side, preferred_element_type=jnp.float32)  34.9 us
  transfers between devices with their start and end apart: 12, of which 11 were waited for; matrix products, arithmetic and copies ran while one was open for 9% of the time, Pallas kernels for 0%

profile of v1, /device:TPU:0, one launch (start us, length us, event | category | flops | bytes accessed | tf_op | source)
XLA Modules:
  0.0 1474.4 jit_solution(3297841349038224058)
XLA Ops:
  9.3 188.0 %shard_map.223 = (bf16[1024,3072]{1,0:T(8,128)(2,1)}, bf16[1024,1024]{1,0:T(8,128)(2,1)S(1)}, bf16[1024,4096]{1,0:T(8,128)(2,1)}, bf16[4096,1024]{1,0:T(8,128)(2...) custom-call(bf16[256,3072]{1,0:T(8,128)(2,1)} %bitcast.233, ...), custom_call_target="tpu_custom_call" | custom-call | tf_op jit(solution)/shard_map/pallas_call | solution.py:655
  198.2 9.1 all-gather
  207.3 4.4 conditional.4
  207.3 4.4 fusion.2
  211.7 9.0 shard_map.222
  221.5 62.1 %conditional.5 = (bf16[256,1024]{1,0:T(8,128)(2,1)}, f32[256,1024]{1,0:T(8,128)S(1)}, bf16[256,1024]{1,0:T(8,128)(2,1)}, bf16[256,3072]{1,0:T(8,128)(2,1)}, f32[...) conditional(s32[]{:T(128)} %convert_element_type.231, () %tuple.39, ...), branch_computations={%region_2.0_spmd, %region_3.11_spmd} | conditional | flops 6789526016 | bytes 111228448 | solution.py:777
  225.6 5.9 convolution_convert_fusion
  231.5 5.1 reshape.296
  236.6 3.8 fusion.111
  240.4 2.8 copy.155
  243.2 2.8 copy.156
  245.9 1.9 fusion.113
  249.6 2.8 copy.154
  252.4 2.2 fusion.14
  256.0 2.8 fusion.114
  260.4 2.3 multiply_convert_fusion
  262.7 15.2 %fusion.5 = (bf16[256,4096]{1,0:T(8,128)(2,1)}, f32[256,4096]{1,0:T(8,128)}) fusion(bf16[256,1024]{1,0:T(8,128)(2,1)} %multiply_convert_fusion, bf16[1024,4096]{1,0:T(8,128)(2,1)} %get-tuple-element.129), kind=kOutput, calls=%fused_computation.9 | convolution fusion | flops 2215641088 | bytes 15204352 | tf_op jit(solution)/shard_map/cond/branch_1_fun/dot_general | solution.py:32
  278.0 5.1 fusion.13
  283.5 80.7 %collective-permute-start = (bf16[256,1024]{1,0:T(8,128)(2,1)}, bf16[256,1024]{1,0:T(8,128)(2,1)S(1)}, u32[]{:S(2)}, u32[]{:S(2)}) collective-permute-start(bf16[256,1024]{1,0:T(8,128)(2,1)} %get-tuple-element.226), channel_id=1, source_target_pairs={{0,16},{1,17},{2,18},{3,19},{4,20},{5,21},{6,22},{7,23},{8,24},{9,... | collective-permute-start | bytes 1572872 | tf_op jit(solution)/shard_map/ppermute | solution.py:28
  364.3 1.7 collective-permute-done
  366.0 27.2 %conditional.6 = (bf16[256,1024]{1,0:T(8,128)(2,1)}, bf16[256]{0:T(256)(128)(2,1)}, bf16[1024]{0:T(1024)(128)(2,1)S(1)}, bf16[1024]{0:T(1024)(128)(2,1)S(1)}, bf...) conditional(s32[]{:T(128)} %convert_element_type.230, () %tuple.38, ...), branch_computations={%region_11.12_spmd, %region_12.34_spmd} | conditional | flops 26765813760 | bytes 534868864 | solution.py:777
  366.0 4.4 broadcast.523
  370.3 4.4 broadcast.524
  374.7 3.5 broadcast.525
  378.3 3.4 broadcast.521
  394.5 108.8 %collective-permute-done.2 = bf16[256,1024]{1,0:T(8,128)(2,1)S(1)} collective-permute-done((bf16[256,1024]{1,0:T(8,128)(2,1)}, bf16[256,1024]{1,0:T(8,128)(2,1)S(1)}, u32[]{:S(2)}, u32[]{:S(2)}) %collective-permute-start.2) | collective-permute-done | bytes 524320 | tf_op jit(solution)/shard_map/ppermute | solution.py:28
  503.4 122.6 %conditional.7 = (bf16[1024]{0:T(1024)(128)(2,1)S(1)}, bf16[1024]{0:T(1024)(128)(2,1)S(1)}, bf16[4096,1024]{1,0:T(8,128)(2,1)}, bf16[16384,256]{1,0:T(8,128)(2,1...) conditional(s32[]{:T(128)} %convert_element_type.231, ...), branch_computations={%region_34.35_spmd, %region_35.48_spmd} | conditional | flops 13601470464 | bytes 297255776 | solution.py:881
  505.1 1.7 multiply_reduce_fusion.14
  506.8 14.7 fusion.77
  521.6 4.6 multiply_reduce_fusion.11
  526.2 1.8 fusion.110
  531.5 1.8 reshape.300
  533.3 1.6 copy.114
  534.9 5.2 reshape.299
  540.2 3.5 fusion.120
  546.9 2.0 subtract_exponential_fusion.1
  548.9 2.8 copy.162
  551.6 1.8 multiply_reduce_fusion.9
  558.0 2.2 multiply_reduce_fusion.10
  561.6 9.0 scatter_custom_fusion
  570.6 8.8 convert_element_type.215
  579.4 5.4 convert_bitcast_fusion.1
  584.9 8.7 copy.139
  594.7 1.8 convert_bitcast_fusion.2
  596.5 2.6 copy.141
  599.1 7.3 convert_bitcast_fusion
  606.4 12.0 copy.143
  618.4 7.3 convolution_convert_fusion.14
  625.9 2.0 copy.125
  631.3 15.7 %reduce-scatter.10.cloned.1.call-done = bf16[64,1024]{1,0:T(8,128)(2,1)} async-done(((bf16[256,1024]{1,0:T(8,128)(2,1)}), bf16[64,1024]{1,0:T(8,128)(2,1)}) %reduce-scatter.10.cloned.1.call-update) | async-done | bytes 131088 | tf_op jit(solution)/shard_map/reduce_scatter | solution.py:888
  647.0 145.2 %reduce-scatter.8.cloned.1.call-done = bf16[4096,256]{1,0:T(8,128)(2,1)} async-done(((bf16[16384,256]{1,0:T(8,128)(2,1)}), bf16[4096,256]{1,0:T(8,128)(2,1)}) %reduce-scatter.8.cloned.1.call-update) | async-done | bytes 2097168 | tf_op jit(solution)/shard_map/reduce_scatter | solution.py:888
  792.3 47.3 %reduce-scatter.14.cloned.1.call-done = bf16[256,1024]{1,0:T(8,128)(2,1)} async-done(((bf16[1024,1024]{1,0:T(8,128)(2,1)}), bf16[256,1024]{1,0:T(8,128)(2,1)}) %reduce-scatter.14.cloned.1.call-update) | async-done | bytes 524304 | tf_op jit(solution)/shard_map/reduce_scatter | solution.py:888
  839.5 112.4 %reduce-scatter.12.cloned.1.call-done = bf16[256,3072]{1,0:T(8,128)(2,1)} async-done(((bf16[1024,3072]{1,0:T(8,128)(2,1)}), bf16[256,3072]{1,0:T(8,128)(2,1)}) %reduce-scatter.12.cloned.1.call-update) | async-done | bytes 1572880 | tf_op jit(solution)/shard_map/reduce_scatter | solution.py:888
  951.9 147.4 %reduce-scatter.16.cloned.1.call-done = bf16[256,4096]{1,0:T(8,128)(2,1)} async-done(((bf16[1024,4096]{1,0:T(8,128)(2,1)}), bf16[256,4096]{1,0:T(8,128)(2,1)}) %reduce-scatter.16.cloned.1.call-update) | async-done | bytes 2097168 | tf_op jit(solution)/shard_map/reduce_scatter | solution.py:888
  1099.3 147.7 %reduce-scatter.18.cloned.1.call-done = bf16[1024,1024]{1,0:T(8,128)(2,1)} async-done(((bf16[4096,1024]{1,0:T(8,128)(2,1)}), bf16[1024,1024]{1,0:T(8,128)(2,1)}) %reduce-scatter.18.cloned.1.call-update) | async-done | bytes 2097168 | tf_op jit(solution)/shard_map/reduce_scatter | solution.py:888
  1250.6 11.3 all-reduce.4
  1262.1 10.1 all-reduce.5
  1273.4 12.6 psum.78
  1286.6 28.5 %all-reduce.10.cloned.1.call-done = (bf16[4096,256]{1,0:T(8,128)(2,1)}, bf16[64,1024]{1,0:T(8,128)(2,1)}, bf16[256,256]{1,0:T(8,128)(2,1)}) async-done(((bf16[4096,256]{1,0:T(8,128)(2,1)}, bf16[64,1024]{1,0:T(8,128)(2,1)}, bf16[256,256]{1,0:T(8,128)(2,1)}), (bf16[4096,256]{1,0:T(8,128)(2,1)}, bf16[64,1024]{1,0:T(8,128)(2,1)}, bf16[256,256]{1,0:T(8,128)(2,1)})) %all-reduce.10.cloned.1.call-update) | async-done | bytes 2359312 | tf_op jit(solution)/shard_map/psum | solution.py:893
  1315.1 4.0 convert_element_type.235
  1320.5 137.3 %all-reduce.12.cloned.1.call-done = (bf16[1,256,3072]{2,1,0:T(8,128)(2,1)}, bf16[1,256,1024]{2,1,0:T(8,128)(2,1)}, bf16[1,256,4096]{2,1,0:T(8,128)(2,1)}, bf16[1,1024,1024]{2,1,0:T(8,128)(2,1)}) async-done(((bf16[1,256,3072]{2,1,0:T(8,128)(2,1)}, bf16[1,256,1024]{2,1,0:T(8,128)(2,1)}, bf16[1,256,4096]{2,1,0:T(8,128)(2,1)}, bf16[1,1024,1024]{2,1,0:T(8,128)(2,1)}), (bf16[1,256,3072]{2,1,0:T(8,128)(2,1)}, ...) | async-done | bytes 6291472 | tf_op jit(solution)/shard_map/psum | solution.py:890
  1457.8 4.2 broadcast_in_dim.177
  1462.1 2.5 broadcast_in_dim.179
  1464.6 2.0 broadcast_in_dim.171
  (177 shorter events, 44.0 us)
Async XLA Ops:
  7.2 624.1 %reduce-scatter.20.cloned.1.call-start = ((), (), s32[]{:S(2)}) async-start(), calls=%async_computation.13 | async-start | bytes 655360 | tf_op jit(solution)/shard_map/reduce_scatter | solution.py:888
  9.3 188.9 %copy-start.48 = (s32[256]{0:T(256)S(1)}, s32[256]{0:T(256)}, u32[]{:S(2)}) copy-start(s32[256]{0:T(256)} %param.22) | copy-start | bytes 3076
  197.4 23.5 %copy-start.6 = (bf16[1024,1024]{1,0:T(8,128)(2,1)}, bf16[1024,1024]{1,0:T(8,128)(2,1)S(1)}, u32[]{:S(2)}) copy-start(bf16[1024,1024]{1,0:T(8,128)(2,1)S(1)} %get-tuple-element.223) | copy-start | bytes 6291460
  207.3 13.4 copy-start.51
  207.3 13.5 copy-start.52
  207.3 13.6 copy-start.44
  220.9 0.6 copy-start.49
  220.9 143.4 %copy-start.47 = (bf16[64,256]{1,0:T(8,128)(2,1)S(1)}, bf16[64,256]{1,0:T(8,128)(2,1)}, u32[]{:S(2)}) copy-start(bf16[64,256]{1,0:T(8,128)(2,1)} %get-tuple-element.221) | copy-start | bytes 98308
  222.8 8.7 copy-start.39
  224.3 31.7 %copy-start.1 = (f32[256,1024]{1,0:T(8,128)}, f32[256,1024]{1,0:T(8,128)S(1)}, u32[]{:S(2)}) copy-start(f32[256,1024]{1,0:T(8,128)S(1)} %get-tuple-element.439) | copy-start | bytes 3145732 | tf_op jit(solution)/shard_map/cond
  247.9 1.3 copy-start.10
  249.6 9.2 copy-start.45
  258.8 19.1 %slice-start.6 = ((s8[8388608]{0:T(1024)(128)(4,1)}), s8[4194304]{0:T(1024)(128)(4,1)S(1)}, s32[]{:S(2)}) async-start(s8[8388608]{0:T(1024)(128)(4,1)} %bitcast.268), calls=%async_computation.22 | async-start | bytes 8388608 | tf_op jit(solution)/shard_map/cond
  262.7 15.2 %slice-start.7 = ((s8[8388608]{0:T(1024)(128)(4,1)}), s8[4194304]{0:T(1024)(128)(4,1)S(1)}, s32[]{:S(2)}) async-start(s8[8388608]{0:T(1024)(128)(4,1)} %bitcast.268), calls=%async_computation.23 | async-start | bytes 8388608 | tf_op jit(solution)/shard_map/cond
  278.0 5.1 copy-start.2
  283.5 82.4 %collective-permute-start = (bf16[256,1024]{1,0:T(8,128)(2,1)}, bf16[256,1024]{1,0:T(8,128)(2,1)S(1)}, u32[]{:S(2)}, u32[]{:S(2)}) collective-permute-start(bf16[256,1024]{1,0:T(8,128)(2,1)} %get-tuple-element.226), channel_id=1, source_target_pairs={{0,16},{1,17},{2,18},{3,19},{4,20},{5,21},{6,22},{7,23},{8,24},{9,... | collective-permute-start | bytes 1572872 | tf_op jit(solution)/shard_map/ppermute | solution.py:28
  366.0 137.4 %copy-start.40 = (bf16[256,256]{1,0:T(8,128)(2,1)S(1)}, bf16[256,256]{1,0:T(8,128)(2,1)}, u32[]{:S(2)}) copy-start(bf16[256,256]{1,0:T(8,128)(2,1)} %get-tuple-element.247) | copy-start | bytes 393220
  366.0 137.4 %copy-start.46 = (f32[2,16,128,1]{2,1,0,3:T(8,128)S(1)}, f32[2,16,128,1]{2,1,0,3:T(8,128)}, u32[]{:S(2)}) copy-start(f32[2,16,128,1]{2,1,0,3:T(8,128)} %get-tuple-element.239) | copy-start | bytes 49156
  366.0 137.4 %copy-start.50 = (f32[2,128]{1,0:T(2,128)S(1)}, f32[2,128]{1,0:T(2,128)}, u32[]{:S(2)}) copy-start(f32[2,128]{1,0:T(2,128)} %copy-done.49) | copy-start | bytes 3076
  393.2 253.8 %reduce-scatter.10.cloned.1.call-start = ((), (), s32[]{:S(2)}) async-start(), calls=%async_computation.8 | async-start | bytes 655360 | tf_op jit(solution)/shard_map/reduce_scatter | solution.py:888
  393.2 110.1 %collective-permute-start.2 = (bf16[256,1024]{1,0:T(8,128)(2,1)}, bf16[256,1024]{1,0:T(8,128)(2,1)S(1)}, u32[]{:S(2)}, u32[]{:S(2)}) collective-permute-start(bf16[256,1024]{1,0:T(8,128)(2,1)} %get-tuple-element.240), channel_id=1, source_target_pairs={{16,0},{17,1},{18,2},{19,3},{20,4},{21,5},{22,6},{23,7},{24,8},{25... | collective-permute-start | bytes 1572872 | tf_op jit(solution)/shard_map/ppermute | solution.py:28
  503.4 18.2 %copy-start.17 = (bf16[256,1024]{1,0:T(8,128)(2,1)}, bf16[256,1024]{1,0:T(8,128)(2,1)S(1)}, u32[]{:S(2)}) copy-start(bf16[256,1024]{1,0:T(8,128)(2,1)S(1)} %get-tuple-element.154) | copy-start | bytes 1572868 | tf_op jit(solution)/shard_map/cond
  505.1 16.5 %slice-start.4 = ((s8[8388608]{0:T(1024)(128)(4,1)}), s8[4194304]{0:T(1024)(128)(4,1)S(1)}, s32[]{:S(2)}) async-start(s8[8388608]{0:T(1024)(128)(4,1)} %bitcast.266), calls=%async_computation.20 | async-start | bytes 8388608 | tf_op jit(solution)/shard_map/cond
  506.8 14.8 %slice-start.5 = ((s8[8388608]{0:T(1024)(128)(4,1)}), s8[4194304]{0:T(1024)(128)(4,1)S(1)}, s32[]{:S(2)}) async-start(s8[8388608]{0:T(1024)(128)(4,1)} %bitcast.266), calls=%async_computation.21 | async-start | bytes 8388608 | tf_op jit(solution)/shard_map/cond
  521.6 4.6 copy-start.29
  521.6 7.4 copy-start.18
  526.2 3.8 copy-start.9
  528.0 1.0 copy-start.13
  529.2 0.8 copy-start.36
  551.6 2.3 copy-start.34
  553.4 1.0 copy-start.35
  553.4 1.9 copy-start.23
  553.4 4.5 slice-start.12
  554.5 3.5 slice-start.13
  558.0 2.6 copy-start.14
  558.0 2.6 copy-start.19
  560.2 1.0 copy-start.32
  584.9 9.8 copy-start.37
  606.4 12.0 copy-start.20
  628.0 164.2 %reduce-scatter.8.cloned.1.call-start = ((), (), s32[]{:S(2)}) async-start(), calls=%async_computation.7 | async-start | bytes 10485760 | tf_op jit(solution)/shard_map/reduce_scatter | solution.py:888
  628.7 210.8 %reduce-scatter.14.cloned.1.call-start = ((), (), s32[]{:S(2)}) async-start(), calls=%async_computation.10 | async-start | bytes 2621440 | tf_op jit(solution)/shard_map/reduce_scatter | solution.py:888
  629.3 322.6 %reduce-scatter.12.cloned.1.call-start = ((), (), s32[]{:S(2)}) async-start(), calls=%async_computation.9 | async-start | bytes 7864320 | tf_op jit(solution)/shard_map/reduce_scatter | solution.py:888
  629.9 469.4 %reduce-scatter.16.cloned.1.call-start = ((), (), s32[]{:S(2)}) async-start(), calls=%async_computation.11 | async-start | bytes 10485760 | tf_op jit(solution)/shard_map/reduce_scatter | solution.py:888
  630.5 616.5 %reduce-scatter.18.cloned.1.call-start = ((), (), s32[]{:S(2)}) async-start(), calls=%async_computation.12 | async-start | bytes 10485760 | tf_op jit(solution)/shard_map/reduce_scatter | solution.py:888
  631.2 683.9 %all-reduce.10.cloned.1.call-start = ((), (), s32[]{:S(2)}) async-start(), calls=%async_computation.14 | async-start | bytes 4718592 | tf_op jit(solution)/shard_map/psum | solution.py:893
  792.2 456.1 %copy-start.53 = (u32[32]{0:T(128)S(1)}, u32[32]{0:T(128)}, u32[]{:S(2)}) copy-start(u32[32]{0:T(128)} %constant.310) | copy-start | bytes 388
  792.2 665.6 %all-reduce.12.cloned.1.call-start = ((), (), s32[]{:S(2)}) async-start(), calls=%async_computation.15 | async-start | bytes 12582912 | tf_op jit(solution)/shard_map/psum | solution.py:890
  1247.0 3.1 collective-permute-start.1
  1315.1 4.0 copy-start.43
  1315.1 4.7 copy-start.42
  1457.8 4.3 copy-start.30
  1462.1 2.5 copy-start.38
  1462.1 4.5 copy-start.41
Sparse Core Ops, SparseCore 0:
  393.3 125.7 reduce-scatter.19
  628.1 18.8 reduce-scatter.9
  649.4 142.7 reduce-scatter.7
  794.9 44.5 reduce-scatter.13
  841.8 110.0 reduce-scatter.11
  954.2 144.9 reduce-scatter.15
  1101.7 145.1 reduce-scatter.17
  1250.9 64.1 all-reduce.9
  1318.8 138.9 all-reduce.11

commit v2 on v1

--- a/solution.py
+++ b/solution.py
@@ -497,175 +497,216 @@
 
 
 MESH = pl.DeviceIdType.MESH
-LAYER_ARRAYS = 4
-
-
-def gather_kernel(count_z, *refs):
-    shards = refs[:8]
-    wholes = refs[8:16]
-    own_sem, zsend, zrecv, psend, precv, gate = refs[16:]
+ANYWHERE = pl.BlockSpec(memory_space=pl.ANY)
+
+
+def pick(index, values):
+    out = values[-1]
+    for at in range(len(values) - 2, -1, -1):
+        out = jnp.where(index == at, values[at], out)
+    return out
+
+
+def rows_at(start, size):
+    return pl.ds(pl.multiple_of(start, 8), size)
+
+
+def remote(src, dst, send_sem, recv_sem, device):
+    return pltpu.make_async_remote_copy(
+        src_ref=src,
+        dst_ref=dst,
+        send_sem=send_sem,
+        recv_sem=recv_sem,
+        device_id=device,
+        device_id_type=MESH,
+    )
+
+
+def gather_kernel(count, first_order, last_order, whole_line, *refs):
+    shards = refs[:count]
+    wholes = refs[count : 2 * count]
+    own_sem, zsend, zrecv, psend, precv, gate = refs[2 * count : 2 * count + 6]
+    stage = refs[2 * count + 6 :]
     sec = lax.axis_index("section")
     grp = lax.axis_index("group")
     pos = lax.axis_index("dp")
-    beside_x = (sec, grp ^ 1, pos)
-    beside_y = (sec, grp ^ 2, pos)
-
-    def along(step):
-        return (sec, grp, lax.rem(pos + step, count_z))
-
+    beside = ((sec, grp ^ 1, pos), (sec, grp ^ 2, pos))
+    above = (sec, grp, pos + 1)
+    below = (sec, grp, pos - 1)
+    partner = (1 - sec, grp, pos)
     barrier = pltpu.get_barrier_semaphore()
-    partners = [beside_x, beside_y, (1 - sec, grp, pos)] + [along(k) for k in range(1, count_z)]
-    for partner in partners:
-        pl.semaphore_signal(barrier, inc=1, device_id=partner, device_id_type=MESH)
-    pl.semaphore_wait(barrier, len(partners))
-
-    def remote(src, dst, send_sem, recv_sem, device):
-        return pltpu.make_async_remote_copy(
-            src_ref=src,
-            dst_ref=dst,
-            send_sem=send_sem,
-            recv_sem=recv_sem,
-            device_id=device,
-            device_id_type=MESH,
-        )
-
-    def run(order, gains, before, middle):
-        own = []
-        for slot, idx in enumerate(order):
+
+    def greet(device):
+        pl.semaphore_signal(barrier, inc=1, device_id=device, device_id_type=MESH)
+
+    for device in beside + (partner,):
+        greet(device)
+
+    @pl.when(pos > 0)
+    def _():
+        greet(below)
+
+    @pl.when(pos < 3)
+    def _():
+        greet(above)
+
+    at_end = (pos == 0) | (pos == 3)
+    pl.semaphore_wait(barrier, jnp.where(at_end, 4, 5))
+
+    turn = [pick(pos, v) for v in ((3, 1, 3, 1), (2, 3, 1, 2), (1, 2, 2, 3))]
+
+    def run(order, before, middle):
+        def part_of(idx):
             rows = shards[idx].shape[0]
-            own.append(
-                pltpu.make_async_copy(
-                    shards[idx], wholes[idx].at[pl.ds(pos * rows, rows)], own_sem.at[slot]
-                )
+            return rows if idx in whole_line else rows // 4
+
+        def shift(idx, who):
+            return 0 if idx in whole_line else who * part_of(idx)
+
+        def block(idx, origin, who):
+            return rows_at(origin * shards[idx].shape[0] + shift(idx, who), part_of(idx))
+
+        def load_own(slot):
+            return pltpu.make_async_copy(shards[order[slot]], stage[order[slot]], own_sem.at[slot])
+
+        def store_own(slot):
+            idx = order[slot]
+            rows = shards[idx].shape[0]
+            return pltpu.make_async_copy(
+                stage[idx], wholes[idx].at[rows_at(pos * rows, rows)], own_sem.at[slot]
             )
+
+        def own_ends(slot):
+            idx = order[slot]
+            src = shards[idx].at[rows_at(shift(idx, grp), part_of(idx))]
+            dst = wholes[idx].at[block(idx, pos, grp)]
+            return (
+                (pos < 3, remote(src, dst, zsend.at[slot, 0], zrecv.at[slot, 1], above)),
+                (pos > 0, remote(src, dst, zsend.at[slot, 1], zrecv.at[slot, 3], below)),
+            )
+
+        def start_own(slot):
+            for goes, copy in own_ends(slot):
+                pl.when(goes)(copy.start)
+
+        def origin_of(j):
+            return lax.rem(pos - turn[j] + 4, 4)
+
+        def arrived(slot, j):
+            here = wholes[order[slot]].at[block(order[slot], origin_of(j), grp)]
+            return remote(here, here, zsend.at[slot, 2 + j], zrecv.at[slot, turn[j]], partner)
+
+        def onward(slot, j):
+            step = jnp.where(turn[j] <= pos, 1, -1)
+            to = pos + step
+            here = wholes[order[slot]].at[block(order[slot], origin_of(j), grp)]
+            landed = jnp.clip(turn[j] + step, 0, 3)
+            copy = remote(
+                here,
+                here,
+                zsend.at[slot, 2 + j],
+                zrecv.at[slot, landed],
+                (sec, grp, jnp.clip(to, 0, 3)),
+            )
+            return (to >= 0) & (to <= 3), copy
+
+        def plane(slot, j, way):
+            idx = order[slot]
+            origin = origin_of(j)
+            if way < 2:
+                here = wholes[idx].at[block(idx, origin, grp)]
+                return remote(here, here, psend.at[slot, j, way], precv.at[slot, j, way], beside[way])
+            half = shards[idx].shape[1] // 2
+            there = wholes[idx].at[
+                block(idx, origin, grp ^ (way - 1)), pl.ds(half * (way - 2), half)
+            ]
+            return remote(
+                there, there, psend.at[slot, j, way], precv.at[slot, j, way], beside[3 - way]
+            )
+
+        items = [(slot, j) for slot in range(len(order)) for j in range(3)]
+        crossing = [item for item in items if order[item[0]] not in whole_line]
+
+        def first(slot, j):
+            arrived(slot, j).wait_recv()
+            goes, copy = onward(slot, j)
+            pl.when(goes)(copy.start)
+            if (slot, j) in crossing:
+                plane(slot, j, 0).start()
+                plane(slot, j, 1).start()
+
+        def second(slot, j):
+            if (slot, j) in crossing:
+                for way in (0, 1):
+                    plane(slot, j, way).wait_recv()
+                    plane(slot, j, way + 2).start()
+
         if before is not None:
             before()
-        sends = []
-        zin = {}
-        rows_g = shards[gains].shape[0]
-        own.append(
-            pltpu.make_async_copy(
-                shards[gains], wholes[gains].at[pl.ds(pos * rows_g, rows_g)], own_sem.at[len(order)]
-            )
-        )
-        for k in range(1, count_z):
-            copy = remote(
-                shards[gains],
-                wholes[gains].at[pl.ds(pos * rows_g, rows_g)],
-                zsend.at[len(order), k],
-                zrecv.at[len(order), k],
-                along(k),
-            )
-            copy.start()
-            zin[len(order), k] = copy
-            sends.append(copy)
-        for slot, idx in enumerate(order):
-            rows = shards[idx].shape[0]
-            part = rows // 4
-            for k in range(1, count_z):
-                copy = remote(
-                    shards[idx].at[pl.ds(grp * part, part)],
-                    wholes[idx].at[pl.ds(pos * rows + grp * part, part)],
-                    zsend.at[slot, k],
-                    zrecv.at[slot, k],
-                    along(k),
-                )
-                copy.start()
-                zin[slot, k] = copy
-                sends.append(copy)
-        for copy in own:
-            copy.start()
-        items = [(slot, idx, k) for slot, idx in enumerate(order) for k in range(1, count_z)]
-        crossing = {}
-
-        def block(idx, k, who):
-            rows = shards[idx].shape[0]
-            part = rows // 4
-            origin = lax.rem(pos - k + count_z, count_z)
-            return pl.ds(origin * rows + who * part, part)
-
-        def first(slot, idx, k):
-            zin[slot, k].wait_recv()
-            here = block(idx, k, grp)
-            for way, device in ((0, beside_x), (1, beside_y)):
-                copy = remote(
-                    wholes[idx].at[here],
-                    wholes[idx].at[here],
-                    psend.at[slot, k, way],
-                    precv.at[slot, k, way],
-                    device,
-                )
-                copy.start()
-                crossing[slot, k, way] = copy
-                sends.append(copy)
-
-        def second(slot, idx, k):
-            half = shards[idx].shape[1] // 2
-            for way, who, lo, device in ((0, grp ^ 1, 0, beside_y), (1, grp ^ 2, half, beside_x)):
-                crossing[slot, k, way].wait_recv()
-                there = block(idx, k, who)
-                copy = remote(
-                    wholes[idx].at[there, pl.ds(lo, half)],
-                    wholes[idx].at[there, pl.ds(lo, half)],
-                    psend.at[slot, k, 2 + way],
-                    precv.at[slot, k, 2 + way],
-                    device,
-                )
-                copy.start()
-                crossing[slot, k, 2 + way] = copy
-                sends.append(copy)
-
+        for slot in range(len(order)):
+            start_own(slot)
+        for slot in range(len(order)):
+            load_own(slot).start()
         lag = 2
         for at in range(len(items) + lag):
             if at < len(items):
-                first(*items[at])
+                slot, j = items[at]
+                if j == 2:
+                    load_own(slot).wait()
+                    store_own(slot).start()
+                first(slot, j)
             if at == len(items) - 1 and middle is not None:
                 middle()
             if at >= lag:
                 second(*items[at - lag])
-        for slot, idx, k in items:
-            crossing[slot, k, 2].wait_recv()
-            crossing[slot, k, 3].wait_recv()
-        for k in range(1, count_z):
-            zin[len(order), k].wait_recv()
-        for copy in sends:
-            copy.wait_send()
-        for copy in own:
-            copy.wait()
+        for slot, j in crossing:
+            plane(slot, j, 2).wait_recv()
+            plane(slot, j, 3).wait_recv()
+        for slot in range(len(order)):
+            store_own(slot).wait()
+            for goes, copy in own_ends(slot):
+                pl.when(goes)(copy.wait_send)
+        for slot, j in items:
+            goes, copy = onward(slot, j)
+            pl.when(goes)(copy.wait_send)
+        for slot, j in crossing:
+            for way in range(4):
+                plane(slot, j, way).wait_send()
 
     def let_go():
-        pl.semaphore_signal(gate, inc=1, device_id=(1 - sec, grp, pos), device_id_type=MESH)
+        pl.semaphore_signal(gate, inc=1, device_id=partner, device_id_type=MESH)
 
     def hold():
         pl.semaphore_wait(gate, 1)
 
     @pl.when(sec == 0)
     def _():
-        run((4, 0, 1, 2, 3), 7, None, let_go)
+        run(first_order, None, let_go)
 
     @pl.when(sec == 1)
     def _():
-        run((0, 1, 2, 3, 5, 6), 7, hold, None)
-
-
-def gather_all(shards, count_z):
-    wholes = tuple(
-        jax.ShapeDtypeStruct((s.shape[0] * count_z, s.shape[1]), s.dtype) for s in shards
-    )
+        run(last_order, hold, None)
+
+
+def gather_all(shards, first_order, last_order, whole_line):
+    count = len(shards)
     return pl.pallas_call(
-        functools.partial(gather_kernel, count_z),
-        out_shape=wholes,
-        in_specs=[pl.BlockSpec(memory_space=pl.ANY)] * len(shards),
-        out_specs=[pl.BlockSpec(memory_space=pl.ANY)] * len(shards),
+        functools.partial(gather_kernel, count, first_order, last_order, whole_line),
+        out_shape=[jax.ShapeDtypeStruct((s.shape[0] * 4, s.shape[1]), s.dtype) for s in shards],
+        in_specs=[ANYWHERE] * count,
+        out_specs=[ANYWHERE] * count,
         scratch_shapes=[
             pltpu.SemaphoreType.DMA((8,)),
+            pltpu.SemaphoreType.DMA((8, 5)),
             pltpu.SemaphoreType.DMA((8, 4)),
-            pltpu.SemaphoreType.DMA((8, 4)),
-            pltpu.SemaphoreType.DMA((8, 4, 4)),
-            pltpu.SemaphoreType.DMA((8, 4, 4)),
+            pltpu.SemaphoreType.DMA((8, 3, 4)),
+            pltpu.SemaphoreType.DMA((8, 3, 4)),
             pltpu.SemaphoreType.REGULAR,
-        ],
-        compiler_params=pltpu.CompilerParams(collective_id=0, has_side_effects=True),
+        ]
+        + [pltpu.VMEM(s.shape, s.dtype) for s in shards],
+        compiler_params=pltpu.CompilerParams(
+            collective_id=0, has_side_effects=True, vmem_limit_bytes=24 << 20
+        ),
     )(*shards)
 
 
@@ -720,8 +761,388 @@
     )(rows)
 
 
-def attend2(qkv_rows, key_valid):
-    return jax.vmap(attend)(qkv_rows, key_valid)
+def strip_of(rows, columns):
+    strip = 16
+    while 2 * strip * columns <= 65536 and rows % (2 * strip) == 0:
+        strip = 2 * strip
+    return strip
+
+
+def add_rows(into, terms, rows, columns):
+    strip = strip_of(rows, columns)
+
+    def body(at, carry):
+        here = rows_at(at * strip, strip)
+        total = terms[0](here).astype(jnp.float32)
+        for term in terms[1:]:
+            total = total + term(here).astype(jnp.float32)
+        into(here, total)
+        return carry
+
+    lax.fori_loop(0, rows // strip, body, 0)
+
+
+def reduce_kernel(kinds, *refs):
+    count = len(kinds)
+    arrays = refs[:count]
+    gains = refs[count]
+    outs = refs[count + 1 : 2 * count + 1]
+    gain_out = refs[2 * count + 1]
+    rest = list(refs[2 * count + 2 :])
+    s1, r1, own_sem, s2, r2, s3, r3, s4, r4, fin_sem, sg, rg = rest[:12]
+    gain_own_sem, gain_in, gain_got = rest[12:15]
+    bufs = rest[15:]
+    own, got1, got2, got3, fin = ([bufs[5 * a + b] for a in range(count)] for b in range(5))
+    sec = lax.axis_index("section")
+    grp = lax.axis_index("group")
+    pos = lax.axis_index("dp")
+    beside = ((sec, grp ^ 1, pos), (sec, grp ^ 2, pos))
+    barrier = pltpu.get_barrier_semaphore()
+    steps = [(jg, jz) for jg in range(4) for jz in range(4)][1:]
+
+    def other(j):
+        return (sec, grp ^ steps[j - 1][0], lax.rem(pos + steps[j - 1][1], 4))
+
+    for j in range(1, 16):
+        pl.semaphore_signal(barrier, inc=1, device_id=other(j), device_id_type=MESH)
+    pl.semaphore_wait(barrier, 15)
+
+    live = [None if kind[1] is None else sec == kind[1] for kind in kinds]
+
+    def when(a, run):
+        if live[a] is None:
+            run()
+        else:
+            pl.when(live[a])(run)
+
+    def rows_of(a):
+        return outs[a].shape[0]
+
+    def part_of(a):
+        return outs[a].shape[0] // 4
+
+    def block(a, line, who):
+        return arrays[a].at[rows_at(line * rows_of(a) + who * part_of(a), part_of(a))]
+
+    def gain_copy(j):
+        device = other(j)
+        return remote(gain_in.at[device[2]], gain_got.at[j - 1], sg.at[j - 1], rg.at[j - 1], device)
+
+    gain_load = pltpu.make_async_copy(gains, gain_in, gain_own_sem)
+
+    def ways(line):
+        first = 0 if line < 2 else 1
+        return first, 1 - first
+
+    def send_first(a, line, b):
+        first, second = ways(line)
+        who = grp ^ (1 + first)
+        if b:
+            who = who ^ (1 + second)
+        return remote(
+            block(a, line, who),
+            got1[a].at[line, b],
+            s1.at[a, line, b],
+            r1.at[a, line, b],
+            beside[first],
+        )
+
+    def load_own(a, line, b):
+        first, second = ways(line)
+        who = grp ^ (1 + second) if b else grp
+        return pltpu.make_async_copy(block(a, line, who), own[a].at[line, b], own_sem.at[a, line, b])
+
+    def send_second(a, line):
+        first, second = ways(line)
+        return remote(own[a].at[line, 1], got2[a].at[line], s2.at[a, line], r2.at[a, line], beside[second])
+
+    def send_line(a, line):
+        k = lax.rem(line - pos + 4, 4)
+        slot = jnp.maximum(k - 1, 0)
+        return remote(
+            own[a].at[line, 0], got3[a].at[slot], s3.at[a, line], r3.at[a, slot], (sec, grp, line)
+        )
+
+    def line_arrival(a, slot):
+        return remote(got3[a].at[slot], got3[a].at[slot], s3.at[a, slot], r3.at[a, slot], beside[0])
+
+    def begin(a, line):
+        def run():
+            for b in (1, 0):
+                send_first(a, line, b).start()
+                load_own(a, line, b).start()
+
+        when(a, run)
+
+    def middle(a, line):
+        def run():
+            columns = outs[a].shape[1]
+            for b in (1, 0):
+                load_own(a, line, b).wait()
+                send_first(a, line, b).wait_recv()
+
+                def into(here, total, b=b):
+                    own[a][line, b, here, :] = total.astype(jnp.bfloat16)
+
+                add_rows(
+                    into,
+                    [lambda here, b=b: own[a][line, b, here, :], lambda here, b=b: got1[a][line, b, here, :]],
+                    part_of(a),
+                    columns,
+                )
+                if b:
+                    send_second(a, line).start()
+
+        when(a, run)
+
+    def late(a, line):
+        def run():
+            send_second(a, line).wait_recv()
+
+            def into(here, total):
+                own[a][line, 0, here, :] = total.astype(jnp.bfloat16)
+
+            add_rows(
+                into,
+                [lambda here: own[a][line, 0, here, :], lambda here: got2[a][line, here, :]],
+                part_of(a),
+                outs[a].shape[1],
+            )
+            pl.when(line != pos)(send_line(a, line).start)
+
+        when(a, run)
+
+    def own_out(a):
+        here = outs[a].at[rows_at(grp * part_of(a), part_of(a))]
+        return pltpu.make_async_copy(fin[a], here, fin_sem.at[a])
+
+    def spread(a, way):
+        part = part_of(a)
+        if way < 2:
+            here = outs[a].at[rows_at(grp * part, part)]
+            return remote(fin[a], here, s4.at[a, way], r4.at[a, way], beside[way])
+        half = outs[a].shape[1] // 2
+        there = outs[a].at[rows_at((grp ^ (way - 1)) * part, part), pl.ds(half * (way - 2), half)]
+        return remote(there, there, s4.at[a, way], r4.at[a, way], beside[3 - way])
+
+    def spread_start(a):
+        spread(a, 0).start()
+        spread(a, 1).start()
+        own_out(a).start()
+
+    def finish(a):
+        def run():
+            for slot in range(3):
+                line_arrival(a, slot).wait_recv()
+
+            def into(here, total):
+                fin[a][here, :] = total.astype(jnp.bfloat16)
+
+            add_rows(
+                into,
+                [lambda here: own[a][pos, 0, here, :]]
+                + [lambda here, slot=slot: got3[a][slot, here, :] for slot in range(3)],
+                part_of(a),
+                outs[a].shape[1],
+            )
+            spread_start(a)
+
+        when(a, run)
+
+    def pass_on(a):
+        def run():
+            for way in (0, 1):
+                spread(a, way).wait_recv()
+                spread(a, way + 2).start()
+
+        when(a, run)
+
+    def line_rows(a, line):
+        return arrays[a].at[rows_at(line * rows_of(a), rows_of(a))]
+
+    def line_first(a, k):
+        to = lax.rem(pos + k, 4)
+        return remote(
+            line_rows(a, to), got1[a].at[k - 1], s1.at[a, k, 0], r1.at[a, k, 0], (sec, grp, to)
+        )
+
+    def line_own(a):
+        return pltpu.make_async_copy(line_rows(a, pos), own[a], own_sem.at[a, 0, 0])
+
+    def cross(a, j):
+        part = part_of(a)
+        to = grp ^ j
+        return remote(
+            own[a].at[rows_at(to * part, part)],
+            got3[a].at[j - 1],
+            s3.at[a, j],
+            r3.at[a, j - 1],
+            (sec, to, pos),
+        )
+
+    def line_begin(a):
+        def run():
+            for k in (2, 1, 3):
+                line_first(a, k).start()
+            line_own(a).start()
+
+        when(a, run)
+
+    def line_middle(a):
+        def run():
+            line_own(a).wait()
+            for k in (1, 2, 3):
+                line_first(a, k).wait_recv()
+
+            def into(here, total):
+                own[a][here, :] = total.astype(jnp.bfloat16)
+
+            add_rows(
+                into,
+                [lambda here: own[a][here, :]]
+                + [lambda here, k=k: got1[a][k, here, :] for k in range(3)],
+                rows_of(a),
+                outs[a].shape[1],
+            )
+            for j in (3, 1, 2):
+                cross(a, j).start()
+
+        when(a, run)
+
+    def line_finish(a):
+        def run():
+            part = part_of(a)
+            for j in (1, 2, 3):
+                cross(a, j).wait_recv()
+
+            def into(here, total):
+                fin[a][here, :] = total.astype(jnp.bfloat16)
+
+            strip = strip_of(part, outs[a].shape[1])
+
+            def body(at, carry):
+                here = rows_at(at * strip, strip)
+                total = own[a][rows_at(grp * part + at * strip, strip), :].astype(jnp.float32)
+                for j in range(3):
+                    total = total + got3[a][j, here, :].astype(jnp.float32)
+                fin[a][here, :] = total.astype(jnp.bfloat16)
+                return carry
+
+            lax.fori_loop(0, part // strip, body, 0)
+            spread_start(a)
+
+        when(a, run)
+
+    plane_arrays = [a for a in range(count) if kinds[a][0] == "plane"]
+    line_arrays = [a for a in range(count) if kinds[a][0] == "line"]
+    units = [(a, line) for a in plane_arrays for line in (0, 2, 1, 3)]
+    gain_load.start()
+    ahead = 6
+    for unit in units[:2]:
+        begin(*unit)
+    for a in line_arrays:
+        line_begin(a)
+    for unit in units[2:ahead]:
+        begin(*unit)
+    gain_load.wait()
+    for j in range(1, 16):
+        gain_copy(j).start()
+    lag = 2
+    finished = []
+    for at in range(len(units) + lag + 4):
+        if at + ahead < len(units):
+            begin(*units[at + ahead])
+        if at < len(units):
+            middle(*units[at])
+        if at == len(units) // 2:
+            for a in line_arrays:
+                line_middle(a)
+        if at == len(units) // 2 + 2:
+            for a in line_arrays:
+                line_finish(a)
+        if at == len(units) // 2 + 4:
+            for a in line_arrays:
+                pass_on(a)
+        if lag <= at < len(units) + lag:
+            late(*units[at - lag])
+        spot = at - lag - 2
+        if 0 <= spot < len(units) and units[spot][1] == 3:
+            if finished:
+                pass_on(finished[-1])
+            finish(units[spot][0])
+            finished.append(units[spot][0])
+    pass_on(finished[-1])
+    for j in range(1, 16):
+        gain_copy(j).wait_recv()
+    total = gain_in[pos]
+    for j in range(15):
+        total = total + gain_got[j]
+    gain_out[...] = total
+    for a in range(count):
+
+        def run(a=a):
+            spread(a, 2).wait_recv()
+            spread(a, 3).wait_recv()
+            own_out(a).wait()
+            for way in range(4):
+                spread(a, way).wait_send()
+            if kinds[a][0] == "plane":
+                for line in range(4):
+                    for b in (0, 1):
+                        send_first(a, line, b).wait_send()
+                    send_second(a, line).wait_send()
+                    pl.when(line != pos)(send_line(a, line).wait_send)
+            else:
+                for k in (1, 2, 3):
+                    line_first(a, k).wait_send()
+                    cross(a, k).wait_send()
+
+        when(a, run)
+    for j in range(1, 16):
+        gain_copy(j).wait_send()
+
+
+def reduce_all(arrays, gains, kinds, collective_id):
+    count = len(arrays)
+    outs = [jax.ShapeDtypeStruct((x.shape[0] // 4, x.shape[1]), x.dtype) for x in arrays]
+    buffers = []
+    for x, kind in zip(arrays, kinds):
+        rows, columns = x.shape[0] // 4, x.shape[1]
+        part = rows // 4
+        if kind[0] == "plane":
+            shapes = [(4, 2, part, columns), (4, 2, part, columns), (4, part, columns)]
+        else:
+            shapes = [(rows, columns), (3, rows, columns), (8, 128)]
+        shapes += [(3, part, columns), (part, columns)]
+        buffers += [pltpu.VMEM(shape, x.dtype) for shape in shapes]
+    dma = pltpu.SemaphoreType.DMA
+    return pl.pallas_call(
+        functools.partial(reduce_kernel, kinds),
+        out_shape=outs + [jax.ShapeDtypeStruct(gains.shape[1:], gains.dtype)],
+        in_specs=[ANYWHERE] * (count + 1),
+        out_specs=[ANYWHERE] * count + [pl.BlockSpec(memory_space=pltpu.VMEM)],
+        scratch_shapes=[
+            dma((count, 4, 2)),
+            dma((count, 4, 2)),
+            dma((count, 4, 2)),
+            dma((count, 4)),
+            dma((count, 4)),
+            dma((count, 4)),
+            dma((count, 4)),
+            dma((count, 4)),
+            dma((count, 4)),
+            dma((count,)),
+            dma((15,)),
+            dma((15,)),
+            dma,
+            pltpu.VMEM(gains.shape, gains.dtype),
+            pltpu.VMEM((15,) + gains.shape[1:], gains.dtype),
+        ]
+        + buffers,
+        compiler_params=pltpu.CompilerParams(
+            collective_id=collective_id, has_side_effects=True, vmem_limit_bytes=58 << 20
+        ),
+    )(*arrays, gains)
 
 
 def block_forward(hidden, key_valid, weights):
@@ -808,8 +1229,11 @@
         [ln_attn, ln_mlp, ln_final[None], jnp.zeros((13, ln_final.shape[0]), jnp.bfloat16)], 0
     )
     shards = (w_qkv[0], w_proj[0], w_up[0], w_down[0], w_in, w_out, embed_table, gains)
-    line_tokens = lax.all_gather(tokens, "dp", axis=0, tiled=True)
-    wholes = gather_all(shards, count_z)
+    wholes = gather_all(shards, (7, 4, 0, 1, 2, 3), (7, 0, 1, 2, 3, 5, 6), (7, 1))
+    all_tokens = lax.all_gather(tokens, ("group", "dp"), axis=0, tiled=True)
+    line_tokens = lax.dynamic_slice_in_dim(
+        all_tokens, lax.axis_index("group") * count_z * rows, count_z * rows, 0
+    )
     qkv_weight, proj_weight, up_weight, down_weight, in_weight, out_weight, table_full, gain_all = wholes
     gain_all = gain_all.reshape(count_z, 16, -1).astype(jnp.float32)
     gain_attn = gain_all[:, 0].reshape(-1)
@@ -874,37 +1298,47 @@
             kept_first, grad_first.astype(jnp.float32), key_valid, weights
         )
         grad_low = grad_start.astype(jnp.bfloat16)
-        looked_grad = product_nt(grad_low, in_weight) * row_scale
-        table_grad = jnp.zeros(table_full.shape, jnp.float32).at[tokens].add(looked_grad)
-        return (gain_pair, grads, table_grad.astype(jnp.bfloat16), product_tn(mixed_in, grad_low).astype(jnp.bfloat16))
-
-    gain_pair, grads, table_g, in_g = lax.cond(
-        first_section,
-        front_back,
-        lambda: (gain_pair_b, grads_b, table_b, jnp.zeros(in_weight.shape, jnp.bfloat16)),
-    )
-
-    def scatter(x):
-        return lax.psum_scatter(x, "dp", scatter_dimension=0, tiled=True)
-
-    layer = [lax.psum(scatter(x), "group").astype(jnp.float32) for x in grads]
-    gain_out = [lax.psum(scatter(x.astype(jnp.bfloat16)), "group").astype(jnp.float32) for x in gain_pair]
-    edge = [
-        lax.psum(scatter(x), ("section", "group")).astype(jnp.float32)
-        for x in (table_g, in_g, gain_final.astype(jnp.bfloat16), out_b)
-    ]
+        looked_grad = (product_nt(grad_low, in_weight) * row_scale).astype(jnp.bfloat16)
+        return gain_pair, grads, product_tn(mixed_in, grad_low).astype(jnp.bfloat16), looked_grad
+
+    def end_back():
+        shape = in_weight.shape
+        packed = out_b.reshape(count_z, shape[0] // count_z, shape[1]).reshape(shape)
+        return gain_pair_b, grads_b, packed, jnp.zeros((rows, emb), jnp.bfloat16)
+
+    gain_pair, grads, edge_g, looked_grad = lax.cond(first_section, front_back, end_back)
+    gain_rows = jnp.stack([gain_pair[0], gain_pair[1], gain_final], 0)
+    gain_rows = jnp.concatenate([gain_rows, jnp.zeros((5, width), jnp.float32)], 0)
+    gain_rows = gain_rows.reshape(8, count_z, width // count_z).transpose(1, 0, 2)
+    order = (table_b, grads[2], grads[3], edge_g, grads[1], grads[0])
+    kinds = (("plane", 1),) + (("plane", None),) * 4 + (("line", None),)
+    table_r, up_r, down_r, edge_r, proj_r, qkv_r, gain_r = reduce_all(order, gain_rows, kinds, 2)
+    looked_all = lax.all_gather(looked_grad, ("group", "dp"), axis=0, tiled=True)
+
+    def add_looked():
+        local = all_tokens - pos * vocab_part
+        hit = lax.broadcasted_iota(jnp.int32, (vocab_part, 1), 0) == local[None, :]
+        return product(hit.astype(jnp.bfloat16), looked_all).astype(jnp.bfloat16)
+
+    looked_sum = only_on(first_section, add_looked)
+    mine = (jnp.where(first_section, looked_sum, table_r), edge_r, gain_r)
+    theirs = lax.ppermute(mine, "section", [(0, 1), (1, 0)])
+    table_out = mine[0].astype(jnp.float32) + theirs[0].astype(jnp.float32)
+    in_r = jnp.where(first_section, edge_r, theirs[1]).astype(jnp.float32)
+    out_r = jnp.where(first_section, theirs[1], edge_r).astype(jnp.float32).reshape(-1, emb)
+    final_r = jnp.where(first_section, theirs[2][2], gain_r[2])
     return (
         token_loss,
-        edge[0],
-        edge[1],
-        gain_out[0][None],
-        layer[0][None],
-        layer[1][None],
-        gain_out[1][None],
-        layer[2][None],
-        layer[3][None],
-        edge[2],
-        edge[3],
+        table_out,
+        in_r,
+        gain_r[0][None],
+        qkv_r.astype(jnp.float32)[None],
+        proj_r.astype(jnp.float32)[None],
+        gain_r[1][None],
+        up_r.astype(jnp.float32)[None],
+        down_r.astype(jnp.float32)[None],
+        final_r,
+        out_r,
     )
 
 
@@ -925,7 +1359,7 @@
         P("dp"),
         P("dp", None),
     )
-    fits = mesh.shape["dp"] == 4 and mesh.shape["group"] == 4 and mesh.shape["section"] == 2
+    fits = (mesh.shape["section"], mesh.shape["group"], mesh.shape["dp"]) == (2, 4, 4)
     return jax.shard_map(
         per_device if fits else per_device_general,
         mesh=mesh,

time: 1480 us -> 922 us (0.62)
  waiting for transfers between devices: 896 us -> 112 us
  Pallas kernels: 197 us -> 416 us
  other arithmetic: 50.4 us -> 32.6 us
    reduce_scatter x7 -> x0, waiting for transfers between devices: 616 us -> none  [scatter(): return lax.psum_scatter(x, 'dp', scatter_dimension=0, tiled=True)]
    pallas_call x1 -> x2, Pallas kernels: 188 us -> 407 us  [the longest x1 295 us: reduce_all(): pl.pallas_call(functools.partial(reduce_kernel, kinds), out_shape=outs +...]
    psum x2 -> x0, waiting for transfers between devices: 166 us -> none  [the longest x1 137 us: per_device(): layer = [lax.psum(scatter(x), 'group').astype(jnp.float32) for x in grads]]
    all_gather x1, blocking collectives: 9.08 us -> 45 us  [per_device(): all_tokens = lax.all_gather(tokens, ('group', 'dp'), axis=0, tiled=True)]
    ppermute x0 -> x3, starting transfers between devices: none -> 29.2 us  [per_device(): theirs = lax.ppermute(mine, 'section', [(0, 1), (1, 0)])]
    ppermute x3, starting transfers between devices: 83.3 us -> 59.9 us  [passed_along(): return lax.ppermute(x, axis, pairs)]
    psum x2 -> x0, blocking collectives: 22.7 us -> none  [the longest x1 12.6 us: per_device(): lax.psum(scatter(x), ('section', 'group')).astype(jnp.float32)]
    convert_element_type x5 -> x0, other arithmetic: 14.8 us -> none  [the longest x1 8.82 us: front_back(): table_grad.astype(jnp.bfloat16)]
  transfers between devices with their start and end apart: 12 -> 7, of which waited for: 11 -> 3; matrix products, arithmetic and copies ran while one was open for 9% -> 3% of each run, Pallas kernels for 0% -> 32%
where the time goes in v2:
time: 922 us; the launch traced here: 913 us
  Pallas kernels  416 us (45%)
  waiting for transfers between devices  112 us (12%)
  matrix products  103 us (11%)
  local copies, waits for them, and re-layouts  90.7 us (10%)
  starting transfers between devices  89.1 us (10%)
  blocking collectives  45 us (5%)
  other arithmetic  32.6 us (4%)
  between operations  14.6 us (2%)
    pallas_call x1, Pallas kernels, reduce_all(): pl.pallas_call(functools.partial(reduce_kernel, kinds), out_shape=outs +...  295 us
    ppermute x3, waiting for transfers between devices, passed_along(): return lax.ppermute(x, axis, pairs)  112 us
    pallas_call x1, Pallas kernels, gather_all(): pl.pallas_call(functools.partial(gather_kernel, count, first_order, last_...  112 us
    ppermute x3, starting transfers between devices, passed_along(): return lax.ppermute(x, axis, pairs)  59.9 us
    dot_general x7, matrix products, product(): return jnp.dot(left_side, right_side, preferred_element_type=jnp.float32)  45.3 us
    all_gather x1, blocking collectives, per_device(): all_tokens = lax.all_gather(tokens, ('group', 'dp'), axis=0, tiled=True)  45 us
    ppermute x3, starting transfers between devices, per_device(): theirs = lax.ppermute(mine, 'section', [(0, 1), (1, 0)])  29.2 us
    dot_general x5, matrix products, product_nt(): lax.dot_general(left_side, right_side, (((1,), (1,)), ((), ())), preferre...  26.1 us
  transfers between devices with their start and end apart: 7, of which 3 were waited for; matrix products, arithmetic and copies ran while one was open for 3% of the time, Pallas kernels for 32%

profile of v2, /device:TPU:0, one launch (start us, length us, event | category | flops | bytes accessed | tf_op | source)
XLA Modules:
  0.0 913.0 jit_solution(14996210325890221015)
XLA Ops:
  7.2 45.0 %all-gather = s32[16,1,256]{2,1,0:T(1,128)} all-gather(s32[1,1,256]{2,1,0:T(1,128)} %bitcast.273), channel_id=1, replica_groups=mesh['section'=2,'group'=4,'dp'=4] {'group','dp'}, dimensions={0}, use_global_device_ids=true | all-gather | bytes 17408 | tf_op jit(solution)/shard_map/all_gather | solution.py:1233
  52.3 6.1 conditional.5
  53.2 5.2 fusion.2
  58.3 9.1 shard_map.222
  67.7 1.6 copy-done.1
  70.7 111.9 %shard_map.223 = (bf16[1024,3072]{1,0:T(8,128)(2,1)S(1)}, bf16[1024,1024]{1,0:T(8,128)(2,1)}, bf16[1024,4096]{1,0:T(8,128)(2,1)}, bf16[4096,1024]{1,0:T(8,128)(2...) custom-call(bf16[256,3072]{1,0:T(8,128)(2,1)S(1)} %bitcast.233, ...), custom_call_target="tpu_custom_call" | custom-call | tf_op jit(solution)/shard_map/pallas_call | solution.py:693
  183.4 2.0 copy-done.60
  185.4 54.4 %conditional.6 = (bf16[256,1024]{1,0:T(8,128)(2,1)}, f32[256,1024]{1,0:T(8,128)S(1)}, bf16[256,1024]{1,0:T(8,128)(2,1)}, bf16[256,3072]{1,0:T(8,128)(2,1)}, f32[...) conditional(s32[]{:T(128)} %convert_element_type.225, () %tuple.54, ...), branch_computations={%region_2.0_spmd, %region_3.11_spmd} | conditional | flops 6789526016 | bytes 125908576 | solution.py:1198
  187.4 2.8 convolution_convert_fusion
  190.3 3.7 reshape.314
  194.0 3.8 fusion.113
  197.8 2.0 copy.164
  199.8 2.8 copy.165
  202.5 1.7 fusion.115
  206.0 3.0 copy.163
  209.0 2.2 fusion.14
  212.6 2.8 fusion.116
  215.4 1.6 multiply_reduce_fusion
  217.1 2.2 multiply_convert_fusion
  219.3 15.3 %fusion.5 = (bf16[256,4096]{1,0:T(8,128)(2,1)}, f32[256,4096]{1,0:T(8,128)}) fusion(bf16[256,1024]{1,0:T(8,128)(2,1)} %multiply_convert_fusion, bf16[1024,4096]{1,0:T(8,128)(2,1)} %get-tuple-element.174), kind=kOutput, calls=%fused_computation.8 | convolution fusion | flops 2215641088 | bytes 15204352 | tf_op jit(solution)/shard_map/cond/branch_1_fun/dot_general | solution.py:32
  234.6 5.1 fusion.13
  239.8 57.3 %collective-permute-start = (bf16[256,1024]{1,0:T(8,128)(2,1)}, bf16[256,1024]{1,0:T(8,128)(2,1)S(1)}, u32[]{:S(2)}, u32[]{:S(2)}) collective-permute-start(bf16[256,1024]{1,0:T(8,128)(2,1)} %get-tuple-element.280), channel_id=1, source_target_pairs={{0,16},{1,17},{2,18},{3,19},{4,20},{5,21},{6,22},{7,23},{8,24},{9,... | collective-permute-start | bytes 1572872 | tf_op jit(solution)/shard_map/ppermute | solution.py:28
  297.2 1.7 collective-permute-done
  298.9 26.9 %conditional.7 = (bf16[256,1024]{1,0:T(8,128)(2,1)}, bf16[256]{0:T(256)(128)(2,1)S(1)}, f32[1024]{0:T(1024)S(1)}, f32[1024]{0:T(1024)S(1)}, bf16[1024,3072]{1,0:...) conditional(s32[]{:T(128)} %convert_element_type.224, () %tuple.53, ...), branch_computations={%region_11.12_spmd, %region_12.34_spmd} | conditional | flops 26765813760 | bytes 534875008 | solution.py:1198
  298.9 4.3 broadcast.525
  303.2 4.3 broadcast.526
  307.5 3.6 broadcast.527
  311.1 3.4 broadcast.523
  314.4 1.6 broadcast.524
  327.0 109.1 %collective-permute-done.2 = bf16[256,1024]{1,0:T(8,128)(2,1)S(1)} collective-permute-done((bf16[256,1024]{1,0:T(8,128)(2,1)}, bf16[256,1024]{1,0:T(8,128)(2,1)S(1)}, u32[]{:S(2)}, u32[]{:S(2)}) %collective-permute-start.2) | collective-permute-done | bytes 524320 | tf_op jit(solution)/shard_map/ppermute | solution.py:28
  436.2 107.2 %conditional.8 = (f32[1024]{0:T(1024)S(1)}, f32[1024]{0:T(1024)S(1)}, bf16[4096,1024]{1,0:T(8,128)(2,1)}, bf16[256,256]{1,0:T(8,128)(2,1)S(1)}, bf16[1024,4096]{...) conditional(s32[]{:T(128)} %convert_element_type.225, ...), branch_computations={%region_34.35_spmd, %region_35.47_spmd} | conditional | flops 13597274112 | bytes 235260672 | solution.py:1309
  436.2 1.5 reduce_sum.340
  437.9 1.7 multiply_reduce_fusion.14
  439.7 14.7 %fusion.75 = bf16[256,4096]{1,0:T(8,128)(2,1)S(1)} fusion(f32[256,4096]{1,0:T(8,128)} %get-tuple-element.200, bf16[256,1024]{1,0:T(8,128)(2,1)S(1)} %get-tuple-element.199, bf16[4096,1024]{1,0:T(8,128)(2,1)} %get-tuple-element.201), kind=kOutput, calls=%fused_computation.175 | convolution fusion | flops 2222981120 | bytes 15204352 | tf_op jit(solution)/shard_map/cond/branch_1_fun/dot_general | solution.py:42
  454.4 4.6 multiply_reduce_fusion.11
  459.0 1.8 fusion.112
  464.3 1.8 reshape.318
  466.1 1.6 copy.118
  467.7 5.3 reshape.317
  473.0 3.5 fusion.122
  476.5 1.6 copy.169
  478.1 1.6 copy.170
  479.8 2.0 subtract_exponential_fusion.1
  481.7 2.8 copy.171
  484.5 1.8 multiply_reduce_fusion.9
  489.2 1.6 copy.123
  490.8 5.5 convert_bitcast_fusion.1
  496.3 8.8 copy.152
  505.1 5.0 multiply_reduce_fusion.10
  512.5 2.0 convert_bitcast_fusion.2
  514.5 2.6 copy.150
  517.1 7.3 convert_bitcast_fusion
  524.4 11.6 %copy.146 = bf16[1024,4096]{1,0:T(8,128)(2,1)} copy(bf16[1024,4096]{0,1:T(8,128)(2,1)} %convert_bitcast_fusion) | data formatting | bytes 16777216 | tf_op jit(solution)/shard_map/cond | solution.py:1309
  536.0 7.2 convolution_convert_fusion.14
  545.5 1.6 collective-permute-done.1
  548.3 295.2 %shard_map.224 = (bf16[4096,256]{1,0:T(8,128)(2,1)}, bf16[256,4096]{1,0:T(8,128)(2,1)}, bf16[1024,1024]{1,0:T(8,128)(2,1)}, bf16[64,1024]{1,0:T(8,128)(2,1)}, bf...) custom-call(bf16[16384,256]{1,0:T(8,128)(2,1)} %get-tuple-element.303.refs_0_, ...), custom_call_target="tpu_custom_call" | custom-call | tf_op jit(solution)/shard_map/pallas_call | solution.py:1119
  843.5 29.1 %collective-permute-start.4 = (bf16[64,1024]{1,0:T(8,128)(2,1)}, bf16[64,1024]{1,0:T(8,128)(2,1)S(1)}, u32[]{:S(2)}, u32[]{:S(2)}) collective-permute-start(bf16[64,1024]{1,0:T(8,128)(2,1)} %get-tuple-element.313), channel_id=1, source_target_pairs={{0,16},{16,0},{1,17},{17,1},{2,18},{18,2},{3,19},{19,3},{4,20},{20... | collective-permute-start | bytes 393224 | tf_op jit(solution)/shard_map/ppermute | solution.py:1325
  872.7 3.4 bitcast_convert_fusion.2
  876.1 14.5 %conditional.9 = (bf16[4096,256]{1,0:T(8,128)(2,1)S(1)}) conditional(s32[]{:T(128)} %convert_element_type.225, () %tuple.59, (s32[]{:T(128)}, s32[4096]{0:T(1024)}, bf16[4096,256]{1,0:T(8,128)(2,1)}) %tuple.62), branch_computations={%region_47.48_spmd, %region_48.49_spmd} | conditional | flops 8607764480 | bytes 4243480 | solution.py:1198
  876.9 13.8 %fusion.107 = bf16[4096,256]{1,0:T(8,128)(2,1)S(1)} fusion(bf16[4096,256]{1,0:T(8,128)(2,1)} %get-tuple-element.217, s32[4096]{0:T(1024)S(1)} %broadcast_subtract_fusion), kind=kOutput, calls=%fused_computation.245 | convolution fusion | flops 8607760384 | bytes 4210688 | tf_op jit(solution)/shard_map/cond/branch_1_fun/dot_general | solution.py:32
  890.6 1.6 broadcast_select_fusion
  893.0 2.5 bitcast_convert_fusion
  895.4 2.5 bitcast_convert_fusion.1
  902.0 4.0 convert_add_fusion.1
  (168 shorter events, 29.1 us)
Async XLA Ops:
  7.2 869.0 %all-gather.3.cloned.1.call-start = ((), (), s32[]{:S(2)}) async-start(), calls=%async_computation | async-start | bytes 2228224 | tf_op jit(solution)/shard_map/all_gather | solution.py:1316
  52.2 15.2 %copy-start.61 = (bf16[256]{0:T(256)(128)(2,1)S(1)}, bf16[256]{0:T(256)(128)(2,1)}, u32[]{:S(2)}) copy-start(bf16[256]{0:T(256)(128)(2,1)} %param.36) | copy-start | bytes 1540
  52.2 15.3 %copy-start.58 = (bf16[1,256]{1,0:T(2,128)(2,1)S(1)}, bf16[1,256]{1,0:T(2,128)(2,1)}, u32[]{:S(2)}) copy-start(bf16[1,256]{1,0:T(2,128)(2,1)} %param.33) | copy-start | bytes 1540
  52.2 15.3 %copy-start.59 = (bf16[1,256]{1,0:T(2,128)(2,1)S(1)}, bf16[1,256]{1,0:T(2,128)(2,1)}, u32[]{:S(2)}) copy-start(bf16[1,256]{1,0:T(2,128)(2,1)} %param.30) | copy-start | bytes 1540
  52.2 15.4 %copy-start = (bf16[1,256,4096]{2,1,0:T(8,128)(2,1)S(1)}, bf16[1,256,4096]{2,1,0:T(8,128)(2,1)}, u32[]{:S(2)}) copy-start(bf16[1,256,4096]{2,1,0:T(8,128)(2,1)} %param.34) | copy-start | bytes 6291460
  52.2 15.4 %copy-start.3 = (bf16[1,256,1024]{2,1,0:T(8,128)(2,1)S(1)}, bf16[1,256,1024]{2,1,0:T(8,128)(2,1)}, u32[]{:S(2)}) copy-start(bf16[1,256,1024]{2,1,0:T(8,128)(2,1)} %param.32) | copy-start | bytes 1572868
  52.3 15.4 %copy-start.4 = (bf16[64,1024]{1,0:T(8,128)(2,1)S(1)}, bf16[64,1024]{1,0:T(8,128)(2,1)}, u32[]{:S(2)}) copy-start(bf16[64,1024]{1,0:T(8,128)(2,1)} %refs_4_.1) | copy-start | bytes 393220
  52.3 15.4 %copy-start.5 = (bf16[256,256]{1,0:T(8,128)(2,1)S(1)}, bf16[256,256]{1,0:T(8,128)(2,1)}, u32[]{:S(2)}) copy-start(bf16[256,256]{1,0:T(8,128)(2,1)} %refs_5_.1) | copy-start | bytes 393220
  67.7 1.6 copy-start.1
  69.3 1.4 copy-start.2
  70.7 112.0 %copy-start.62 = (s32[2]{0:T(128)S(1)}, s32[2]{0:T(128)}, u32[]{:S(2)}) copy-start(s32[2]{0:T(128)} %param.26) | copy-start | bytes 28
  70.7 112.0 %copy-start.63 = (s32[2]{0:T(128)S(1)}, s32[2]{0:T(128)}, u32[]{:S(2)}) copy-start(s32[2]{0:T(128)} %param.25) | copy-start | bytes 28
  70.7 112.1 %copy-start.42 = (bf16[4,256,256]{2,1,0:T(8,128)(2,1)S(1)}, bf16[4,256,256]{2,1,0:T(8,128)(2,1)}, u32[]{:S(2)}) copy-start(bf16[4,256,256]{2,1,0:T(8,128)(2,1)} %shard_map.222) | copy-start | bytes 1572868
  70.7 112.1 %copy-start.51 = (bf16[256,256]{1,0:T(8,128)(2,1)S(1)}, bf16[256,256]{1,0:T(8,128)(2,1)}, u32[]{:S(2)}) copy-start(bf16[256,256]{1,0:T(8,128)(2,1)} %param.27) | copy-start | bytes 393220
  182.6 0.8 copy-start.40
  182.6 2.8 copy-start.60
  182.8 2.6 copy-start.56
  182.8 116.0 %copy-start.55 = (s32[256]{0:T(256)S(1)}, s32[256]{0:T(256)}, u32[]{:S(2)}) copy-start(s32[256]{0:T(256)} %param.24) | copy-start | bytes 3076
  185.7 4.5 copy-start.47
  186.1 26.5 %copy-start.7 = (f32[256,1024]{1,0:T(8,128)}, f32[256,1024]{1,0:T(8,128)S(1)}, u32[]{:S(2)}) copy-start(f32[256,1024]{1,0:T(8,128)S(1)} %get-tuple-element.509) | copy-start | bytes 3145732 | tf_op jit(solution)/shard_map/cond
  190.2 14.1 %copy-start.19 = (bf16[256,3072]{1,0:T(8,128)(2,1)}, bf16[256,3072]{1,0:T(8,128)(2,1)S(1)}, u32[]{:S(2)}) copy-start(bf16[256,3072]{1,0:T(8,128)(2,1)S(1)} %convolution_convert_fusion) | copy-start | bytes 4718596 | tf_op jit(solution)/shard_map/cond
  204.3 1.3 copy-start.16
  205.6 7.0 copy-start.12
  206.0 9.4 %copy-start.53 = (f32[2,16,128]{2,1,0:T(8,128)}, f32[2,16,128]{2,1,0:T(8,128)S(1)}, u32[]{:S(2)}) copy-start(f32[2,16,128]{2,1,0:T(8,128)S(1)} %log_add_fusion) | copy-start | bytes 49156 | tf_op jit(solution)/shard_map/cond
  215.4 19.2 %slice-start.6 = ((s8[8388608]{0:T(1024)(128)(4,1)}), s8[4194304]{0:T(1024)(128)(4,1)S(1)}, s32[]{:S(2)}) async-start(s8[8388608]{0:T(1024)(128)(4,1)} %bitcast.281), calls=%async_computation.7 | async-start | bytes 8388608 | tf_op jit(solution)/shard_map/cond
  219.3 15.3 %slice-start.7 = ((s8[8388608]{0:T(1024)(128)(4,1)}), s8[4194304]{0:T(1024)(128)(4,1)S(1)}, s32[]{:S(2)}) async-start(s8[8388608]{0:T(1024)(128)(4,1)} %bitcast.281), calls=%async_computation.8 | async-start | bytes 8388608 | tf_op jit(solution)/shard_map/cond
  234.6 5.1 copy-start.8
  239.8 59.0 %collective-permute-start = (bf16[256,1024]{1,0:T(8,128)(2,1)}, bf16[256,1024]{1,0:T(8,128)(2,1)S(1)}, u32[]{:S(2)}, u32[]{:S(2)}) collective-permute-start(bf16[256,1024]{1,0:T(8,128)(2,1)} %get-tuple-element.280), channel_id=1, source_target_pairs={{0,16},{1,17},{2,18},{3,19},{4,20},{5,21},{6,22},{7,23},{8,24},{9,... | collective-permute-start | bytes 1572872 | tf_op jit(solution)/shard_map/ppermute | solution.py:28
  298.9 137.3 %copy-start.48 = (bf16[256,256]{1,0:T(8,128)(2,1)S(1)}, bf16[256,256]{1,0:T(8,128)(2,1)}, u32[]{:S(2)}) copy-start(bf16[256,256]{1,0:T(8,128)(2,1)} %get-tuple-element.301) | copy-start | bytes 393220
  298.9 137.3 %copy-start.54 = (f32[2,16,128,1]{2,1,0,3:T(8,128)S(1)}, f32[2,16,128,1]{2,1,0,3:T(8,128)}, u32[]{:S(2)}) copy-start(f32[2,16,128,1]{2,1,0,3:T(8,128)} %get-tuple-element.293) | copy-start | bytes 49156
  298.9 137.3 %copy-start.57 = (f32[2,128]{1,0:T(2,128)S(1)}, f32[2,128]{1,0:T(2,128)}, u32[]{:S(2)}) copy-start(f32[2,128]{1,0:T(2,128)} %copy-done.56) | copy-start | bytes 3076
  325.7 110.4 %collective-permute-start.2 = (bf16[256,1024]{1,0:T(8,128)(2,1)}, bf16[256,1024]{1,0:T(8,128)(2,1)S(1)}, u32[]{:S(2)}, u32[]{:S(2)}) collective-permute-start(bf16[256,1024]{1,0:T(8,128)(2,1)} %get-tuple-element.294), channel_id=1, source_target_pairs={{16,0},{17,1},{18,2},{19,3},{20,4},{21,5},{22,6},{23,7},{24,8},{25... | collective-permute-start | bytes 1572872 | tf_op jit(solution)/shard_map/ppermute | solution.py:28
  436.2 18.2 %copy-start.24 = (bf16[256,1024]{1,0:T(8,128)(2,1)}, bf16[256,1024]{1,0:T(8,128)(2,1)S(1)}, u32[]{:S(2)}) copy-start(bf16[256,1024]{1,0:T(8,128)(2,1)S(1)} %get-tuple-element.199) | copy-start | bytes 1572868 | tf_op jit(solution)/shard_map/cond
  437.9 16.5 %slice-start.4 = ((s8[8388608]{0:T(1024)(128)(4,1)}), s8[4194304]{0:T(1024)(128)(4,1)S(1)}, s32[]{:S(2)}) async-start(s8[8388608]{0:T(1024)(128)(4,1)} %bitcast.279), calls=%async_computation.5 | async-start | bytes 8388608 | tf_op jit(solution)/shard_map/cond
  439.7 14.8 %slice-start.5 = ((s8[8388608]{0:T(1024)(128)(4,1)}), s8[4194304]{0:T(1024)(128)(4,1)S(1)}, s32[]{:S(2)}) async-start(s8[8388608]{0:T(1024)(128)(4,1)} %bitcast.279), calls=%async_computation.6 | async-start | bytes 8388608 | tf_op jit(solution)/shard_map/cond
  454.4 4.6 copy-start.36
  454.4 7.4 copy-start.25
  459.0 3.8 copy-start.15
  460.8 1.0 copy-start.20
  462.0 0.8 copy-start.46
  484.5 2.3 copy-start.43
  486.3 1.0 copy-start.44
  486.3 1.9 copy-start.30
  505.1 5.4 copy-start.21
  505.1 5.4 copy-start.26
  510.1 2.1 copy-start.41
  524.4 11.6 %copy-start.27 = (bf16[256,1024]{1,0:T(8,128)(2,1)S(1)}, bf16[256,1024]{1,0:T(8,128)(2,1)}, u32[]{:S(2)}) copy-start(bf16[256,1024]{1,0:T(8,128)(2,1)} %copy-done.24) | copy-start | bytes 1572868 | tf_op jit(solution)/shard_map/cond
  543.4 0.7 copy-start.50
  544.1 3.0 collective-permute-start.1
  843.5 56.9 %collective-permute-start.4 = (bf16[64,1024]{1,0:T(8,128)(2,1)}, bf16[64,1024]{1,0:T(8,128)(2,1)S(1)}, u32[]{:S(2)}, u32[]{:S(2)}) collective-permute-start(bf16[64,1024]{1,0:T(8,128)(2,1)} %get-tuple-element.313), channel_id=1, source_target_pairs={{0,16},{16,0},{1,17},{17,1},{2,18},{18,2},{3,19},{19,3},{4,20},{20... | collective-permute-start | bytes 393224 | tf_op jit(solution)/shard_map/ppermute | solution.py:1325
  872.6 26.4 %collective-permute-start.5 = (f32[8,256]{1,0:T(8,128)}, f32[8,256]{1,0:T(8,128)S(1)}, u32[]{:S(2)}, u32[]{:S(2)}) collective-permute-start(f32[8,256]{1,0:T(8,128)} %get-tuple-element.314), channel_id=1, source_target_pairs={{0,16},{16,0},{1,17},{17,1},{2,18},{18,2},{3,19},{19,3},{4,20},{20... | collective-permute-start | bytes 24584 | tf_op jit(solution)/shard_map/ppermute | solution.py:1325
  890.6 2.3 copy-start.38
  892.2 3.3 copy-start.37
  892.2 9.8 %collective-permute-start.3 = (bf16[4096,256]{1,0:T(8,128)(2,1)}, bf16[4096,256]{1,0:T(8,128)(2,1)S(1)}, u32[]{:S(2)}, u32[]{:S(2)}) collective-permute-start(bf16[4096,256]{1,0:T(8,128)(2,1)} %broadcast_select_fusion), channel_id=1, source_target_pairs={{0,16},{16,0},{1,17},{17,1},{2,18},{18,2},{3,19},{19,3},{4,20},{20... | collective-permute-start | bytes 6291464 | tf_op jit(solution)/shard_map/ppermute | solution.py:1325
  895.4 2.5 copy-start.49
  895.4 5.0 copy-start.52
Sparse Core Ops, SparseCore 0:
  544.2 184.4 all-gather.2

commit v3 on v2

--- a/solution.py
+++ b/solution.py
@@ -535,23 +535,25 @@
     below = (sec, grp, pos - 1)
     partner = (1 - sec, grp, pos)
     barrier = pltpu.get_barrier_semaphore()
+    both = bool(last_order)
 
     def greet(device):
         pl.semaphore_signal(barrier, inc=1, device_id=device, device_id_type=MESH)
 
-    for device in beside + (partner,):
-        greet(device)
-
-    @pl.when(pos > 0)
-    def _():
-        greet(below)
-
-    @pl.when(pos < 3)
-    def _():
-        greet(above)
-
-    at_end = (pos == 0) | (pos == 3)
-    pl.semaphore_wait(barrier, jnp.where(at_end, 4, 5))
+    def meet():
+        for device in beside + ((partner,) if both else ()):
+            greet(device)
+
+        @pl.when(pos > 0)
+        def _():
+            greet(below)
+
+        @pl.when(pos < 3)
+        def _():
+            greet(above)
+
+        at_end = (pos == 0) | (pos == 3)
+        pl.semaphore_wait(barrier, jnp.where(at_end, 3, 4) + (1 if both else 0))
 
     turn = [pick(pos, v) for v in ((3, 1, 3, 1), (2, 3, 1, 2), (1, 2, 2, 3))]
 
@@ -679,16 +681,26 @@
     def hold():
         pl.semaphore_wait(gate, 1)
 
-    @pl.when(sec == 0)
-    def _():
-        run(first_order, None, let_go)
-
-    @pl.when(sec == 1)
-    def _():
-        run(last_order, hold, None)
-
-
-def gather_all(shards, first_order, last_order, whole_line):
+    if both:
+        meet()
+
+        @pl.when(sec == 0)
+        def _():
+            run(first_order, None, let_go)
+
+        @pl.when(sec == 1)
+        def _():
+            run(last_order, hold, None)
+
+    else:
+
+        @pl.when(sec == 0)
+        def _():
+            meet()
+            run(first_order, None, None)
+
+
+def gather_all(shards, first_order, last_order, whole_line, collective_id):
     count = len(shards)
     return pl.pallas_call(
         functools.partial(gather_kernel, count, first_order, last_order, whole_line),
@@ -696,21 +708,21 @@
         in_specs=[ANYWHERE] * count,
         out_specs=[ANYWHERE] * count,
         scratch_shapes=[
-            pltpu.SemaphoreType.DMA((8,)),
-            pltpu.SemaphoreType.DMA((8, 5)),
-            pltpu.SemaphoreType.DMA((8, 4)),
-            pltpu.SemaphoreType.DMA((8, 3, 4)),
-            pltpu.SemaphoreType.DMA((8, 3, 4)),
+            pltpu.SemaphoreType.DMA((count,)),
+            pltpu.SemaphoreType.DMA((count, 5)),
+            pltpu.SemaphoreType.DMA((count, 4)),
+            pltpu.SemaphoreType.DMA((count, 3, 4)),
+            pltpu.SemaphoreType.DMA((count, 3, 4)),
             pltpu.SemaphoreType.REGULAR,
         ]
         + [pltpu.VMEM(s.shape, s.dtype) for s in shards],
         compiler_params=pltpu.CompilerParams(
-            collective_id=0, has_side_effects=True, vmem_limit_bytes=24 << 20
+            collective_id=collective_id, has_side_effects=True, vmem_limit_bytes=24 << 20
         ),
     )(*shards)
 
 
-def swap_kernel(count_z, rows_ref, out_ref, own_sem, send_sem, recv_sem):
+def swap_kernel(rows_ref, ids_ref, out_ref, ids_out, own_sem, send_sem, recv_sem):
     sec = lax.axis_index("section")
     grp = lax.axis_index("group")
     pos = lax.axis_index("dp")
@@ -718,47 +730,49 @@
     @pl.when(sec == 0)
     def _():
         barrier = pltpu.get_barrier_semaphore()
-        for k in range(1, count_z):
-            pl.semaphore_signal(
-                barrier,
-                inc=1,
-                device_id=(sec, grp, lax.rem(pos + k, count_z)),
-                device_id_type=MESH,
+        peers = [(sec, grp, lax.rem(pos + k, 4)) for k in (1, 2, 3)]
+        sides = [(sec, grp ^ j, pos) for j in (1, 2, 3)]
+        for device in peers + sides:
+            pl.semaphore_signal(barrier, inc=1, device_id=device, device_id_type=MESH)
+        pl.semaphore_wait(barrier, 6)
+        copies = []
+        for k, device in enumerate(peers):
+            copies.append(
+                remote(rows_ref.at[device[2]], out_ref.at[pos], send_sem.at[k], recv_sem.at[k], device)
             )
-        pl.semaphore_wait(barrier, count_z - 1)
-        copies = []
-        for k in range(1, count_z):
-            to = lax.rem(pos + k, count_z)
-            copy = pltpu.make_async_remote_copy(
-                src_ref=rows_ref.at[to],
-                dst_ref=out_ref.at[pos],
-                send_sem=send_sem.at[k],
-                recv_sem=recv_sem.at[k],
-                device_id=(sec, grp, to),
-                device_id_type=MESH,
+        for k, device in enumerate(sides):
+            copies.append(
+                remote(ids_ref, ids_out.at[grp], send_sem.at[3 + k], recv_sem.at[3 + k], device)
             )
+        for copy in copies:
             copy.start()
-            copies.append(copy)
-        own = pltpu.make_async_copy(rows_ref.at[pos], out_ref.at[pos], own_sem)
-        own.start()
-        own.wait()
+        own_rows = pltpu.make_async_copy(rows_ref.at[pos], out_ref.at[pos], own_sem.at[0])
+        own_ids = pltpu.make_async_copy(ids_ref, ids_out.at[grp], own_sem.at[1])
+        own_rows.start()
+        own_ids.start()
+        own_rows.wait()
+        own_ids.wait()
         for copy in copies:
             copy.wait()
 
 
-def swap_rows(rows, count_z):
+def swap_rows(rows, ids, collective_id):
+    in_vmem = pl.BlockSpec(memory_space=pltpu.VMEM)
     return pl.pallas_call(
-        functools.partial(swap_kernel, count_z),
-        out_shape=jax.ShapeDtypeStruct(rows.shape, rows.dtype),
-        in_specs=[pl.BlockSpec(memory_space=pl.ANY)],
-        out_specs=pl.BlockSpec(memory_space=pl.ANY),
+        swap_kernel,
+        out_shape=[
+            jax.ShapeDtypeStruct(rows.shape, rows.dtype),
+            jax.ShapeDtypeStruct((4,) + ids.shape, ids.dtype),
+        ],
+        in_specs=[in_vmem] * 2,
+        out_specs=[in_vmem] * 2,
         scratch_shapes=[
-            pltpu.SemaphoreType.DMA,
-            pltpu.SemaphoreType.DMA((4,)),
-            pltpu.SemaphoreType.DMA((4,)),
+            pltpu.SemaphoreType.DMA((2,)),
+            pltpu.SemaphoreType.DMA((6,)),
+            pltpu.SemaphoreType.DMA((6,)),
         ],
-        compiler_params=pltpu.CompilerParams(collective_id=1, has_side_effects=True),
-    )(rows)
+        compiler_params=pltpu.CompilerParams(collective_id=collective_id, has_side_effects=True),
+    )(rows, ids)
 
 
 def strip_of(rows, columns):
@@ -782,16 +796,27 @@
     lax.fori_loop(0, rows // strip, body, 0)
 
 
-def reduce_kernel(kinds, *refs):
+def reduce_kernel(kinds, with_gains, only, *refs):
+    if only is None:
+        reduce_body(kinds, with_gains, *refs)
+    else:
+        pl.when(lax.axis_index("section") == only)(
+            functools.partial(reduce_body, kinds, with_gains, *refs)
+        )
+
+
+def reduce_body(kinds, with_gains, *refs):
     count = len(kinds)
+    more = 1 if with_gains else 0
     arrays = refs[:count]
-    gains = refs[count]
-    outs = refs[count + 1 : 2 * count + 1]
-    gain_out = refs[2 * count + 1]
-    rest = list(refs[2 * count + 2 :])
-    s1, r1, own_sem, s2, r2, s3, r3, s4, r4, fin_sem, sg, rg = rest[:12]
-    gain_own_sem, gain_in, gain_got = rest[12:15]
-    bufs = rest[15:]
+    outs = refs[count + more : 2 * count + more]
+    rest = list(refs[2 * count + 2 * more :])
+    s1, r1, own_sem, s2, r2, s3, r3, s4, r4, fin_sem = rest[:10]
+    bufs = rest[10 : 10 + 5 * count]
+    if with_gains:
+        gains = refs[count]
+        gain_out = refs[2 * count + 1]
+        gain_own_sem, sg, rg, gain_in, gain_got = rest[10 + 5 * count :]
     own, got1, got2, got3, fin = ([bufs[5 * a + b] for a in range(count)] for b in range(5))
     sec = lax.axis_index("section")
     grp = lax.axis_index("group")
@@ -803,17 +828,16 @@
     def other(j):
         return (sec, grp ^ steps[j - 1][0], lax.rem(pos + steps[j - 1][1], 4))
 
-    for j in range(1, 16):
-        pl.semaphore_signal(barrier, inc=1, device_id=other(j), device_id_type=MESH)
-    pl.semaphore_wait(barrier, 15)
-
-    live = [None if kind[1] is None else sec == kind[1] for kind in kinds]
+    if with_gains:
+        peers = [other(j) for j in range(1, 16)]
+    else:
+        peers = [(sec, grp ^ j, pos) for j in (1, 2, 3)] + [other(j) for j in (1, 2, 3)]
+    for device in peers:
+        pl.semaphore_signal(barrier, inc=1, device_id=device, device_id_type=MESH)
+    pl.semaphore_wait(barrier, len(peers))
 
     def when(a, run):
-        if live[a] is None:
-            run()
-        else:
-            pl.when(live[a])(run)
+        run()
 
     def rows_of(a):
         return outs[a].shape[0]
@@ -828,7 +852,8 @@
         device = other(j)
         return remote(gain_in.at[device[2]], gain_got.at[j - 1], sg.at[j - 1], rg.at[j - 1], device)
 
-    gain_load = pltpu.make_async_copy(gains, gain_in, gain_own_sem)
+    def gain_load():
+        return pltpu.make_async_copy(gains, gain_in, gain_own_sem)
 
     def ways(line):
         first = 0 if line < 2 else 1
@@ -1033,20 +1058,22 @@
 
         when(a, run)
 
-    plane_arrays = [a for a in range(count) if kinds[a][0] == "plane"]
-    line_arrays = [a for a in range(count) if kinds[a][0] == "line"]
+    plane_arrays = [a for a in range(count) if kinds[a] == "plane"]
+    line_arrays = [a for a in range(count) if kinds[a] == "line"]
     units = [(a, line) for a in plane_arrays for line in (0, 2, 1, 3)]
-    gain_load.start()
     ahead = 6
+    if with_gains:
+        gain_load().start()
     for unit in units[:2]:
         begin(*unit)
     for a in line_arrays:
         line_begin(a)
     for unit in units[2:ahead]:
         begin(*unit)
-    gain_load.wait()
-    for j in range(1, 16):
-        gain_copy(j).start()
+    if with_gains:
+        gain_load().wait()
+        for j in range(1, 16):
+            gain_copy(j).start()
     lag = 2
     finished = []
     for at in range(len(units) + lag + 4):
@@ -1072,12 +1099,13 @@
             finish(units[spot][0])
             finished.append(units[spot][0])
     pass_on(finished[-1])
-    for j in range(1, 16):
-        gain_copy(j).wait_recv()
-    total = gain_in[pos]
-    for j in range(15):
-        total = total + gain_got[j]
-    gain_out[...] = total
+    if with_gains:
+        for j in range(1, 16):
+            gain_copy(j).wait_recv()
+        total = gain_in[pos]
+        for j in range(15):
+            total = total + gain_got[j]
+        gain_out[...] = total
     for a in range(count):
 
         def run(a=a):
@@ -1086,7 +1114,7 @@
             own_out(a).wait()
             for way in range(4):
                 spread(a, way).wait_send()
-            if kinds[a][0] == "plane":
+            if kinds[a] == "plane":
                 for line in range(4):
                     for b in (0, 1):
                         send_first(a, line, b).wait_send()
@@ -1098,51 +1126,46 @@
                     cross(a, k).wait_send()
 
         when(a, run)
-    for j in range(1, 16):
-        gain_copy(j).wait_send()
-
-
-def reduce_all(arrays, gains, kinds, collective_id):
+    if with_gains:
+        for j in range(1, 16):
+            gain_copy(j).wait_send()
+
+
+def reduce_all(arrays, gains, kinds, only, collective_id):
     count = len(arrays)
+    more = 0 if gains is None else 1
     outs = [jax.ShapeDtypeStruct((x.shape[0] // 4, x.shape[1]), x.dtype) for x in arrays]
     buffers = []
     for x, kind in zip(arrays, kinds):
         rows, columns = x.shape[0] // 4, x.shape[1]
         part = rows // 4
-        if kind[0] == "plane":
+        if kind == "plane":
             shapes = [(4, 2, part, columns), (4, 2, part, columns), (4, part, columns)]
         else:
             shapes = [(rows, columns), (3, rows, columns), (8, 128)]
         shapes += [(3, part, columns), (part, columns)]
         buffers += [pltpu.VMEM(shape, x.dtype) for shape in shapes]
     dma = pltpu.SemaphoreType.DMA
-    return pl.pallas_call(
-        functools.partial(reduce_kernel, kinds),
-        out_shape=outs + [jax.ShapeDtypeStruct(gains.shape[1:], gains.dtype)],
-        in_specs=[ANYWHERE] * (count + 1),
-        out_specs=[ANYWHERE] * count + [pl.BlockSpec(memory_space=pltpu.VMEM)],
-        scratch_shapes=[
-            dma((count, 4, 2)),
-            dma((count, 4, 2)),
-            dma((count, 4, 2)),
-            dma((count, 4)),
-            dma((count, 4)),
-            dma((count, 4)),
-            dma((count, 4)),
-            dma((count, 4)),
-            dma((count, 4)),
-            dma((count,)),
+    scratch = [dma((count, 4, 2))] * 3 + [dma((count, 4))] * 6 + [dma((count,))] + buffers
+    if more:
+        outs.append(jax.ShapeDtypeStruct(gains.shape[1:], gains.dtype))
+        scratch += [
+            dma,
             dma((15,)),
             dma((15,)),
-            dma,
             pltpu.VMEM(gains.shape, gains.dtype),
             pltpu.VMEM((15,) + gains.shape[1:], gains.dtype),
         ]
-        + buffers,
+    return pl.pallas_call(
+        functools.partial(reduce_kernel, kinds, bool(more), only),
+        out_shape=outs,
+        in_specs=[ANYWHERE] * (count + more),
+        out_specs=[ANYWHERE] * count + [pl.BlockSpec(memory_space=pltpu.VMEM)] * more,
+        scratch_shapes=scratch,
         compiler_params=pltpu.CompilerParams(
             collective_id=collective_id, has_side_effects=True, vmem_limit_bytes=58 << 20
         ),
-    )(*arrays, gains)
+    )(*arrays, *((gains,) if more else ()))
 
 
 def block_forward(hidden, key_valid, weights):
@@ -1181,13 +1204,12 @@
     ).reshape(seqs * length, -1)
     grad_normed = product_nt(grad_qkv, qkv_weight)
     grad_in_norm, grad_gain_attn = norm_back(hidden, gain_attn, grad_normed)
-    grads = (
-        product_tn(normed_in, grad_qkv).astype(jnp.bfloat16),
-        product_tn(mixed_rows, grad_mid_low).astype(jnp.bfloat16),
-        product_tn(mlp_in, grad_pre).astype(jnp.bfloat16),
-        product_tn(activated, grad_low).astype(jnp.bfloat16),
-    )
-    return grad_mid + grad_in_norm, (grad_gain_attn, grad_gain_mlp), grads
+    pairs = (normed_in, grad_qkv), (mixed_rows, grad_mid_low), (mlp_in, grad_pre), (activated, grad_low)
+    return grad_mid + grad_in_norm, (grad_gain_attn, grad_gain_mlp), pairs
+
+
+def weight_grads(pairs):
+    return tuple(product_tn(rows, grads).astype(jnp.bfloat16) for rows, grads in pairs)
 
 
 def nothing_like(run):
@@ -1196,6 +1218,10 @@
 
 def only_on(live, run):
     return lax.cond(live, run, lambda: nothing_like(run))
+
+
+def after(value, *others):
+    return lax.optimization_barrier((value,) + others)[0]
 
 
 def per_device(
@@ -1214,7 +1240,6 @@
     ln_final,
     w_out,
 ):
-    count_z = lax.axis_size("dp")
     sec = lax.axis_index("section")
     pos = lax.axis_index("dp")
     first_section = sec == 0
@@ -1222,20 +1247,17 @@
     rows = tokens.shape[0]
     seqs = lengths.shape[0]
     length = rows // seqs
-    width = w_out.shape[0] * count_z
+    width = w_out.shape[0] * 4
     emb = w_out.shape[1]
     vocab_part = embed_table.shape[0]
     gains = jnp.concatenate(
         [ln_attn, ln_mlp, ln_final[None], jnp.zeros((13, ln_final.shape[0]), jnp.bfloat16)], 0
     )
-    shards = (w_qkv[0], w_proj[0], w_up[0], w_down[0], w_in, w_out, embed_table, gains)
-    wholes = gather_all(shards, (7, 4, 0, 1, 2, 3), (7, 0, 1, 2, 3, 5, 6), (7, 1))
-    all_tokens = lax.all_gather(tokens, ("group", "dp"), axis=0, tiled=True)
-    line_tokens = lax.dynamic_slice_in_dim(
-        all_tokens, lax.axis_index("group") * count_z * rows, count_z * rows, 0
-    )
-    qkv_weight, proj_weight, up_weight, down_weight, in_weight, out_weight, table_full, gain_all = wholes
-    gain_all = gain_all.reshape(count_z, 16, -1).astype(jnp.float32)
+    ids = jnp.concatenate([tokens.reshape(-1, 128), jnp.zeros((8 - rows // 128, 128), jnp.int32)], 0)
+    shards = (w_qkv[0], w_proj[0], w_up[0], w_down[0], w_in, w_out, gains, ids)
+    wholes = gather_all(shards, (7, 6, 4, 0, 1, 2, 3), (6, 0, 1, 2, 3, 5), (6, 7, 1), 0)
+    qkv_weight, proj_weight, up_weight, down_weight, in_weight, out_weight, gain_all, line_ids = wholes
+    gain_all = gain_all.reshape(4, 16, -1).astype(jnp.float32)
     gain_attn = gain_all[:, 0].reshape(-1)
     gain_mlp = gain_all[:, 1].reshape(-1)
     final_gain = gain_all[:, 2].reshape(-1)
@@ -1244,12 +1266,13 @@
     loss_scale = LOSS_GAIN / math.sqrt(rows * lax.axis_size(("group", "dp")))
 
     def look_up():
-        local = line_tokens - pos * vocab_part
+        local = line_ids.reshape(4, 8, 128)[:, : rows // 128].reshape(-1) - pos * vocab_part
         hit = local[:, None] == lax.broadcasted_iota(jnp.int32, (1, vocab_part), 1)
         return product(hit.astype(jnp.bfloat16), embed_table).astype(jnp.bfloat16)
 
-    looked_parts = only_on(first_section, look_up).reshape(count_z, rows, emb)
-    looked_parts = swap_rows(looked_parts, count_z)
+    looked_parts = only_on(first_section, look_up).reshape(4, rows, emb)
+    looked_parts, all_ids = swap_rows(looked_parts, line_ids, 1)
+    all_tokens = all_ids.reshape(16, 8, 128)[:, : rows // 128].reshape(-1)
     noise_level = jnp.exp(LOG_LOW + levels.astype(jnp.float32) * (LOG_SPAN / (LEVELS - 1)))
     scale_in = lax.rsqrt(EMB_VAR + noise_level * noise_level)
     row_level = jnp.repeat(noise_level, length)[:, None]
@@ -1265,72 +1288,96 @@
 
     out_first, kept_first, mixed_in = only_on(first_section, front)
     x_second = passed_along(out_first, "section", 1)
+    (table_full,) = gather_all((after(embed_table, x_second),), (0,), (), (), 2)
 
     def back():
         hidden_out, kept = block_forward(x_second.astype(jnp.float32), key_valid, weights)
-        grad_top, entropy, gain_step, tail_now = tail_pass(
-            hidden_out,
-            tokens,
-            key_valid.reshape(-1),
-            final_gain,
-            out_weight,
-            table_full,
-            loss_scale,
-        )
-        grad_logits, projected, final_in, grad_proj = tail_now
-        grad_start, gain_pair, grads = block_backward(kept, grad_top, key_valid, weights)
-        return (
-            grad_start.astype(jnp.bfloat16),
-            entropy.astype(jnp.bfloat16),
-            gain_pair,
-            grads,
-            product_tn(grad_logits, projected).astype(jnp.bfloat16),
-            product_tn(final_in, grad_proj).astype(jnp.bfloat16),
-            gain_step,
-        )
-
-    grad_second, loss_low, gain_pair_b, grads_b, table_b, out_b, gain_final = only_on(last_section, back)
-    grad_first, loss_first = passed_along((grad_second, loss_low), "section", -1)
-    token_loss = jnp.where(first_section, loss_first, loss_low)
+        final_in = normed(hidden_out, final_gain).astype(jnp.bfloat16)
+        projected = product(final_in, out_weight).astype(jnp.bfloat16)
+        return projected, final_in, hidden_out, kept
+
+    projected_b, final_in, hidden_out, kept_second = only_on(last_section, back)
+    projected = passed_along(after(projected_b, table_full), "section", -1)
+
+    def vocabulary():
+        logits = product_nt(projected, table_full)
+        row_max = jnp.max(logits, -1, keepdims=True)
+        log_total = row_max + jnp.log(jnp.sum(jnp.exp(logits - row_max), -1, keepdims=True))
+        vocab_ids = lax.broadcasted_iota(jnp.int32, logits.shape, 1)
+        target_hit = vocab_ids == tokens[:, None]
+        picked = jnp.sum(jnp.where(target_hit, logits, 0.0), -1)
+        valid = key_valid.reshape(-1)
+        entropy = jnp.where(valid, log_total[:, 0] - picked, 0.0).astype(jnp.bfloat16)
+        scale = jnp.where(valid, loss_scale, 0.0)[:, None]
+        grad_logits = (
+            (jnp.exp(logits - log_total) - target_hit.astype(jnp.float32)) * scale
+        ).astype(jnp.bfloat16)
+        grad_proj = product(grad_logits, table_full).astype(jnp.bfloat16)
+        return grad_proj, entropy, grad_logits
+
+    grad_proj_a, loss_low, grad_logits = only_on(first_section, vocabulary)
+    grad_proj = passed_along(grad_proj_a, "section", 1)
+    grad_logits = after(grad_logits, grad_proj)
+    table_g = only_on(
+        first_section, lambda: product_tn(grad_logits, projected).astype(jnp.bfloat16)
+    )
+    (table_r,) = reduce_all((table_g,), None, ("plane",), 0, 3)
+
+    def back_again():
+        grad_final = product_nt(grad_proj, out_weight)
+        grad_top, gain_final = norm_back(hidden_out, final_gain, grad_final)
+        grad_start, gain_pair, pairs = block_backward(kept_second, grad_top, key_valid, weights)
+        return grad_start.astype(jnp.bfloat16), gain_pair + (gain_final,), pairs
+
+    grad_second, gains_b, pairs_b = only_on(last_section, back_again)
+    grad_first = passed_along(after(grad_second, table_r), "section", -1)
+    pairs_b = after(pairs_b, grad_first)
+    shape = in_weight.shape
 
     def front_back():
-        grad_start, gain_pair, grads = block_backward(
+        grad_start, gain_pair, pairs = block_backward(
             kept_first, grad_first.astype(jnp.float32), key_valid, weights
         )
         grad_low = grad_start.astype(jnp.bfloat16)
         looked_grad = (product_nt(grad_low, in_weight) * row_scale).astype(jnp.bfloat16)
-        return gain_pair, grads, product_tn(mixed_in, grad_low).astype(jnp.bfloat16), looked_grad
+        edge = product_tn(mixed_in, grad_low).astype(jnp.bfloat16)
+        return gain_pair + (jnp.zeros_like(final_gain),), weight_grads(pairs), edge, looked_grad
 
     def end_back():
-        shape = in_weight.shape
-        packed = out_b.reshape(count_z, shape[0] // count_z, shape[1]).reshape(shape)
-        return gain_pair_b, grads_b, packed, jnp.zeros((rows, emb), jnp.bfloat16)
-
-    gain_pair, grads, edge_g, looked_grad = lax.cond(first_section, front_back, end_back)
-    gain_rows = jnp.stack([gain_pair[0], gain_pair[1], gain_final], 0)
-    gain_rows = jnp.concatenate([gain_rows, jnp.zeros((5, width), jnp.float32)], 0)
-    gain_rows = gain_rows.reshape(8, count_z, width // count_z).transpose(1, 0, 2)
-    order = (table_b, grads[2], grads[3], edge_g, grads[1], grads[0])
-    kinds = (("plane", 1),) + (("plane", None),) * 4 + (("line", None),)
-    table_r, up_r, down_r, edge_r, proj_r, qkv_r, gain_r = reduce_all(order, gain_rows, kinds, 2)
+        edge = product_tn(final_in, grad_proj).astype(jnp.bfloat16)
+        edge = edge.reshape(4, shape[0] // 4, shape[1]).reshape(shape)
+        return gains_b, weight_grads(pairs_b), edge, jnp.zeros((rows, emb), jnp.bfloat16)
+
+    gain_set, grads, edge_g, looked_grad = lax.cond(first_section, front_back, end_back)
+    gain_rows = jnp.concatenate([jnp.stack(gain_set, 0), jnp.zeros((5, width), jnp.float32)], 0)
+    gain_rows = gain_rows.reshape(8, 4, width // 4).transpose(1, 0, 2)
+    order = (grads[2], grads[3], edge_g, grads[1], grads[0])
+    kinds = ("plane",) * 4 + ("line",)
+    up_r, down_r, edge_r, proj_r, qkv_r, gain_r = reduce_all(order, gain_rows, kinds, None, 4)
     looked_all = lax.all_gather(looked_grad, ("group", "dp"), axis=0, tiled=True)
 
     def add_looked():
         local = all_tokens - pos * vocab_part
         hit = lax.broadcasted_iota(jnp.int32, (vocab_part, 1), 0) == local[None, :]
-        return product(hit.astype(jnp.bfloat16), looked_all).astype(jnp.bfloat16)
-
-    looked_sum = only_on(first_section, add_looked)
-    mine = (jnp.where(first_section, looked_sum, table_r), edge_r, gain_r)
+        looked_sum = product(hit.astype(jnp.bfloat16), looked_all)
+        return (looked_sum + table_r.astype(jnp.float32)).astype(jnp.bfloat16)
+
+    mine = (only_on(first_section, add_looked), edge_r, gain_r, loss_low)
     theirs = lax.ppermute(mine, "section", [(0, 1), (1, 0)])
-    table_out = mine[0].astype(jnp.float32) + theirs[0].astype(jnp.float32)
-    in_r = jnp.where(first_section, edge_r, theirs[1]).astype(jnp.float32)
-    out_r = jnp.where(first_section, theirs[1], edge_r).astype(jnp.float32).reshape(-1, emb)
-    final_r = jnp.where(first_section, theirs[2][2], gain_r[2])
+
+    def pair_of(at):
+        low = jnp.where(first_section, mine[at], theirs[at])
+        high = jnp.where(first_section, theirs[at], mine[at])
+        return low, high
+
+    table_out = pair_of(0)[0].astype(jnp.float32)
+    in_r, out_r = pair_of(1)
+    final_r = pair_of(2)[1][2]
+    token_loss = pair_of(3)[0]
     return (
         token_loss,
         table_out,
-        in_r,
+        in_r.astype(jnp.float32),
         gain_r[0][None],
         qkv_r.astype(jnp.float32)[None],
         proj_r.astype(jnp.float32)[None],
@@ -1338,7 +1385,7 @@
         up_r.astype(jnp.float32)[None],
         down_r.astype(jnp.float32)[None],
         final_r,
-        out_r,
+        out_r.astype(jnp.float32).reshape(-1, emb),
     )
 
 

time: 922 us -> 913 us (level)
  Pallas kernels: 416 us -> 554 us
  waiting for transfers between devices: 112 us -> 8.15 us
  starting transfers between devices: 89.1 us -> 21.8 us
  blocking collectives: 45 us -> 0 us
  matrix products: 103 us -> 128 us
  loops' own time: 8.9 us -> 28.2 us
  other arithmetic: 32.6 us -> 47.1 us
    ppermute x3 -> x4, waiting for transfers between devices: 112 us -> 7.1 us  [passed_along(): return lax.ppermute(x, axis, pairs)]
    pallas_call x2 -> x3, Pallas kernels: 304 us -> 386 us  [the longest x2 376 us: reduce_all(): pl.pallas_call(functools.partial(reduce_kernel, kinds, bool(more), only),...]
    pallas_call x1 -> x2, Pallas kernels: 112 us -> 168 us  [gather_all(): pl.pallas_call(functools.partial(gather_kernel, count, first_order, last_...]
    all_gather x1 -> x0, blocking collectives: 45 us -> none  [per_device(): all_tokens = lax.all_gather(tokens, ('group', 'dp'), axis=0, tiled=True)]
    ppermute x3 -> x4, starting transfers between devices: 59.9 us -> 21.1 us  [passed_along(): return lax.ppermute(x, axis, pairs)]
    another operation x10 -> x68, local copies, waits for them, and re-layouts: 18.8 us -> 52.3 us
    cond x59 -> x26, local copies, waits for them, and re-layouts: 41.9 us -> 10.1 us  [the longest x4 24 us: per_device(): lax.cond(first_section, front_back, end_back)]
    ppermute x3 -> x4, starting transfers between devices: 29.2 us -> 0.71 us  [per_device(): theirs = lax.ppermute(mine, 'section', [(0, 1), (1, 0)])]
  transfers between devices with their start and end apart: 7 -> 9, of which waited for: 3 -> 5; matrix products, arithmetic and copies ran while one was open for 3% -> 3% of each run, Pallas kernels for 32% -> 35%
where the time goes in v3:
time: 913 us; the launch traced here: 896 us
  Pallas kernels  554 us (61%)
  matrix products  128 us (14%)
  local copies, waits for them, and re-layouts  94.5 us (10%)
  other arithmetic  47.1 us (5%)
  loops' own time  28.2 us (3%)
  starting transfers between devices  21.8 us (2%)
  between operations  14.6 us (2%)
    pallas_call x2, Pallas kernels, reduce_all(): pl.pallas_call(functools.partial(reduce_kernel, kinds, bool(more), only),...  376 us
    pallas_call x2, Pallas kernels, gather_all(): pl.pallas_call(functools.partial(gather_kernel, count, first_order, last_...  168 us
    another operation x68, local copies, waits for them, and re-layouts  52.3 us
    dot_general x8, matrix products, product(): return jnp.dot(left_side, right_side, preferred_element_type=jnp.float32)  51 us
    dot_general x6, matrix products, product_nt(): lax.dot_general(left_side, right_side, (((1,), (1,)), ((), ())), preferre...  34 us
    dot_general x6, matrix products, product_tn(): lax.dot_general(left_side, right_side, (((0,), (0,)), ((), ())), preferre...  32 us
    another operation x7, loops' own time, only_on(): return lax.cond(live, run, lambda: nothing_like(run))  24.1 us
    ppermute x4, starting transfers between devices, passed_along(): return lax.ppermute(x, axis, pairs)  21.1 us
  transfers between devices with their start and end apart: 9, of which 5 were waited for; matrix products, arithmetic and copies ran while one was open for 3% of the time, Pallas kernels for 35%

profile of v3, /device:TPU:0, one launch (start us, length us, event | category | flops | bytes accessed | tf_op | source)
XLA Modules:
  0.0 896.4 jit_solution(18028930880972738442)
XLA Ops:
  16.9 123.7 %shard_map.222 = (bf16[1024,3072]{1,0:T(8,128)(2,1)}, bf16[1024,1024]{1,0:T(8,128)(2,1)}, bf16[1024,4096]{1,0:T(8,128)(2,1)}, bf16[4096,1024]{1,0:T(8,128)(2,1)}...) custom-call(bf16[256,3072]{1,0:T(8,128)(2,1)S(1)} %bitcast.254, ...), custom_call_target="tpu_custom_call" | custom-call | tf_op jit(solution)/shard_map/pallas_call | solution.py:705
  140.6 2.9 conditional.9
  140.7 2.9 fusion.2
  143.5 10.0 %shard_map.223 = (bf16[4,256,256]{2,1,0:T(8,128)(2,1)S(1)}, s32[4,32,128]{2,1,0:T(8,128)}) custom-call(bf16[4,256,256]{2,1,0:T(8,128)(2,1)S(1)} %get-tuple-element.724.rows_ref, s32[32,128]{1,0:T(8,128)S(1)} %get-tuple-element.375.ids_ref), custom_call_target="tpu_custom_call" | custom-call | tf_op jit(solution)/shard_map/pallas_call | solution.py:761
  154.4 55.1 %conditional.10 = (bf16[256,1024]{1,0:T(8,128)(2,1)}, f32[256,1024]{1,0:T(8,128)S(1)}, bf16[256,1024]{1,0:T(8,128)(2,1)}, bf16[256,3072]{1,0:T(8,128)(2,1)}, f32...) conditional(s32[]{:T(128)} %convert_element_type.226, () %tuple.78, ...), branch_computations={%region_2.0_spmd, %region_3.11_spmd} | conditional | flops 6789526016 | bytes 117519936 | solution.py:1220
  156.3 4.8 convolution_convert_fusion
  161.1 3.7 reshape.383
  164.9 3.8 fusion.106
  168.7 2.8 copy.131
  171.4 2.8 copy.130
  174.2 1.9 fusion.108
  176.5 2.8 copy.129
  182.3 2.8 fusion.109
  185.1 1.6 multiply_reduce_fusion
  186.7 2.2 multiply_convert_fusion
  188.9 15.2 %fusion.5 = (bf16[256,4096]{1,0:T(8,128)(2,1)}, f32[256,4096]{1,0:T(8,128)}) fusion(bf16[256,1024]{1,0:T(8,128)(2,1)} %multiply_convert_fusion, bf16[1024,4096]{1,0:T(8,128)(2,1)} %get-tuple-element.214), kind=kOutput, calls=%fused_computation.8 | convolution fusion | flops 2215641088 | bytes 15204352 | tf_op jit(solution)/shard_map/cond/branch_1_fun/dot_general | solution.py:32
  204.2 5.1 fusion.13
  209.4 17.2 %collective-permute-start = (bf16[256,1024]{1,0:T(8,128)(2,1)}, bf16[256,1024]{1,0:T(8,128)(2,1)S(1)}, u32[]{:S(2)}, u32[]{:S(2)}) collective-permute-start(bf16[256,1024]{1,0:T(8,128)(2,1)} %get-tuple-element.383), channel_id=1, source_target_pairs={{0,16},{1,17},{2,18},{3,19},{4,20},{5,21},{6,22},{7,23},{8,24},{9,... | collective-permute-start | bytes 1572872 | tf_op jit(solution)/shard_map/ppermute | solution.py:28
  226.7 1.7 collective-permute-done
  228.4 44.0 %shard_map.224 = bf16[16384,256]{1,0:T(8,128)(2,1)} custom-call(bf16[4096,256]{1,0:T(8,128)(2,1)} %refs_0_), custom_call_target="tpu_custom_call" | custom-call | tf_op jit(solution)/shard_map/pallas_call | solution.py:705
  272.4 19.5 %conditional.11 = (bf16[256,256]{1,0:T(8,128)(2,1)S(1)}, bf16[256,1024]{1,0:T(8,128)(2,1)}, f32[256,1024]{1,0:T(8,128)}, f32[256,1024]{1,0:T(8,128)S(1)}, bf16[2...) conditional(s32[]{:T(128)} %convert_element_type.227, () %tuple.77, ...), branch_computations={%region_11.12_spmd, %region_12.21_spmd} | conditional | flops 6790902272 | bytes 117333608 | solution.py:1220
  279.5 2.5 broadcast.660
  293.2 1.9 collective-permute-done.1
  295.2 33.9 %conditional.24 = (bf16[256,256]{1,0:T(8,128)(2,1)S(1)}, bf16[256]{0:T(256)(128)(2,1)S(1)}, bf16[256,16384]{1,0:T(8,128)(2,1)}) conditional(s32[]{:T(128)} %convert_element_type.226, () %tuple.76, (bf16[256,256]{1,0:T(8,128)(2,1)S(1)}, bf16[16384,256]{1,0:T(8,128)(2,1)}, s32[256]{0:T(256)S(1)}, pred[2,128]{1,0:T(4,128)(4,1)S(1)}) %tuple.184), branch_computations={%region_21.22_spmd, %region_22.26_spmd} | conditional | flops 4345364992 | bytes 176437120 | solution.py:1220
  295.2 11.5 %fusion.114 = (f32[256]{0:T(256)S(1)}, f32[256,16384]{1,0:T(8,128)}) fusion(bf16[256,256]{1,0:T(8,128)(2,1)S(1)} %get-tuple-element.226, bf16[16384,256]{1,0:T(8,128)(2,1)} %get-tuple-element.227), kind=kOutput, calls=%fused_computation.290 | convolution fusion | flops 2151677696 | bytes 25297920 | tf_op jit(solution)/shard_map/cond/branch_1_fun/dot_general | solution.py:42
  306.7 9.8 %select_reduce_fusion = (f32[256]{0:T(256)S(1)}, f32[256]{0:T(256)S(1)}) fusion(f32[256,16384]{1,0:T(8,128)} %get-tuple-element.600, s32[256]{0:T(256)S(1)} %get-tuple-element.228, f32[256]{0:T(256)S(1)} %get-tuple-element.599), kind=kLoop, calls=%fused_computation.96 | loop fusion | flops 20971008 | bytes 16781312 | tf_op jit(solution)/shard_map/cond/branch_1_fun/reduce_sum | solution.py:1308
  317.3 6.0 multiply_convert_fusion.6
  323.4 5.7 convolution_convert_fusion.5
  331.4 9.0 %conditional.26 = (bf16[16384,256]{1,0:T(8,128)(2,1)}) conditional(s32[]{:T(128)} %convert_element_type.226, () %tuple.89, (bf16[256,16384]{1,0:T(8,128)(2,1)}, bf16[256,256]{1,0:T(8,128)(2,1)S(1)}) %tuple.91), branch_computations={%region_44.45_spmd, %region_45.46_spmd} | conditional | flops 2151677952 | bytes 16908296 | solution.py:1220
  331.4 9.0 %convolution_convert_fusion.8 = bf16[16384,256]{1,0:T(8,128)(2,1)} fusion(bf16[256,16384]{1,0:T(8,128)(2,1)} %get-tuple-element.250, bf16[256,256]{1,0:T(8,128)(2,1)S(1)} %get-tuple-element.251), kind=kOutput, calls=%fused_computation.178 | convolution fusion | flops 2151677952 | bytes 16908288 | tf_op jit(solution)/shard_map/cond/branch_1_fun/dot_general | solution.py:36
  340.4 66.8 %shard_map.225 = bf16[4096,256]{1,0:T(8,128)(2,1)} custom-call(bf16[16384,256]{1,0:T(8,128)(2,1)} %get-tuple-element.725.refs_0_), custom_call_target="tpu_custom_call" | custom-call | tf_op jit(solution)/shard_map/pallas_call | solution.py:1159
  407.3 24.3 %conditional.25 = (bf16[256,1024]{1,0:T(8,128)(2,1)S(1)}, f32[1024]{0:T(1024)S(1)}, f32[1024]{0:T(1024)S(1)}, f32[1024]{0:T(1024)S(1)}, bf16[256,1024]{1,0:T(8,1...) conditional(s32[]{:T(128)} %convert_element_type.227, () %tuple.87, ...), branch_computations={%region_26.27_spmd, %region_27.44_spmd} | conditional | flops 7012873728 | bytes 227823360 | solution.py:1220
  432.8 2.5 collective-permute-done.4
  435.4 109.4 %conditional.27 = (f32[1024]{0:T(1024)S(1)}, f32[1024]{0:T(1024)S(1)}, f32[1024]{0:T(1024)S(1)}, bf16[4096,1024]{1,0:T(8,128)(2,1)}, bf16[256,256]{1,0:T(8,128)(...) conditional(s32[]{:T(128)} %convert_element_type.226, ...), branch_computations={%region_46.47_spmd, %region_47.59_spmd} | conditional | flops 13593079808 | bytes 266722144
  440.6 1.7 multiply_reduce_fusion.20
  442.3 14.7 %fusion.67 = bf16[256,4096]{1,0:T(8,128)(2,1)S(1)} fusion(f32[256,4096]{1,0:T(8,128)} %get-tuple-element.270, bf16[256,1024]{1,0:T(8,128)(2,1)S(1)} %get-tuple-element.269, bf16[4096,1024]{1,0:T(8,128)(2,1)} %get-tuple-element.271), kind=kOutput, calls=%fused_computation.190 | convolution fusion | flops 2222981120 | bytes 15204352 | tf_op jit(solution)/shard_map/cond/branch_1_fun/dot_general | solution.py:42
  457.1 4.5 multiply_reduce_fusion.17
  461.6 1.8 fusion.105
  466.1 1.6 reshape.388
  467.8 2.8 copy.84
  470.5 3.4 reshape.387
  474.0 3.5 fusion.116
  477.4 1.6 copy.138
  479.1 1.6 copy.139
  480.7 2.0 subtract_exponential_fusion.1
  482.7 2.7 fusion.82
  485.3 2.8 copy.140
  488.1 1.8 multiply_reduce_fusion.15
  491.8 1.6 copy.89
  493.5 2.2 multiply_reduce_fusion.16
  495.7 7.3 fusion.119
  504.8 6.7 convert_bitcast_fusion
  511.4 11.3 %copy.110 = bf16[1024,4096]{1,0:T(8,128)(2,1)} copy(bf16[1024,4096]{0,1:T(8,128)(2,1)} %convert_bitcast_fusion) | data formatting | bytes 16777216 | tf_op jit(solution)/shard_map/conditional
  523.4 3.1 convert_bitcast_fusion.2
  526.5 3.9 copy.114
  530.4 5.5 convert_bitcast_fusion.1
  536.0 8.7 copy.116
  547.9 309.3 %shard_map.226 = (bf16[256,4096]{1,0:T(8,128)(2,1)}, bf16[1024,1024]{1,0:T(8,128)(2,1)}, bf16[64,1024]{1,0:T(8,128)(2,1)}, bf16[256,1024]{1,0:T(8,128)(2,1)}, bf...) custom-call(bf16[1024,4096]{1,0:T(8,128)(2,1)} %get-tuple-element.546.refs_0_, bf16[4096,1024]{1,0:T(8,128)(2,1)} %get-tuple-element.437.refs_1_, ...), custom_call_target="tpu_custom_call" | custom-call | tf_op jit(solution)/shard_map/pallas_call | solution.py:1159
  857.8 3.4 bitcast_convert_fusion.2
  861.2 15.1 %conditional.28 = (bf16[4096,256]{1,0:T(8,128)(2,1)S(1)}) conditional(s32[]{:T(128)} %convert_element_type.226, () %tuple.86, (s32[4,32,128]{2,1,0:T(8,128)}, s32[]{:T(128)}, bf16[4096,256]{1,0:T(8,128)(2,1)}, bf16[4096,256]{1,0:T(8,128)(2,1)}) %tuple.96), branch_computations={%region_59.60_spmd, %region_60.61_spmd} | conditional | flops 8609861632 | bytes 6340632 | solution.py:1220
  862.1 14.2 %fusion.100 = bf16[4096,256]{1,0:T(8,128)(2,1)S(1)} fusion(bf16[4096,256]{1,0:T(8,128)(2,1)} %get-tuple-element.287, s32[4096]{0:T(1024)S(1)} %bitcast.290, bf16[4096,256]{1,0:T(8,128)(2,1)} %get-tuple-element.288), kind=kOutput, calls=%fused_computation.261 | convolution fusion | flops 8609857536 | bytes 6307840 | tf_op jit(solution)/shard_map/cond/branch_1_fun/dot_general | solution.py:32
  876.4 4.2 bitcast_convert_fusion
  880.6 2.5 bitcast_convert_fusion.1
  887.1 2.3 select_convert_fusion
  (207 shorter events, 56.1 us)
Async XLA Ops:
  7.2 854.1 %all-gather.2.cloned.1.call-start = ((), (), s32[]{:S(2)}) async-start(), calls=%async_computation | async-start | bytes 2228224 | tf_op jit(solution)/shard_map/all_gather | solution.py:1357
  9.4 1.6 copy-start
  11.0 1.6 copy-start.1
  12.6 1.4 copy-start.2
  14.0 1.0 copy-start.3
  15.1 0.9 copy-start.4
  16.0 0.9 copy-start.5
  16.9 123.7 %copy-start.30 = (bf16[4096,256]{1,0:T(8,128)(2,1)S(1)}, bf16[4096,256]{1,0:T(8,128)(2,1)}, u32[]{:S(2)}) copy-start(bf16[4096,256]{1,0:T(8,128)(2,1)} %refs_0_) | copy-start | bytes 6291460
  140.6 13.2 %copy-start.32 = (bf16[256,1024]{1,0:T(8,128)(2,1)}, bf16[256,1024]{1,0:T(8,128)(2,1)S(1)}, u32[]{:S(2)}) copy-start(bf16[256,1024]{1,0:T(8,128)(2,1)S(1)} %get-tuple-element.377) | copy-start | bytes 1572868
  140.6 13.0 %copy-start.60 = (s32[2]{0:T(128)S(1)}, s32[2]{0:T(128)}, u32[]{:S(2)}) copy-start(s32[2]{0:T(128)} %param.32) | copy-start | bytes 28
  140.6 13.0 %copy-start.61 = (s32[2]{0:T(128)S(1)}, s32[2]{0:T(128)}, u32[]{:S(2)}) copy-start(s32[2]{0:T(128)} %param.31) | copy-start | bytes 28
  140.6 13.2 %copy-start.48 = (bf16[256,256]{1,0:T(8,128)(2,1)S(1)}, bf16[256,256]{1,0:T(8,128)(2,1)}, u32[]{:S(2)}) copy-start(bf16[256,256]{1,0:T(8,128)(2,1)} %param.33) | copy-start | bytes 393220
  153.8 0.6 copy-start.55
  154.6 6.5 copy-start.44
  155.0 27.3 %copy-start.7 = (f32[256,1024]{1,0:T(8,128)}, f32[256,1024]{1,0:T(8,128)S(1)}, u32[]{:S(2)}) copy-start(f32[256,1024]{1,0:T(8,128)S(1)} %get-tuple-element.642) | copy-start | bytes 3145732 | tf_op jit(solution)/shard_map/cond
  161.1 7.5 copy-start.16
  176.5 8.6 copy-start.52
  179.3 3.0 copy-start.22
  185.1 19.1 %slice-start.6 = ((s8[8388608]{0:T(1024)(128)(4,1)}), s8[4194304]{0:T(1024)(128)(4,1)S(1)}, s32[]{:S(2)}) async-start(s8[8388608]{0:T(1024)(128)(4,1)} %bitcast.303), calls=%async_computation.7 | async-start | bytes 8388608 | tf_op jit(solution)/shard_map/cond
  188.9 15.2 %slice-start.7 = ((s8[8388608]{0:T(1024)(128)(4,1)}), s8[4194304]{0:T(1024)(128)(4,1)S(1)}, s32[]{:S(2)}) async-start(s8[8388608]{0:T(1024)(128)(4,1)} %bitcast.303), calls=%async_computation.8 | async-start | bytes 8388608 | tf_op jit(solution)/shard_map/cond
  204.2 5.1 copy-start.8
  209.4 62.9 %copy-start.9 = (f32[256,1024]{1,0:T(8,128)}, f32[256,1024]{1,0:T(8,128)S(1)}, u32[]{:S(2)}) copy-start(f32[256,1024]{1,0:T(8,128)S(1)} %get-tuple-element.425) | copy-start | bytes 3145732
  209.4 18.9 %collective-permute-start = (bf16[256,1024]{1,0:T(8,128)(2,1)}, bf16[256,1024]{1,0:T(8,128)(2,1)S(1)}, u32[]{:S(2)}, u32[]{:S(2)}) collective-permute-start(bf16[256,1024]{1,0:T(8,128)(2,1)} %get-tuple-element.383), channel_id=1, source_target_pairs={{0,16},{1,17},{2,18},{3,19},{4,20},{5,21},{6,22},{7,23},{8,24},{9,... | collective-permute-start | bytes 1572872 | tf_op jit(solution)/shard_map/ppermute | solution.py:28
  272.4 22.8 %copy-start.54 = (s32[256]{0:T(256)S(1)}, s32[256]{0:T(256)}, u32[]{:S(2)}) copy-start(s32[256]{0:T(256)} %param.30) | copy-start | bytes 3076
  291.9 3.2 collective-permute-start.1
  306.7 10.7 %copy-start.6 = (f32[256,16384]{1,0:T(8,128)S(1)}, f32[256,16384]{1,0:T(8,128)}, u32[]{:S(2)}) copy-start(f32[256,16384]{1,0:T(8,128)} %get-tuple-element.600) | copy-start | bytes 50331652 | tf_op jit(solution)/shard_map/cond
  306.7 16.7 %slice-start = ((s8[8388608]{0:T(1024)(128)(4,1)}), s8[4194304]{0:T(1024)(128)(4,1)S(1)}, s32[]{:S(2)}) async-start(s8[8388608]{0:T(1024)(128)(4,1)} %bitcast.257), calls=%async_computation.1 | async-start | bytes 8388608 | tf_op jit(solution)/shard_map/cond
  317.3 6.0 slice-start.1
  329.1 2.3 copy-start.57
  329.1 2.3 collective-permute-start.3
  340.4 66.8 %copy-start.38 = (bf16[1024,256]{1,0:T(8,128)(2,1)S(1)}, bf16[1024,256]{1,0:T(8,128)(2,1)}, u32[]{:S(2)}) copy-start(bf16[1024,256]{1,0:T(8,128)(2,1)} %get-tuple-element.384) | copy-start | bytes 1572868
  407.2 28.1 %copy-start.10 = (f32[256,1024]{1,0:T(8,128)S(1)}, f32[256,1024]{1,0:T(8,128)}, u32[]{:S(2)}) copy-start(f32[256,1024]{1,0:T(8,128)} %copy-done.9) | copy-start | bytes 3145732
  407.2 28.1 %copy-start.45 = (bf16[256,256]{1,0:T(8,128)(2,1)S(1)}, bf16[256,256]{1,0:T(8,128)(2,1)}, u32[]{:S(2)}) copy-start(bf16[256,256]{1,0:T(8,128)(2,1)} %get-tuple-element.434) | copy-start | bytes 393220
  407.3 28.1 %copy-start.53 = (f32[2,16,128,1]{2,1,0,3:T(8,128)S(1)}, f32[2,16,128,1]{2,1,0,3:T(8,128)}, u32[]{:S(2)}) copy-start(f32[2,16,128,1]{2,1,0,3:T(8,128)} %get-tuple-element.427) | copy-start | bytes 49156
  407.3 28.1 %copy-start.56 = (f32[2,128]{1,0:T(2,128)S(1)}, f32[2,128]{1,0:T(2,128)}, u32[]{:S(2)}) copy-start(f32[2,128]{1,0:T(2,128)} %copy-done.55) | copy-start | bytes 3076
  431.5 3.8 collective-permute-start.4
  435.4 110.1 %copy-start.58 = (bf16[256]{0:T(256)(128)(2,1)S(1)}, bf16[256]{0:T(256)(128)(2,1)}, u32[]{:S(2)}) copy-start(bf16[256]{0:T(256)(128)(2,1)} %copy-done.57) | copy-start | bytes 1540
  439.0 24.4 %copy-start.25 = (bf16[256,1024]{1,0:T(8,128)(2,1)}, bf16[256,1024]{1,0:T(8,128)(2,1)S(1)}, u32[]{:S(2)}) copy-start(bf16[256,1024]{1,0:T(8,128)(2,1)S(1)} %get-tuple-element.269) | copy-start | bytes 1572868 | tf_op jit(solution)/shard_map/conditional
  440.5 16.5 %slice-start.4 = ((s8[8388608]{0:T(1024)(128)(4,1)}), s8[4194304]{0:T(1024)(128)(4,1)S(1)}, s32[]{:S(2)}) async-start(s8[8388608]{0:T(1024)(128)(4,1)} %bitcast.301), calls=%async_computation.5 | async-start | bytes 8388608 | tf_op jit(solution)/shard_map/conditional
  442.3 14.7 %slice-start.5 = ((s8[8388608]{0:T(1024)(128)(4,1)}), s8[4194304]{0:T(1024)(128)(4,1)S(1)}, s32[]{:S(2)}) async-start(s8[8388608]{0:T(1024)(128)(4,1)} %bitcast.301), calls=%async_computation.6 | async-start | bytes 8388608 | tf_op jit(solution)/shard_map/conditional
  457.0 4.6 copy-start.28
  461.6 3.7 copy-start.24
  463.4 1.0 copy-start.20
  464.4 6.1 copy-start.17
  464.6 0.8 copy-start.40
  488.1 2.3 copy-start.37
  489.9 1.3 copy-start.35
  489.9 1.7 copy-start.43
  489.9 3.6 slice-start.12
  491.2 2.3 slice-start.13
  493.5 2.2 copy-start.26
  495.7 8.1 copy-start.21
  503.0 1.1 copy-start.33
  503.0 1.8 copy-start.29
  511.4 11.9 %copy-start.41 = (bf16[256,1024]{1,0:T(8,128)(2,1)S(1)}, bf16[256,1024]{1,0:T(8,128)(2,1)}, u32[]{:S(2)}) copy-start(bf16[256,1024]{1,0:T(8,128)(2,1)} %copy-done.40) | copy-start | bytes 1572868 | tf_op jit(solution)/shard_map/conditional
  544.8 0.7 copy-start.47
  545.5 1.2 collective-permute-start.2
  857.2 28.3 %collective-permute-start.6 = (bf16[64,1024]{1,0:T(8,128)(2,1)}, bf16[64,1024]{1,0:T(8,128)(2,1)S(1)}, u32[]{:S(2)}, u32[]{:S(2)}) collective-permute-start(bf16[64,1024]{1,0:T(8,128)(2,1)} %get-tuple-element.444), channel_id=1, source_target_pairs={{0,16},{16,0},{1,17},{17,1},{2,18},{18,2},{3,19},{19,3},{4,20},{20... | collective-permute-start | bytes 393224 | tf_op jit(solution)/shard_map/ppermute | solution.py:1366
  857.3 26.9 %collective-permute-start.7 = (f32[8,256]{1,0:T(8,128)}, f32[8,256]{1,0:T(8,128)S(1)}, u32[]{:S(2)}, u32[]{:S(2)}) collective-permute-start(f32[8,256]{1,0:T(8,128)} %get-tuple-element.445), channel_id=1, source_target_pairs={{0,16},{16,0},{1,17},{17,1},{2,18},{18,2},{3,19},{19,3},{4,20},{20... | collective-permute-start | bytes 24584 | tf_op jit(solution)/shard_map/ppermute | solution.py:1366
  876.3 4.3 copy-start.31
  876.3 10.8 %collective-permute-start.5 = (bf16[4096,256]{1,0:T(8,128)(2,1)S(1)}, bf16[4096,256]{1,0:T(8,128)(2,1)}, u32[]{:S(2)}, u32[]{:S(2)}) collective-permute-start(bf16[4096,256]{1,0:T(8,128)(2,1)S(1)} %get-tuple-element.726), channel_id=1, source_target_pairs={{0,16},{16,0},{1,17},{17,1},{2,18},{18,2},{3,19},{19,3},{4,20},{20... | collective-permute-start | bytes 6291464 | tf_op jit(solution)/shard_map/ppermute | solution.py:1366
  880.6 2.5 copy-start.46
  880.6 5.0 copy-start.49
Sparse Core Ops, SparseCore 0:
  545.6 189.2 all-gather.1

commit v4 on v3

--- a/solution.py
+++ b/solution.py
@@ -1168,48 +1168,446 @@
     )(*arrays, *((gains,) if more else ()))
 
 
-def block_forward(hidden, key_valid, weights):
-    gain_attn, qkv_weight, proj_weight, gain_mlp, up_weight, down_weight = weights
-    seqs, length = key_valid.shape
-    normed_in = normed(hidden, gain_attn).astype(jnp.bfloat16)
-    qkv_rows = product(normed_in, qkv_weight).astype(jnp.bfloat16)
-    mixed_rows, log_total = jax.vmap(attend)(qkv_rows.reshape(seqs, length, -1), key_valid)
-    mixed_rows = mixed_rows.reshape(seqs * length, -1)
-    hidden_mid = hidden + product(mixed_rows, proj_weight)
-    mlp_in = normed(hidden_mid, gain_mlp).astype(jnp.bfloat16)
-    pre_act = product(mlp_in, up_weight)
-    activated = gelu_exact(pre_act).astype(jnp.bfloat16)
-    hidden_out = hidden_mid + product(activated, down_weight)
-    kept = (hidden, normed_in, qkv_rows, log_total, mixed_rows, hidden_mid, mlp_in, pre_act, activated)
-    return hidden_out, kept
-
-
-def block_backward(kept, grad_out, key_valid, weights):
-    hidden, normed_in, qkv_rows, log_total, mixed_rows, hidden_mid, mlp_in, pre_act, activated = kept
-    gain_attn, qkv_weight, proj_weight, gain_mlp, up_weight, down_weight = weights
-    seqs, length = key_valid.shape
-    grad_low = grad_out.astype(jnp.bfloat16)
-    grad_activated = product_nt(grad_low, down_weight)
-    grad_pre = jax.vjp(gelu_exact, pre_act)[1](grad_activated)[0].astype(jnp.bfloat16)
-    grad_mlp_in = product_nt(grad_pre, up_weight)
-    grad_mid_norm, grad_gain_mlp = norm_back(hidden_mid, gain_mlp, grad_mlp_in)
-    grad_mid = grad_out + grad_mid_norm
-    grad_mid_low = grad_mid.astype(jnp.bfloat16)
-    grad_mixed = product_nt(grad_mid_low, proj_weight).astype(jnp.bfloat16)
-    grad_qkv = jax.vmap(attend_back)(
-        qkv_rows.reshape(seqs, length, -1),
-        key_valid,
-        log_total,
-        grad_mixed.reshape(seqs, length, -1),
-    ).reshape(seqs * length, -1)
-    grad_normed = product_nt(grad_qkv, qkv_weight)
-    grad_in_norm, grad_gain_attn = norm_back(hidden, gain_attn, grad_normed)
-    pairs = (normed_in, grad_qkv), (mixed_rows, grad_mid_low), (mlp_in, grad_pre), (activated, grad_low)
-    return grad_mid + grad_in_norm, (grad_gain_attn, grad_gain_mlp), pairs
-
-
-def weight_grads(pairs):
-    return tuple(product_tn(rows, grads).astype(jnp.bfloat16) for rows, grads in pairs)
+IN_VMEM = pl.BlockSpec(memory_space=pltpu.VMEM)
+IN_SMEM = pl.BlockSpec(memory_space=pltpu.SMEM)
+ROOT_HALF = 0.7071067811865476
+ROOT_TWO_PI = 0.3989422804014327
+
+
+def dot_nn(left, right):
+    return lax.dot_general(
+        left, right, (((1,), (0,)), ((), ())), preferred_element_type=jnp.float32
+    )
+
+
+def dot_nt(left, right):
+    return lax.dot_general(
+        left, right, (((1,), (1,)), ((), ())), preferred_element_type=jnp.float32
+    )
+
+
+def dot_tn(left, right):
+    return lax.dot_general(
+        left, right, (((0,), (0,)), ((), ())), preferred_element_type=jnp.float32
+    )
+
+
+def unit_rows(v):
+    center = v - jnp.mean(v, -1, keepdims=True)
+    scale = lax.rsqrt(jnp.mean(center * center, -1, keepdims=True) + EPS)
+    return center * scale, scale
+
+
+def split_heads(pair):
+    low = lax.broadcasted_iota(jnp.int32, pair.shape, 1) < HEAD
+    nothing = jnp.zeros_like(pair)
+    return jnp.concatenate([jnp.where(low, pair, nothing), jnp.where(low, nothing, pair)], 0)
+
+
+def join_heads(stacked):
+    half = stacked.shape[0] // 2
+    low = lax.broadcasted_iota(jnp.int32, (half, stacked.shape[1]), 1) < HEAD
+    return jnp.where(low, stacked[:half], stacked[half:])
+
+
+def pair_scores(keys, stacked_queries, key_count):
+    scores = dot_nt(keys, stacked_queries) * 0.125
+    valid = lax.broadcasted_iota(jnp.int32, scores.shape, 0) < key_count
+    return jnp.where(valid, scores, MASKED)
+
+
+STRIP = 64
+
+
+def forward_kernel(only, tile, given, *refs):
+    x, gain_attn, gain_mlp, counts, wq, wp, wu, wd = refs[:8]
+    rest = refs[8 + given :]
+    outs = rest[:KEPT_COUNT]
+    qv, pv, uv, dv = rest[KEPT_COUNT : KEPT_COUNT + 4]
+    kept = rest[KEPT_COUNT + 4 : 2 * KEPT_COUNT + 4]
+    a, att, m, acc, wsem, osem = rest[2 * KEPT_COUNT + 4 :]
+    xv, at_t, qkv, lse, att_t, mid, m_t, pre, act_t, out = kept
+    rows, width = a.shape
+    units = dv.shape[0]
+
+    def store(idx):
+        return pltpu.make_async_copy(kept[idx], outs[idx], osem.at[idx])
+
+    def run():
+        loads = []
+
+        def load(src, dst):
+            copy = pltpu.make_async_copy(src, dst, wsem.at[len(loads)])
+            copy.start()
+            loads.append(copy)
+
+        for lo in range(0, 3 * width, tile):
+            load(wq.at[:, pl.ds(lo, tile)], qv.at[:, pl.ds(lo, tile)])
+        load(wp, pv)
+        for lo in range(0, units, tile):
+            load(wu.at[:, pl.ds(lo, tile)], uv.at[:, pl.ds(lo, tile)])
+            load(wd.at[pl.ds(lo, tile)], dv.at[pl.ds(lo, tile)])
+        loads = iter(loads)
+        for lo in range(0, rows, STRIP):
+            here = pl.ds(lo, STRIP)
+            xv[here, :] = x[here, :].astype(jnp.float32)
+            a[here, :] = (unit_rows(xv[here, :])[0] * gain_attn[...]).astype(jnp.bfloat16)
+        store(0).start()
+        for lo in range(0, 3 * width, tile):
+            next(loads).wait()
+            cols = pl.ds(lo, tile)
+            qkv[:, cols] = dot_nn(a[...], qv[:, cols]).astype(jnp.bfloat16)
+        store(2).start()
+        for lo in range(0, width, 256):
+            at_t[pl.ds(lo, 256), :] = a[:, pl.ds(lo, 256)].T
+        store(1).start()
+        pairs = width // 128
+        for seq in range(rows // LEN):
+            here = pl.ds(seq * LEN, LEN)
+            for pair in range(pairs):
+                stacked = split_heads(qkv[here, pl.ds(pair * 128, 128)])
+                scores = pair_scores(qkv[here, pl.ds(width + pair * 128, 128)], stacked, counts[seq])
+                top = jnp.max(scores, 0, keepdims=True)
+                power = jnp.exp(scores - top)
+                total = jnp.sum(power, 0, keepdims=True)
+                lse[seq * pairs + pair] = top + jnp.log(total)
+                probs = (power * (1.0 / total)).astype(jnp.bfloat16)
+                mixed = dot_tn(probs, qkv[here, pl.ds(2 * width + pair * 128, 128)])
+                att[here, pl.ds(pair * 128, 128)] = join_heads(mixed).astype(jnp.bfloat16)
+        store(3).start()
+        for lo in range(0, width, 256):
+            att_t[pl.ds(lo, 256), :] = att[:, pl.ds(lo, 256)].T
+        store(4).start()
+        next(loads).wait()
+        for lo in range(0, width, tile):
+            cols = pl.ds(lo, tile)
+            mid[:, cols] = xv[:, cols] + dot_nn(att[...], pv[:, cols])
+        for lo in range(0, rows, STRIP):
+            here = pl.ds(lo, STRIP)
+            m[here, :] = (unit_rows(mid[here, :])[0] * gain_mlp[...]).astype(jnp.bfloat16)
+        store(5).start()
+        acc[...] = mid[...]
+        for lo in range(0, units, tile):
+            cols = pl.ds(lo, tile)
+            next(loads).wait()
+            before = dot_nn(m[...], uv[:, cols])
+            pre[:, cols] = before
+            active = (0.5 * before * (1.0 + lax.erf(before * ROOT_HALF))).astype(jnp.bfloat16)
+            act_t[cols, :] = active.T
+            next(loads).wait()
+            acc[...] += dot_nn(active, dv[cols, :])
+        store(7).start()
+        store(8).start()
+        for lo in range(0, width, 256):
+            m_t[pl.ds(lo, 256), :] = m[:, pl.ds(lo, 256)].T
+        store(6).start()
+        out[...] = acc[...]
+        store(9).start()
+        for idx in range(KEPT_COUNT):
+            store(idx).wait()
+
+    pl.when(lax.axis_index("section") == only)(run)
+
+
+KEPT_COUNT = 10
+
+
+def kept_shapes(rows, width, units):
+    f32, low = jnp.float32, jnp.bfloat16
+    return [
+        jax.ShapeDtypeStruct(shape, kind)
+        for shape, kind in (
+            ((rows, width), f32),
+            ((width, rows), low),
+            ((rows, 3 * width), low),
+            ((rows // LEN * width // 128, 1, 2 * LEN), f32),
+            ((width, rows), low),
+            ((rows, width), f32),
+            ((width, rows), low),
+            ((rows, units), f32),
+            ((units, rows), low),
+            ((rows, width), f32),
+        )
+    ]
+
+
+def run_forward(only, x, gain_attn, gain_mlp, counts, weights, kept):
+    wq, wp, wu, wd = weights
+    rows, width = x.shape
+    units = wd.shape[0]
+    tile = 512
+    shapes = kept_shapes(rows, width, units)
+    low = jnp.bfloat16
+    given = 0 if kept is None else KEPT_COUNT
+    in_specs = [IN_VMEM] * 3 + [IN_SMEM] + [ANYWHERE] * (4 + given)
+    return pl.pallas_call(
+        functools.partial(forward_kernel, only, tile, given),
+        out_shape=shapes,
+        in_specs=in_specs,
+        out_specs=[ANYWHERE] * KEPT_COUNT,
+        input_output_aliases={8 + idx: idx for idx in range(given)},
+        scratch_shapes=[pltpu.VMEM(w.shape, w.dtype) for w in weights]
+        + [pltpu.VMEM(s.shape, s.dtype) for s in shapes]
+        + [
+            pltpu.VMEM((rows, width), low),
+            pltpu.VMEM((rows, width), low),
+            pltpu.VMEM((rows, width), low),
+            pltpu.VMEM((rows, width), jnp.float32),
+            pltpu.SemaphoreType.DMA((3 * width // tile + 1 + 2 * units // tile,)),
+            pltpu.SemaphoreType.DMA((KEPT_COUNT,)),
+        ],
+        compiler_params=pltpu.CompilerParams(vmem_limit_bytes=56 << 20),
+    )(x, gain_attn, gain_mlp, counts, wq, wp, wu, wd, *(kept or ()))
+
+
+GRAD_COUNT = 6
+
+
+def grad_shapes(rows, width, units):
+    f32, low = jnp.float32, jnp.bfloat16
+    return [
+        jax.ShapeDtypeStruct(shape, kind)
+        for shape, kind in (
+            ((rows, width), low),
+            ((rows, units), low),
+            ((rows, width), low),
+            ((rows, 3 * width), low),
+            ((rows, width), low),
+            ((8, width), f32),
+        )
+    ]
+
+
+def norm_pull(v, gain, upstream):
+    unit, scale = unit_rows(v)
+    pulled = upstream * gain
+    inner = jnp.mean(pulled * unit, -1, keepdims=True)
+    grad = (pulled - jnp.mean(pulled, -1, keepdims=True) - unit * inner) * scale
+    return grad, jnp.sum(upstream * unit, 0, keepdims=True)
+
+
+def backward_kernel(only, tile, given, *refs):
+    grad, gain_attn, gain_mlp, counts, x_in, qkv_in, lse_in, mid_in, pre_in, wq, wp, wu, wd = refs[:13]
+    rest = refs[13 + given :]
+    outs = rest[:GRAD_COUNT]
+    qv, pv, uv, dv = rest[GRAD_COUNT : GRAD_COUNT + 4]
+    made = rest[GRAD_COUNT + 4 : 2 * GRAD_COUNT + 4]
+    x, qkv, lse, mid, pre, gm, gmid, gatt, wsem, ksem, osem = rest[2 * GRAD_COUNT + 4 :]
+    gy, gpre, gz, gqkv, gx, gains = made
+    rows, width = gm.shape
+    units = dv.shape[0]
+
+    def store(idx):
+        return pltpu.make_async_copy(made[idx], outs[idx], osem.at[idx])
+
+    def run():
+        loads = []
+
+        def load(src, dst):
+            copy = pltpu.make_async_copy(src, dst, wsem.at[len(loads)])
+            copy.start()
+            loads.append(copy)
+
+        kept = [
+            pltpu.make_async_copy(src, dst, ksem.at[idx])
+            for idx, (src, dst) in enumerate(
+                ((pre_in, pre), (mid_in, mid), (qkv_in, qkv), (lse_in, lse), (x_in, x))
+            )
+        ]
+        kept[0].start()
+        for lo in range(0, units, tile):
+            load(wd.at[pl.ds(lo, tile)], dv.at[pl.ds(lo, tile)])
+            load(wu.at[:, pl.ds(lo, tile)], uv.at[:, pl.ds(lo, tile)])
+        for copy in kept[1:]:
+            copy.start()
+        load(wp, pv)
+        load(wq, qv)
+        loads = iter(loads)
+        gy[...] = grad[...].astype(jnp.bfloat16)
+        store(0).start()
+        gains[...] = jnp.zeros_like(gains)
+        kept[0].wait()
+        gm[...] = jnp.zeros_like(gm)
+        for lo in range(0, units, tile):
+            cols = pl.ds(lo, tile)
+            next(loads).wait()
+            pulled = dot_nt(gy[...], dv[cols, :])
+            before = pre[:, cols]
+            slope = 0.5 * (1.0 + lax.erf(before * ROOT_HALF)) + before * (
+                ROOT_TWO_PI * jnp.exp(-0.5 * before * before)
+            )
+            low = (pulled * slope).astype(jnp.bfloat16)
+            gpre[:, cols] = low
+            next(loads).wait()
+            gm[...] += dot_nt(low, uv[:, cols])
+        store(1).start()
+        kept[1].wait()
+        for lo in range(0, rows, STRIP):
+            here = pl.ds(lo, STRIP)
+            step, gain = norm_pull(mid[here, :], gain_mlp[...], gm[here, :])
+            total = grad[here, :].astype(jnp.float32) + step
+            gmid[here, :] = total
+            gz[here, :] = total.astype(jnp.bfloat16)
+            gains[1:2, :] += gain
+        store(2).start()
+        next(loads).wait()
+        gatt[...] = dot_nt(gz[...], pv[...]).astype(jnp.bfloat16)
+        kept[2].wait()
+        kept[3].wait()
+        pairs = width // 128
+        for seq in range(rows // LEN):
+            here = pl.ds(seq * LEN, LEN)
+            for pair in range(pairs):
+                own = pl.ds(pair * 128, 128)
+                stacked = split_heads(qkv[here, own])
+                pulled = split_heads(gatt[here, own])
+                keys = qkv[here, pl.ds(width + pair * 128, 128)]
+                values = qkv[here, pl.ds(2 * width + pair * 128, 128)]
+                probs = jnp.exp(pair_scores(keys, stacked, counts[seq]) - lse[seq * pairs + pair])
+                gprobs = dot_nt(values, pulled)
+                inner = jnp.sum(probs * gprobs, 0, keepdims=True)
+                gscores = (probs * (gprobs - inner)).astype(jnp.bfloat16)
+                gqkv[here, own] = (join_heads(dot_tn(gscores, keys)) * 0.125).astype(jnp.bfloat16)
+                gqkv[here, pl.ds(width + pair * 128, 128)] = (dot_nn(gscores, stacked) * 0.125).astype(
+                    jnp.bfloat16
+                )
+                gqkv[here, pl.ds(2 * width + pair * 128, 128)] = dot_nn(
+                    probs.astype(jnp.bfloat16), pulled
+                ).astype(jnp.bfloat16)
+        store(3).start()
+        next(loads).wait()
+        for lo in range(0, width, 256):
+            gm[:, pl.ds(lo, 256)] = dot_nt(gqkv[...], qv[pl.ds(lo, 256), :])
+        kept[4].wait()
+        for lo in range(0, rows, STRIP):
+            here = pl.ds(lo, STRIP)
+            step, gain = norm_pull(x[here, :], gain_attn[...], gm[here, :])
+            gx[here, :] = (gmid[here, :] + step).astype(jnp.bfloat16)
+            gains[0:1, :] += gain
+        store(4).start()
+        store(5).start()
+        for idx in range(GRAD_COUNT):
+            store(idx).wait()
+
+    pl.when(lax.axis_index("section") == only)(run)
+
+
+def run_backward(only, grad, gain_attn, gain_mlp, counts, kept, weights, made):
+    wq, wp, wu, wd = weights
+    x, _, qkv, lse, _, mid, _, pre, _, _ = kept
+    rows, width = x.shape
+    units = wd.shape[0]
+    tile = 512
+    shapes = grad_shapes(rows, width, units)
+    low, f32 = jnp.bfloat16, jnp.float32
+    given = 0 if made is None else GRAD_COUNT
+    in_specs = [IN_VMEM] * 3 + [IN_SMEM] + [ANYWHERE] * (9 + given)
+    return pl.pallas_call(
+        functools.partial(backward_kernel, only, tile, given),
+        out_shape=shapes,
+        in_specs=in_specs,
+        out_specs=[ANYWHERE] * GRAD_COUNT,
+        input_output_aliases={13 + idx: idx for idx in range(given)},
+        scratch_shapes=[pltpu.VMEM(w.shape, w.dtype) for w in weights]
+        + [pltpu.VMEM(s.shape, s.dtype) for s in shapes]
+        + [pltpu.VMEM(s.shape, s.dtype) for s in (x, qkv, lse, mid, pre)]
+        + [
+            pltpu.VMEM((rows, width), f32),
+            pltpu.VMEM((rows, width), f32),
+            pltpu.VMEM((rows, width), low),
+            pltpu.SemaphoreType.DMA((2 + 2 * units // tile,)),
+            pltpu.SemaphoreType.DMA((5,)),
+            pltpu.SemaphoreType.DMA((GRAD_COUNT,)),
+        ],
+        compiler_params=pltpu.CompilerParams(vmem_limit_bytes=56 << 20),
+    )(grad, gain_attn, gain_mlp, counts, x, qkv, lse, mid, pre, wq, wp, wu, wd, *(made or ()))
+
+
+def vocabulary_kernel(only, tile, proj, ids, scale, table, gproj_out, loss_out, gtable, tv, gt, gp, tsem, gsem):
+    rows, emb = proj.shape
+    vocab = tv.shape[0]
+    count = vocab // tile
+
+    def run():
+        for at in range(count):
+            here = pl.ds(at * tile, tile)
+            pltpu.make_async_copy(table.at[here], tv.at[here], tsem.at[at]).start()
+
+        def logits_of(at):
+            return dot_nt(tv[rows_at(at * tile, tile), :], proj[...])
+
+        def hits_of(at):
+            names = lax.broadcasted_iota(jnp.int32, (tile, rows), 0) + at * tile
+            return names == ids[...]
+
+        def stats(at, carry):
+            top, total, picked = carry
+            here = rows_at(at * tile, tile)
+            pltpu.make_async_copy(table.at[here], tv.at[here], tsem.at[at]).wait()
+            logits = logits_of(at)
+            higher = jnp.maximum(top, jnp.max(logits, 0, keepdims=True))
+            total = total * jnp.exp(top - higher) + jnp.sum(jnp.exp(logits - higher), 0, keepdims=True)
+            picked = picked + jnp.sum(jnp.where(hits_of(at), logits, 0.0), 0, keepdims=True)
+            return higher, total, picked
+
+        start = (
+            jnp.full((1, rows), MASKED, jnp.float32),
+            jnp.zeros((1, rows), jnp.float32),
+            jnp.zeros((1, rows), jnp.float32),
+        )
+        top, total, picked = lax.fori_loop(0, count, stats, start)
+        log_total = top + jnp.log(total)
+        loss_out[...] = jnp.where(scale[...] > 0, log_total - picked, 0.0)
+        gp[...] = jnp.zeros_like(gp)
+
+        def gstore(at):
+            return pltpu.make_async_copy(
+                gt.at[rows_at(at * tile, tile)], gtable.at[rows_at(at * tile, tile)], gsem.at[at]
+            )
+
+        def pull(at, carry):
+            here = rows_at(at * tile, tile)
+            probs = jnp.exp(logits_of(at) - log_total)
+            grads = ((probs - jnp.where(hits_of(at), 1.0, 0.0)) * scale[...]).astype(jnp.bfloat16)
+            gp[...] += dot_tn(grads, tv[here, :])
+            gt[here, :] = dot_nn(grads, proj[...]).astype(jnp.bfloat16)
+            gstore(at).start()
+            return carry
+
+        lax.fori_loop(0, count, pull, 0)
+        gproj_out[...] = gp[...].astype(jnp.bfloat16)
+
+        def done(at, carry):
+            gstore(at).wait()
+            return carry
+
+        lax.fori_loop(0, count, done, 0)
+
+    pl.when(lax.axis_index("section") == only)(run)
+
+
+def run_vocabulary(only, proj, ids, scale, table):
+    rows, emb = proj.shape
+    vocab = table.shape[0]
+    tile = 1024
+    return pl.pallas_call(
+        functools.partial(vocabulary_kernel, only, tile),
+        out_shape=[
+            jax.ShapeDtypeStruct((rows, emb), jnp.bfloat16),
+            jax.ShapeDtypeStruct((1, rows), jnp.float32),
+            jax.ShapeDtypeStruct(table.shape, jnp.bfloat16),
+        ],
+        in_specs=[IN_VMEM] * 3 + [ANYWHERE],
+        out_specs=[IN_VMEM] * 2 + [ANYWHERE],
+        scratch_shapes=[
+            pltpu.VMEM(table.shape, table.dtype),
+            pltpu.VMEM(table.shape, jnp.bfloat16),
+            pltpu.VMEM((rows, emb), jnp.float32),
+            pltpu.SemaphoreType.DMA((vocab // tile,)),
+            pltpu.SemaphoreType.DMA((vocab // tile,)),
+        ],
+        compiler_params=pltpu.CompilerParams(vmem_limit_bytes=40 << 20),
+    )(proj, ids, scale, table)
 
 
 def nothing_like(run):
@@ -1261,7 +1659,9 @@
     gain_attn = gain_all[:, 0].reshape(-1)
     gain_mlp = gain_all[:, 1].reshape(-1)
     final_gain = gain_all[:, 2].reshape(-1)
-    weights = (gain_attn, qkv_weight, proj_weight, gain_mlp, up_weight, down_weight)
+    weights = (qkv_weight, proj_weight, up_weight, down_weight)
+    gain_attn = gain_attn[None]
+    gain_mlp = gain_mlp[None]
     key_valid = jnp.arange(length, dtype=jnp.int32)[None, :] < lengths[:, None]
     loss_scale = LOSS_GAIN / math.sqrt(rows * lax.axis_size(("group", "dp")))
 
@@ -1283,75 +1683,53 @@
         mixed_in = ((looked + row_level * noise_rows.astype(jnp.float32)) * row_scale).astype(
             jnp.bfloat16
         )
-        out, kept = block_forward(product(mixed_in, in_weight), key_valid, weights)
-        return out.astype(jnp.bfloat16), kept, mixed_in
-
-    out_first, kept_first, mixed_in = only_on(first_section, front)
-    x_second = passed_along(out_first, "section", 1)
+        return mixed_in, product(mixed_in, in_weight)
+
+    mixed_in, x_first = only_on(first_section, front)
+    kept = run_forward(0, x_first, gain_attn, gain_mlp, lengths, weights, None)
+    x_second = passed_along(kept[9].astype(jnp.bfloat16), "section", 1)
     (table_full,) = gather_all((after(embed_table, x_second),), (0,), (), (), 2)
-
-    def back():
-        hidden_out, kept = block_forward(x_second.astype(jnp.float32), key_valid, weights)
-        final_in = normed(hidden_out, final_gain).astype(jnp.bfloat16)
-        projected = product(final_in, out_weight).astype(jnp.bfloat16)
-        return projected, final_in, hidden_out, kept
-
-    projected_b, final_in, hidden_out, kept_second = only_on(last_section, back)
-    projected = passed_along(after(projected_b, table_full), "section", -1)
-
-    def vocabulary():
-        logits = product_nt(projected, table_full)
-        row_max = jnp.max(logits, -1, keepdims=True)
-        log_total = row_max + jnp.log(jnp.sum(jnp.exp(logits - row_max), -1, keepdims=True))
-        vocab_ids = lax.broadcasted_iota(jnp.int32, logits.shape, 1)
-        target_hit = vocab_ids == tokens[:, None]
-        picked = jnp.sum(jnp.where(target_hit, logits, 0.0), -1)
-        valid = key_valid.reshape(-1)
-        entropy = jnp.where(valid, log_total[:, 0] - picked, 0.0).astype(jnp.bfloat16)
-        scale = jnp.where(valid, loss_scale, 0.0)[:, None]
-        grad_logits = (
-            (jnp.exp(logits - log_total) - target_hit.astype(jnp.float32)) * scale
-        ).astype(jnp.bfloat16)
-        grad_proj = product(grad_logits, table_full).astype(jnp.bfloat16)
-        return grad_proj, entropy, grad_logits
-
-    grad_proj_a, loss_low, grad_logits = only_on(first_section, vocabulary)
+    kept = run_forward(1, x_second, gain_attn, gain_mlp, lengths, weights, kept)
+    final_in = normed(kept[9], final_gain).astype(jnp.bfloat16)
+    projected = product(final_in, out_weight).astype(jnp.bfloat16)
+    projected = passed_along(after(projected, table_full), "section", -1)
+    valid_scale = jnp.where(key_valid.reshape(1, -1), loss_scale, 0.0)
+    grad_proj_a, entropy, table_g = run_vocabulary(
+        0, projected, tokens[None], valid_scale, table_full
+    )
     grad_proj = passed_along(grad_proj_a, "section", 1)
-    grad_logits = after(grad_logits, grad_proj)
-    table_g = only_on(
-        first_section, lambda: product_tn(grad_logits, projected).astype(jnp.bfloat16)
-    )
-    (table_r,) = reduce_all((table_g,), None, ("plane",), 0, 3)
-
-    def back_again():
-        grad_final = product_nt(grad_proj, out_weight)
-        grad_top, gain_final = norm_back(hidden_out, final_gain, grad_final)
-        grad_start, gain_pair, pairs = block_backward(kept_second, grad_top, key_valid, weights)
-        return grad_start.astype(jnp.bfloat16), gain_pair + (gain_final,), pairs
-
-    grad_second, gains_b, pairs_b = only_on(last_section, back_again)
-    grad_first = passed_along(after(grad_second, table_r), "section", -1)
-    pairs_b = after(pairs_b, grad_first)
+    (table_r,) = reduce_all((after(table_g, grad_proj),), None, ("plane",), 0, 3)
+    grad_top, gain_final = norm_back(kept[9], final_gain, product_nt(grad_proj, out_weight))
+    made = run_backward(1, grad_top, gain_attn, gain_mlp, lengths, kept, weights, None)
+    grad_first = passed_along(after(made[4], table_r), "section", -1)
+    made = run_backward(0, grad_first, gain_attn, gain_mlp, lengths, kept, weights, made)
     shape = in_weight.shape
 
-    def front_back():
-        grad_start, gain_pair, pairs = block_backward(
-            kept_first, grad_first.astype(jnp.float32), key_valid, weights
-        )
-        grad_low = grad_start.astype(jnp.bfloat16)
-        looked_grad = (product_nt(grad_low, in_weight) * row_scale).astype(jnp.bfloat16)
-        edge = product_tn(mixed_in, grad_low).astype(jnp.bfloat16)
-        return gain_pair + (jnp.zeros_like(final_gain),), weight_grads(pairs), edge, looked_grad
-
-    def end_back():
+    def front_edge():
+        looked_grad = (product_nt(made[4], in_weight) * row_scale).astype(jnp.bfloat16)
+        return product_tn(mixed_in, made[4]).astype(jnp.bfloat16), looked_grad
+
+    def back_edge():
         edge = product_tn(final_in, grad_proj).astype(jnp.bfloat16)
         edge = edge.reshape(4, shape[0] // 4, shape[1]).reshape(shape)
-        return gains_b, weight_grads(pairs_b), edge, jnp.zeros((rows, emb), jnp.bfloat16)
-
-    gain_set, grads, edge_g, looked_grad = lax.cond(first_section, front_back, end_back)
-    gain_rows = jnp.concatenate([jnp.stack(gain_set, 0), jnp.zeros((5, width), jnp.float32)], 0)
+        return edge, jnp.zeros((rows, emb), jnp.bfloat16)
+
+    edge_g, looked_grad = lax.cond(first_section, front_edge, back_edge)
+    gain_rows = made[5] + jnp.concatenate(
+        [jnp.zeros((2, width)), gain_final[None], jnp.zeros((5, width))], 0
+    )
     gain_rows = gain_rows.reshape(8, 4, width // 4).transpose(1, 0, 2)
-    order = (grads[2], grads[3], edge_g, grads[1], grads[0])
+
+    def grads_of(rows_at_once, grads):
+        return product(rows_at_once, grads).astype(jnp.bfloat16)
+
+    order = (
+        grads_of(kept[6], made[1]),
+        grads_of(kept[8], made[0]),
+        edge_g,
+        grads_of(kept[4], made[2]),
+        grads_of(kept[1], made[3]),
+    )
     kinds = ("plane",) * 4 + ("line",)
     up_r, down_r, edge_r, proj_r, qkv_r, gain_r = reduce_all(order, gain_rows, kinds, None, 4)
     looked_all = lax.all_gather(looked_grad, ("group", "dp"), axis=0, tiled=True)
@@ -1362,6 +1740,7 @@
         looked_sum = product(hit.astype(jnp.bfloat16), looked_all)
         return (looked_sum + table_r.astype(jnp.float32)).astype(jnp.bfloat16)
 
+    loss_low = after(entropy, gain_r)[0].astype(jnp.bfloat16)
     mine = (only_on(first_section, add_looked), edge_r, gain_r, loss_low)
     theirs = lax.ppermute(mine, "section", [(0, 1), (1, 0)])
 

time: 913 us -> 785 us (0.86)
  matrix products: 128 us -> 40.2 us
  local copies, waits for them, and re-layouts: 94.5 us -> 26.7 us
  Pallas kernels: 554 us -> 613 us
  loops' own time: 28.2 us -> 0.24 us
  other arithmetic: 47.1 us -> 24.9 us
  starting transfers between devices: 21.8 us -> 44 us
    pallas_call x0 -> x5, Pallas kernels: none -> 81.8 us  [the longest x2 36.6 us: run_backward(): pl.pallas_call(functools.partial(backward_kernel, only, tile, given), out...]
    another operation x69 -> x0, local copies, waits for them, and re-layouts: 53.9 us -> none
    dot_general x6 -> x2, matrix products: 34 us -> 0.91 us  [product_nt(): lax.dot_general(left_side, right_side, (((1,), (1,)), ((), ())), preferre...]
    dot_general x6 -> x1, matrix products: 32 us -> 2.1 us  [product_tn(): lax.dot_general(left_side, right_side, (((0,), (0,)), ((), ())), preferre...]
    another operation x7 -> x3, loops' own time: 24.1 us -> 0.22 us  [only_on(): return lax.cond(live, run, lambda: nothing_like(run))]
    ppermute x4, starting transfers between devices: 21.1 us -> 42.7 us  [passed_along(): return lax.ppermute(x, axis, pairs)]
    pallas_call x2, Pallas kernels: 376 us -> 357 us  [reduce_all(): pl.pallas_call(functools.partial(reduce_kernel, kinds, bool(more), only),...]
    unnamed x50 -> x66, local copies, waits for them, and re-layouts: 8.73 us -> 23.6 us
  transfers between devices with their start and end apart: 9 -> 9, of which waited for: 5 -> 4; matrix products, arithmetic and copies ran while one was open for 3% -> 6% of each run, Pallas kernels for 35% -> 37%
where the time goes in v4:
time: 785 us; the launch traced here: 770 us
  Pallas kernels  613 us (78%)
  starting transfers between devices  44 us (6%)
  matrix products  40.2 us (5%)
  local copies, waits for them, and re-layouts  26.7 us (3%)
  other arithmetic  24.9 us (3%)
  between operations  14.7 us (2%)
    pallas_call x2, Pallas kernels, reduce_all(): pl.pallas_call(functools.partial(reduce_kernel, kinds, bool(more), only),...  357 us
    pallas_call x2, Pallas kernels, gather_all(): pl.pallas_call(functools.partial(gather_kernel, count, first_order, last_...  164 us
    ppermute x4, starting transfers between devices, passed_along(): return lax.ppermute(x, axis, pairs)  42.7 us
    dot_general x8, matrix products, product(): return jnp.dot(left_side, right_side, preferred_element_type=jnp.float32)  37.2 us
    pallas_call x2, Pallas kernels, run_backward(): pl.pallas_call(functools.partial(backward_kernel, only, tile, given), out...  36.6 us
    pallas_call x1, Pallas kernels, run_vocabulary(): pl.pallas_call(functools.partial(vocabulary_kernel, only, tile), out_shap...  25.8 us
    unnamed x66, local copies, waits for them, and re-layouts  23.6 us
    pallas_call x2, Pallas kernels, run_forward(): pl.pallas_call(functools.partial(forward_kernel, only, tile, given), out_...  19.4 us
  transfers between devices with their start and end apart: 9, of which 4 were waited for; matrix products, arithmetic and copies ran while one was open for 6% of the time, Pallas kernels for 37%

profile of v4, /device:TPU:0, one launch (start us, length us, event | category | flops | bytes accessed | tf_op | source)
XLA Modules:
  0.0 770.3 jit_solution(12741396285847788033)
XLA Ops:
  7.2 0.7 broadcast_in_dim.70
  7.9 0.7 concatenate.10.refs_7_
  8.7 0.8 maximum_maximum_fusion.refs_6_
  9.4 1.6 copy-done.5
  11.0 1.6 copy-done.6
  12.6 1.4 copy-done.7
  14.0 1.0 copy-done.8
  15.1 0.9 copy-done.9
  16.0 0.9 copy-done.10
  16.9 122.9 %shard_map.222 = (bf16[1024,3072]{1,0:T(8,128)(2,1)S(1)}, bf16[1024,1024]{1,0:T(8,128)(2,1)S(1)}, bf16[1024,4096]{1,0:T(8,128)(2,1)S(1)}, bf16[4096,1024]{1,0:T(...) custom-call(bf16[256,3072]{1,0:T(8,128)(2,1)S(1)} %bitcast.63, ...), custom_call_target="tpu_custom_call" | custom-call | tf_op jit(solution)/shard_map/pallas_call | solution.py:705
  139.8 3.2 copy-done
  143.0 2.7 copy-done.1
  145.7 1.3 copy-done.3
  147.0 3.7 conditional.4
  147.0 3.6 fusion.2
  150.6 10.7 %shard_map.223 = (bf16[4,256,256]{2,1,0:T(8,128)(2,1)S(1)}, s32[4,32,128]{2,1,0:T(8,128)S(1)}) custom-call(bf16[4,256,256]{2,1,0:T(8,128)(2,1)} %get-tuple-element.222.rows_ref, s32[32,128]{1,0:T(8,128)S(1)} %get-tuple-element.137.ids_ref), custom_call_target="tpu_custom_call" | custom-call | tf_op jit(solution)/shard_map/pallas_call | solution.py:761
  161.4 0.6 fusion.10
  162.1 2.1 conditional.5
  162.2 0.8 multiply_convert_fusion
  163.0 1.2 fusion.11
  164.2 17.7 %shard_map.224 = (f32[256,1024]{1,0:T(8,128)}, bf16[1024,256]{1,0:T(8,128)(2,1)}, bf16[256,3072]{1,0:T(8,128)(2,1)}, f32[16,1,256]{2,1,0:T(1,128)}, bf16[1024,25...) custom-call(f32[256,1024]{1,0:T(8,128)S(1)} %get-tuple-element.140.r, ...), custom_call_target="tpu_custom_call" | custom-call | tf_op jit(solution)/shard_map/pallas_call | solution.py:1343
  181.9 1.3 convert_element_type.86
  183.2 38.9 %collective-permute-start = (bf16[256,1024]{1,0:T(8,128)(2,1)S(1)}, bf16[256,1024]{1,0:T(8,128)(2,1)S(1)}, u32[]{:S(2)}, u32[]{:S(2)}) collective-permute-start(bf16[256,1024]{1,0:T(8,128)(2,1)S(1)} %convert_element_type.86), channel_id=1, source_target_pairs={{0,16},{1,17},{2,18},{3,19},{4,20},{5,21},{6,22},{7,23},{8,24},{9,... | collective-permute-start | bytes 1572872 | tf_op jit(solution)/shard_map/ppermute | solution.py:28
  222.0 1.5 collective-permute-done.refs_0_
  223.5 0.8 copy-done.25
  224.3 1.8 shard_map.225
  226.1 1.5 reduce_sum.52
  227.6 1.5 multiply_reduce_fusion.2
  229.1 40.9 %shard_map.226.table = bf16[16384,256]{1,0:T(8,128)(2,1)S(1)} custom-call(bf16[4096,256]{1,0:T(8,128)(2,1)S(1)} %copy-done.22), custom_call_target="tpu_custom_call" | custom-call | tf_op jit(solution)/shard_map/pallas_call | solution.py:705
  270.0 3.3 copy-done.2
  273.9 1.3 collective-permute-start.1
  275.3 1.9 collective-permute-done.1.proj
  277.1 25.8 %shard_map.227 = (bf16[256,256]{1,0:T(8,128)(2,1)S(1)}, f32[1,256]{1,0:T(1,128)S(1)}, bf16[16384,256]{1,0:T(8,128)(2,1)S(1)}) custom-call(bf16[256,256]{1,0:T(8,128)(2,1)S(1)} %collective-permute-done.1.proj, s32[1,256]{1,0:T(1,128)S(1)} %bitcast.67, f32[1,256]{1,0:T(1,128)S(1)} %bitcast.68, bf16[16384,256]{1,0:T(8,128)(2,1)} %copy-done.2), custom_call_target="tpu_custom_call" | custom-call | tf_op jit(solution)/shard_map/pallas_call | solution.py:1593
  303.0 3.3 copy-done.4
  306.3 1.3 collective-permute-start.2
  307.6 1.0 collective-permute-done.2
  308.6 69.2 %shard_map.229 = bf16[4096,256]{1,0:T(8,128)(2,1)} custom-call(bf16[16384,256]{1,0:T(8,128)(2,1)} %copy-done.4), custom_call_target="tpu_custom_call" | custom-call | tf_op jit(solution)/shard_map/pallas_call | solution.py:1159
  377.8 0.6 multiply_reduce_fusion
  378.8 1.1 broadcast_add_fusion.refs_0_
  379.9 11.2 %shard_map.228 = (bf16[256,1024]{1,0:T(8,128)(2,1)}, bf16[256,4096]{1,0:T(8,128)(2,1)}, bf16[256,1024]{1,0:T(8,128)(2,1)}, bf16[256,3072]{1,0:T(8,128)(2,1)}, bf...) custom-call(f32[256,1024]{1,0:T(8,128)} %broadcast_add_fusion.refs_0_, f32[1,1024]{1,0:T(1,128)} %bitcast.76, ...), custom_call_target="tpu_custom_call" | custom-call | tf_op jit(solution)/shard_map/pallas_call | solution.py:1505
  391.1 1.3 collective-permute-start.3
  392.4 2.5 collective-permute-done.3.refs_0_
  395.0 0.8 copy-done.24
  395.8 25.4 %shard_map.230 = (bf16[256,1024]{1,0:T(8,128)(2,1)}, bf16[256,4096]{1,0:T(8,128)(2,1)}, bf16[256,1024]{1,0:T(8,128)(2,1)}, bf16[256,3072]{1,0:T(8,128)(2,1)}, bf...) custom-call(bf16[256,1024]{1,0:T(8,128)(2,1)} %copy-done.24, ...), custom_call_target="tpu_custom_call", output_to_operand_aliasing={{0}: (13, {}), {1}: (14, {}), {2}: (15, {}), {3}: (16, {}),... | custom-call | tf_op jit(solution)/shard_map/pallas_call | solution.py:1505
  421.2 2.5 conditional.6
  421.2 2.1 convolution_convert_fusion.1
  423.7 0.6 copy-done.27
  424.5 0.7 maximum_add_fusion
  425.2 2.0 convolution_convert_fusion.5.refs_3_
  427.2 4.5 convolution_convert_fusion.4.refs_4_
  431.7 5.6 convolution_convert_fusion.2.refs_1_
  437.3 5.7 convolution_convert_fusion.3.refs_0_
  443.0 287.3 %shard_map.231 = (bf16[256,4096]{1,0:T(8,128)(2,1)}, bf16[1024,1024]{1,0:T(8,128)(2,1)}, bf16[64,1024]{1,0:T(8,128)(2,1)}, bf16[256,1024]{1,0:T(8,128)(2,1)}, bf...) custom-call(bf16[1024,4096]{1,0:T(8,128)(2,1)} %convolution_convert_fusion.3.refs_0_, ...), custom_call_target="tpu_custom_call" | custom-call | tf_op jit(solution)/shard_map/pallas_call | solution.py:1159
  730.9 4.2 bitcast_convert_fusion
  735.1 2.0 bitcast_convert_fusion.2
  737.2 14.5 %conditional.7 = (bf16[4096,256]{1,0:T(8,128)(2,1)S(1)}) conditional(s32[]{:T(128)} %convert_element_type.82, () %tuple.54, (s32[4,32,128]{2,1,0:T(8,128)S(1)}, s32[]{:T(128)}, bf16[4096,256]{1,0:T(8,128)(2,1)}, bf16[4096,256]{1,0:T(8,128)(2,1)}) %tuple.55), branch_computations={%region_12.13_spmd, %region_13.14_spmd} | conditional | flops 8609861632 | bytes 6340632 | solution.py:1618
  737.4 14.2 %fusion.7 = bf16[4096,256]{1,0:T(8,128)(2,1)S(1)} fusion(bf16[4096,256]{1,0:T(8,128)(2,1)} %get-tuple-element.64, s32[4096]{0:T(1024)S(1)} %bitcast.83, bf16[4096,256]{1,0:T(8,128)(2,1)} %get-tuple-element.65), kind=kOutput, calls=%fused_computation.16 | convolution fusion | flops 8609857536 | bytes 6307840 | tf_op jit(solution)/shard_map/cond/branch_1_fun/dot_general | solution.py:32
  751.7 0.6 collective-permute-start.4
  752.3 4.2 bitcast_convert_fusion.1
  756.5 1.1 bitcast_convert_fusion.3
  758.1 1.4 broadcast_select_fusion
  759.4 0.7 select_convert_fusion.1
  760.2 0.8 reshape.138
  761.0 2.3 select_convert_fusion
  (85 shorter events, 3.1 us)
Async XLA Ops:
  7.2 730.0 %all-gather.2.cloned.1.call-start = ((), (), s32[]{:S(2)}) async-start(), calls=%async_computation | async-start | bytes 2228224 | tf_op jit(solution)/shard_map/all_gather | solution.py:1735
  9.4 1.6 copy-start.5
  11.0 1.6 copy-start.6
  12.6 1.4 copy-start.7
  14.0 1.0 copy-start.8
  15.1 0.9 copy-start.9
  16.0 0.9 copy-start.10
  16.9 130.1 %copy-start.21 = (bf16[4096,256]{1,0:T(8,128)(2,1)S(1)}, bf16[4096,256]{1,0:T(8,128)(2,1)}, u32[]{:S(2)}) copy-start(bf16[4096,256]{1,0:T(8,128)(2,1)} %refs_0_) | copy-start | bytes 6291460
  139.8 3.2 copy-start
  143.0 2.7 copy-start.1
  145.7 1.3 copy-start.3
  147.0 14.4 %copy-start.32 = (s32[2]{0:T(128)S(1)}, s32[2]{0:T(128)}, u32[]{:S(2)}) copy-start(s32[2]{0:T(128)} %param.24) | copy-start | bytes 28
  147.0 15.1 %copy-start.29 = (bf16[256,256]{1,0:T(8,128)(2,1)S(1)}, bf16[256,256]{1,0:T(8,128)(2,1)}, u32[]{:S(2)}) copy-start(bf16[256,256]{1,0:T(8,128)(2,1)} %param.25) | copy-start | bytes 393220
  183.2 40.3 %collective-permute-start = (bf16[256,1024]{1,0:T(8,128)(2,1)S(1)}, bf16[256,1024]{1,0:T(8,128)(2,1)S(1)}, u32[]{:S(2)}, u32[]{:S(2)}) collective-permute-start(bf16[256,1024]{1,0:T(8,128)(2,1)S(1)} %convert_element_type.86), channel_id=1, source_target_pairs={{0,16},{1,17},{2,18},{3,19},{4,20},{5,21},{6,22},{7,23},{8,24},{9,... | collective-permute-start | bytes 1572872 | tf_op jit(solution)/shard_map/ppermute | solution.py:28
  223.5 0.8 copy-start.25
  226.1 3.0 copy-start.22
  229.1 44.2 %copy-start.12 = (f32[256,1024]{1,0:T(8,128)S(1)}, f32[256,1024]{1,0:T(8,128)}, u32[]{:S(2)}) copy-start(f32[256,1024]{1,0:T(8,128)} %get-tuple-element.156) | copy-start | bytes 3145732
  270.0 3.4 copy-start.2
  273.4 1.8 copy-start.31
  273.4 3.8 copy-start.11
  273.9 3.2 collective-permute-start.1
  303.0 3.4 copy-start.4
  306.3 2.3 collective-permute-start.2
  391.1 3.8 collective-permute-start.3
  394.9 0.8 copy-start.24
  421.2 3.3 copy-start.28
  421.2 4.0 copy-start.18
  421.2 4.0 copy-start.19
  423.7 0.7 copy-start.27
  423.7 3.5 copy-start.15
  423.7 3.5 copy-start.16
  427.2 4.5 copy-start.13
  427.2 4.5 copy-start.17
  431.7 5.6 copy-start.14
  431.7 5.6 copy-start.20
  730.4 29.1 %collective-permute-start.6 = (bf16[64,1024]{1,0:T(8,128)(2,1)}, bf16[64,1024]{1,0:T(8,128)(2,1)S(1)}, u32[]{:S(2)}, u32[]{:S(2)}) collective-permute-start(bf16[64,1024]{1,0:T(8,128)(2,1)} %get-tuple-element.192), channel_id=1, source_target_pairs={{0,16},{16,0},{1,17},{17,1},{2,18},{18,2},{3,19},{19,3},{4,20},{20... | collective-permute-start | bytes 393224 | tf_op jit(solution)/shard_map/ppermute | solution.py:1745
  730.4 27.6 %collective-permute-start.7 = (f32[8,256]{1,0:T(8,128)}, f32[8,256]{1,0:T(8,128)S(1)}, u32[]{:S(2)}, u32[]{:S(2)}) collective-permute-start(f32[8,256]{1,0:T(8,128)} %get-tuple-element.188), channel_id=1, source_target_pairs={{0,16},{16,0},{1,17},{17,1},{2,18},{18,2},{3,19},{19,3},{4,20},{20... | collective-permute-start | bytes 24584 | tf_op jit(solution)/shard_map/ppermute | solution.py:1745
  730.9 4.2 copy-start.23
  751.6 9.3 %collective-permute-start.5 = (bf16[4096,256]{1,0:T(8,128)(2,1)S(1)}, bf16[4096,256]{1,0:T(8,128)(2,1)}, u32[]{:S(2)}, u32[]{:S(2)}) collective-permute-start(bf16[4096,256]{1,0:T(8,128)(2,1)S(1)} %get-tuple-element.223), channel_id=1, source_target_pairs={{0,16},{16,0},{1,17},{17,1},{2,18},{18,2},{3,19},{19,3},{4,20},{20... | collective-permute-start | bytes 6291464 | tf_op jit(solution)/shard_map/ppermute | solution.py:1745
  751.7 5.8 collective-permute-start.4
  752.3 4.2 copy-start.26
  752.3 7.2 copy-start.30
Sparse Core Ops, SparseCore 0:
  424.5 152.0 all-gather.1

commit v5 on v4

--- a/solution.py
+++ b/solution.py
@@ -522,7 +522,7 @@
     )
 
 
-def gather_kernel(count, first_order, last_order, whole_line, *refs):
+def gather_kernel(count, first_order, last_order, *refs):
     shards = refs[:count]
     wholes = refs[count : 2 * count]
     own_sem, zsend, zrecv, psend, precv, gate = refs[2 * count : 2 * count + 6]
@@ -558,30 +558,35 @@
     turn = [pick(pos, v) for v in ((3, 1, 3, 1), (2, 3, 1, 2), (1, 2, 2, 3))]
 
     def run(order, before, middle):
-        def part_of(idx):
-            rows = shards[idx].shape[0]
-            return rows if idx in whole_line else rows // 4
-
-        def shift(idx, who):
-            return 0 if idx in whole_line else who * part_of(idx)
-
-        def block(idx, origin, who):
-            return rows_at(origin * shards[idx].shape[0] + shift(idx, who), part_of(idx))
-
-        def load_own(slot):
-            return pltpu.make_async_copy(shards[order[slot]], stage[order[slot]], own_sem.at[slot])
-
-        def store_own(slot):
-            idx = order[slot]
+        def rows_of(slot):
+            return shards[order[slot][0]].shape[0]
+
+        def part_of(slot):
+            _, _, size, whole_line = order[slot]
+            return size if whole_line else size // 4
+
+        def shift(slot, who):
+            _, lo, _, whole_line = order[slot]
+            return lo if whole_line else lo + who * part_of(slot)
+
+        def block(slot, origin, who):
+            return rows_at(origin * rows_of(slot) + shift(slot, who), part_of(slot))
+
+        staged = sorted({entry[0] for entry in order})
+
+        def load_own(idx):
+            return pltpu.make_async_copy(shards[idx], stage[idx], own_sem.at[idx])
+
+        def store_own(idx):
             rows = shards[idx].shape[0]
             return pltpu.make_async_copy(
-                stage[idx], wholes[idx].at[rows_at(pos * rows, rows)], own_sem.at[slot]
+                stage[idx], wholes[idx].at[rows_at(pos * rows, rows)], own_sem.at[idx]
             )
 
         def own_ends(slot):
-            idx = order[slot]
-            src = shards[idx].at[rows_at(shift(idx, grp), part_of(idx))]
-            dst = wholes[idx].at[block(idx, pos, grp)]
+            idx = order[slot][0]
+            src = shards[idx].at[rows_at(shift(slot, grp), part_of(slot))]
+            dst = wholes[idx].at[block(slot, pos, grp)]
             return (
                 (pos < 3, remote(src, dst, zsend.at[slot, 0], zrecv.at[slot, 1], above)),
                 (pos > 0, remote(src, dst, zsend.at[slot, 1], zrecv.at[slot, 3], below)),
@@ -595,13 +600,13 @@
             return lax.rem(pos - turn[j] + 4, 4)
 
         def arrived(slot, j):
-            here = wholes[order[slot]].at[block(order[slot], origin_of(j), grp)]
+            here = wholes[order[slot][0]].at[block(slot, origin_of(j), grp)]
             return remote(here, here, zsend.at[slot, 2 + j], zrecv.at[slot, turn[j]], partner)
 
         def onward(slot, j):
             step = jnp.where(turn[j] <= pos, 1, -1)
             to = pos + step
-            here = wholes[order[slot]].at[block(order[slot], origin_of(j), grp)]
+            here = wholes[order[slot][0]].at[block(slot, origin_of(j), grp)]
             landed = jnp.clip(turn[j] + step, 0, 3)
             copy = remote(
                 here,
@@ -613,21 +618,21 @@
             return (to >= 0) & (to <= 3), copy
 
         def plane(slot, j, way):
-            idx = order[slot]
+            idx = order[slot][0]
             origin = origin_of(j)
             if way < 2:
-                here = wholes[idx].at[block(idx, origin, grp)]
+                here = wholes[idx].at[block(slot, origin, grp)]
                 return remote(here, here, psend.at[slot, j, way], precv.at[slot, j, way], beside[way])
             half = shards[idx].shape[1] // 2
             there = wholes[idx].at[
-                block(idx, origin, grp ^ (way - 1)), pl.ds(half * (way - 2), half)
+                block(slot, origin, grp ^ (way - 1)), pl.ds(half * (way - 2), half)
             ]
             return remote(
                 there, there, psend.at[slot, j, way], precv.at[slot, j, way], beside[3 - way]
             )
 
         items = [(slot, j) for slot in range(len(order)) for j in range(3)]
-        crossing = [item for item in items if order[item[0]] not in whole_line]
+        crossing = [item for item in items if not order[item[0]][3]]
 
         def first(slot, j):
             arrived(slot, j).wait_recv()
@@ -647,15 +652,15 @@
             before()
         for slot in range(len(order)):
             start_own(slot)
-        for slot in range(len(order)):
-            load_own(slot).start()
+        for idx in staged:
+            load_own(idx).start()
         lag = 2
         for at in range(len(items) + lag):
             if at < len(items):
                 slot, j = items[at]
-                if j == 2:
-                    load_own(slot).wait()
-                    store_own(slot).start()
+                if j == 2 and slot < len(staged):
+                    load_own(staged[slot]).wait()
+                    store_own(staged[slot]).start()
                 first(slot, j)
             if at == len(items) - 1 and middle is not None:
                 middle()
@@ -664,8 +669,9 @@
         for slot, j in crossing:
             plane(slot, j, 2).wait_recv()
             plane(slot, j, 3).wait_recv()
+        for idx in staged:
+            store_own(idx).wait()
         for slot in range(len(order)):
-            store_own(slot).wait()
             for goes, copy in own_ends(slot):
                 pl.when(goes)(copy.wait_send)
         for slot, j in items:
@@ -700,24 +706,25 @@
             run(first_order, None, None)
 
 
-def gather_all(shards, first_order, last_order, whole_line, collective_id):
+def gather_all(shards, first_order, last_order, collective_id):
     count = len(shards)
+    slots = max(len(first_order), len(last_order))
     return pl.pallas_call(
-        functools.partial(gather_kernel, count, first_order, last_order, whole_line),
+        functools.partial(gather_kernel, count, first_order, last_order),
         out_shape=[jax.ShapeDtypeStruct((s.shape[0] * 4, s.shape[1]), s.dtype) for s in shards],
         in_specs=[ANYWHERE] * count,
         out_specs=[ANYWHERE] * count,
         scratch_shapes=[
             pltpu.SemaphoreType.DMA((count,)),
-            pltpu.SemaphoreType.DMA((count, 5)),
-            pltpu.SemaphoreType.DMA((count, 4)),
-            pltpu.SemaphoreType.DMA((count, 3, 4)),
-            pltpu.SemaphoreType.DMA((count, 3, 4)),
+            pltpu.SemaphoreType.DMA((slots, 5)),
+            pltpu.SemaphoreType.DMA((slots, 4)),
+            pltpu.SemaphoreType.DMA((slots, 3, 4)),
+            pltpu.SemaphoreType.DMA((slots, 3, 4)),
             pltpu.SemaphoreType.REGULAR,
         ]
         + [pltpu.VMEM(s.shape, s.dtype) for s in shards],
         compiler_params=pltpu.CompilerParams(
-            collective_id=collective_id, has_side_effects=True, vmem_limit_bytes=24 << 20
+            collective_id=collective_id, has_side_effects=True, vmem_limit_bytes=60 << 20
         ),
     )(*shards)
 
@@ -773,399 +780,6 @@
         ],
         compiler_params=pltpu.CompilerParams(collective_id=collective_id, has_side_effects=True),
     )(rows, ids)
-
-
-def strip_of(rows, columns):
-    strip = 16
-    while 2 * strip * columns <= 65536 and rows % (2 * strip) == 0:
-        strip = 2 * strip
-    return strip
-
-
-def add_rows(into, terms, rows, columns):
-    strip = strip_of(rows, columns)
-
-    def body(at, carry):
-        here = rows_at(at * strip, strip)
-        total = terms[0](here).astype(jnp.float32)
-        for term in terms[1:]:
-            total = total + term(here).astype(jnp.float32)
-        into(here, total)
-        return carry
-
-    lax.fori_loop(0, rows // strip, body, 0)
-
-
-def reduce_kernel(kinds, with_gains, only, *refs):
-    if only is None:
-        reduce_body(kinds, with_gains, *refs)
-    else:
-        pl.when(lax.axis_index("section") == only)(
-            functools.partial(reduce_body, kinds, with_gains, *refs)
-        )
-
-
-def reduce_body(kinds, with_gains, *refs):
-    count = len(kinds)
-    more = 1 if with_gains else 0
-    arrays = refs[:count]
-    outs = refs[count + more : 2 * count + more]
-    rest = list(refs[2 * count + 2 * more :])
-    s1, r1, own_sem, s2, r2, s3, r3, s4, r4, fin_sem = rest[:10]
-    bufs = rest[10 : 10 + 5 * count]
-    if with_gains:
-        gains = refs[count]
-        gain_out = refs[2 * count + 1]
-        gain_own_sem, sg, rg, gain_in, gain_got = rest[10 + 5 * count :]
-    own, got1, got2, got3, fin = ([bufs[5 * a + b] for a in range(count)] for b in range(5))
-    sec = lax.axis_index("section")
-    grp = lax.axis_index("group")
-    pos = lax.axis_index("dp")
-    beside = ((sec, grp ^ 1, pos), (sec, grp ^ 2, pos))
-    barrier = pltpu.get_barrier_semaphore()
-    steps = [(jg, jz) for jg in range(4) for jz in range(4)][1:]
-
-    def other(j):
-        return (sec, grp ^ steps[j - 1][0], lax.rem(pos + steps[j - 1][1], 4))
-
-    if with_gains:
-        peers = [other(j) for j in range(1, 16)]
-    else:
-        peers = [(sec, grp ^ j, pos) for j in (1, 2, 3)] + [other(j) for j in (1, 2, 3)]
-    for device in peers:
-        pl.semaphore_signal(barrier, inc=1, device_id=device, device_id_type=MESH)
-    pl.semaphore_wait(barrier, len(peers))
-
-    def when(a, run):
-        run()
-
-    def rows_of(a):
-        return outs[a].shape[0]
-
-    def part_of(a):
-        return outs[a].shape[0] // 4
-
-    def block(a, line, who):
-        return arrays[a].at[rows_at(line * rows_of(a) + who * part_of(a), part_of(a))]
-
-    def gain_copy(j):
-        device = other(j)
-        return remote(gain_in.at[device[2]], gain_got.at[j - 1], sg.at[j - 1], rg.at[j - 1], device)
-
-    def gain_load():
-        return pltpu.make_async_copy(gains, gain_in, gain_own_sem)
-
-    def ways(line):
-        first = 0 if line < 2 else 1
-        return first, 1 - first
-
-    def send_first(a, line, b):
-        first, second = ways(line)
-        who = grp ^ (1 + first)
-        if b:
-            who = who ^ (1 + second)
-        return remote(
-            block(a, line, who),
-            got1[a].at[line, b],
-            s1.at[a, line, b],
-            r1.at[a, line, b],
-            beside[first],
-        )
-
-    def load_own(a, line, b):
-        first, second = ways(line)
-        who = grp ^ (1 + second) if b else grp
-        return pltpu.make_async_copy(block(a, line, who), own[a].at[line, b], own_sem.at[a, line, b])
-
-    def send_second(a, line):
-        first, second = ways(line)
-        return remote(own[a].at[line, 1], got2[a].at[line], s2.at[a, line], r2.at[a, line], beside[second])
-
-    def send_line(a, line):
-        k = lax.rem(line - pos + 4, 4)
-        slot = jnp.maximum(k - 1, 0)
-        return remote(
-            own[a].at[line, 0], got3[a].at[slot], s3.at[a, line], r3.at[a, slot], (sec, grp, line)
-        )
-
-    def line_arrival(a, slot):
-        return remote(got3[a].at[slot], got3[a].at[slot], s3.at[a, slot], r3.at[a, slot], beside[0])
-
-    def begin(a, line):
-        def run():
-            for b in (1, 0):
-                send_first(a, line, b).start()
-                load_own(a, line, b).start()
-
-        when(a, run)
-
-    def middle(a, line):
-        def run():
-            columns = outs[a].shape[1]
-            for b in (1, 0):
-                load_own(a, line, b).wait()
-                send_first(a, line, b).wait_recv()
-
-                def into(here, total, b=b):
-                    own[a][line, b, here, :] = total.astype(jnp.bfloat16)
-
-                add_rows(
-                    into,
-                    [lambda here, b=b: own[a][line, b, here, :], lambda here, b=b: got1[a][line, b, here, :]],
-                    part_of(a),
-                    columns,
-                )
-                if b:
-                    send_second(a, line).start()
-
-        when(a, run)
-
-    def late(a, line):
-        def run():
-            send_second(a, line).wait_recv()
-
-            def into(here, total):
-                own[a][line, 0, here, :] = total.astype(jnp.bfloat16)
-
-            add_rows(
-                into,
-                [lambda here: own[a][line, 0, here, :], lambda here: got2[a][line, here, :]],
-                part_of(a),
-                outs[a].shape[1],
-            )
-            pl.when(line != pos)(send_line(a, line).start)
-
-        when(a, run)
-
-    def own_out(a):
-        here = outs[a].at[rows_at(grp * part_of(a), part_of(a))]
-        return pltpu.make_async_copy(fin[a], here, fin_sem.at[a])
-
-    def spread(a, way):
-        part = part_of(a)
-        if way < 2:
-            here = outs[a].at[rows_at(grp * part, part)]
-            return remote(fin[a], here, s4.at[a, way], r4.at[a, way], beside[way])
-        half = outs[a].shape[1] // 2
-        there = outs[a].at[rows_at((grp ^ (way - 1)) * part, part), pl.ds(half * (way - 2), half)]
-        return remote(there, there, s4.at[a, way], r4.at[a, way], beside[3 - way])
-
-    def spread_start(a):
-        spread(a, 0).start()
-        spread(a, 1).start()
-        own_out(a).start()
-
-    def finish(a):
-        def run():
-            for slot in range(3):
-                line_arrival(a, slot).wait_recv()
-
-            def into(here, total):
-                fin[a][here, :] = total.astype(jnp.bfloat16)
-
-            add_rows(
-                into,
-                [lambda here: own[a][pos, 0, here, :]]
-                + [lambda here, slot=slot: got3[a][slot, here, :] for slot in range(3)],
-                part_of(a),
-                outs[a].shape[1],
-            )
-            spread_start(a)
-
-        when(a, run)
-
-    def pass_on(a):
-        def run():
-            for way in (0, 1):
-                spread(a, way).wait_recv()
-                spread(a, way + 2).start()
-
-        when(a, run)
-
-    def line_rows(a, line):
-        return arrays[a].at[rows_at(line * rows_of(a), rows_of(a))]
-
-    def line_first(a, k):
-        to = lax.rem(pos + k, 4)
-        return remote(
-            line_rows(a, to), got1[a].at[k - 1], s1.at[a, k, 0], r1.at[a, k, 0], (sec, grp, to)
-        )
-
-    def line_own(a):
-        return pltpu.make_async_copy(line_rows(a, pos), own[a], own_sem.at[a, 0, 0])
-
-    def cross(a, j):
-        part = part_of(a)
-        to = grp ^ j
-        return remote(
-            own[a].at[rows_at(to * part, part)],
-            got3[a].at[j - 1],
-            s3.at[a, j],
-            r3.at[a, j - 1],
-            (sec, to, pos),
-        )
-
-    def line_begin(a):
-        def run():
-            for k in (2, 1, 3):
-                line_first(a, k).start()
-            line_own(a).start()
-
-        when(a, run)
-
-    def line_middle(a):
-        def run():
-            line_own(a).wait()
-            for k in (1, 2, 3):
-                line_first(a, k).wait_recv()
-
-            def into(here, total):
-                own[a][here, :] = total.astype(jnp.bfloat16)
-
-            add_rows(
-                into,
-                [lambda here: own[a][here, :]]
-                + [lambda here, k=k: got1[a][k, here, :] for k in range(3)],
-                rows_of(a),
-                outs[a].shape[1],
-            )
-            for j in (3, 1, 2):
-                cross(a, j).start()
-
-        when(a, run)
-
-    def line_finish(a):
-        def run():
-            part = part_of(a)
-            for j in (1, 2, 3):
-                cross(a, j).wait_recv()
-
-            def into(here, total):
-                fin[a][here, :] = total.astype(jnp.bfloat16)
-
-            strip = strip_of(part, outs[a].shape[1])
-
-            def body(at, carry):
-                here = rows_at(at * strip, strip)
-                total = own[a][rows_at(grp * part + at * strip, strip), :].astype(jnp.float32)
-                for j in range(3):
-                    total = total + got3[a][j, here, :].astype(jnp.float32)
-                fin[a][here, :] = total.astype(jnp.bfloat16)
-                return carry
-
-            lax.fori_loop(0, part // strip, body, 0)
-            spread_start(a)
-
-        when(a, run)
-
-    plane_arrays = [a for a in range(count) if kinds[a] == "plane"]
-    line_arrays = [a for a in range(count) if kinds[a] == "line"]
-    units = [(a, line) for a in plane_arrays for line in (0, 2, 1, 3)]
-    ahead = 6
-    if with_gains:
-        gain_load().start()
-    for unit in units[:2]:
-        begin(*unit)
-    for a in line_arrays:
-        line_begin(a)
-    for unit in units[2:ahead]:
-        begin(*unit)
-    if with_gains:
-        gain_load().wait()
-        for j in range(1, 16):
-            gain_copy(j).start()
-    lag = 2
-    finished = []
-    for at in range(len(units) + lag + 4):
-        if at + ahead < len(units):
-            begin(*units[at + ahead])
-        if at < len(units):
-            middle(*units[at])
-        if at == len(units) // 2:
-            for a in line_arrays:
-                line_middle(a)
-        if at == len(units) // 2 + 2:
-            for a in line_arrays:
-                line_finish(a)
-        if at == len(units) // 2 + 4:
-            for a in line_arrays:
-                pass_on(a)
-        if lag <= at < len(units) + lag:
-            late(*units[at - lag])
-        spot = at - lag - 2
-        if 0 <= spot < len(units) and units[spot][1] == 3:
-            if finished:
-                pass_on(finished[-1])
-            finish(units[spot][0])
-            finished.append(units[spot][0])
-    pass_on(finished[-1])
-    if with_gains:
-        for j in range(1, 16):
-            gain_copy(j).wait_recv()
-        total = gain_in[pos]
-        for j in range(15):
-            total = total + gain_got[j]
-        gain_out[...] = total
-    for a in range(count):
-
-        def run(a=a):
-            spread(a, 2).wait_recv()
-            spread(a, 3).wait_recv()
-            own_out(a).wait()
-            for way in range(4):
-                spread(a, way).wait_send()
-            if kinds[a] == "plane":
-                for line in range(4):
-                    for b in (0, 1):
-                        send_first(a, line, b).wait_send()
-                    send_second(a, line).wait_send()
-                    pl.when(line != pos)(send_line(a, line).wait_send)
-            else:
-                for k in (1, 2, 3):
-                    line_first(a, k).wait_send()
-                    cross(a, k).wait_send()
-
-        when(a, run)
-    if with_gains:
-        for j in range(1, 16):
-            gain_copy(j).wait_send()
-
-
-def reduce_all(arrays, gains, kinds, only, collective_id):
-    count = len(arrays)
-    more = 0 if gains is None else 1
-    outs = [jax.ShapeDtypeStruct((x.shape[0] // 4, x.shape[1]), x.dtype) for x in arrays]
-    buffers = []
-    for x, kind in zip(arrays, kinds):
-        rows, columns = x.shape[0] // 4, x.shape[1]
-        part = rows // 4
-        if kind == "plane":
-            shapes = [(4, 2, part, columns), (4, 2, part, columns), (4, part, columns)]
-        else:
-            shapes = [(rows, columns), (3, rows, columns), (8, 128)]
-        shapes += [(3, part, columns), (part, columns)]
-        buffers += [pltpu.VMEM(shape, x.dtype) for shape in shapes]
-    dma = pltpu.SemaphoreType.DMA
-    scratch = [dma((count, 4, 2))] * 3 + [dma((count, 4))] * 6 + [dma((count,))] + buffers
-    if more:
-        outs.append(jax.ShapeDtypeStruct(gains.shape[1:], gains.dtype))
-        scratch += [
-            dma,
-            dma((15,)),
-            dma((15,)),
-            pltpu.VMEM(gains.shape, gains.dtype),
-            pltpu.VMEM((15,) + gains.shape[1:], gains.dtype),
-        ]
-    return pl.pallas_call(
-        functools.partial(reduce_kernel, kinds, bool(more), only),
-        out_shape=outs,
-        in_specs=[ANYWHERE] * (count + more),
-        out_specs=[ANYWHERE] * count + [pl.BlockSpec(memory_space=pltpu.VMEM)] * more,
-        scratch_shapes=scratch,
-        compiler_params=pltpu.CompilerParams(
-            collective_id=collective_id, has_side_effects=True, vmem_limit_bytes=58 << 20
-        ),
-    )(*arrays, *((gains,) if more else ()))
 
 
 IN_VMEM = pl.BlockSpec(memory_space=pltpu.VMEM)
@@ -1610,12 +1224,594 @@
     )(proj, ids, scale, table)
 
 
+def strip_of(rows, columns):
+    strip = 16
+    while 2 * strip * columns <= 65536 and rows % (2 * strip) == 0:
+        strip = 2 * strip
+    return strip
+
+
+def add_rows(store, terms, rows, columns):
+    strip = strip_of(rows, columns)
+
+    def body(at, carry):
+        here = rows_at(at * strip, strip)
+        total = terms[0](here).astype(jnp.float32)
+        for term in terms[1:]:
+            total = total + term(here).astype(jnp.float32)
+        store(here, total)
+        return carry
+
+    lax.fori_loop(0, rows // strip, body, 0)
+
+
+def reduce_kernel(plan, spots, only, extras, ahead, refs_of, *refs):
+    body = functools.partial(reduce_body, plan, spots, extras, ahead, refs_of(refs))
+    if only is None:
+        body()
+    else:
+        pl.when(lax.axis_index("section") == only)(body)
+
+
+def reduce_body(plan, spots, extras, ahead, named):
+    arrays, outs = named["arrays"], named["outs"]
+    own, got1, got2, got3, land = (named[k] for k in ("own", "got1", "got2", "got3", "land"))
+    s1, r1, own_sem, s2, r2, s3, r3, s4, r4, fin_sem = named["sems"]
+    count = len(plan)
+    sec = lax.axis_index("section")
+    grp = lax.axis_index("group")
+    pos = lax.axis_index("dp")
+    beside = ((sec, grp ^ 1, pos), (sec, grp ^ 2, pos))
+    sides = [(sec, grp ^ j, pos) for j in (1, 2, 3)]
+    line_peers = [(sec, grp, lax.rem(pos + k, 4)) for k in (1, 2, 3)]
+    steps = [(jg, jz) for jg in range(4) for jz in range(4)][1:]
+
+    def other(j):
+        return (sec, grp ^ steps[j][0], lax.rem(pos + steps[j][1], 4))
+
+    with_gains = "gains" in extras
+    spreads = "spread" in extras
+    looked = "looked" in extras
+    peers = [other(j) for j in range(15)] if with_gains else sides + line_peers
+    barrier = pltpu.get_barrier_semaphore()
+    for device in peers:
+        pl.semaphore_signal(barrier, inc=1, device_id=device, device_id_type=MESH)
+    pl.semaphore_wait(barrier, len(peers))
+
+    def rows_of(p):
+        return arrays[plan[p][0]].shape[0] // 4
+
+    def columns_of(p):
+        return arrays[plan[p][0]].shape[1]
+
+    def sub_of(p):
+        return rows_of(p) // 4 // plan[p][3]
+
+    def block(p, line, who):
+        start = line * rows_of(p) + who * (rows_of(p) // 4) + plan[p][2] * sub_of(p)
+        return arrays[plan[p][0]].at[rows_at(start, sub_of(p))]
+
+    def ways(line):
+        return (0, 1) if line < 2 else (1, 0)
+
+    def send_first(p, line, b):
+        first, second = ways(line)
+        who = grp ^ (1 + first)
+        if b:
+            who = who ^ (1 + second)
+        return remote(
+            block(p, line, who),
+            got1[p].at[line, b],
+            s1.at[p, line, b],
+            r1.at[p, line, b],
+            beside[first],
+        )
+
+    def load_own(p, line, b):
+        who = grp ^ (1 + ways(line)[1]) if b else grp
+        return pltpu.make_async_copy(block(p, line, who), own[p].at[line, b], own_sem.at[p, line, b])
+
+    def send_second(p, line):
+        second = ways(line)[1]
+        return remote(own[p].at[line, 1], got2[p].at[line], s2.at[p, line], r2.at[p, line], beside[second])
+
+    def send_line(p, line):
+        slot = jnp.maximum(lax.rem(line - pos + 4, 4) - 1, 0)
+        return remote(
+            own[p].at[line, 0], got3[p].at[slot], s3.at[p, line], r3.at[p, slot], (sec, grp, line)
+        )
+
+    def line_arrival(p, slot):
+        return remote(got3[p].at[slot], got3[p].at[slot], s3.at[p, slot], r3.at[p, slot], beside[0])
+
+    def begin(p, line):
+        for b in (1, 0):
+            send_first(p, line, b).start()
+            load_own(p, line, b).start()
+
+    def middle(p, line):
+        for b in (1, 0):
+            load_own(p, line, b).wait()
+            send_first(p, line, b).wait_recv()
+
+            def store(here, total, b=b):
+                own[p][line, b, here, :] = total.astype(jnp.bfloat16)
+
+            add_rows(
+                store,
+                [
+                    lambda here, b=b: own[p][line, b, here, :],
+                    lambda here, b=b: got1[p][line, b, here, :],
+                ],
+                sub_of(p),
+                columns_of(p),
+            )
+            if b:
+                send_second(p, line).start()
+
+    def late(p, line):
+        send_second(p, line).wait_recv()
+
+        def store(here, total):
+            own[p][line, 0, here, :] = total.astype(jnp.bfloat16)
+
+        add_rows(
+            store,
+            [lambda here: own[p][line, 0, here, :], lambda here: got2[p][line, here, :]],
+            sub_of(p),
+            columns_of(p),
+        )
+        pl.when(line != pos)(send_line(p, line).start)
+
+    pending = {}
+
+    def write_out(p, who, term):
+        rings = named["rings"][spots[p]]
+        turn = pending.setdefault(spots[p], [])
+        slot = len(turn) % 2
+        if len(turn) >= 2:
+            turn[-2].wait()
+        ring = rings.at[slot]
+
+        def store(here, total):
+            rings[slot, here, :] = total
+
+        add_rows(store, term, sub_of(p), columns_of(p))
+        start = who * (rows_of(p) // 4) + plan[p][2] * sub_of(p)
+        copy = pltpu.make_async_copy(
+            ring, outs[plan[p][0]].at[rows_at(start, sub_of(p))], named["ring_sem"].at[spots[p], slot]
+        )
+        copy.start()
+        turn.append(copy)
+
+    def drain():
+        for turn in pending.values():
+            for copy in turn[-2:]:
+                copy.wait()
+
+    def spread(p, way):
+        if way < 2:
+            here = land[p].at[grp]
+            return remote(here, here, s4.at[p, way], r4.at[p, way], beside[way])
+        half = columns_of(p) // 2
+        there = land[p].at[grp ^ (way - 1), :, pl.ds(half * (way - 2), half)]
+        return remote(there, there, s4.at[p, way], r4.at[p, way], beside[3 - way])
+
+    def settle(p, terms):
+        def store(here, total):
+            land[p][grp, here, :] = total.astype(jnp.bfloat16)
+
+        add_rows(store, terms, sub_of(p), columns_of(p))
+        if spreads:
+            spread(p, 0).start()
+            spread(p, 1).start()
+        else:
+            own_out(p).start()
+
+    def own_out(p):
+        return pltpu.make_async_copy(
+            land[p].at[grp], outs[plan[p][0]].at[rows_at(plan[p][2] * sub_of(p), sub_of(p))], fin_sem.at[p]
+        )
+
+    def arrival(p, way):
+        who = (grp ^ 1, grp ^ 2)[way]
+        return remote(land[p].at[who], land[p].at[who], s4.at[p, way], r4.at[p, way], beside[way])
+
+    def finish(p):
+        for slot in range(3):
+            line_arrival(p, slot).wait_recv()
+        settle(
+            p,
+            [lambda here: own[p][pos, 0, here, :]]
+            + [lambda here, slot=slot: got3[p][slot, here, :] for slot in range(3)],
+        )
+
+    def pass_on(p):
+        if spreads:
+            for way in (0, 1):
+                arrival(p, way).wait_recv()
+                spread(p, way + 2).start()
+
+    def write_near(p):
+        if spreads:
+            for who in (grp, grp ^ 1, grp ^ 2):
+                write_out(p, who, [lambda here, who=who: land[p][who, here, :]])
+
+    def write_far(p):
+        if spreads:
+            spread(p, 2).wait_recv()
+            spread(p, 3).wait_recv()
+            write_out(p, grp ^ 3, [lambda here: land[p][grp ^ 3, here, :]])
+
+    def line_rows(p, line):
+        return arrays[plan[p][0]].at[rows_at(line * rows_of(p), rows_of(p))]
+
+    def line_first(p, k):
+        to = lax.rem(pos + k, 4)
+        return remote(
+            line_rows(p, to), got1[p].at[k - 1], s1.at[p, k, 0], r1.at[p, k, 0], (sec, grp, to)
+        )
+
+    def line_own(p):
+        return pltpu.make_async_copy(line_rows(p, pos), own[p], own_sem.at[p, 0, 0])
+
+    def cross(p, j):
+        to = grp ^ j
+        return remote(
+            own[p].at[rows_at(to * sub_of(p), sub_of(p))],
+            got3[p].at[j - 1],
+            s3.at[p, j],
+            r3.at[p, j - 1],
+            (sec, to, pos),
+        )
+
+    def line_begin(p):
+        for k in (2, 1, 3):
+            line_first(p, k).start()
+        line_own(p).start()
+
+    def line_middle(p):
+        line_own(p).wait()
+        for k in (1, 2, 3):
+            line_first(p, k).wait_recv()
+
+        def store(here, total):
+            own[p][here, :] = total.astype(jnp.bfloat16)
+
+        add_rows(
+            store,
+            [lambda here: own[p][here, :]] + [lambda here, k=k: got1[p][k, here, :] for k in range(3)],
+            rows_of(p),
+            columns_of(p),
+        )
+        for j in (3, 1, 2):
+            cross(p, j).start()
+
+    def line_finish(p):
+        for j in (1, 2, 3):
+            cross(p, j).wait_recv()
+        base = grp * sub_of(p)
+        strip = strip_of(sub_of(p), columns_of(p))
+        settle(
+            p,
+            [lambda here: own[p][rows_at(base + here.start, strip), :]]
+            + [lambda here, j=j: got3[p][j, here, :] for j in range(3)],
+        )
+
+    if with_gains:
+        gain_in, gain_got, sg, rg, gain_sem = named["gain_scratch"]
+
+        def gain_copy(j):
+            device = other(j)
+            return remote(gain_in.at[device[2]], gain_got.at[j], sg.at[j], rg.at[j], device)
+
+        gain_load = pltpu.make_async_copy(named["gains"], gain_in, gain_sem)
+        gain_load.start()
+
+    if looked:
+        looks, looks_own, sl, rl, table_fin, tland, tsum = named["look_scratch"]
+        ids, look_in, fin_in = named["look_in"]
+        vocab_quarter = fin_in.shape[0]
+        look_load = pltpu.make_async_copy(look_in, looks.at[grp, pos], looks_own.at[0])
+        fin_load = pltpu.make_async_copy(fin_in, table_fin, looks_own.at[1])
+
+        def look_line(k):
+            here = looks.at[grp, pos]
+            return remote(here, here, sl.at[k], rl.at[k], line_peers[k])
+
+        def look_side(k):
+            here = looks.at[grp]
+            return remote(here, here, sl.at[3 + k], rl.at[3 + k], sides[k])
+
+        def table_spread(way):
+            if way < 2:
+                here = tland.at[grp]
+                return remote(here, here, sl.at[6 + way], rl.at[6 + way], beside[way])
+            half = tland.shape[2] // 2
+            there = tland.at[grp ^ (way - 1), :, pl.ds(half * (way - 2), half)]
+            return remote(there, there, sl.at[6 + way], rl.at[6 + way], beside[3 - way])
+
+        def table_out(who):
+            return pltpu.make_async_copy(
+                tland.at[who],
+                named["table_out"].at[rows_at(who * vocab_quarter, vocab_quarter)],
+                looks_own.at[2 + who],
+            )
+
+        def look_begin():
+            look_load.start()
+            fin_load.start()
+            look_load.wait()
+            for k in range(3):
+                look_line(k).start()
+
+        def look_middle():
+            for k in range(3):
+                look_line(k).wait_recv()
+            for k in range(3):
+                look_side(k).start()
+
+        def look_sum():
+            for k in range(3):
+                look_side(k).wait_recv()
+            fin_load.wait()
+            base = pos * (4 * vocab_quarter) + grp * vocab_quarter
+            tall = 256
+            names = lax.broadcasted_iota(jnp.int32, (tall, ids.shape[2]), 0)
+
+            def body(at, carry):
+                here = rows_at(at * tall, tall)
+                total = table_fin[here, :].astype(jnp.float32)
+                for g in range(4):
+                    for z in range(4):
+                        hit = names + (base + at * tall) == ids[g * 4 + z]
+                        total = total + dot_nn(
+                            jnp.where(hit, 1.0, 0.0).astype(jnp.bfloat16), looks[g, z]
+                        )
+                tland[grp, here, :] = total.astype(jnp.bfloat16)
+                return carry
+
+            lax.fori_loop(0, vocab_quarter // tall, body, 0)
+            table_spread(0).start()
+            table_spread(1).start()
+
+        def look_pass():
+            for way in (0, 1):
+                who = (grp ^ 1, grp ^ 2)[way]
+                remote(
+                    tland.at[who], tland.at[who], sl.at[6 + way], rl.at[6 + way], beside[way]
+                ).wait_recv()
+                table_spread(way + 2).start()
+
+        def look_end():
+            table_spread(2).wait_recv()
+            table_spread(3).wait_recv()
+            for who in range(4):
+                table_out(who).start()
+            for who in range(4):
+                table_out(who).wait()
+            for k in range(3):
+                look_line(k).wait_send()
+                look_side(k).wait_send()
+            for way in range(4):
+                table_spread(way).wait_send()
+
+        def on_first(run):
+            pl.when(sec == 0)(run)
+
+    else:
+
+        def on_first(run):
+            pass
+
+        look_begin = look_middle = look_sum = look_pass = look_end = None
+
+    planes = [p for p in range(count) if plan[p][1] == "plane"]
+    lines = [p for p in range(count) if plan[p][1] == "line"]
+    units = [(p, line) for p in planes for line in (0, 2, 1, 3)]
+    for unit in units[:2]:
+        begin(*unit)
+    for p in lines:
+        line_begin(p)
+    on_first(look_begin)
+    for unit in units[2:ahead]:
+        begin(*unit)
+    if with_gains:
+        gain_load.wait()
+        for j in range(15):
+            gain_copy(j).start()
+    lag = 3
+    total_steps = len(units) + lag
+    done = []
+    for at in range(total_steps):
+        if at + ahead < len(units):
+            begin(*units[at + ahead])
+        if at < len(units):
+            middle(*units[at])
+        if at >= lag:
+            p, line = units[at - lag]
+            late(p, line)
+            if line == 1 and len(done) >= 1:
+                finish(done[-1])
+            if line == 2 and len(done) >= 2:
+                pass_on(done[-2])
+            if line == 0 and len(done) >= 3:
+                write_near(done[-3])
+            if line == 3:
+                done.append(p)
+        if at == len(units) // 4:
+            on_first(look_middle)
+        if at == len(units) // 2:
+            on_first(look_sum)
+        if at == 3 * len(units) // 4:
+            on_first(look_pass)
+    for p in lines:
+        line_middle(p)
+    finish(done[-1])
+    written = max(len(done) - 3, 0)
+    passed = max(len(done) - 2, 0)
+    for p in done[passed:]:
+        pass_on(p)
+    for p in lines:
+        line_finish(p)
+    for p in done[written:]:
+        write_near(p)
+    for p in lines:
+        pass_on(p)
+    for p in done:
+        write_far(p)
+    for p in lines:
+        write_near(p)
+        write_far(p)
+    if with_gains:
+        for j in range(15):
+            gain_copy(j).wait_recv()
+        total = gain_in[pos]
+        for j in range(15):
+            total = total + gain_got[j]
+        named["gain_out"][...] = total
+    on_first(look_end)
+    drain()
+    for p in range(count):
+        if spreads:
+            for way in range(4):
+                spread(p, way).wait_send()
+        else:
+            own_out(p).wait()
+        if plan[p][1] == "plane":
+            for line in range(4):
+                for b in (0, 1):
+                    send_first(p, line, b).wait_send()
+                send_second(p, line).wait_send()
+                pl.when(line != pos)(send_line(p, line).wait_send)
+        else:
+            for k in (1, 2, 3):
+                line_first(p, k).wait_send()
+                cross(p, k).wait_send()
+    if with_gains:
+        for j in range(15):
+            gain_copy(j).wait_send()
+
+
+def reduce_all(arrays, plan, only, collective_id, ahead, gains=None, look=None, spread=True):
+    low, f32, dma = jnp.bfloat16, jnp.float32, pltpu.SemaphoreType.DMA
+    extras = ("spread",) * spread + ("gains",) * (gains is not None) + ("looked",) * (look is not None)
+    count = len(plan)
+    inputs = list(arrays)
+    kind = f32 if spread else low
+    share = 4 if spread else 16
+    outs = [jax.ShapeDtypeStruct((x.shape[0] // share, x.shape[1]), kind) for x in arrays]
+    out_specs = [ANYWHERE] * len(arrays)
+    in_specs = [ANYWHERE] * len(arrays)
+    names = ["own", "got1", "got2", "got3", "land"]
+    scratch = {name: [] for name in names}
+    ring_shapes = []
+    spots = []
+    for src, way, _, chunks in plan:
+        rows, columns = arrays[src].shape[0] // 4, arrays[src].shape[1]
+        sub = rows // 4 // chunks
+        if way == "plane":
+            shapes = [(4, 2, sub, columns), (4, 2, sub, columns), (4, sub, columns)]
+        else:
+            shapes = [(rows, columns), (3, rows, columns), (8, 128)]
+        for name, shape in zip(names, shapes + [(3, sub, columns), (4, sub, columns)]):
+            scratch[name].append(pltpu.VMEM(shape, low))
+        if (sub, columns) not in ring_shapes:
+            ring_shapes.append((sub, columns))
+        spots.append(ring_shapes.index((sub, columns)))
+    flat = [item for name in names for item in scratch[name]]
+    sems = [dma((count, 4, 2))] * 3 + [dma((count, 4))] * 6 + [dma((count,))]
+    tail = []
+    if spread:
+        tail += [pltpu.VMEM((2,) + shape, f32) for shape in ring_shapes] + [dma((len(ring_shapes), 2))]
+    if gains is not None:
+        inputs.append(gains)
+        in_specs.append(ANYWHERE)
+        outs.append(jax.ShapeDtypeStruct(gains.shape[1:], f32))
+        out_specs.append(IN_VMEM)
+        tail += [
+            pltpu.VMEM(gains.shape, f32),
+            pltpu.VMEM((15,) + gains.shape[1:], f32),
+            dma((15,)),
+            dma((15,)),
+            dma,
+        ]
+    if look is not None:
+        ids, rows_in, fin_in = look
+        inputs += [ids, rows_in, fin_in]
+        in_specs += [IN_VMEM, ANYWHERE, ANYWHERE]
+        quarter, emb = fin_in.shape
+        outs.append(jax.ShapeDtypeStruct((4 * quarter, emb), low))
+        out_specs.append(ANYWHERE)
+        tail += [
+            pltpu.VMEM((4, 4) + rows_in.shape, low),
+            dma((6,)),
+            dma((10,)),
+            dma((10,)),
+            pltpu.VMEM(fin_in.shape, low),
+            pltpu.VMEM((4, quarter, emb), low),
+            pltpu.VMEM((8, 128), f32),
+        ]
+
+    def refs_of(refs):
+        at = 0
+
+        def take(n):
+            nonlocal at
+            at += n
+            return list(refs[at - n : at])
+
+        named = {"arrays": take(len(arrays))}
+        if gains is not None:
+            named["gains"] = take(1)[0]
+        if look is not None:
+            named["look_in"] = take(3)
+        named["outs"] = take(len(arrays))
+        if gains is not None:
+            named["gain_out"] = take(1)[0]
+        if look is not None:
+            named["table_out"] = take(1)[0]
+        for name in names:
+            named[name] = take(count)
+        named["sems"] = take(10)
+        if spread:
+            named["rings"] = take(len(ring_shapes))
+            named["ring_sem"] = take(1)[0]
+        if gains is not None:
+            named["gain_scratch"] = take(5)
+        if look is not None:
+            named["look_scratch"] = take(7)
+        return named
+
+    return pl.pallas_call(
+        functools.partial(reduce_kernel, plan, tuple(spots), only, extras, ahead, refs_of),
+        out_shape=outs,
+        in_specs=in_specs,
+        out_specs=out_specs,
+        scratch_shapes=flat + sems + tail,
+        compiler_params=pltpu.CompilerParams(
+            collective_id=collective_id, has_side_effects=True, vmem_limit_bytes=60 << 20
+        ),
+    )(*inputs)
+
+
 def nothing_like(run):
     return jax.tree.map(lambda a: jnp.zeros(a.shape, a.dtype), jax.eval_shape(run))
 
 
 def only_on(live, run):
     return lax.cond(live, run, lambda: nothing_like(run))
+
+
+LAYER_PLAN = (
+    (0, "plane", 0, 1),
+    (1, "plane", 0, 1),
+    (2, "plane", 0, 1),
+    (3, "plane", 0, 1),
+    (4, "line", 0, 1),
+)
+LAYER_AHEAD = 6
+TABLE_AHEAD = 8
 
 
 def after(value, *others):
@@ -1653,7 +1849,18 @@
     )
     ids = jnp.concatenate([tokens.reshape(-1, 128), jnp.zeros((8 - rows // 128, 128), jnp.int32)], 0)
     shards = (w_qkv[0], w_proj[0], w_up[0], w_down[0], w_in, w_out, gains, ids)
-    wholes = gather_all(shards, (7, 6, 4, 0, 1, 2, 3), (6, 0, 1, 2, 3, 5), (6, 7, 1), 0)
+    sizes = [s.shape[0] for s in shards]
+
+    def entry(idx, whole=False):
+        return (idx, 0, sizes[idx], whole)
+
+    half = sizes[3] // 2
+    wholes = gather_all(
+        shards,
+        (entry(7, True), entry(6, True), entry(4), entry(0), entry(1), entry(2), entry(3)),
+        (entry(6, True), entry(0), entry(1, True), entry(2), (3, 0, half, True), (3, half, half, False), entry(5)),
+        0,
+    )
     qkv_weight, proj_weight, up_weight, down_weight, in_weight, out_weight, gain_all, line_ids = wholes
     gain_all = gain_all.reshape(4, 16, -1).astype(jnp.float32)
     gain_attn = gain_all[:, 0].reshape(-1)
@@ -1687,21 +1894,31 @@
 
     mixed_in, x_first = only_on(first_section, front)
     kept = run_forward(0, x_first, gain_attn, gain_mlp, lengths, weights, None)
-    x_second = passed_along(kept[9].astype(jnp.bfloat16), "section", 1)
-    (table_full,) = gather_all((after(embed_table, x_second),), (0,), (), (), 2)
+    out_first = kept[9].astype(jnp.bfloat16)
+    (table_full,) = gather_all(
+        (after(embed_table, out_first),), ((0, 0, vocab_part, False),), (), 2
+    )
+    x_second = passed_along(after(out_first, table_full), "section", 1)
     kept = run_forward(1, x_second, gain_attn, gain_mlp, lengths, weights, kept)
     final_in = normed(kept[9], final_gain).astype(jnp.bfloat16)
     projected = product(final_in, out_weight).astype(jnp.bfloat16)
-    projected = passed_along(after(projected, table_full), "section", -1)
+    projected = passed_along(projected, "section", -1)
     valid_scale = jnp.where(key_valid.reshape(1, -1), loss_scale, 0.0)
     grad_proj_a, entropy, table_g = run_vocabulary(
         0, projected, tokens[None], valid_scale, table_full
     )
     grad_proj = passed_along(grad_proj_a, "section", 1)
-    (table_r,) = reduce_all((after(table_g, grad_proj),), None, ("plane",), 0, 3)
+    (table_fin,) = reduce_all(
+        (after(table_g, grad_proj),),
+        tuple((0, "plane", chunk, 4) for chunk in range(4)),
+        0,
+        3,
+        TABLE_AHEAD,
+        spread=False,
+    )
     grad_top, gain_final = norm_back(kept[9], final_gain, product_nt(grad_proj, out_weight))
     made = run_backward(1, grad_top, gain_attn, gain_mlp, lengths, kept, weights, None)
-    grad_first = passed_along(after(made[4], table_r), "section", -1)
+    grad_first = passed_along(after(made[4], table_fin), "section", -1)
     made = run_backward(0, grad_first, gain_attn, gain_mlp, lengths, kept, weights, made)
     shape = in_weight.shape
 
@@ -1730,18 +1947,17 @@
         grads_of(kept[4], made[2]),
         grads_of(kept[1], made[3]),
     )
-    kinds = ("plane",) * 4 + ("line",)
-    up_r, down_r, edge_r, proj_r, qkv_r, gain_r = reduce_all(order, gain_rows, kinds, None, 4)
-    looked_all = lax.all_gather(looked_grad, ("group", "dp"), axis=0, tiled=True)
-
-    def add_looked():
-        local = all_tokens - pos * vocab_part
-        hit = lax.broadcasted_iota(jnp.int32, (vocab_part, 1), 0) == local[None, :]
-        looked_sum = product(hit.astype(jnp.bfloat16), looked_all)
-        return (looked_sum + table_r.astype(jnp.float32)).astype(jnp.bfloat16)
-
+    up_r, down_r, edge_r, proj_r, qkv_r, gain_r, table_r = reduce_all(
+        order,
+        LAYER_PLAN,
+        None,
+        4,
+        LAYER_AHEAD,
+        gains=gain_rows,
+        look=(all_tokens.reshape(16, 1, rows), looked_grad, table_fin),
+    )
     loss_low = after(entropy, gain_r)[0].astype(jnp.bfloat16)
-    mine = (only_on(first_section, add_looked), edge_r, gain_r, loss_low)
+    mine = (table_r, edge_r, gain_r, loss_low)
     theirs = lax.ppermute(mine, "section", [(0, 1), (1, 0)])
 
     def pair_of(at):
@@ -1756,15 +1972,15 @@
     return (
         token_loss,
         table_out,
-        in_r.astype(jnp.float32),
+        in_r,
         gain_r[0][None],
-        qkv_r.astype(jnp.float32)[None],
-        proj_r.astype(jnp.float32)[None],
+        qkv_r[None],
+        proj_r[None],
         gain_r[1][None],
-        up_r.astype(jnp.float32)[None],
-        down_r.astype(jnp.float32)[None],
+        up_r[None],
+        down_r[None],
         final_r,
-        out_r.astype(jnp.float32).reshape(-1, emb),
+        out_r.reshape(-1, emb),
     )
 
 

time: 785 us -> 706 us (0.90)
  starting transfers between devices: 44 us -> 10.7 us
  Pallas kernels: 613 us -> 595 us
  waiting for transfers between devices: 6.84 us -> 23.9 us
  matrix products: 40.2 us -> 24.4 us
  between operations: 14.7 us -> 1.26 us
    ppermute x4, starting transfers between devices: 42.7 us -> 9.58 us  [passed_along(): return lax.ppermute(x, axis, pairs)]
    pallas_call x2, Pallas kernels: 357 us -> 328 us  [reduce_all(): pl.pallas_call(functools.partial(reduce_kernel, plan, tuple(spots), only,...]
    pallas_call x2, Pallas kernels: 164 us -> 184 us  [gather_all(): pl.pallas_call(functools.partial(gather_kernel, count, first_order, last_...]
    dot_general x8 -> x7, matrix products: 37.2 us -> 22.2 us  [product(): return jnp.dot(left_side, right_side, preferred_element_type=jnp.float32)]
    ppermute x4, waiting for transfers between devices: 6.81 us -> 20.9 us  [passed_along(): return lax.ppermute(x, axis, pairs)]
    broadcast_in_dim x4 -> x0, other arithmetic: 11.5 us -> none  [the longest x1 4.19 us: per_device(): down_r.astype(jnp.float32)[None]]
    pallas_call x2, Pallas kernels: 36.6 us -> 27.4 us  [run_backward(): pl.pallas_call(functools.partial(backward_kernel, only, tile, given), out...]
    unnamed x66 -> x50, local copies, waits for them, and re-layouts: 23.6 us -> 14.7 us
  transfers between devices with their start and end apart: 9 -> 8, of which waited for: 4 -> 5; matrix products, arithmetic and copies ran while one was open for 6% -> 1% of each run, Pallas kernels for 37% -> 0%
where the time goes in v5:
time: 706 us; the launch traced here: 695 us
  Pallas kernels  595 us (84%)
  matrix products  24.4 us (3%)
  waiting for transfers between devices  23.9 us (3%)
  local copies, waits for them, and re-layouts  20.6 us (3%)
  other arithmetic  18.7 us (3%)
  starting transfers between devices  10.7 us (2%)
    pallas_call x2, Pallas kernels, reduce_all(): pl.pallas_call(functools.partial(reduce_kernel, plan, tuple(spots), only,...  328 us
    pallas_call x2, Pallas kernels, gather_all(): pl.pallas_call(functools.partial(gather_kernel, count, first_order, last_...  184 us
    pallas_call x2, Pallas kernels, run_backward(): pl.pallas_call(functools.partial(backward_kernel, only, tile, given), out...  27.4 us
    pallas_call x1, Pallas kernels, run_vocabulary(): pl.pallas_call(functools.partial(vocabulary_kernel, only, tile), out_shap...  25.8 us
    dot_general x7, matrix products, product(): return jnp.dot(left_side, right_side, preferred_element_type=jnp.float32)  22.2 us
    ppermute x4, waiting for transfers between devices, passed_along(): return lax.ppermute(x, axis, pairs)  20.9 us
    pallas_call x2, Pallas kernels, run_forward(): pl.pallas_call(functools.partial(forward_kernel, only, tile, given), out_...  19.4 us
    unnamed x50, local copies, waits for them, and re-layouts  14.7 us
  transfers between devices with their start and end apart: 8, of which 5 were waited for; matrix products, arithmetic and copies ran while one was open for 1% of the time, Pallas kernels for 0%

profile of v5, /device:TPU:0, one launch (start us, length us, event | category | flops | bytes accessed | tf_op | source)
XLA Modules:
  0.0 695.0 jit_solution(16313017713660249795)
XLA Ops:
  0.7 0.7 broadcast_in_dim.57
  1.3 0.7 add_rsqrt_fusion
  2.0 1.3 concatenate.10.refs_7_
  3.3 1.4 maximum_maximum_fusion.refs_6_
  4.7 118.3 %shard_map.222 = (bf16[1024,3072]{1,0:T(8,128)(2,1)}, bf16[1024,1024]{1,0:T(8,128)(2,1)}, bf16[1024,4096]{1,0:T(8,128)(2,1)}, bf16[4096,1024]{1,0:T(8,128)(2,1)}...) custom-call(bf16[256,3072]{1,0:T(8,128)(2,1)} %bitcast.61, ...), custom_call_target="tpu_custom_call" | custom-call | tf_op jit(solution)/shard_map/pallas_call | solution.py:712
  123.1 1.4 fusion.6
  124.5 2.9 conditional.3
  124.5 2.9 fusion.2
  127.4 10.8 %shard_map.223 = (bf16[4,256,256]{2,1,0:T(8,128)(2,1)}, s32[4,32,128]{2,1,0:T(8,128)}) custom-call(bf16[4,256,256]{2,1,0:T(8,128)(2,1)S(1)} %get-tuple-element.228.rows_ref, s32[32,128]{1,0:T(8,128)S(1)} %get-tuple-element.120.ids_ref), custom_call_target="tpu_custom_call" | custom-call | tf_op jit(solution)/shard_map/pallas_call | solution.py:768
  138.3 3.4 conditional.4
  138.3 1.1 convert_reduce_fusion
  139.5 0.8 multiply_convert_fusion
  140.3 1.4 fusion.7
  141.7 17.6 %shard_map.224 = (f32[256,1024]{1,0:T(8,128)}, bf16[1024,256]{1,0:T(8,128)(2,1)}, bf16[256,3072]{1,0:T(8,128)(2,1)}, f32[16,1,256]{2,1,0:T(1,128)}, bf16[1024,25...) custom-call(f32[256,1024]{1,0:T(8,128)S(1)} %get-tuple-element.123.r, ...), custom_call_target="tpu_custom_call" | custom-call | tf_op jit(solution)/shard_map/pallas_call | solution.py:957
  159.3 1.3 convert_element_type.70
  160.6 65.5 %shard_map.225.table = bf16[16384,256]{1,0:T(8,128)(2,1)} custom-call(bf16[4096,256]{1,0:T(8,128)(2,1)S(1)} %copy-done.14), custom_call_target="tpu_custom_call" | custom-call | tf_op jit(solution)/shard_map/pallas_call | solution.py:712
  226.2 5.7 collective-permute-start
  231.9 1.5 collective-permute-done.refs_0_
  233.4 0.8 copy-done.19
  234.2 1.8 shard_map.226
  236.0 1.5 reduce_sum.52
  237.5 1.5 multiply_reduce_fusion.2
  239.0 0.2 multiply_convert_fusion.1
  239.2 0.3 convolution_convert_fusion.6
  239.5 1.3 collective-permute-start.1
  240.9 17.5 %collective-permute-done.1.proj = bf16[256,256]{1,0:T(8,128)(2,1)S(1)} collective-permute-done((bf16[256,256]{1,0:T(8,128)(2,1)S(1)}, bf16[256,256]{1,0:T(8,128)(2,1)S(1)}, u32[]{:S(2)}, u32[]{:S(2)}) %collective-permute-start.1) | collective-permute-done | bytes 131104 | tf_op jit(solution)/shard_map/ppermute | solution.py:28
  258.4 25.8 %shard_map.227 = (bf16[256,256]{1,0:T(8,128)(2,1)S(1)}, f32[1,256]{1,0:T(1,128)S(1)}, bf16[16384,256]{1,0:T(8,128)(2,1)S(1)}) custom-call(bf16[256,256]{1,0:T(8,128)(2,1)S(1)} %collective-permute-done.1.proj, s32[1,256]{1,0:T(1,128)S(1)} %bitcast.53, f32[1,256]{1,0:T(1,128)S(1)} %bitcast.54, bf16[16384,256]{1,0:T(8,128)(2,1)} %shard_map.225.table), custom_call_target="tpu_custom_call" | custom-call | tf_op jit(solution)/shard_map/pallas_call | solution.py:1207
  284.3 3.3 copy-done
  287.5 1.3 collective-permute-start.2
  288.8 1.0 collective-permute-done.2
  289.8 48.5 %shard_map.229.refs_8_ = bf16[1024,256]{1,0:T(8,128)(2,1)} custom-call(bf16[16384,256]{1,0:T(8,128)(2,1)} %copy-done), custom_call_target="tpu_custom_call" | custom-call | tf_op jit(solution)/shard_map/pallas_call | solution.py:1786
  338.3 0.6 multiply_reduce_fusion
  338.9 0.4 fusion.5
  339.3 1.1 broadcast_add_fusion.refs_0_
  340.4 1.9 shard_map.228
  342.3 1.3 collective-permute-start.3
  343.7 1.4 slice.35
  345.2 1.0 collective-permute-done.3.refs_0_
  346.1 0.8 copy-done.18
  347.0 25.4 %shard_map.230 = (bf16[256,1024]{1,0:T(8,128)(2,1)}, bf16[256,4096]{1,0:T(8,128)(2,1)}, bf16[256,1024]{1,0:T(8,128)(2,1)}, bf16[256,3072]{1,0:T(8,128)(2,1)}, bf...) custom-call(bf16[256,1024]{1,0:T(8,128)(2,1)} %copy-done.18, ...), custom_call_target="tpu_custom_call", output_to_operand_aliasing={{0}: (13, {}), {1}: (14, {}), {2}: (15, {}), {3}: (16, {}),... | custom-call | tf_op jit(solution)/shard_map/pallas_call | solution.py:1119
  372.4 1.6 conditional.5
  372.4 0.3 fusion.3
  372.8 1.2 convolution_convert_fusion.1
  374.1 2.0 convolution_convert_fusion.5.refs_3_
  376.1 5.6 convolution_convert_fusion.3.refs_0_
  381.7 4.4 convolution_convert_fusion.4.refs_4_
  386.2 5.6 convolution_convert_fusion.2.refs_1_
  391.8 0.7 maximum_add_fusion
  392.5 279.6 %shard_map.231 = (f32[256,4096]{1,0:T(8,128)}, f32[1024,1024]{1,0:T(8,128)}, f32[64,1024]{1,0:T(8,128)}, f32[256,1024]{1,0:T(8,128)}, f32[256,3072]{1,0:T(8,128)...) custom-call(bf16[1024,4096]{1,0:T(8,128)(2,1)} %convolution_convert_fusion.3.refs_0_, ...), custom_call_target="tpu_custom_call" | custom-call | tf_op jit(solution)/shard_map/pallas_call | solution.py:1786
  672.2 0.5 collective-permute-start.7
  672.8 0.4 collective-permute-start.6
  673.3 3.0 collective-permute-done.4
  676.3 0.5 broadcast_select_fusion.3
  676.8 1.4 broadcast_select_fusion.2
  678.2 1.7 broadcast_select_fusion
  679.9 0.8 reshape.122
  680.7 4.3 select_convert_fusion
  685.0 1.7 copy.76
  686.7 0.3 copy-done.17
  686.9 1.0 copy.77
  687.9 1.1 copy-done.7
  689.0 2.1 copy.78
  691.1 1.6 copy-done.6
  692.7 2.0 copy.79
  (60 shorter events, 0.7 us)
Async XLA Ops:
  4.7 119.8 %copy-start.14 = (bf16[4096,256]{1,0:T(8,128)(2,1)S(1)}, bf16[4096,256]{1,0:T(8,128)(2,1)}, u32[]{:S(2)}) copy-start(bf16[4096,256]{1,0:T(8,128)(2,1)} %refs_0_) | copy-start | bytes 6291460
  124.5 13.8 %copy-start.21 = (bf16[256,256]{1,0:T(8,128)(2,1)S(1)}, bf16[256,256]{1,0:T(8,128)(2,1)}, u32[]{:S(2)}) copy-start(bf16[256,256]{1,0:T(8,128)(2,1)} %param.23) | copy-start | bytes 393220
  226.2 7.2 %collective-permute-start = (bf16[256,1024]{1,0:T(8,128)(2,1)S(1)}, bf16[256,1024]{1,0:T(8,128)(2,1)S(1)}, u32[]{:S(2)}, u32[]{:S(2)}) collective-permute-start(bf16[256,1024]{1,0:T(8,128)(2,1)S(1)} %convert_element_type.70), channel_id=1, source_target_pairs={{0,16},{1,17},{2,18},{3,19},{4,20},{5,21},{6,22},{7,23},{8,24},{9,... | collective-permute-start | bytes 1572872 | tf_op jit(solution)/shard_map/ppermute | solution.py:28
  233.4 0.8 copy-start.19
  236.0 3.0 copy-start.2
  236.0 3.2 copy-start.16
  237.5 3.4 copy-start.22
  237.5 20.9 %copy-start.1 = (s32[256]{0:T(256)S(1)}, s32[256]{0:T(256)}, u32[]{:S(2)}) copy-start(s32[256]{0:T(256)} %param.20) | copy-start | bytes 3076
  239.5 18.9 %collective-permute-start.1 = (bf16[256,256]{1,0:T(8,128)(2,1)S(1)}, bf16[256,256]{1,0:T(8,128)(2,1)S(1)}, u32[]{:S(2)}, u32[]{:S(2)}) collective-permute-start(bf16[256,256]{1,0:T(8,128)(2,1)S(1)} %convolution_convert_fusion.6), channel_id=1, source_target_pairs={{16,0},{17,1},{18,2},{19,3},{20,4},{21,5},{22,6},{23,7},{24,8},{25... | collective-permute-start | bytes 393224 | tf_op jit(solution)/shard_map/ppermute | solution.py:28
  284.2 3.3 copy-start
  287.5 2.3 collective-permute-start.2
  342.3 3.8 collective-permute-start.3
  346.1 0.8 copy-start.18
  347.0 25.4 %copy-start.15 = (bf16[256,1024]{1,0:T(8,128)(2,1)S(1)}, bf16[256,1024]{1,0:T(8,128)(2,1)}, u32[]{:S(2)}) copy-start(bf16[256,1024]{1,0:T(8,128)(2,1)} %get-tuple-element.122) | copy-start | bytes 1572868
  372.4 1.6 copy-start.11
  372.4 1.6 copy-start.12
  374.0 2.1 copy-start.4
  374.0 2.1 copy-start.13
  376.1 5.6 copy-start.5
  376.1 5.6 copy-start.9
  381.7 4.4 copy-start.3
  381.7 4.4 copy-start.10
  386.2 5.6 copy-start.20
  672.1 8.6 %collective-permute-start.5 = (bf16[4096,256]{1,0:T(8,128)(2,1)}, bf16[4096,256]{1,0:T(8,128)(2,1)S(1)}, u32[]{:S(2)}, u32[]{:S(2)}) collective-permute-start(bf16[4096,256]{1,0:T(8,128)(2,1)} %get-tuple-element.175), channel_id=1, source_target_pairs={{0,16},{16,0},{1,17},{17,1},{2,18},{18,2},{3,19},{19,3},{4,20},{20... | collective-permute-start | bytes 6291464 | tf_op jit(solution)/shard_map/ppermute | solution.py:1961
  672.2 4.6 collective-permute-start.7
  672.7 3.6 collective-permute-start.4
  672.8 5.4 collective-permute-start.6
  680.7 4.3 copy-start.8
  685.0 2.0 copy-start.17
  685.0 4.0 copy-start.7
  689.0 3.7 copy-start.6

commit v6 on v5

--- a/solution.py
+++ b/solution.py
@@ -1245,26 +1245,40 @@
     lax.fori_loop(0, rows // strip, body, 0)
 
 
-def reduce_kernel(plan, spots, only, extras, ahead, refs_of, *refs):
-    body = functools.partial(reduce_body, plan, spots, extras, ahead, refs_of(refs))
+def reduce_kernel(plan, spots, only, extras, pace, refs_of, *refs):
+    body = functools.partial(reduce_body, plan, spots, extras, pace, refs_of(refs))
     if only is None:
         body()
     else:
         pl.when(lax.axis_index("section") == only)(body)
 
 
-def reduce_body(plan, spots, extras, ahead, named):
+def stage_blocks(order):
+    left = list(range(16))
+    kept = []
+    for bit in order:
+        left = [r for r in left if not (r >> bit) & 1]
+        kept.append(left)
+    return kept
+
+
+def reduce_body(plan, spots, extras, pace, named):
     arrays, outs = named["arrays"], named["outs"]
-    own, got1, got2, got3, land = (named[k] for k in ("own", "got1", "got2", "got3", "land"))
-    s1, r1, own_sem, s2, r2, s3, r3, s4, r4, fin_sem = named["sems"]
+    own, got1, got2, got3, got4, land = (
+        named[k] for k in ("own", "got1", "got2", "got3", "got4", "land")
+    )
+    ssem, rsem, own_sem, s4, r4, fin_sem = named["sems"]
+    got = (got1, got2, got3, got4)
     count = len(plan)
     sec = lax.axis_index("section")
     grp = lax.axis_index("group")
     pos = lax.axis_index("dp")
     beside = ((sec, grp ^ 1, pos), (sec, grp ^ 2, pos))
+    swaps = beside + ((sec, grp, pos ^ 1), (sec, grp, pos ^ 2))
     sides = [(sec, grp ^ j, pos) for j in (1, 2, 3)]
     line_peers = [(sec, grp, lax.rem(pos + k, 4)) for k in (1, 2, 3)]
     steps = [(jg, jz) for jg in range(4) for jz in range(4)][1:]
+    kept = [stage_blocks(piece[1]) for piece in plan]
 
     def other(j):
         return (sec, grp ^ steps[j][0], lax.rem(pos + steps[j][1], 4))
@@ -1272,7 +1286,12 @@
     with_gains = "gains" in extras
     spreads = "spread" in extras
     looked = "looked" in extras
-    peers = [other(j) for j in range(15)] if with_gains else sides + line_peers
+    if with_gains:
+        peers = [other(j) for j in range(15)]
+    elif looked:
+        peers = sides + line_peers
+    else:
+        peers = list(swaps)
     barrier = pltpu.get_barrier_semaphore()
     for device in peers:
         pl.semaphore_signal(barrier, inc=1, device_id=device, device_id_type=MESH)
@@ -1287,81 +1306,59 @@
     def sub_of(p):
         return rows_of(p) // 4 // plan[p][3]
 
-    def block(p, line, who):
+    def block(p, r):
+        line, who = pos ^ (r >> 2), grp ^ (r & 3)
         start = line * rows_of(p) + who * (rows_of(p) // 4) + plan[p][2] * sub_of(p)
         return arrays[plan[p][0]].at[rows_at(start, sub_of(p))]
 
-    def ways(line):
-        return (0, 1) if line < 2 else (1, 0)
-
-    def send_first(p, line, b):
-        first, second = ways(line)
-        who = grp ^ (1 + first)
-        if b:
-            who = who ^ (1 + second)
+    def spot(p, r):
+        return kept[p][0].index(r)
+
+    def swap(p, stage, at):
+        bit = plan[p][1][stage]
+        r = kept[p][stage][at] | (1 << bit)
+        src = block(p, r) if stage == 0 else own[p].at[spot(p, r)]
         return remote(
-            block(p, line, who),
-            got1[p].at[line, b],
-            s1.at[p, line, b],
-            r1.at[p, line, b],
-            beside[first],
+            src, got[stage][p].at[at], ssem.at[p, stage, at], rsem.at[p, stage, at], swaps[bit]
         )
 
-    def load_own(p, line, b):
-        who = grp ^ (1 + ways(line)[1]) if b else grp
-        return pltpu.make_async_copy(block(p, line, who), own[p].at[line, b], own_sem.at[p, line, b])
-
-    def send_second(p, line):
-        second = ways(line)[1]
-        return remote(own[p].at[line, 1], got2[p].at[line], s2.at[p, line], r2.at[p, line], beside[second])
-
-    def send_line(p, line):
-        slot = jnp.maximum(lax.rem(line - pos + 4, 4) - 1, 0)
-        return remote(
-            own[p].at[line, 0], got3[p].at[slot], s3.at[p, line], r3.at[p, slot], (sec, grp, line)
-        )
-
-    def line_arrival(p, slot):
-        return remote(got3[p].at[slot], got3[p].at[slot], s3.at[p, slot], r3.at[p, slot], beside[0])
-
-    def begin(p, line):
-        for b in (1, 0):
-            send_first(p, line, b).start()
-            load_own(p, line, b).start()
-
-    def middle(p, line):
-        for b in (1, 0):
-            load_own(p, line, b).wait()
-            send_first(p, line, b).wait_recv()
-
-            def store(here, total, b=b):
-                own[p][line, b, here, :] = total.astype(jnp.bfloat16)
-
-            add_rows(
-                store,
-                [
-                    lambda here, b=b: own[p][line, b, here, :],
-                    lambda here, b=b: got1[p][line, b, here, :],
-                ],
-                sub_of(p),
-                columns_of(p),
-            )
-            if b:
-                send_second(p, line).start()
-
-    def late(p, line):
-        send_second(p, line).wait_recv()
-
-        def store(here, total):
-            own[p][line, 0, here, :] = total.astype(jnp.bfloat16)
-
-        add_rows(
-            store,
-            [lambda here: own[p][line, 0, here, :], lambda here: got2[p][line, here, :]],
-            sub_of(p),
-            columns_of(p),
-        )
-        pl.when(line != pos)(send_line(p, line).start)
+    def load_own(p, at):
+        return pltpu.make_async_copy(block(p, kept[p][0][at]), own[p].at[at], own_sem.at[p, at])
+
+    def order_of(p, stage):
+        places = range(len(kept[p][stage]))
+        if stage == 3:
+            return list(places)
+        bit = plan[p][1][stage + 1]
+        return sorted(places, key=lambda at: 1 - ((kept[p][stage][at] >> bit) & 1))
+
+    def begin(p):
+        for at in order_of(p, 0):
+            swap(p, 0, at).start()
+            load_own(p, at).start()
+
+    def advance(p, stage):
+        for at in order_of(p, stage):
+            r = kept[p][stage][at]
+            place = spot(p, r)
+            if stage == 0:
+                load_own(p, at).wait()
+            swap(p, stage, at).wait_recv()
+            terms = [
+                lambda here, place=place: own[p][place, here, :],
+                lambda here, at=at: got[stage][p][at, here, :],
+            ]
+            if stage == 3:
+                settle(p, terms)
+                return
+
+            def store(here, total, place=place):
+                own[p][place, here, :] = total.astype(jnp.bfloat16)
+
+            add_rows(store, terms, sub_of(p), columns_of(p))
+            bit = plan[p][1][stage + 1]
+            if (r >> bit) & 1:
+                swap(p, stage + 1, kept[p][stage + 1].index(r ^ (1 << bit))).start()
 
     pending = {}
 
@@ -1398,8 +1395,10 @@
         return remote(there, there, s4.at[p, way], r4.at[p, way], beside[3 - way])
 
     def settle(p, terms):
+        mine = grp if spreads else 0
+
         def store(here, total):
-            land[p][grp, here, :] = total.astype(jnp.bfloat16)
+            land[p][mine, here, :] = total.astype(jnp.bfloat16)
 
         add_rows(store, terms, sub_of(p), columns_of(p))
         if spreads:
@@ -1410,21 +1409,12 @@
 
     def own_out(p):
         return pltpu.make_async_copy(
-            land[p].at[grp], outs[plan[p][0]].at[rows_at(plan[p][2] * sub_of(p), sub_of(p))], fin_sem.at[p]
+            land[p].at[0], outs[plan[p][0]].at[rows_at(plan[p][2] * sub_of(p), sub_of(p))], fin_sem.at[p]
         )
 
     def arrival(p, way):
         who = (grp ^ 1, grp ^ 2)[way]
         return remote(land[p].at[who], land[p].at[who], s4.at[p, way], r4.at[p, way], beside[way])
-
-    def finish(p):
-        for slot in range(3):
-            line_arrival(p, slot).wait_recv()
-        settle(
-            p,
-            [lambda here: own[p][pos, 0, here, :]]
-            + [lambda here, slot=slot: got3[p][slot, here, :] for slot in range(3)],
-        )
 
     def pass_on(p):
         if spreads:
@@ -1442,61 +1432,6 @@
             spread(p, 2).wait_recv()
             spread(p, 3).wait_recv()
             write_out(p, grp ^ 3, [lambda here: land[p][grp ^ 3, here, :]])
-
-    def line_rows(p, line):
-        return arrays[plan[p][0]].at[rows_at(line * rows_of(p), rows_of(p))]
-
-    def line_first(p, k):
-        to = lax.rem(pos + k, 4)
-        return remote(
-            line_rows(p, to), got1[p].at[k - 1], s1.at[p, k, 0], r1.at[p, k, 0], (sec, grp, to)
-        )
-
-    def line_own(p):
-        return pltpu.make_async_copy(line_rows(p, pos), own[p], own_sem.at[p, 0, 0])
-
-    def cross(p, j):
-        to = grp ^ j
-        return remote(
-            own[p].at[rows_at(to * sub_of(p), sub_of(p))],
-            got3[p].at[j - 1],
-            s3.at[p, j],
-            r3.at[p, j - 1],
-            (sec, to, pos),
-        )
-
-    def line_begin(p):
-        for k in (2, 1, 3):
-            line_first(p, k).start()
-        line_own(p).start()
-
-    def line_middle(p):
-        line_own(p).wait()
-        for k in (1, 2, 3):
-            line_first(p, k).wait_recv()
-
-        def store(here, total):
-            own[p][here, :] = total.astype(jnp.bfloat16)
-
-        add_rows(
-            store,
-            [lambda here: own[p][here, :]] + [lambda here, k=k: got1[p][k, here, :] for k in range(3)],
-            rows_of(p),
-            columns_of(p),
-        )
-        for j in (3, 1, 2):
-            cross(p, j).start()
-
-    def line_finish(p):
-        for j in (1, 2, 3):
-            cross(p, j).wait_recv()
-        base = grp * sub_of(p)
-        strip = strip_of(sub_of(p), columns_of(p))
-        settle(
-            p,
-            [lambda here: own[p][rows_at(base + here.start, strip), :]]
-            + [lambda here, j=j: got3[p][j, here, :] for j in range(3)],
-        )
 
     if with_gains:
         gain_in, gain_got, sg, rg, gain_sem = named["gain_scratch"]
@@ -1606,63 +1541,27 @@
 
         look_begin = look_middle = look_sum = look_pass = look_end = None
 
-    planes = [p for p in range(count) if plan[p][1] == "plane"]
-    lines = [p for p in range(count) if plan[p][1] == "line"]
-    units = [(p, line) for p in planes for line in (0, 2, 1, 3)]
-    for unit in units[:2]:
-        begin(*unit)
-    for p in lines:
-        line_begin(p)
+    ahead, lag, lag_end = pace
     on_first(look_begin)
-    for unit in units[2:ahead]:
-        begin(*unit)
+    for p in range(min(ahead, count)):
+        begin(p)
     if with_gains:
         gain_load.wait()
         for j in range(15):
             gain_copy(j).start()
-    lag = 3
-    total_steps = len(units) + lag
-    done = []
-    for at in range(total_steps):
-        if at + ahead < len(units):
-            begin(*units[at + ahead])
-        if at < len(units):
-            middle(*units[at])
-        if at >= lag:
-            p, line = units[at - lag]
-            late(p, line)
-            if line == 1 and len(done) >= 1:
-                finish(done[-1])
-            if line == 2 and len(done) >= 2:
-                pass_on(done[-2])
-            if line == 0 and len(done) >= 3:
-                write_near(done[-3])
-            if line == 3:
-                done.append(p)
-        if at == len(units) // 4:
-            on_first(look_middle)
-        if at == len(units) // 2:
-            on_first(look_sum)
-        if at == 3 * len(units) // 4:
-            on_first(look_pass)
-    for p in lines:
-        line_middle(p)
-    finish(done[-1])
-    written = max(len(done) - 3, 0)
-    passed = max(len(done) - 2, 0)
-    for p in done[passed:]:
-        pass_on(p)
-    for p in lines:
-        line_finish(p)
-    for p in done[written:]:
-        write_near(p)
-    for p in lines:
-        pass_on(p)
-    for p in done:
-        write_far(p)
-    for p in lines:
-        write_near(p)
-        write_far(p)
+    delays = [0, lag, 2 * lag, 3 * lag, 3 * lag + lag_end, 3 * lag + 2 * lag_end, 3 * lag + 3 * lag_end]
+    for at in range(count + delays[-1]):
+        if ahead + at < count:
+            begin(ahead + at)
+        for stage in range(4):
+            if 0 <= at - delays[stage] < count:
+                advance(at - delays[stage], stage)
+        for run, delay in zip((pass_on, write_near, write_far), delays[4:]):
+            if 0 <= at - delay < count:
+                run(at - delay)
+        for when, run in ((1, look_middle), (3, look_sum), (5, look_pass)):
+            if at == when * (count + delays[3]) // 6:
+                on_first(run)
     if with_gains:
         for j in range(15):
             gain_copy(j).wait_recv()
@@ -1678,22 +1577,15 @@
                 spread(p, way).wait_send()
         else:
             own_out(p).wait()
-        if plan[p][1] == "plane":
-            for line in range(4):
-                for b in (0, 1):
-                    send_first(p, line, b).wait_send()
-                send_second(p, line).wait_send()
-                pl.when(line != pos)(send_line(p, line).wait_send)
-        else:
-            for k in (1, 2, 3):
-                line_first(p, k).wait_send()
-                cross(p, k).wait_send()
+        for stage in range(4):
+            for at in range(len(kept[p][stage])):
+                swap(p, stage, at).wait_send()
     if with_gains:
         for j in range(15):
             gain_copy(j).wait_send()
 
 
-def reduce_all(arrays, plan, only, collective_id, ahead, gains=None, look=None, spread=True):
+def reduce_all(arrays, plan, only, collective_id, pace, gains=None, look=None, spread=True):
     low, f32, dma = jnp.bfloat16, jnp.float32, pltpu.SemaphoreType.DMA
     extras = ("spread",) * spread + ("gains",) * (gains is not None) + ("looked",) * (look is not None)
     count = len(plan)
@@ -1703,24 +1595,20 @@
     outs = [jax.ShapeDtypeStruct((x.shape[0] // share, x.shape[1]), kind) for x in arrays]
     out_specs = [ANYWHERE] * len(arrays)
     in_specs = [ANYWHERE] * len(arrays)
-    names = ["own", "got1", "got2", "got3", "land"]
+    names = ["own", "got1", "got2", "got3", "got4", "land"]
     scratch = {name: [] for name in names}
     ring_shapes = []
     spots = []
-    for src, way, _, chunks in plan:
+    for src, _, _, chunks in plan:
         rows, columns = arrays[src].shape[0] // 4, arrays[src].shape[1]
         sub = rows // 4 // chunks
-        if way == "plane":
-            shapes = [(4, 2, sub, columns), (4, 2, sub, columns), (4, sub, columns)]
-        else:
-            shapes = [(rows, columns), (3, rows, columns), (8, 128)]
-        for name, shape in zip(names, shapes + [(3, sub, columns), (4, sub, columns)]):
-            scratch[name].append(pltpu.VMEM(shape, low))
+        for name, blocks in zip(names, (8, 8, 4, 2, 1, 4 if spread else 1)):
+            scratch[name].append(pltpu.VMEM((blocks, sub, columns), low))
         if (sub, columns) not in ring_shapes:
             ring_shapes.append((sub, columns))
         spots.append(ring_shapes.index((sub, columns)))
     flat = [item for name in names for item in scratch[name]]
-    sems = [dma((count, 4, 2))] * 3 + [dma((count, 4))] * 6 + [dma((count,))]
+    sems = [dma((count, 4, 8))] * 2 + [dma((count, 8))] + [dma((count, 4))] * 2 + [dma((count,))]
     tail = []
     if spread:
         tail += [pltpu.VMEM((2,) + shape, f32) for shape in ring_shapes] + [dma((len(ring_shapes), 2))]
@@ -1773,7 +1661,7 @@
             named["table_out"] = take(1)[0]
         for name in names:
             named[name] = take(count)
-        named["sems"] = take(10)
+        named["sems"] = take(6)
         if spread:
             named["rings"] = take(len(ring_shapes))
             named["ring_sem"] = take(1)[0]
@@ -1784,7 +1672,7 @@
         return named
 
     return pl.pallas_call(
-        functools.partial(reduce_kernel, plan, tuple(spots), only, extras, ahead, refs_of),
+        functools.partial(reduce_kernel, plan, tuple(spots), only, extras, pace, refs_of),
         out_shape=outs,
         in_specs=in_specs,
         out_specs=out_specs,
@@ -1803,15 +1691,20 @@
     return lax.cond(live, run, lambda: nothing_like(run))
 
 
+X_FIRST = (0, 1, 2, 3)
+Y_FIRST = (1, 0, 2, 3)
+Z_THEN_X = (2, 0, 1, 3)
+Z_THEN_Y = (2, 1, 0, 3)
+ORDERS = (X_FIRST, Z_THEN_Y, Y_FIRST, Z_THEN_X)
 LAYER_PLAN = (
-    (0, "plane", 0, 1),
-    (1, "plane", 0, 1),
-    (2, "plane", 0, 1),
-    (3, "plane", 0, 1),
-    (4, "line", 0, 1),
+    tuple((0, ORDERS[chunk], chunk, 4) for chunk in range(4))
+    + tuple((1, ORDERS[chunk], chunk, 4) for chunk in range(4))
+    + tuple((4, ORDERS[chunk], chunk, 4) for chunk in range(4))
+    + ((3, Y_FIRST, 0, 2), (3, Z_THEN_X, 1, 2), (2, X_FIRST, 0, 1))
 )
-LAYER_AHEAD = 6
-TABLE_AHEAD = 8
+TABLE_PLAN = tuple((0, ORDERS[chunk], chunk, 4) for chunk in range(4))
+LAYER_PACE = (8, 4, 2)
+TABLE_PACE = (4, 2, 1)
 
 
 def after(value, *others):
@@ -1910,10 +1803,10 @@
     grad_proj = passed_along(grad_proj_a, "section", 1)
     (table_fin,) = reduce_all(
         (after(table_g, grad_proj),),
-        tuple((0, "plane", chunk, 4) for chunk in range(4)),
+        TABLE_PLAN,
         0,
         3,
-        TABLE_AHEAD,
+        TABLE_PACE,
         spread=False,
     )
     grad_top, gain_final = norm_back(kept[9], final_gain, product_nt(grad_proj, out_weight))
@@ -1952,7 +1845,7 @@
         LAYER_PLAN,
         None,
         4,
-        LAYER_AHEAD,
+        LAYER_PACE,
         gains=gain_rows,
         look=(all_tokens.reshape(16, 1, rows), looked_grad, table_fin),
     )

time: 706 us -> 652 us (0.924)
  Pallas kernels: 595 us -> 547 us
    pallas_call x2, Pallas kernels: 328 us -> 280 us  [reduce_all(): pl.pallas_call(functools.partial(reduce_kernel, plan, tuple(spots), only,...]
where the time goes in v6:
time: 652 us; the launch traced here: 647 us
  Pallas kernels  547 us (84%)
  matrix products  24.4 us (4%)
  waiting for transfers between devices  23.9 us (4%)
  local copies, waits for them, and re-layouts  20.6 us (3%)
  other arithmetic  18.7 us (3%)
  starting transfers between devices  10.7 us (2%)
    pallas_call x2, Pallas kernels, reduce_all(): pl.pallas_call(functools.partial(reduce_kernel, plan, tuple(spots), only,...  280 us
    pallas_call x2, Pallas kernels, gather_all(): pl.pallas_call(functools.partial(gather_kernel, count, first_order, last_...  184 us
    pallas_call x2, Pallas kernels, run_backward(): pl.pallas_call(functools.partial(backward_kernel, only, tile, given), out...  27.3 us
    pallas_call x1, Pallas kernels, run_vocabulary(): pl.pallas_call(functools.partial(vocabulary_kernel, only, tile), out_shap...  25.8 us
    dot_general x7, matrix products, product(): return jnp.dot(left_side, right_side, preferred_element_type=jnp.float32)  22.2 us
    ppermute x4, waiting for transfers between devices, passed_along(): return lax.ppermute(x, axis, pairs)  20.9 us
    pallas_call x2, Pallas kernels, run_forward(): pl.pallas_call(functools.partial(forward_kernel, only, tile, given), out_...  19.4 us
    unnamed x50, local copies, waits for them, and re-layouts  14.7 us
  transfers between devices with their start and end apart: 8, of which 5 were waited for; matrix products, arithmetic and copies ran while one was open for 1% of the time, Pallas kernels for 0%

profile of v6, /device:TPU:0, one launch (start us, length us, event | category | flops | bytes accessed | tf_op | source)
XLA Modules:
  0.0 646.7 jit_solution(6021000715005708836)
XLA Ops:
  0.7 0.7 broadcast_in_dim.57
  1.3 0.7 add_rsqrt_fusion
  2.0 1.3 concatenate.10.refs_7_
  3.3 1.4 maximum_maximum_fusion.refs_6_
  4.7 118.3 %shard_map.222 = (bf16[1024,3072]{1,0:T(8,128)(2,1)}, bf16[1024,1024]{1,0:T(8,128)(2,1)}, bf16[1024,4096]{1,0:T(8,128)(2,1)}, bf16[4096,1024]{1,0:T(8,128)(2,1)}...) custom-call(bf16[256,3072]{1,0:T(8,128)(2,1)} %bitcast.61, ...), custom_call_target="tpu_custom_call" | custom-call | tf_op jit(solution)/shard_map/pallas_call | solution.py:712
  123.1 1.4 fusion.6
  124.5 2.9 conditional.3
  124.5 2.9 fusion.2
  127.4 10.8 %shard_map.223 = (bf16[4,256,256]{2,1,0:T(8,128)(2,1)}, s32[4,32,128]{2,1,0:T(8,128)}) custom-call(bf16[4,256,256]{2,1,0:T(8,128)(2,1)S(1)} %get-tuple-element.228.rows_ref, s32[32,128]{1,0:T(8,128)S(1)} %get-tuple-element.120.ids_ref), custom_call_target="tpu_custom_call" | custom-call | tf_op jit(solution)/shard_map/pallas_call | solution.py:768
  138.3 3.4 conditional.4
  138.3 1.1 convert_reduce_fusion
  139.5 0.8 multiply_convert_fusion
  140.3 1.4 fusion.7
  141.7 17.6 %shard_map.224 = (f32[256,1024]{1,0:T(8,128)}, bf16[1024,256]{1,0:T(8,128)(2,1)}, bf16[256,3072]{1,0:T(8,128)(2,1)}, f32[16,1,256]{2,1,0:T(1,128)}, bf16[1024,25...) custom-call(f32[256,1024]{1,0:T(8,128)S(1)} %get-tuple-element.123.r, ...), custom_call_target="tpu_custom_call" | custom-call | tf_op jit(solution)/shard_map/pallas_call | solution.py:957
  159.3 1.3 convert_element_type.70
  160.6 65.5 %shard_map.225.table = bf16[16384,256]{1,0:T(8,128)(2,1)} custom-call(bf16[4096,256]{1,0:T(8,128)(2,1)S(1)} %copy-done.14), custom_call_target="tpu_custom_call" | custom-call | tf_op jit(solution)/shard_map/pallas_call | solution.py:712
  226.2 5.7 collective-permute-start
  231.9 1.5 collective-permute-done.refs_0_
  233.4 0.8 copy-done.19
  234.2 1.8 shard_map.226
  236.0 1.5 reduce_sum.52
  237.5 1.5 multiply_reduce_fusion.2
  239.0 0.2 multiply_convert_fusion.1
  239.2 0.3 convolution_convert_fusion.6
  239.5 1.3 collective-permute-start.1
  240.9 17.5 %collective-permute-done.1.proj = bf16[256,256]{1,0:T(8,128)(2,1)S(1)} collective-permute-done((bf16[256,256]{1,0:T(8,128)(2,1)S(1)}, bf16[256,256]{1,0:T(8,128)(2,1)S(1)}, u32[]{:S(2)}, u32[]{:S(2)}) %collective-permute-start.1) | collective-permute-done | bytes 131104 | tf_op jit(solution)/shard_map/ppermute | solution.py:28
  258.4 25.8 %shard_map.227 = (bf16[256,256]{1,0:T(8,128)(2,1)S(1)}, f32[1,256]{1,0:T(1,128)S(1)}, bf16[16384,256]{1,0:T(8,128)(2,1)S(1)}) custom-call(bf16[256,256]{1,0:T(8,128)(2,1)S(1)} %collective-permute-done.1.proj, s32[1,256]{1,0:T(1,128)S(1)} %bitcast.53, f32[1,256]{1,0:T(1,128)S(1)} %bitcast.54, bf16[16384,256]{1,0:T(8,128)(2,1)} %shard_map.225.table), custom_call_target="tpu_custom_call" | custom-call | tf_op jit(solution)/shard_map/pallas_call | solution.py:1207
  284.3 3.3 copy-done
  287.5 1.3 collective-permute-start.2
  288.8 1.0 collective-permute-done.2
  289.8 47.7 %shard_map.229.refs_8_ = bf16[1024,256]{1,0:T(8,128)(2,1)} custom-call(bf16[16384,256]{1,0:T(8,128)(2,1)} %copy-done), custom_call_target="tpu_custom_call" | custom-call | tf_op jit(solution)/shard_map/pallas_call | solution.py:1674
  337.4 0.6 multiply_reduce_fusion
  338.0 0.4 fusion.5
  338.4 1.1 broadcast_add_fusion.refs_0_
  339.6 1.9 shard_map.228
  341.5 1.3 collective-permute-start.3
  342.9 1.4 slice.35
  344.3 1.0 collective-permute-done.3.refs_0_
  345.3 0.8 copy-done.18
  346.1 25.4 %shard_map.230 = (bf16[256,1024]{1,0:T(8,128)(2,1)}, bf16[256,4096]{1,0:T(8,128)(2,1)}, bf16[256,1024]{1,0:T(8,128)(2,1)}, bf16[256,3072]{1,0:T(8,128)(2,1)}, bf...) custom-call(bf16[256,1024]{1,0:T(8,128)(2,1)} %copy-done.18, ...), custom_call_target="tpu_custom_call", output_to_operand_aliasing={{0}: (13, {}), {1}: (14, {}), {2}: (15, {}), {3}: (16, {}),... | custom-call | tf_op jit(solution)/shard_map/pallas_call | solution.py:1119
  371.6 1.6 conditional.5
  371.6 0.3 fusion.3
  371.9 1.2 convolution_convert_fusion.1
  373.2 2.0 convolution_convert_fusion.5.refs_3_
  375.3 5.6 convolution_convert_fusion.3.refs_0_
  380.9 4.4 convolution_convert_fusion.4.refs_4_
  385.3 5.6 convolution_convert_fusion.2.refs_1_
  390.9 0.7 maximum_add_fusion
  391.6 232.2 %shard_map.231 = (f32[256,4096]{1,0:T(8,128)}, f32[1024,1024]{1,0:T(8,128)}, f32[64,1024]{1,0:T(8,128)}, f32[256,1024]{1,0:T(8,128)}, f32[256,3072]{1,0:T(8,128)...) custom-call(bf16[1024,4096]{1,0:T(8,128)(2,1)} %convolution_convert_fusion.3.refs_0_, ...), custom_call_target="tpu_custom_call" | custom-call | tf_op jit(solution)/shard_map/pallas_call | solution.py:1674
  623.9 0.5 collective-permute-start.7
  624.6 0.4 collective-permute-start.6
  625.0 3.0 collective-permute-done.4
  628.0 0.5 broadcast_select_fusion.3
  628.6 1.4 broadcast_select_fusion.2
  630.0 1.7 broadcast_select_fusion
  631.7 0.8 reshape.122
  632.4 4.3 select_convert_fusion
  636.7 1.7 copy.76
  638.4 0.3 copy-done.17
  638.7 1.0 copy.77
  639.7 1.1 copy-done.7
  640.8 2.1 copy.78
  642.9 1.6 copy-done.6
  644.5 2.0 copy.79
  (60 shorter events, 0.7 us)
Async XLA Ops:
  4.7 119.8 %copy-start.14 = (bf16[4096,256]{1,0:T(8,128)(2,1)S(1)}, bf16[4096,256]{1,0:T(8,128)(2,1)}, u32[]{:S(2)}) copy-start(bf16[4096,256]{1,0:T(8,128)(2,1)} %refs_0_) | copy-start | bytes 6291460
  124.5 13.8 %copy-start.21 = (bf16[256,256]{1,0:T(8,128)(2,1)S(1)}, bf16[256,256]{1,0:T(8,128)(2,1)}, u32[]{:S(2)}) copy-start(bf16[256,256]{1,0:T(8,128)(2,1)} %param.23) | copy-start | bytes 393220
  226.2 7.2 %collective-permute-start = (bf16[256,1024]{1,0:T(8,128)(2,1)S(1)}, bf16[256,1024]{1,0:T(8,128)(2,1)S(1)}, u32[]{:S(2)}, u32[]{:S(2)}) collective-permute-start(bf16[256,1024]{1,0:T(8,128)(2,1)S(1)} %convert_element_type.70), channel_id=1, source_target_pairs={{0,16},{1,17},{2,18},{3,19},{4,20},{5,21},{6,22},{7,23},{8,24},{9,... | collective-permute-start | bytes 1572872 | tf_op jit(solution)/shard_map/ppermute | solution.py:28
  233.4 0.8 copy-start.19
  236.0 3.0 copy-start.2
  236.0 3.2 copy-start.16
  237.5 3.4 copy-start.22
  237.5 20.9 %copy-start.1 = (s32[256]{0:T(256)S(1)}, s32[256]{0:T(256)}, u32[]{:S(2)}) copy-start(s32[256]{0:T(256)} %param.20) | copy-start | bytes 3076
  239.5 18.9 %collective-permute-start.1 = (bf16[256,256]{1,0:T(8,128)(2,1)S(1)}, bf16[256,256]{1,0:T(8,128)(2,1)S(1)}, u32[]{:S(2)}, u32[]{:S(2)}) collective-permute-start(bf16[256,256]{1,0:T(8,128)(2,1)S(1)} %convolution_convert_fusion.6), channel_id=1, source_target_pairs={{16,0},{17,1},{18,2},{19,3},{20,4},{21,5},{22,6},{23,7},{24,8},{25... | collective-permute-start | bytes 393224 | tf_op jit(solution)/shard_map/ppermute | solution.py:28
  284.2 3.3 copy-start
  287.5 2.3 collective-permute-start.2
  341.5 3.8 collective-permute-start.3
  345.3 0.8 copy-start.18
  346.1 25.4 %copy-start.15 = (bf16[256,1024]{1,0:T(8,128)(2,1)S(1)}, bf16[256,1024]{1,0:T(8,128)(2,1)}, u32[]{:S(2)}) copy-start(bf16[256,1024]{1,0:T(8,128)(2,1)} %get-tuple-element.122) | copy-start | bytes 1572868
  371.6 1.6 copy-start.11
  371.6 1.6 copy-start.12
  373.2 2.1 copy-start.4
  373.2 2.1 copy-start.13
  375.3 5.6 copy-start.5
  375.3 5.6 copy-start.9
  380.9 4.4 copy-start.3
  380.9 4.4 copy-start.10
  385.3 5.6 copy-start.20
  623.9 8.6 %collective-permute-start.5 = (bf16[4096,256]{1,0:T(8,128)(2,1)}, bf16[4096,256]{1,0:T(8,128)(2,1)S(1)}, u32[]{:S(2)}, u32[]{:S(2)}) collective-permute-start(bf16[4096,256]{1,0:T(8,128)(2,1)} %get-tuple-element.175), channel_id=1, source_target_pairs={{0,16},{16,0},{1,17},{17,1},{2,18},{18,2},{3,19},{19,3},{4,20},{20... | collective-permute-start | bytes 6291464 | tf_op jit(solution)/shard_map/ppermute | solution.py:1854
  623.9 4.6 collective-permute-start.7
  624.5 3.6 collective-permute-start.4
  624.6 5.4 collective-permute-start.6
  632.4 4.3 copy-start.8
  636.7 2.0 copy-start.17
  636.7 4.0 copy-start.7
  640.8 3.7 copy-start.6

commit v7 on v6

--- a/solution.py
+++ b/solution.py
@@ -631,7 +631,7 @@
                 there, there, psend.at[slot, j, way], precv.at[slot, j, way], beside[3 - way]
             )
 
-        items = [(slot, j) for slot in range(len(order)) for j in range(3)]
+        items = [(slot, j) for j in range(3) for slot in range(len(order))]
         crossing = [item for item in items if not order[item[0]][3]]
 
         def first(slot, j):
@@ -654,11 +654,11 @@
             start_own(slot)
         for idx in staged:
             load_own(idx).start()
-        lag = 2
+        lag = 4
         for at in range(len(items) + lag):
             if at < len(items):
                 slot, j = items[at]
-                if j == 2 and slot < len(staged):
+                if j == 1 and slot < len(staged):
                     load_own(staged[slot]).wait()
                     store_own(staged[slot]).start()
                 first(slot, j)
@@ -1137,90 +1137,138 @@
     )(grad, gain_attn, gain_mlp, counts, x, qkv, lse, mid, pre, wq, wp, wu, wd, *(made or ()))
 
 
-def vocabulary_kernel(only, tile, proj, ids, scale, table, gproj_out, loss_out, gtable, tv, gt, gp, tsem, gsem):
-    rows, emb = proj.shape
+def vocabulary_kernel(only, tile, proj, ids, scale, table, gproj_out, loss_out, gtable, *scratch):
+    tv, gt, pall, gp, gsend, gin, stat, stats, whole, tsem, gsem, psem, prem, ssem, srem, qsem, qrem = scratch
+    rows = proj.shape[0]
     vocab = tv.shape[0]
     count = vocab // tile
+    sec = lax.axis_index("section")
+    grp = lax.axis_index("group")
+    pos = lax.axis_index("dp")
+    peers = [(sec, grp, lax.rem(pos + k, 4)) for k in (1, 2, 3)]
+    places = [lax.rem(pos + k, 4) for k in (1, 2, 3)]
 
     def run():
-        for at in range(count):
-            here = pl.ds(at * tile, tile)
-            pltpu.make_async_copy(table.at[here], tv.at[here], tsem.at[at]).start()
+        load = pltpu.make_async_copy(table, tv, tsem)
+        load.start()
+        barrier = pltpu.get_barrier_semaphore()
+        for device in peers:
+            pl.semaphore_signal(barrier, inc=1, device_id=device, device_id_type=MESH)
+        pall[pos] = proj[...]
+        pl.semaphore_wait(barrier, 3)
+        first = [
+            remote(pall.at[pos], pall.at[pos], psem.at[k], prem.at[k], peers[k]) for k in range(3)
+        ]
+        for copy in first:
+            copy.start()
+        load.wait()
+        for copy in first:
+            copy.wait()
+        line_rows = pall[...].reshape(4 * rows, pall.shape[2])
 
         def logits_of(at):
-            return dot_nt(tv[rows_at(at * tile, tile), :], proj[...])
+            return dot_nt(tv[rows_at(at * tile, tile), :], line_rows)
 
         def hits_of(at):
-            names = lax.broadcasted_iota(jnp.int32, (tile, rows), 0) + at * tile
+            names = lax.broadcasted_iota(jnp.int32, (tile, 4 * rows), 0) + (at * tile + pos * vocab)
             return names == ids[...]
 
-        def stats(at, carry):
-            top, total, picked = carry
-            here = rows_at(at * tile, tile)
-            pltpu.make_async_copy(table.at[here], tv.at[here], tsem.at[at]).wait()
+        stat[0:1, :] = jnp.full((1, 4 * rows), MASKED, jnp.float32)
+        stat[1:8, :] = jnp.zeros((7, 4 * rows), jnp.float32)
+
+        def measure(at, carry):
             logits = logits_of(at)
+            top = stat[0:1, :]
             higher = jnp.maximum(top, jnp.max(logits, 0, keepdims=True))
-            total = total * jnp.exp(top - higher) + jnp.sum(jnp.exp(logits - higher), 0, keepdims=True)
-            picked = picked + jnp.sum(jnp.where(hits_of(at), logits, 0.0), 0, keepdims=True)
-            return higher, total, picked
-
-        start = (
-            jnp.full((1, rows), MASKED, jnp.float32),
-            jnp.zeros((1, rows), jnp.float32),
-            jnp.zeros((1, rows), jnp.float32),
-        )
-        top, total, picked = lax.fori_loop(0, count, stats, start)
+            stat[1:2, :] = stat[1:2, :] * jnp.exp(top - higher) + jnp.sum(
+                jnp.exp(logits - higher), 0, keepdims=True
+            )
+            stat[2:3, :] += jnp.sum(jnp.where(hits_of(at), logits, 0.0), 0, keepdims=True)
+            stat[0:1, :] = higher
+            return carry
+
+        lax.fori_loop(0, count, measure, 0)
+        second = [
+            remote(stat, stats.at[pos], ssem.at[k], srem.at[k], peers[k]) for k in range(3)
+        ]
+        for copy in second:
+            copy.start()
+        stats[pos] = stat[...]
+        for copy in second:
+            copy.wait()
+        top = stats[0, 0:1, :]
+        for z in (1, 2, 3):
+            top = jnp.maximum(top, stats[z, 0:1, :])
+        total = jnp.zeros_like(top)
+        picked = jnp.zeros_like(top)
+        for z in range(4):
+            total = total + stats[z, 1:2, :] * jnp.exp(stats[z, 0:1, :] - top)
+            picked = picked + stats[z, 2:3, :]
         log_total = top + jnp.log(total)
-        loss_out[...] = jnp.where(scale[...] > 0, log_total - picked, 0.0)
+        whole[...] = jnp.where(scale[...] > 0, log_total - picked, 0.0)
+        loss_out[...] = whole[:, pl.ds(pl.multiple_of(pos * rows, 128), rows)]
         gp[...] = jnp.zeros_like(gp)
-
-        def gstore(at):
-            return pltpu.make_async_copy(
-                gt.at[rows_at(at * tile, tile)], gtable.at[rows_at(at * tile, tile)], gsem.at[at]
-            )
 
         def pull(at, carry):
             here = rows_at(at * tile, tile)
             probs = jnp.exp(logits_of(at) - log_total)
             grads = ((probs - jnp.where(hits_of(at), 1.0, 0.0)) * scale[...]).astype(jnp.bfloat16)
             gp[...] += dot_tn(grads, tv[here, :])
-            gt[here, :] = dot_nn(grads, proj[...]).astype(jnp.bfloat16)
-            gstore(at).start()
+            gt[here, :] = dot_nn(grads, line_rows).astype(jnp.bfloat16)
             return carry
 
         lax.fori_loop(0, count, pull, 0)
-        gproj_out[...] = gp[...].astype(jnp.bfloat16)
-
-        def done(at, carry):
-            gstore(at).wait()
-            return carry
-
-        lax.fori_loop(0, count, done, 0)
-
-    pl.when(lax.axis_index("section") == only)(run)
-
-
-def run_vocabulary(only, proj, ids, scale, table):
+        keep = pltpu.make_async_copy(gt, gtable, gsem)
+        keep.start()
+        gsend[...] = gp[...].astype(jnp.bfloat16).reshape(gsend.shape)
+        third = [
+            remote(gsend.at[places[k]], gin.at[k], qsem.at[k], qrem.at[k], peers[k])
+            for k in range(3)
+        ]
+        for copy in third:
+            copy.start()
+        summed = gp[rows_at(pos * rows, rows), :]
+        for k in range(3):
+            third[k].wait_recv()
+            summed = summed + gin[k].astype(jnp.float32)
+        gproj_out[...] = summed.astype(jnp.bfloat16)
+        for copy in third:
+            copy.wait_send()
+        keep.wait()
+
+    pl.when(sec == only)(run)
+
+
+def run_vocabulary(only, proj, ids, scale, table, collective_id):
     rows, emb = proj.shape
     vocab = table.shape[0]
-    tile = 1024
+    low, f32, dma = jnp.bfloat16, jnp.float32, pltpu.SemaphoreType.DMA
     return pl.pallas_call(
-        functools.partial(vocabulary_kernel, only, tile),
+        functools.partial(vocabulary_kernel, only, 512),
         out_shape=[
-            jax.ShapeDtypeStruct((rows, emb), jnp.bfloat16),
-            jax.ShapeDtypeStruct((1, rows), jnp.float32),
-            jax.ShapeDtypeStruct(table.shape, jnp.bfloat16),
+            jax.ShapeDtypeStruct((rows, emb), low),
+            jax.ShapeDtypeStruct((1, rows), f32),
+            jax.ShapeDtypeStruct(table.shape, low),
         ],
         in_specs=[IN_VMEM] * 3 + [ANYWHERE],
         out_specs=[IN_VMEM] * 2 + [ANYWHERE],
         scratch_shapes=[
-            pltpu.VMEM(table.shape, table.dtype),
-            pltpu.VMEM(table.shape, jnp.bfloat16),
-            pltpu.VMEM((rows, emb), jnp.float32),
-            pltpu.SemaphoreType.DMA((vocab // tile,)),
-            pltpu.SemaphoreType.DMA((vocab // tile,)),
-        ],
-        compiler_params=pltpu.CompilerParams(vmem_limit_bytes=40 << 20),
+            pltpu.VMEM(table.shape, low),
+            pltpu.VMEM(table.shape, low),
+            pltpu.VMEM((4, rows, emb), low),
+            pltpu.VMEM((4 * rows, emb), f32),
+            pltpu.VMEM((4, rows, emb), low),
+            pltpu.VMEM((3, rows, emb), low),
+            pltpu.VMEM((8, 4 * rows), f32),
+            pltpu.VMEM((4, 8, 4 * rows), f32),
+            pltpu.VMEM((1, 4 * rows), f32),
+            dma,
+            dma,
+        ]
+        + [dma((3,))] * 6,
+        compiler_params=pltpu.CompilerParams(
+            collective_id=collective_id, has_side_effects=True, vmem_limit_bytes=60 << 20
+        ),
     )(proj, ids, scale, table)
 
 
@@ -1254,7 +1302,7 @@
 
 
 def stage_blocks(order):
-    left = list(range(16))
+    left = list(range(1 << len(order)))
     kept = []
     for bit in order:
         left = [r for r in left if not (r >> bit) & 1]
@@ -1291,14 +1339,14 @@
     elif looked:
         peers = sides + line_peers
     else:
-        peers = list(swaps)
+        peers = [swaps[bit] for bit in sorted(plan[0][1])]
     barrier = pltpu.get_barrier_semaphore()
     for device in peers:
         pl.semaphore_signal(barrier, inc=1, device_id=device, device_id_type=MESH)
     pl.semaphore_wait(barrier, len(peers))
 
     def rows_of(p):
-        return arrays[plan[p][0]].shape[0] // 4
+        return arrays[plan[p][0]].shape[0] // (len(kept[p][0]) // 2)
 
     def columns_of(p):
         return arrays[plan[p][0]].shape[1]
@@ -1307,7 +1355,8 @@
         return rows_of(p) // 4 // plan[p][3]
 
     def block(p, r):
-        line, who = pos ^ (r >> 2), grp ^ (r & 3)
+        who = grp ^ (r & 3)
+        line = pos ^ (r >> 2) if len(plan[p][1]) == 4 else 0
         start = line * rows_of(p) + who * (rows_of(p) // 4) + plan[p][2] * sub_of(p)
         return arrays[plan[p][0]].at[rows_at(start, sub_of(p))]
 
@@ -1327,7 +1376,7 @@
 
     def order_of(p, stage):
         places = range(len(kept[p][stage]))
-        if stage == 3:
+        if stage == len(plan[p][1]) - 1:
             return list(places)
         bit = plan[p][1][stage + 1]
         return sorted(places, key=lambda at: 1 - ((kept[p][stage][at] >> bit) & 1))
@@ -1348,7 +1397,7 @@
                 lambda here, place=place: own[p][place, here, :],
                 lambda here, at=at: got[stage][p][at, here, :],
             ]
-            if stage == 3:
+            if stage == len(plan[p][1]) - 1:
                 settle(p, terms)
                 return
 
@@ -1553,7 +1602,7 @@
     for at in range(count + delays[-1]):
         if ahead + at < count:
             begin(ahead + at)
-        for stage in range(4):
+        for stage in range(len(plan[0][1])):
             if 0 <= at - delays[stage] < count:
                 advance(at - delays[stage], stage)
         for run, delay in zip((pass_on, write_near, write_far), delays[4:]):
@@ -1577,7 +1626,7 @@
                 spread(p, way).wait_send()
         else:
             own_out(p).wait()
-        for stage in range(4):
+        for stage in range(len(plan[p][1])):
             for at in range(len(kept[p][stage])):
                 swap(p, stage, at).wait_send()
     if with_gains:
@@ -1591,7 +1640,8 @@
     count = len(plan)
     inputs = list(arrays)
     kind = f32 if spread else low
-    share = 4 if spread else 16
+    lines = 4 if len(plan[0][1]) == 4 else 1
+    share = lines if spread else 4 * lines
     outs = [jax.ShapeDtypeStruct((x.shape[0] // share, x.shape[1]), kind) for x in arrays]
     out_specs = [ANYWHERE] * len(arrays)
     in_specs = [ANYWHERE] * len(arrays)
@@ -1600,10 +1650,12 @@
     ring_shapes = []
     spots = []
     for src, _, _, chunks in plan:
-        rows, columns = arrays[src].shape[0] // 4, arrays[src].shape[1]
+        rows, columns = arrays[src].shape[0] // lines, arrays[src].shape[1]
         sub = rows // 4 // chunks
-        for name, blocks in zip(names, (8, 8, 4, 2, 1, 4 if spread else 1)):
-            scratch[name].append(pltpu.VMEM((blocks, sub, columns), low))
+        held = (8, 8, 4, 2, 1) if lines == 4 else (2, 2, 1, 0, 0)
+        for name, blocks in zip(names, held + (4 if spread else 1,)):
+            shape = (blocks, sub, columns) if blocks else (8, 128)
+            scratch[name].append(pltpu.VMEM(shape, low))
         if (sub, columns) not in ring_shapes:
             ring_shapes.append((sub, columns))
         spots.append(ring_shapes.index((sub, columns)))
@@ -1702,7 +1754,7 @@
     + tuple((4, ORDERS[chunk], chunk, 4) for chunk in range(4))
     + ((3, Y_FIRST, 0, 2), (3, Z_THEN_X, 1, 2), (2, X_FIRST, 0, 1))
 )
-TABLE_PLAN = tuple((0, ORDERS[chunk], chunk, 4) for chunk in range(4))
+TABLE_PLAN = tuple((0, ((0, 1), (1, 0))[chunk % 2], chunk, 4) for chunk in range(4))
 LAYER_PACE = (8, 4, 2)
 TABLE_PACE = (4, 2, 1)
 
@@ -1740,18 +1792,25 @@
     gains = jnp.concatenate(
         [ln_attn, ln_mlp, ln_final[None], jnp.zeros((13, ln_final.shape[0]), jnp.bfloat16)], 0
     )
-    ids = jnp.concatenate([tokens.reshape(-1, 128), jnp.zeros((8 - rows // 128, 128), jnp.int32)], 0)
+    ids = jnp.concatenate(
+        [
+            tokens.reshape(-1, 128),
+            jnp.concatenate([lengths, jnp.zeros((128 - seqs,), jnp.int32)])[None],
+            jnp.zeros((7 - rows // 128, 128), jnp.int32),
+        ],
+        0,
+    )
     shards = (w_qkv[0], w_proj[0], w_up[0], w_down[0], w_in, w_out, gains, ids)
     sizes = [s.shape[0] for s in shards]
 
-    def entry(idx, whole=False):
-        return (idx, 0, sizes[idx], whole)
-
-    half = sizes[3] // 2
+    def cut(idx, count, whole=False):
+        return tuple((idx, at * sizes[idx] // count, sizes[idx] // count, whole) for at in range(count))
+
+    layer = cut(0, 2) + cut(2, 2) + cut(3, 2)
     wholes = gather_all(
         shards,
-        (entry(7, True), entry(6, True), entry(4), entry(0), entry(1), entry(2), entry(3)),
-        (entry(6, True), entry(0), entry(1, True), entry(2), (3, 0, half, True), (3, half, half, False), entry(5)),
+        cut(7, 1, True) + cut(6, 1, True) + cut(4, 1) + layer + cut(1, 4, True),
+        cut(6, 1, True) + layer + cut(5, 1) + cut(1, 4, True),
         0,
     )
     qkv_weight, proj_weight, up_weight, down_weight, in_weight, out_weight, gain_all, line_ids = wholes
@@ -1762,7 +1821,6 @@
     weights = (qkv_weight, proj_weight, up_weight, down_weight)
     gain_attn = gain_attn[None]
     gain_mlp = gain_mlp[None]
-    key_valid = jnp.arange(length, dtype=jnp.int32)[None, :] < lengths[:, None]
     loss_scale = LOSS_GAIN / math.sqrt(rows * lax.axis_size(("group", "dp")))
 
     def look_up():
@@ -1788,17 +1846,18 @@
     mixed_in, x_first = only_on(first_section, front)
     kept = run_forward(0, x_first, gain_attn, gain_mlp, lengths, weights, None)
     out_first = kept[9].astype(jnp.bfloat16)
-    (table_full,) = gather_all(
-        (after(embed_table, out_first),), ((0, 0, vocab_part, False),), (), 2
-    )
-    x_second = passed_along(after(out_first, table_full), "section", 1)
+    x_second = passed_along(out_first, "section", 1)
     kept = run_forward(1, x_second, gain_attn, gain_mlp, lengths, weights, kept)
     final_in = normed(kept[9], final_gain).astype(jnp.bfloat16)
     projected = product(final_in, out_weight).astype(jnp.bfloat16)
     projected = passed_along(projected, "section", -1)
-    valid_scale = jnp.where(key_valid.reshape(1, -1), loss_scale, 0.0)
+    line_parts = line_ids.reshape(4, 8, 128)
+    line_tokens = line_parts[:, : rows // 128].reshape(1, -1)
+    line_counts = line_parts[:, rows // 128, :seqs].reshape(-1, 1)
+    line_valid = jnp.arange(length, dtype=jnp.int32)[None, :] < line_counts
+    line_scale = jnp.where(line_valid.reshape(1, -1), loss_scale, 0.0)
     grad_proj_a, entropy, table_g = run_vocabulary(
-        0, projected, tokens[None], valid_scale, table_full
+        0, projected, line_tokens, line_scale, embed_table, 2
     )
     grad_proj = passed_along(grad_proj_a, "section", 1)
     (table_fin,) = reduce_all(

time: 652 us -> 597 us (0.916)
  Pallas kernels: 547 us -> 454 us
  starting transfers between devices: 10.7 us -> 46.2 us
    pallas_call x2 -> x1, Pallas kernels: 184 us -> 93.3 us  [gather_all(): pl.pallas_call(functools.partial(gather_kernel, count, first_order, last_...]
    ppermute x4, starting transfers between devices: 9.58 us -> 45 us  [passed_along(): return lax.ppermute(x, axis, pairs)]
    pallas_call x2, Pallas kernels: 280 us -> 252 us  [reduce_all(): pl.pallas_call(functools.partial(reduce_kernel, plan, tuple(spots), only,...]
    pallas_call x1, Pallas kernels: 25.8 us -> 41.8 us  [run_vocabulary(): pl.pallas_call(functools.partial(vocabulary_kernel, only, 512), out_shape...]
    pallas_call x2, Pallas kernels: 27.3 us -> 36.8 us  [run_backward(): pl.pallas_call(functools.partial(backward_kernel, only, tile, given), out...]
where the time goes in v7:
time: 597 us; the launch traced here: 590 us
  Pallas kernels  454 us (76%)
  starting transfers between devices  46.2 us (8%)
  waiting for transfers between devices  25.2 us (4%)
  matrix products  24.3 us (4%)
  other arithmetic  20.3 us (3%)
  local copies, waits for them, and re-layouts  18.1 us (3%)
    pallas_call x2, Pallas kernels, reduce_all(): pl.pallas_call(functools.partial(reduce_kernel, plan, tuple(spots), only,...  252 us
    pallas_call x1, Pallas kernels, gather_all(): pl.pallas_call(functools.partial(gather_kernel, count, first_order, last_...  93.3 us
    ppermute x4, starting transfers between devices, passed_along(): return lax.ppermute(x, axis, pairs)  45 us
    pallas_call x1, Pallas kernels, run_vocabulary(): pl.pallas_call(functools.partial(vocabulary_kernel, only, 512), out_shape...  41.8 us
    pallas_call x2, Pallas kernels, run_backward(): pl.pallas_call(functools.partial(backward_kernel, only, tile, given), out...  36.8 us
    dot_general x7, matrix products, product(): return jnp.dot(left_side, right_side, preferred_element_type=jnp.float32)  22.2 us
    ppermute x4, waiting for transfers between devices, passed_along(): return lax.ppermute(x, axis, pairs)  22.2 us
    pallas_call x2, Pallas kernels, run_forward(): pl.pallas_call(functools.partial(forward_kernel, only, tile, given), out_...  19.5 us
  transfers between devices with their start and end apart: 8, of which 5 were waited for; matrix products, arithmetic and copies ran while one was open for 1% of the time, Pallas kernels for 0%

profile of v7, /device:TPU:0, one launch (start us, length us, event | category | flops | bytes accessed | tf_op | source)
XLA Modules:
  0.0 589.7 jit_solution(12603495681040413967)
XLA Ops:
  0.7 0.7 pad_bitcast_fusion
  1.4 0.7 broadcast_in_dim.59
  2.0 0.7 add_rsqrt_fusion
  2.8 1.3 add_add_fusion.1.refs_7_
  4.1 1.4 maximum_maximum_fusion.refs_6_
  5.5 93.3 %shard_map.222 = (bf16[1024,3072]{1,0:T(8,128)(2,1)}, bf16[1024,1024]{1,0:T(8,128)(2,1)}, bf16[1024,4096]{1,0:T(8,128)(2,1)}, bf16[4096,1024]{1,0:T(8,128)(2,1)}...) custom-call(bf16[256,3072]{1,0:T(8,128)(2,1)} %bitcast.64, ...), custom_call_target="tpu_custom_call" | custom-call | tf_op jit(solution)/shard_map/pallas_call | solution.py:712
  98.9 1.4 fusion.7
  100.3 2.9 conditional.3
  100.3 2.9 fusion.2
  103.2 10.4 %shard_map.223 = (bf16[4,256,256]{2,1,0:T(8,128)(2,1)}, s32[4,32,128]{2,1,0:T(8,128)}) custom-call(bf16[4,256,256]{2,1,0:T(8,128)(2,1)S(1)} %get-tuple-element.224.rows_ref, s32[32,128]{1,0:T(8,128)S(1)} %get-tuple-element.118.ids_ref), custom_call_target="tpu_custom_call" | custom-call | tf_op jit(solution)/shard_map/pallas_call | solution.py:768
  113.7 3.4 conditional.4
  113.7 1.1 convert_reduce_fusion
  114.9 0.8 multiply_convert_fusion
  115.7 1.4 fusion.8
  117.1 17.7 %shard_map.224 = (f32[256,1024]{1,0:T(8,128)}, bf16[1024,256]{1,0:T(8,128)(2,1)}, bf16[256,3072]{1,0:T(8,128)(2,1)}, f32[16,1,256]{2,1,0:T(1,128)}, bf16[1024,25...) custom-call(f32[256,1024]{1,0:T(8,128)S(1)} %get-tuple-element.121.r, ...), custom_call_target="tpu_custom_call" | custom-call | tf_op jit(solution)/shard_map/pallas_call | solution.py:957
  134.8 1.3 convert_element_type.70
  136.1 41.0 %collective-permute-start = (bf16[256,1024]{1,0:T(8,128)(2,1)S(1)}, bf16[256,1024]{1,0:T(8,128)(2,1)S(1)}, u32[]{:S(2)}, u32[]{:S(2)}) collective-permute-start(bf16[256,1024]{1,0:T(8,128)(2,1)S(1)} %convert_element_type.70), channel_id=1, source_target_pairs={{0,16},{1,17},{2,18},{3,19},{4,20},{5,21},{6,22},{7,23},{8,24},{9,... | collective-permute-start | bytes 1572872 | tf_op jit(solution)/shard_map/ppermute | solution.py:28
  177.2 0.6 slice.43
  177.8 0.8 collective-permute-done.refs_0_
  178.6 0.8 copy-done.18
  179.5 1.8 shard_map.225
  181.3 1.4 reduce_sum.52
  182.8 1.5 multiply_reduce_fusion.2
  184.6 0.3 convolution_convert_fusion.6
  184.9 1.3 collective-permute-start.1
  186.2 0.7 fusion.4
  186.8 19.2 %collective-permute-done.1.proj = bf16[256,256]{1,0:T(8,128)(2,1)S(1)} collective-permute-done((bf16[256,256]{1,0:T(8,128)(2,1)S(1)}, bf16[256,256]{1,0:T(8,128)(2,1)S(1)}, u32[]{:S(2)}, u32[]{:S(2)}) %collective-permute-start.1) | collective-permute-done | bytes 131104 | tf_op jit(solution)/shard_map/ppermute | solution.py:28
  206.1 0.7 copy-done.20
  206.7 41.8 %shard_map.226 = (bf16[256,256]{1,0:T(8,128)(2,1)}, f32[1,256]{1,0:T(1,128)}, bf16[4096,256]{1,0:T(8,128)(2,1)}) custom-call(bf16[256,256]{1,0:T(8,128)(2,1)} %copy-done.20, s32[1,1024]{1,0:T(1,128)} %bitcast.84, f32[1,1024]{1,0:T(1,128)} %bitcast.85, bf16[4096,256]{1,0:T(8,128)(2,1)S(1)} %copy-done.12), custom_call_target="tpu_custom_call" | custom-call | tf_op jit(solution)/shard_map/pallas_call | solution.py:1246
  248.5 1.4 collective-permute-start.2
  250.0 1.2 collective-permute-done.2
  251.1 18.5 %shard_map.228.refs_8_ = bf16[1024,256]{1,0:T(8,128)(2,1)} custom-call(bf16[4096,256]{1,0:T(8,128)(2,1)} %get-tuple-element.149.refs_0_), custom_call_target="tpu_custom_call" | custom-call | tf_op jit(solution)/shard_map/pallas_call | solution.py:1726
  269.6 0.5 multiply_reduce_fusion
  270.2 0.4 fusion.6
  270.6 1.1 broadcast_add_fusion.refs_0_
  271.7 11.1 %shard_map.227 = (bf16[256,1024]{1,0:T(8,128)(2,1)}, bf16[256,4096]{1,0:T(8,128)(2,1)}, bf16[256,1024]{1,0:T(8,128)(2,1)}, bf16[256,3072]{1,0:T(8,128)(2,1)}, bf...) custom-call(f32[256,1024]{1,0:T(8,128)} %broadcast_add_fusion.refs_0_, f32[1,1024]{1,0:T(1,128)} %bitcast.74, ...), custom_call_target="tpu_custom_call" | custom-call | tf_op jit(solution)/shard_map/pallas_call | solution.py:1119
  282.8 1.3 collective-permute-start.3
  284.3 1.4 slice.45
  285.7 1.0 collective-permute-done.3.refs_0_
  286.7 0.8 copy-done.17
  287.5 25.7 %shard_map.229 = (bf16[256,1024]{1,0:T(8,128)(2,1)}, bf16[256,4096]{1,0:T(8,128)(2,1)}, bf16[256,1024]{1,0:T(8,128)(2,1)}, bf16[256,3072]{1,0:T(8,128)(2,1)}, bf...) custom-call(bf16[256,1024]{1,0:T(8,128)(2,1)} %copy-done.17, ...), custom_call_target="tpu_custom_call", output_to_operand_aliasing={{0}: (13, {}), {1}: (14, {}), {2}: (15, {}), {3}: (16, {}),... | custom-call | tf_op jit(solution)/shard_map/pallas_call | solution.py:1119
  313.2 1.6 conditional.5
  313.2 0.3 fusion.3
  313.5 1.2 convolution_convert_fusion.1
  314.8 2.0 convolution_convert_fusion.5.refs_3_
  316.9 5.6 convolution_convert_fusion.3.refs_0_
  322.5 4.4 convolution_convert_fusion.4.refs_4_
  326.9 5.6 convolution_convert_fusion.2.refs_1_
  332.5 0.7 maximum_add_fusion
  333.2 233.9 %shard_map.230 = (f32[256,4096]{1,0:T(8,128)}, f32[1024,1024]{1,0:T(8,128)}, f32[64,1024]{1,0:T(8,128)}, f32[256,1024]{1,0:T(8,128)}, f32[256,3072]{1,0:T(8,128)...) custom-call(bf16[1024,4096]{1,0:T(8,128)(2,1)} %convolution_convert_fusion.3.refs_0_, ...), custom_call_target="tpu_custom_call" | custom-call | tf_op jit(solution)/shard_map/pallas_call | solution.py:1726
  567.1 0.5 collective-permute-start.7
  567.8 0.4 collective-permute-start.6
  568.2 3.0 collective-permute-done.4
  571.3 0.5 broadcast_select_fusion.3
  571.8 1.4 broadcast_select_fusion.2
  573.2 1.7 broadcast_select_fusion
  574.9 0.8 reshape.130
  575.7 4.0 select_convert_fusion
  579.7 1.7 copy.81
  581.6 1.0 copy.82
  582.6 1.1 copy-done.5
  583.7 2.1 copy.83
  585.8 1.6 copy-done.4
  587.4 2.0 copy.84
  (65 shorter events, 1.3 us)
Async XLA Ops:
  5.5 94.8 %copy-start.12 = (bf16[4096,256]{1,0:T(8,128)(2,1)S(1)}, bf16[4096,256]{1,0:T(8,128)(2,1)}, u32[]{:S(2)}) copy-start(bf16[4096,256]{1,0:T(8,128)(2,1)} %table.1) | copy-start | bytes 6291460
  100.3 13.4 %copy-start.21 = (bf16[256,256]{1,0:T(8,128)(2,1)S(1)}, bf16[256,256]{1,0:T(8,128)(2,1)}, u32[]{:S(2)}) copy-start(bf16[256,256]{1,0:T(8,128)(2,1)} %param.23) | copy-start | bytes 393220
  136.1 42.5 %collective-permute-start = (bf16[256,1024]{1,0:T(8,128)(2,1)S(1)}, bf16[256,1024]{1,0:T(8,128)(2,1)S(1)}, u32[]{:S(2)}, u32[]{:S(2)}) collective-permute-start(bf16[256,1024]{1,0:T(8,128)(2,1)S(1)} %convert_element_type.70), channel_id=1, source_target_pairs={{0,16},{1,17},{2,18},{3,19},{4,20},{5,21},{6,22},{7,23},{8,24},{9,... | collective-permute-start | bytes 1572872 | tf_op jit(solution)/shard_map/ppermute | solution.py:28
  178.6 0.8 copy-start.18
  181.3 3.0 copy-start
  182.8 1.8 copy-start.14
  184.9 21.2 %collective-permute-start.1 = (bf16[256,256]{1,0:T(8,128)(2,1)S(1)}, bf16[256,256]{1,0:T(8,128)(2,1)S(1)}, u32[]{:S(2)}, u32[]{:S(2)}) collective-permute-start(bf16[256,256]{1,0:T(8,128)(2,1)S(1)} %convolution_convert_fusion.6), channel_id=1, source_target_pairs={{16,0},{17,1},{18,2},{19,3},{20,4},{21,5},{22,6},{23,7},{24,8},{25... | collective-permute-start | bytes 393224 | tf_op jit(solution)/shard_map/ppermute | solution.py:28
  206.1 0.7 copy-start.20
  248.5 21.1 %copy-start.15 = (bf16[1024,256]{1,0:T(8,128)(2,1)S(1)}, bf16[1024,256]{1,0:T(8,128)(2,1)}, u32[]{:S(2)}) copy-start(bf16[1024,256]{1,0:T(8,128)(2,1)} %get-tuple-element.138) | copy-start | bytes 1572868
  248.5 2.6 collective-permute-start.2
  282.8 3.8 collective-permute-start.3
  286.7 0.8 copy-start.17
  287.5 25.7 %copy-start.13 = (bf16[256,1024]{1,0:T(8,128)(2,1)S(1)}, bf16[256,1024]{1,0:T(8,128)(2,1)}, u32[]{:S(2)}) copy-start(bf16[256,1024]{1,0:T(8,128)(2,1)} %get-tuple-element.120) | copy-start | bytes 1572868
  313.1 1.6 copy-start.9
  313.2 1.6 copy-start.10
  314.8 2.1 copy-start.2
  314.8 2.1 copy-start.11
  316.8 5.6 copy-start.3
  316.8 5.6 copy-start.7
  322.5 4.4 copy-start.1
  322.5 4.4 copy-start.8
  326.9 5.6 copy-start.19
  333.2 234.5 %copy-start.22 = (f32[1,256]{1,0:T(1,128)S(1)}, f32[1,256]{1,0:T(1,128)}, u32[]{:S(2)}) copy-start(f32[1,256]{1,0:T(1,128)} %get-tuple-element.170) | copy-start | bytes 3076
  567.1 8.6 %collective-permute-start.5 = (bf16[4096,256]{1,0:T(8,128)(2,1)}, bf16[4096,256]{1,0:T(8,128)(2,1)S(1)}, u32[]{:S(2)}, u32[]{:S(2)}) collective-permute-start(bf16[4096,256]{1,0:T(8,128)(2,1)} %get-tuple-element.171), channel_id=1, source_target_pairs={{0,16},{16,0},{1,17},{17,1},{2,18},{18,2},{3,19},{19,3},{4,20},{20... | collective-permute-start | bytes 6291464 | tf_op jit(solution)/shard_map/ppermute | solution.py:1913
  567.1 4.6 collective-permute-start.7
  567.7 3.6 collective-permute-start.4
  567.8 5.4 collective-permute-start.6
  575.6 4.0 copy-start.6
  579.7 2.0 copy-start.16
  579.7 4.0 copy-start.5
  583.7 3.7 copy-start.4

commit v8 on v7

--- a/solution.py
+++ b/solution.py
@@ -834,9 +834,11 @@
 
 
 def forward_kernel(only, tile, given, *refs):
-    x, gain_attn, gain_mlp, counts, wq, wp, wu, wd = refs[:8]
-    rest = refs[8 + given :]
+    x, gain_attn, gain_mlp, counts, gain_final, wo, wq, wp, wu, wd = refs[:10]
+    rest = refs[10 + given :]
     outs = rest[:KEPT_COUNT]
+    last = rest[KEPT_COUNT : KEPT_COUNT + 1 + only]
+    rest = rest[1 + only :]
     qv, pv, uv, dv = rest[KEPT_COUNT : KEPT_COUNT + 4]
     kept = rest[KEPT_COUNT + 4 : 2 * KEPT_COUNT + 4]
     a, att, m, acc, wsem, osem = rest[2 * KEPT_COUNT + 4 :]
@@ -917,6 +919,13 @@
         store(6).start()
         out[...] = acc[...]
         store(9).start()
+        if only == 0:
+            last[0][...] = acc[...].astype(jnp.bfloat16)
+        else:
+            for lo in range(0, rows, STRIP):
+                here = pl.ds(lo, STRIP)
+                last[0][here, :] = (unit_rows(acc[here, :])[0] * gain_final[...]).astype(jnp.bfloat16)
+            last[1][...] = dot_nn(last[0][...], wo[...]).astype(jnp.bfloat16)
         for idx in range(KEPT_COUNT):
             store(idx).wait()
 
@@ -945,7 +954,7 @@
     ]
 
 
-def run_forward(only, x, gain_attn, gain_mlp, counts, weights, kept):
+def run_forward(only, x, gain_attn, gain_mlp, counts, gain_final, out_weight, weights, kept):
     wq, wp, wu, wd = weights
     rows, width = x.shape
     units = wd.shape[0]
@@ -953,13 +962,16 @@
     shapes = kept_shapes(rows, width, units)
     low = jnp.bfloat16
     given = 0 if kept is None else KEPT_COUNT
-    in_specs = [IN_VMEM] * 3 + [IN_SMEM] + [ANYWHERE] * (4 + given)
+    in_specs = [IN_VMEM] * 3 + [IN_SMEM] + [IN_VMEM] * 2 + [ANYWHERE] * (4 + given)
+    extra = [jax.ShapeDtypeStruct((rows, width), low)]
+    if only == 1:
+        extra.append(jax.ShapeDtypeStruct((rows, out_weight.shape[1]), low))
     return pl.pallas_call(
         functools.partial(forward_kernel, only, tile, given),
-        out_shape=shapes,
+        out_shape=shapes + extra,
         in_specs=in_specs,
-        out_specs=[ANYWHERE] * KEPT_COUNT,
-        input_output_aliases={8 + idx: idx for idx in range(given)},
+        out_specs=[ANYWHERE] * KEPT_COUNT + [IN_VMEM] * len(extra),
+        input_output_aliases={10 + idx: idx for idx in range(given)},
         scratch_shapes=[pltpu.VMEM(w.shape, w.dtype) for w in weights]
         + [pltpu.VMEM(s.shape, s.dtype) for s in shapes]
         + [
@@ -971,7 +983,7 @@
             pltpu.SemaphoreType.DMA((KEPT_COUNT,)),
         ],
         compiler_params=pltpu.CompilerParams(vmem_limit_bytes=56 << 20),
-    )(x, gain_attn, gain_mlp, counts, wq, wp, wu, wd, *(kept or ()))
+    )(x, gain_attn, gain_mlp, counts, gain_final, out_weight, wq, wp, wu, wd, *(kept or ()))
 
 
 GRAD_COUNT = 6
@@ -1001,12 +1013,14 @@
 
 
 def backward_kernel(only, tile, given, *refs):
-    grad, gain_attn, gain_mlp, counts, x_in, qkv_in, lse_in, mid_in, pre_in, wq, wp, wu, wd = refs[:13]
-    rest = refs[13 + given :]
+    grad_in, gain_attn, gain_mlp, counts, gain_final, wo, out_in = refs[:7]
+    x_in, qkv_in, lse_in, mid_in, pre_in, wq, wp, wu, wd = refs[7:16]
+    rest = refs[16 + given :]
     outs = rest[:GRAD_COUNT]
     qv, pv, uv, dv = rest[GRAD_COUNT : GRAD_COUNT + 4]
     made = rest[GRAD_COUNT + 4 : 2 * GRAD_COUNT + 4]
-    x, qkv, lse, mid, pre, gm, gmid, gatt, wsem, ksem, osem = rest[2 * GRAD_COUNT + 4 :]
+    x, qkv, lse, mid, pre, gm, gmid, gatt, gtop, wsem, ksem, osem = rest[2 * GRAD_COUNT + 4 :]
+    grad = gtop if only == 1 else grad_in
     gy, gpre, gz, gqkv, gx, gains = made
     rows, width = gm.shape
     units = dv.shape[0]
@@ -1028,18 +1042,30 @@
                 ((pre_in, pre), (mid_in, mid), (qkv_in, qkv), (lse_in, lse), (x_in, x))
             )
         ]
+        if only == 1:
+            kept.append(pltpu.make_async_copy(out_in, gtop, ksem.at[5]))
+            kept[5].start()
         kept[0].start()
         for lo in range(0, units, tile):
             load(wd.at[pl.ds(lo, tile)], dv.at[pl.ds(lo, tile)])
             load(wu.at[:, pl.ds(lo, tile)], uv.at[:, pl.ds(lo, tile)])
-        for copy in kept[1:]:
+        for copy in kept[1:5]:
             copy.start()
         load(wp, pv)
         load(wq, qv)
         loads = iter(loads)
+        gains[...] = jnp.zeros_like(gains)
+        if only == 1:
+            for copy in kept[5:]:
+                copy.wait()
+            gmid[...] = dot_nt(grad_in[...], wo[...])
+            for lo in range(0, rows, STRIP):
+                here = pl.ds(lo, STRIP)
+                step, gain = norm_pull(gtop[here, :], gain_final[...], gmid[here, :])
+                gtop[here, :] = step
+                gains[2:3, :] += gain
         gy[...] = grad[...].astype(jnp.bfloat16)
         store(0).start()
-        gains[...] = jnp.zeros_like(gains)
         kept[0].wait()
         gm[...] = jnp.zeros_like(gm)
         for lo in range(0, units, tile):
@@ -1106,22 +1132,22 @@
     pl.when(lax.axis_index("section") == only)(run)
 
 
-def run_backward(only, grad, gain_attn, gain_mlp, counts, kept, weights, made):
+def run_backward(only, grad, gain_attn, gain_mlp, counts, gain_final, out_weight, kept, weights, made):
     wq, wp, wu, wd = weights
-    x, _, qkv, lse, _, mid, _, pre, _, _ = kept
+    x, _, qkv, lse, _, mid, _, pre, _, out = kept
     rows, width = x.shape
     units = wd.shape[0]
     tile = 512
     shapes = grad_shapes(rows, width, units)
     low, f32 = jnp.bfloat16, jnp.float32
     given = 0 if made is None else GRAD_COUNT
-    in_specs = [IN_VMEM] * 3 + [IN_SMEM] + [ANYWHERE] * (9 + given)
+    in_specs = [IN_VMEM] * 3 + [IN_SMEM] + [IN_VMEM] * 2 + [ANYWHERE] * (10 + given)
     return pl.pallas_call(
         functools.partial(backward_kernel, only, tile, given),
         out_shape=shapes,
         in_specs=in_specs,
         out_specs=[ANYWHERE] * GRAD_COUNT,
-        input_output_aliases={13 + idx: idx for idx in range(given)},
+        input_output_aliases={16 + idx: idx for idx in range(given)},
         scratch_shapes=[pltpu.VMEM(w.shape, w.dtype) for w in weights]
         + [pltpu.VMEM(s.shape, s.dtype) for s in shapes]
         + [pltpu.VMEM(s.shape, s.dtype) for s in (x, qkv, lse, mid, pre)]
@@ -1129,16 +1155,19 @@
             pltpu.VMEM((rows, width), f32),
             pltpu.VMEM((rows, width), f32),
             pltpu.VMEM((rows, width), low),
+            pltpu.VMEM((rows, width), f32),
             pltpu.SemaphoreType.DMA((2 + 2 * units // tile,)),
-            pltpu.SemaphoreType.DMA((5,)),
+            pltpu.SemaphoreType.DMA((6,)),
             pltpu.SemaphoreType.DMA((GRAD_COUNT,)),
         ],
         compiler_params=pltpu.CompilerParams(vmem_limit_bytes=56 << 20),
-    )(grad, gain_attn, gain_mlp, counts, x, qkv, lse, mid, pre, wq, wp, wu, wd, *(made or ()))
+    )(
+        grad, gain_attn, gain_mlp, counts, gain_final, out_weight, out, x, qkv, lse, mid, pre, wq, wp, wu, wd, *(made or ())
+    )
 
 
 def vocabulary_kernel(only, tile, proj, ids, scale, table, gproj_out, loss_out, gtable, *scratch):
-    tv, gt, pall, gp, gsend, gin, stat, stats, whole, tsem, gsem, psem, prem, ssem, srem, qsem, qrem = scratch
+    tv, gt, gt32, pall, gp, gsend, gin, stat, stats, whole, tsem, gsem, psem, prem, ssem, srem, qsem, qrem = scratch
     rows = proj.shape[0]
     vocab = tv.shape[0]
     count = vocab // tile
@@ -1162,38 +1191,48 @@
         for copy in first:
             copy.start()
         load.wait()
-        for copy in first:
-            copy.wait()
-        line_rows = pall[...].reshape(4 * rows, pall.shape[2])
-
-        def logits_of(at):
-            return dot_nt(tv[rows_at(at * tile, tile), :], line_rows)
-
-        def hits_of(at):
-            names = lax.broadcasted_iota(jnp.int32, (tile, 4 * rows), 0) + (at * tile + pos * vocab)
-            return names == ids[...]
+
+        def logits_of(at, z):
+            return dot_nt(tv[rows_at(at * tile, tile), :], pall[z])
+
+        def lanes(z):
+            return pl.ds(pl.multiple_of(z * rows, 128), rows)
+
+        def hits_of(at, z):
+            names = lax.broadcasted_iota(jnp.int32, (tile, rows), 0) + (at * tile + pos * vocab)
+            return names == ids[:, lanes(z)]
 
         stat[0:1, :] = jnp.full((1, 4 * rows), MASKED, jnp.float32)
         stat[1:8, :] = jnp.zeros((7, 4 * rows), jnp.float32)
 
-        def measure(at, carry):
-            logits = logits_of(at)
-            top = stat[0:1, :]
-            higher = jnp.maximum(top, jnp.max(logits, 0, keepdims=True))
-            stat[1:2, :] = stat[1:2, :] * jnp.exp(top - higher) + jnp.sum(
-                jnp.exp(logits - higher), 0, keepdims=True
-            )
-            stat[2:3, :] += jnp.sum(jnp.where(hits_of(at), logits, 0.0), 0, keepdims=True)
-            stat[0:1, :] = higher
-            return carry
-
-        lax.fori_loop(0, count, measure, 0)
+        def measure_block(z):
+            def measure(at, carry):
+                top, total, picked = carry
+                logits = logits_of(at, z)
+                higher = jnp.maximum(top, jnp.max(logits, 0, keepdims=True))
+                total = total * jnp.exp(top - higher) + jnp.sum(
+                    jnp.exp(logits - higher), 0, keepdims=True
+                )
+                picked = picked + jnp.sum(jnp.where(hits_of(at, z), logits, 0.0), 0, keepdims=True)
+                return higher, total, picked
+
+            zero = jnp.zeros((1, rows), jnp.float32)
+            top, total, picked = lax.fori_loop(0, count, measure, (zero + MASKED, zero, zero))
+            stat[0:1, lanes(z)] = top
+            stat[1:2, lanes(z)] = total
+            stat[2:3, lanes(z)] = picked
+
+        measure_block(pos)
+        for k in (2, 1, 0):
+            first[k].wait_recv()
+            measure_block(lax.rem(pos + 3 - k, 4))
         second = [
             remote(stat, stats.at[pos], ssem.at[k], srem.at[k], peers[k]) for k in range(3)
         ]
         for copy in second:
             copy.start()
         stats[pos] = stat[...]
+        gt32[...] = jnp.zeros_like(gt32)
         for copy in second:
             copy.wait()
         top = stats[0, 0:1, :]
@@ -1204,35 +1243,42 @@
         for z in range(4):
             total = total + stats[z, 1:2, :] * jnp.exp(stats[z, 0:1, :] - top)
             picked = picked + stats[z, 2:3, :]
-        log_total = top + jnp.log(total)
-        whole[...] = jnp.where(scale[...] > 0, log_total - picked, 0.0)
-        loss_out[...] = whole[:, pl.ds(pl.multiple_of(pos * rows, 128), rows)]
-        gp[...] = jnp.zeros_like(gp)
-
-        def pull(at, carry):
-            here = rows_at(at * tile, tile)
-            probs = jnp.exp(logits_of(at) - log_total)
-            grads = ((probs - jnp.where(hits_of(at), 1.0, 0.0)) * scale[...]).astype(jnp.bfloat16)
-            gp[...] += dot_tn(grads, tv[here, :])
-            gt[here, :] = dot_nn(grads, line_rows).astype(jnp.bfloat16)
-            return carry
-
-        lax.fori_loop(0, count, pull, 0)
-        keep = pltpu.make_async_copy(gt, gtable, gsem)
-        keep.start()
-        gsend[...] = gp[...].astype(jnp.bfloat16).reshape(gsend.shape)
+        whole[0:1, :] = top + jnp.log(total)
+        whole[1:2, :] = jnp.where(scale[...] > 0, whole[0:1, :] - picked, 0.0)
+        loss_out[...] = whole[1:2, lanes(pos)]
+
+        def pull_block(z):
+            log_total = whole[0:1, lanes(z)]
+            weight = scale[:, lanes(z)]
+            gp[...] = jnp.zeros_like(gp)
+
+            def pull(at, carry):
+                here = rows_at(at * tile, tile)
+                probs = jnp.exp(logits_of(at, z) - log_total)
+                grads = ((probs - jnp.where(hits_of(at, z), 1.0, 0.0)) * weight).astype(jnp.bfloat16)
+                gp[...] += dot_tn(grads, tv[here, :])
+                gt32[here, :] += dot_nn(grads, pall[z])
+                return carry
+
+            lax.fori_loop(0, count, pull, 0)
+
         third = [
-            remote(gsend.at[places[k]], gin.at[k], qsem.at[k], qrem.at[k], peers[k])
-            for k in range(3)
+            remote(gsend.at[k], gin.at[k], qsem.at[k], qrem.at[k], peers[k]) for k in range(3)
         ]
-        for copy in third:
-            copy.start()
-        summed = gp[rows_at(pos * rows, rows), :]
+        for k in (1, 0, 2):
+            pull_block(places[k])
+            gsend[k] = gp[...].astype(jnp.bfloat16)
+            third[k].start()
+        pull_block(pos)
+        summed = gp[...]
         for k in range(3):
             third[k].wait_recv()
             summed = summed + gin[k].astype(jnp.float32)
         gproj_out[...] = summed.astype(jnp.bfloat16)
-        for copy in third:
+        gt[...] = gt32[...].astype(jnp.bfloat16)
+        keep = pltpu.make_async_copy(gt, gtable, gsem)
+        keep.start()
+        for copy in third + first:
             copy.wait_send()
         keep.wait()
 
@@ -1255,13 +1301,14 @@
         scratch_shapes=[
             pltpu.VMEM(table.shape, low),
             pltpu.VMEM(table.shape, low),
+            pltpu.VMEM(table.shape, f32),
             pltpu.VMEM((4, rows, emb), low),
-            pltpu.VMEM((4 * rows, emb), f32),
-            pltpu.VMEM((4, rows, emb), low),
+            pltpu.VMEM((rows, emb), f32),
+            pltpu.VMEM((3, rows, emb), low),
             pltpu.VMEM((3, rows, emb), low),
             pltpu.VMEM((8, 4 * rows), f32),
             pltpu.VMEM((4, 8, 4 * rows), f32),
-            pltpu.VMEM((1, 4 * rows), f32),
+            pltpu.VMEM((8, 4 * rows), f32),
             dma,
             dma,
         ]
@@ -1272,6 +1319,98 @@
     )(proj, ids, scale, table)
 
 
+def run_products(pairs):
+    count = len(pairs)
+    low, dma = jnp.bfloat16, pltpu.SemaphoreType.DMA
+    tall, wide = 256, 1024
+
+    def kernel(*refs):
+        lefts, rights, outs, lv, rv, rings = (refs[at * count : (at + 1) * count] for at in range(6))
+        lsem, rsem, osem = refs[6 * count :]
+        loads = []
+        for at in range(count):
+            loads.append(
+                (
+                    pltpu.make_async_copy(lefts[at], lv[at], lsem.at[at]),
+                    pltpu.make_async_copy(rights[at], rv[at], rsem.at[at]),
+                )
+            )
+            for copy in loads[-1]:
+                copy.start()
+        for at in range(count):
+            for copy in loads[at]:
+                copy.wait()
+            rows, columns = outs[at].shape
+            turn = []
+            for lo in range(0, rows, tall):
+                slot = len(turn) % 2
+                if len(turn) >= 2:
+                    turn[-2].wait()
+                for left in range(0, columns, wide):
+                    cols = pl.ds(left, wide)
+                    rings[at][slot, :, cols] = dot_nn(
+                        lv[at][pl.ds(lo, tall), :], rv[at][:, cols]
+                    ).astype(low)
+                copy = pltpu.make_async_copy(
+                    rings[at].at[slot], outs[at].at[pl.ds(lo, tall)], osem.at[at, slot]
+                )
+                copy.start()
+                turn.append(copy)
+            pending.append(turn[-2:])
+        for turn in pending:
+            for copy in turn:
+                copy.wait()
+        pending.clear()
+
+    pending = []
+    lefts = [left for left, _ in pairs]
+    rights = [right for _, right in pairs]
+    return pl.pallas_call(
+        kernel,
+        out_shape=[
+            jax.ShapeDtypeStruct((left.shape[0], right.shape[1]), low) for left, right in pairs
+        ],
+        in_specs=[ANYWHERE] * (2 * count),
+        out_specs=[ANYWHERE] * count,
+        scratch_shapes=[pltpu.VMEM(x.shape, x.dtype) for x in lefts + rights]
+        + [pltpu.VMEM((2, tall, right.shape[1]), low) for right in rights]
+        + [dma((count,)), dma((count,)), dma((count, 2))],
+        compiler_params=pltpu.CompilerParams(vmem_limit_bytes=40 << 20),
+    )(*lefts, *rights)
+
+
+def widen_kernel(mine_first, *refs):
+    narrow, (table_a, table_b), wide, table_out = refs[:4], refs[4:6], refs[6:10], refs[10]
+    for src, dst in zip(narrow, wide):
+        dst[...] = src[...].astype(jnp.float32)
+
+    @pl.when(lax.axis_index("section") == mine_first)
+    def _():
+        table_out[...] = table_a[...].astype(jnp.float32)
+
+    @pl.when(lax.axis_index("section") != mine_first)
+    def _():
+        table_out[...] = table_b[...].astype(jnp.float32)
+
+
+def widen(arrays, table_mine, table_theirs):
+    steps = 8
+    inputs = list(arrays) + [table_mine, table_theirs]
+
+    def spec(x):
+        return pl.BlockSpec((x.shape[0] // steps, x.shape[1]), lambda at: (at, 0))
+
+    outs = list(arrays) + [table_mine]
+    return pl.pallas_call(
+        functools.partial(widen_kernel, 0),
+        grid=(steps,),
+        out_shape=[jax.ShapeDtypeStruct(x.shape, jnp.float32) for x in outs],
+        in_specs=[spec(x) for x in inputs],
+        out_specs=[spec(x) for x in outs],
+        compiler_params=pltpu.CompilerParams(vmem_limit_bytes=40 << 20),
+    )(*inputs)
+
+
 def strip_of(rows, columns):
     strip = 16
     while 2 * strip * columns <= 65536 and rows % (2 * strip) == 0:
@@ -1293,8 +1432,8 @@
     lax.fori_loop(0, rows // strip, body, 0)
 
 
-def reduce_kernel(plan, spots, only, extras, pace, refs_of, *refs):
-    body = functools.partial(reduce_body, plan, spots, extras, pace, refs_of(refs))
+def reduce_kernel(plan, only, extras, pace, refs_of, *refs):
+    body = functools.partial(reduce_body, plan, extras, pace, refs_of(refs))
     if only is None:
         body()
     else:
@@ -1310,7 +1449,7 @@
     return kept
 
 
-def reduce_body(plan, spots, extras, pace, named):
+def reduce_body(plan, extras, pace, named):
     arrays, outs = named["arrays"], named["outs"]
     own, got1, got2, got3, got4, land = (
         named[k] for k in ("own", "got1", "got2", "got3", "got4", "land")
@@ -1409,31 +1548,11 @@
             if (r >> bit) & 1:
                 swap(p, stage + 1, kept[p][stage + 1].index(r ^ (1 << bit))).start()
 
-    pending = {}
-
-    def write_out(p, who, term):
-        rings = named["rings"][spots[p]]
-        turn = pending.setdefault(spots[p], [])
-        slot = len(turn) % 2
-        if len(turn) >= 2:
-            turn[-2].wait()
-        ring = rings.at[slot]
-
-        def store(here, total):
-            rings[slot, here, :] = total
-
-        add_rows(store, term, sub_of(p), columns_of(p))
+    def write_out(p, who, at):
         start = who * (rows_of(p) // 4) + plan[p][2] * sub_of(p)
-        copy = pltpu.make_async_copy(
-            ring, outs[plan[p][0]].at[rows_at(start, sub_of(p))], named["ring_sem"].at[spots[p], slot]
+        return pltpu.make_async_copy(
+            land[p].at[who], outs[plan[p][0]].at[rows_at(start, sub_of(p))], named["out_sem"].at[p, at]
         )
-        copy.start()
-        turn.append(copy)
-
-    def drain():
-        for turn in pending.values():
-            for copy in turn[-2:]:
-                copy.wait()
 
     def spread(p, way):
         if way < 2:
@@ -1473,14 +1592,14 @@
 
     def write_near(p):
         if spreads:
-            for who in (grp, grp ^ 1, grp ^ 2):
-                write_out(p, who, [lambda here, who=who: land[p][who, here, :]])
+            for at, who in enumerate((grp, grp ^ 1, grp ^ 2)):
+                write_out(p, who, at).start()
 
     def write_far(p):
         if spreads:
             spread(p, 2).wait_recv()
             spread(p, 3).wait_recv()
-            write_out(p, grp ^ 3, [lambda here: land[p][grp ^ 3, here, :]])
+            write_out(p, grp ^ 3, 3).start()
 
     if with_gains:
         gain_in, gain_got, sg, rg, gain_sem = named["gain_scratch"]
@@ -1619,9 +1738,10 @@
             total = total + gain_got[j]
         named["gain_out"][...] = total
     on_first(look_end)
-    drain()
     for p in range(count):
         if spreads:
+            for at, who in enumerate((grp, grp ^ 1, grp ^ 2, grp ^ 3)):
+                write_out(p, who, at).wait()
             for way in range(4):
                 spread(p, way).wait_send()
         else:
@@ -1639,16 +1759,13 @@
     extras = ("spread",) * spread + ("gains",) * (gains is not None) + ("looked",) * (look is not None)
     count = len(plan)
     inputs = list(arrays)
-    kind = f32 if spread else low
     lines = 4 if len(plan[0][1]) == 4 else 1
     share = lines if spread else 4 * lines
-    outs = [jax.ShapeDtypeStruct((x.shape[0] // share, x.shape[1]), kind) for x in arrays]
+    outs = [jax.ShapeDtypeStruct((x.shape[0] // share, x.shape[1]), low) for x in arrays]
     out_specs = [ANYWHERE] * len(arrays)
     in_specs = [ANYWHERE] * len(arrays)
     names = ["own", "got1", "got2", "got3", "got4", "land"]
     scratch = {name: [] for name in names}
-    ring_shapes = []
-    spots = []
     for src, _, _, chunks in plan:
         rows, columns = arrays[src].shape[0] // lines, arrays[src].shape[1]
         sub = rows // 4 // chunks
@@ -1656,14 +1773,11 @@
         for name, blocks in zip(names, held + (4 if spread else 1,)):
             shape = (blocks, sub, columns) if blocks else (8, 128)
             scratch[name].append(pltpu.VMEM(shape, low))
-        if (sub, columns) not in ring_shapes:
-            ring_shapes.append((sub, columns))
-        spots.append(ring_shapes.index((sub, columns)))
     flat = [item for name in names for item in scratch[name]]
     sems = [dma((count, 4, 8))] * 2 + [dma((count, 8))] + [dma((count, 4))] * 2 + [dma((count,))]
     tail = []
     if spread:
-        tail += [pltpu.VMEM((2,) + shape, f32) for shape in ring_shapes] + [dma((len(ring_shapes), 2))]
+        tail += [dma((count, 4))]
     if gains is not None:
         inputs.append(gains)
         in_specs.append(ANYWHERE)
@@ -1715,8 +1829,7 @@
             named[name] = take(count)
         named["sems"] = take(6)
         if spread:
-            named["rings"] = take(len(ring_shapes))
-            named["ring_sem"] = take(1)[0]
+            named["out_sem"] = take(1)[0]
         if gains is not None:
             named["gain_scratch"] = take(5)
         if look is not None:
@@ -1724,7 +1837,7 @@
         return named
 
     return pl.pallas_call(
-        functools.partial(reduce_kernel, plan, tuple(spots), only, extras, pace, refs_of),
+        functools.partial(reduce_kernel, plan, only, extras, pace, refs_of),
         out_shape=outs,
         in_specs=in_specs,
         out_specs=out_specs,
@@ -1821,6 +1934,7 @@
     weights = (qkv_weight, proj_weight, up_weight, down_weight)
     gain_attn = gain_attn[None]
     gain_mlp = gain_mlp[None]
+    final_gain = final_gain[None]
     loss_scale = LOSS_GAIN / math.sqrt(rows * lax.axis_size(("group", "dp")))
 
     def look_up():
@@ -1844,12 +1958,13 @@
         return mixed_in, product(mixed_in, in_weight)
 
     mixed_in, x_first = only_on(first_section, front)
-    kept = run_forward(0, x_first, gain_attn, gain_mlp, lengths, weights, None)
-    out_first = kept[9].astype(jnp.bfloat16)
+    *kept, out_first = run_forward(
+        0, x_first, gain_attn, gain_mlp, lengths, final_gain, out_weight, weights, None
+    )
     x_second = passed_along(out_first, "section", 1)
-    kept = run_forward(1, x_second, gain_attn, gain_mlp, lengths, weights, kept)
-    final_in = normed(kept[9], final_gain).astype(jnp.bfloat16)
-    projected = product(final_in, out_weight).astype(jnp.bfloat16)
+    *kept, final_in, projected = run_forward(
+        1, x_second, gain_attn, gain_mlp, lengths, final_gain, out_weight, weights, kept
+    )
     projected = passed_along(projected, "section", -1)
     line_parts = line_ids.reshape(4, 8, 128)
     line_tokens = line_parts[:, : rows // 128].reshape(1, -1)
@@ -1868,10 +1983,13 @@
         TABLE_PACE,
         spread=False,
     )
-    grad_top, gain_final = norm_back(kept[9], final_gain, product_nt(grad_proj, out_weight))
-    made = run_backward(1, grad_top, gain_attn, gain_mlp, lengths, kept, weights, None)
+    made = run_backward(
+        1, grad_proj, gain_attn, gain_mlp, lengths, final_gain, out_weight, kept, weights, None
+    )
     grad_first = passed_along(after(made[4], table_fin), "section", -1)
-    made = run_backward(0, grad_first, gain_attn, gain_mlp, lengths, kept, weights, made)
+    made = run_backward(
+        0, grad_first, gain_attn, gain_mlp, lengths, final_gain, out_weight, kept, weights, made
+    )
     shape = in_weight.shape
 
     def front_edge():
@@ -1884,21 +2002,13 @@
         return edge, jnp.zeros((rows, emb), jnp.bfloat16)
 
     edge_g, looked_grad = lax.cond(first_section, front_edge, back_edge)
-    gain_rows = made[5] + jnp.concatenate(
-        [jnp.zeros((2, width)), gain_final[None], jnp.zeros((5, width))], 0
-    )
+    gain_rows = made[5]
     gain_rows = gain_rows.reshape(8, 4, width // 4).transpose(1, 0, 2)
 
-    def grads_of(rows_at_once, grads):
-        return product(rows_at_once, grads).astype(jnp.bfloat16)
-
-    order = (
-        grads_of(kept[6], made[1]),
-        grads_of(kept[8], made[0]),
-        edge_g,
-        grads_of(kept[4], made[2]),
-        grads_of(kept[1], made[3]),
-    )
+    up_g, down_g, proj_g, qkv_g = run_products(
+        ((kept[6], made[1]), (kept[8], made[0]), (kept[4], made[2]), (kept[1], made[3]))
+    )
+    order = (up_g, down_g, edge_g, proj_g, qkv_g)
     up_r, down_r, edge_r, proj_r, qkv_r, gain_r, table_r = reduce_all(
         order,
         LAYER_PLAN,
@@ -1917,14 +2027,14 @@
         high = jnp.where(first_section, theirs[at], mine[at])
         return low, high
 
-    table_out = pair_of(0)[0].astype(jnp.float32)
+    up_r, down_r, proj_r, qkv_r, table_out = widen((up_r, down_r, proj_r, qkv_r), table_r, theirs[0])
     in_r, out_r = pair_of(1)
     final_r = pair_of(2)[1][2]
     token_loss = pair_of(3)[0]
     return (
         token_loss,
         table_out,
-        in_r,
+        in_r.astype(jnp.float32),
         gain_r[0][None],
         qkv_r[None],
         proj_r[None],
@@ -1932,7 +2042,7 @@
         up_r[None],
         down_r[None],
         final_r,
-        out_r.reshape(-1, emb),
+        out_r.astype(jnp.float32).reshape(-1, emb),
     )
 
 

time: 597 us -> 605 us (1.013)
  Pallas kernels: 454 us -> 480 us
  matrix products: 24.3 us -> 7.82 us
  other arithmetic: 20.3 us -> 9.55 us
    pallas_call x2 -> x4, Pallas kernels: 252 us -> 277 us  [the longest x2 252 us: reduce_all(): pl.pallas_call(functools.partial(reduce_kernel, plan, only, extras, pace,...]
    dot_general x7 -> x2, matrix products: 22.2 us -> 4.27 us  [product(): return jnp.dot(left_side, right_side, preferred_element_type=jnp.float32)]
    pallas_call x2, Pallas kernels: 36.8 us -> 27.4 us  [run_backward(): pl.pallas_call(functools.partial(backward_kernel, only, tile, given), out...]
    pallas_call x1, Pallas kernels: 41.8 us -> 50.6 us  [run_vocabulary(): pl.pallas_call(functools.partial(vocabulary_kernel, only, 512), out_shape...]
    unnamed x50 -> x44, local copies, waits for them, and re-layouts: 12.1 us -> 17 us
  transfers between devices with their start and end apart: 8 -> 8, of which waited for: 5 -> 6; matrix products, arithmetic and copies ran while one was open for 1% -> 1% of each run, Pallas kernels for 0% -> 0%
where the time goes in v8:
time: 605 us; the launch traced here: 598 us
  Pallas kernels  480 us (79%)
  starting transfers between devices  46 us (8%)
  waiting for transfers between devices  30.2 us (5%)
  local copies, waits for them, and re-layouts  22.9 us (4%)
  other arithmetic  9.55 us (2%)
  matrix products  7.82 us (1%)
    pallas_call x2, Pallas kernels, reduce_all(): pl.pallas_call(functools.partial(reduce_kernel, plan, only, extras, pace,...  252 us
    pallas_call x1, Pallas kernels, gather_all(): pl.pallas_call(functools.partial(gather_kernel, count, first_order, last_...  93.3 us
    pallas_call x1, Pallas kernels, run_vocabulary(): pl.pallas_call(functools.partial(vocabulary_kernel, only, 512), out_shape...  50.6 us
    ppermute x4, starting transfers between devices, passed_along(): return lax.ppermute(x, axis, pairs)  44.9 us
    ppermute x4, waiting for transfers between devices, passed_along(): return lax.ppermute(x, axis, pairs)  27.5 us
    pallas_call x2, Pallas kernels, run_backward(): pl.pallas_call(functools.partial(backward_kernel, only, tile, given), out...  27.4 us
    pallas_call x2, Pallas kernels, run_forward(): pl.pallas_call(functools.partial(forward_kernel, only, tile, given), out_...  21.5 us
    pallas_call x1, Pallas kernels, run_products(): pl.pallas_call(kernel, out_shape=[jax.ShapeDtypeStruct((left.shape[0], ri...  18.5 us
  transfers between devices with their start and end apart: 8, of which 6 were waited for; matrix products, arithmetic and copies ran while one was open for 1% of the time, Pallas kernels for 0%

profile of v8, /device:TPU:0, one launch (start us, length us, event | category | flops | bytes accessed | tf_op | source)
XLA Modules:
  0.0 598.1 jit_solution(9916487417885493724)
XLA Ops:
  0.7 0.7 pad_bitcast_fusion
  1.3 0.1 pad.3.clone
  1.4 0.7 broadcast_in_dim.42
  2.0 0.7 add_rsqrt_fusion
  2.7 0.1 pad.7.clone
  2.8 1.3 add_add_fusion.refs_7_
  4.1 1.4 maximum_maximum_fusion.refs_6_
  5.5 93.3 %shard_map.222 = (bf16[1024,3072]{1,0:T(8,128)(2,1)}, bf16[1024,1024]{1,0:T(8,128)(2,1)}, bf16[1024,4096]{1,0:T(8,128)(2,1)}, bf16[4096,1024]{1,0:T(8,128)(2,1)}...) custom-call(bf16[256,3072]{1,0:T(8,128)(2,1)} %bitcast.48, ...), custom_call_target="tpu_custom_call" | custom-call | tf_op jit(solution)/shard_map/pallas_call | solution.py:712
  98.9 1.4 fusion.5
  100.3 2.9 conditional.3
  100.3 2.9 fusion.2
  103.2 10.4 %shard_map.223 = (bf16[4,256,256]{2,1,0:T(8,128)(2,1)}, s32[4,32,128]{2,1,0:T(8,128)}) custom-call(bf16[4,256,256]{2,1,0:T(8,128)(2,1)S(1)} %get-tuple-element.221.rows_ref, s32[32,128]{1,0:T(8,128)S(1)} %get-tuple-element.130.ids_ref), custom_call_target="tpu_custom_call" | custom-call | tf_op jit(solution)/shard_map/pallas_call | solution.py:768
  113.7 3.4 conditional.4
  113.7 1.1 convert_reduce_fusion
  114.9 0.8 multiply_convert_fusion
  115.7 1.4 fusion.6
  117.1 18.7 %shard_map.224 = (f32[256,1024]{1,0:T(8,128)}, bf16[1024,256]{1,0:T(8,128)(2,1)}, bf16[256,3072]{1,0:T(8,128)(2,1)}, f32[16,1,256]{2,1,0:T(1,128)}, bf16[1024,25...) custom-call(f32[256,1024]{1,0:T(8,128)S(1)} %get-tuple-element.133.r, ...), custom_call_target="tpu_custom_call" | custom-call | tf_op jit(solution)/shard_map/pallas_call | solution.py:969
  135.9 41.0 %collective-permute-start = (bf16[256,1024]{1,0:T(8,128)(2,1)}, bf16[256,1024]{1,0:T(8,128)(2,1)S(1)}, u32[]{:S(2)}, u32[]{:S(2)}) collective-permute-start(bf16[256,1024]{1,0:T(8,128)(2,1)} %get-tuple-element.140), channel_id=1, source_target_pairs={{0,16},{1,17},{2,18},{3,19},{4,20},{5,21},{6,22},{7,23},{8,24},{9,... | collective-permute-start | bytes 1572872 | tf_op jit(solution)/shard_map/ppermute | solution.py:28
  176.9 0.6 slice.43
  177.5 0.1 lt.25
  177.6 1.0 collective-permute-done.refs_0_
  178.6 0.8 copy-done.17
  179.4 2.8 shard_map.225
  182.1 1.3 collective-permute-start.1
  183.4 0.7 fusion.4
  184.1 17.2 %collective-permute-done.1.proj = bf16[256,256]{1,0:T(8,128)(2,1)S(1)} collective-permute-done((bf16[256,256]{1,0:T(8,128)(2,1)}, bf16[256,256]{1,0:T(8,128)(2,1)S(1)}, u32[]{:S(2)}, u32[]{:S(2)}) %collective-permute-start.1) | collective-permute-done | bytes 131104 | tf_op jit(solution)/shard_map/ppermute | solution.py:28
  201.3 0.7 copy-done.19
  201.9 50.6 %shard_map.226 = (bf16[256,256]{1,0:T(8,128)(2,1)}, f32[1,256]{1,0:T(1,128)}, bf16[4096,256]{1,0:T(8,128)(2,1)}) custom-call(bf16[256,256]{1,0:T(8,128)(2,1)} %copy-done.19, s32[1,1024]{1,0:T(1,128)} %bitcast.67, f32[1,1024]{1,0:T(1,128)} %bitcast.68, bf16[4096,256]{1,0:T(8,128)(2,1)S(1)} %copy-done.15), custom_call_target="tpu_custom_call" | custom-call | tf_op jit(solution)/shard_map/pallas_call | solution.py:1292
  252.6 1.3 collective-permute-start.2
  253.9 1.2 collective-permute-done.2.refs_0_
  255.0 18.5 %shard_map.228.refs_8_ = bf16[1024,256]{1,0:T(8,128)(2,1)} custom-call(bf16[4096,256]{1,0:T(8,128)(2,1)} %get-tuple-element.166.refs_0_), custom_call_target="tpu_custom_call" | custom-call | tf_op jit(solution)/shard_map/pallas_call | solution.py:1839
  273.5 1.8 shard_map.227
  275.3 1.3 collective-permute-start.3
  276.6 1.4 slice.45
  278.1 8.1 %collective-permute-done.3.refs_0_ = bf16[256,1024]{1,0:T(8,128)(2,1)S(1)} collective-permute-done((bf16[256,1024]{1,0:T(8,128)(2,1)S(1)}, bf16[256,1024]{1,0:T(8,128)(2,1)S(1)}, u32[]{:S(2)}, u32[]{:S(2)}) %collective-permute-start.3) | collective-permute-done | bytes 524320 | tf_op jit(solution)/shard_map/ppermute | solution.py:28
  286.1 0.8 copy-done.16
  287.0 25.6 %shard_map.229 = (bf16[256,1024]{1,0:T(8,128)(2,1)}, bf16[256,4096]{1,0:T(8,128)(2,1)}, bf16[256,1024]{1,0:T(8,128)(2,1)}, bf16[256,3072]{1,0:T(8,128)(2,1)}, bf...) custom-call(bf16[256,1024]{1,0:T(8,128)(2,1)} %copy-done.16, ...), custom_call_target="tpu_custom_call", output_to_operand_aliasing={{0}: (16, {}), {1}: (17, {}), {2}: (18, {}), {3}: (19, {}),... | custom-call | tf_op jit(solution)/shard_map/pallas_call | solution.py:1145
  312.6 3.6 conditional.5
  312.6 1.5 fusion.3
  314.2 2.0 convolution_convert_fusion.1
  316.2 1.6 copy-done.1
  317.8 1.4 copy-done.2
  319.2 1.0 copy-done.5
  320.3 1.0 copy-done.6
  321.3 1.0 copy-done.7
  322.3 18.5 %shard_map.230 = (bf16[1024,4096]{1,0:T(8,128)(2,1)}, bf16[4096,1024]{1,0:T(8,128)(2,1)}, bf16[1024,1024]{1,0:T(8,128)(2,1)S(1)}, bf16[1024,3072]{1,0:T(8,128)(2,1)}) custom-call(bf16[1024,256]{1,0:T(8,128)(2,1)S(1)} %copy-done.7, bf16[4096,256]{1,0:T(8,128)(2,1)S(1)} %copy-done.1, bf16[1024,256]{1,0:T(8,128)(2,1)S(1)} %copy-done.6, ...), custom_call_target="tpu_custom_call" | custom-call | tf_op jit(solution)/shard_map/pallas_call | solution.py:1368
  340.9 1.3 copy-done.11
  342.2 233.8 %shard_map.231 = (bf16[256,4096]{1,0:T(8,128)(2,1)}, bf16[1024,1024]{1,0:T(8,128)(2,1)}, bf16[64,1024]{1,0:T(8,128)(2,1)}, bf16[256,1024]{1,0:T(8,128)(2,1)}, bf...) custom-call(bf16[1024,4096]{1,0:T(8,128)(2,1)} %get-tuple-element.177.refs_0_, ...), custom_call_target="tpu_custom_call" | custom-call | tf_op jit(solution)/shard_map/pallas_call | solution.py:1839
  576.0 0.1 collective-permute-start.5
  576.1 0.5 collective-permute-start.4
  576.7 0.1 collective-permute-start.7
  576.8 0.4 collective-permute-start.6
  577.2 2.7 collective-permute-done.4
  579.9 0.5 broadcast_select_fusion.1
  580.4 0.1 collective-permute-done.7
  580.5 1.4 broadcast_select_fusion
  581.9 1.6 select_convert_fusion
  583.5 0.8 reshape.106
  584.3 1.6 copy-done.8
  585.9 1.6 copy-done.9
  587.5 1.6 copy-done.10
  589.1 1.4 copy-done.12
  590.5 1.0 copy-done.13
  591.5 6.4 %shard_map.232 = (f32[256,4096]{1,0:T(8,128)}, f32[1024,1024]{1,0:T(8,128)}, f32[256,1024]{1,0:T(8,128)}, f32[256,3072]{1,0:T(8,128)}, f32[4096,256]{1,0:T(8,128)}) custom-call(bf16[256,4096]{1,0:T(8,128)(2,1)S(1)} %copy-done.8, bf16[1024,1024]{1,0:T(8,128)(2,1)S(1)} %copy-done.9, bf16[256,1024]{1,0:T(8,128)(2,1)S(1)} %copy-done.13, ...), custom_call_target="tpu_custom_call" | custom-call | tf_op jit(solution)/shard_map/pallas_call | solution.py:1404
  (39 shorter events, 0.2 us)
Async XLA Ops:
  5.5 94.8 %copy-start.15 = (bf16[4096,256]{1,0:T(8,128)(2,1)S(1)}, bf16[4096,256]{1,0:T(8,128)(2,1)}, u32[]{:S(2)}) copy-start(bf16[4096,256]{1,0:T(8,128)(2,1)} %table.1) | copy-start | bytes 6291460
  100.3 13.4 %copy-start.20 = (bf16[256,256]{1,0:T(8,128)(2,1)S(1)}, bf16[256,256]{1,0:T(8,128)(2,1)}, u32[]{:S(2)}) copy-start(bf16[256,256]{1,0:T(8,128)(2,1)} %param.23) | copy-start | bytes 393220
  135.9 42.7 %collective-permute-start = (bf16[256,1024]{1,0:T(8,128)(2,1)}, bf16[256,1024]{1,0:T(8,128)(2,1)S(1)}, u32[]{:S(2)}, u32[]{:S(2)}) collective-permute-start(bf16[256,1024]{1,0:T(8,128)(2,1)} %get-tuple-element.140), channel_id=1, source_target_pairs={{0,16},{1,17},{2,18},{3,19},{4,20},{5,21},{6,22},{7,23},{8,24},{9,... | collective-permute-start | bytes 1572872 | tf_op jit(solution)/shard_map/ppermute | solution.py:28
  178.6 0.8 copy-start.17
  182.1 19.2 %collective-permute-start.1 = (bf16[256,256]{1,0:T(8,128)(2,1)}, bf16[256,256]{1,0:T(8,128)(2,1)S(1)}, u32[]{:S(2)}, u32[]{:S(2)}) collective-permute-start(bf16[256,256]{1,0:T(8,128)(2,1)} %get-tuple-element.151), channel_id=1, source_target_pairs={{16,0},{17,1},{18,2},{19,3},{20,4},{21,5},{22,6},{23,7},{24,8},{25... | collective-permute-start | bytes 393224 | tf_op jit(solution)/shard_map/ppermute | solution.py:28
  201.3 0.7 copy-start.19
  252.6 2.5 collective-permute-start.2
  275.3 10.8 %collective-permute-start.3 = (bf16[256,1024]{1,0:T(8,128)(2,1)S(1)}, bf16[256,1024]{1,0:T(8,128)(2,1)S(1)}, u32[]{:S(2)}, u32[]{:S(2)}) collective-permute-start(bf16[256,1024]{1,0:T(8,128)(2,1)S(1)} %get-tuple-element.167.refs_20_), channel_id=1, source_target_pairs={{16,0},{17,1},{18,2},{19,3},{20,4},{21,5},{22,6},{23,7},{24,8},{25... | collective-permute-start | bytes 1572872 | tf_op jit(solution)/shard_map/ppermute | solution.py:28
  286.1 0.8 copy-start.16
  287.0 25.6 %copy-start.18 = (bf16[256,1024]{1,0:T(8,128)(2,1)S(1)}, bf16[256,1024]{1,0:T(8,128)(2,1)}, u32[]{:S(2)}) copy-start(bf16[256,1024]{1,0:T(8,128)(2,1)} %get-tuple-element.179) | copy-start | bytes 1572868
  312.6 3.6 copy-start
  312.6 3.6 copy-start.3
  312.6 3.6 copy-start.4
  316.2 1.6 copy-start.1
  317.8 1.4 copy-start.2
  319.2 1.0 copy-start.5
  320.3 1.0 copy-start.6
  321.3 1.0 copy-start.7
  322.3 19.9 %copy-start.14 = (bf16[256,1024]{1,0:T(8,128)(2,1)S(1)}, bf16[256,1024]{1,0:T(8,128)(2,1)}, u32[]{:S(2)}) copy-start(bf16[256,1024]{1,0:T(8,128)(2,1)} %get-tuple-element.182.refs_2_) | copy-start | bytes 1572868
  340.9 1.3 copy-start.11
  342.2 233.9 %copy-start.21 = (f32[1,256]{1,0:T(1,128)S(1)}, f32[1,256]{1,0:T(1,128)}, u32[]{:S(2)}) copy-start(f32[1,256]{1,0:T(1,128)} %get-tuple-element.189) | copy-start | bytes 3076
  576.0 8.3 %collective-permute-start.5 = (bf16[4096,256]{1,0:T(8,128)(2,1)}, bf16[4096,256]{1,0:T(8,128)(2,1)S(1)}, u32[]{:S(2)}, u32[]{:S(2)}) collective-permute-start(bf16[4096,256]{1,0:T(8,128)(2,1)} %get-tuple-element.194.refs_4_), channel_id=1, source_target_pairs={{0,16},{16,0},{1,17},{17,1},{2,18},{18,2},{3,19},{19,3},{4,20},{20... | collective-permute-start | bytes 6291464 | tf_op jit(solution)/shard_map/ppermute | solution.py:2023
  576.1 3.7 collective-permute-start.4
  576.7 3.8 collective-permute-start.7
  576.8 5.1 collective-permute-start.6
  584.3 1.6 copy-start.8
  585.9 1.6 copy-start.9
  587.5 1.6 copy-start.10
  589.1 1.4 copy-start.12
  590.5 1.0 copy-start.13

commit v9 on v7

--- a/solution.py
+++ b/solution.py
@@ -834,9 +834,11 @@
 
 
 def forward_kernel(only, tile, given, *refs):
-    x, gain_attn, gain_mlp, counts, wq, wp, wu, wd = refs[:8]
-    rest = refs[8 + given :]
+    x, gain_attn, gain_mlp, counts, gain_final, wo, wq, wp, wu, wd = refs[:10]
+    rest = refs[10 + given :]
     outs = rest[:KEPT_COUNT]
+    last = rest[KEPT_COUNT : KEPT_COUNT + 1 + only]
+    rest = rest[1 + only :]
     qv, pv, uv, dv = rest[KEPT_COUNT : KEPT_COUNT + 4]
     kept = rest[KEPT_COUNT + 4 : 2 * KEPT_COUNT + 4]
     a, att, m, acc, wsem, osem = rest[2 * KEPT_COUNT + 4 :]
@@ -917,6 +919,13 @@
         store(6).start()
         out[...] = acc[...]
         store(9).start()
+        if only == 0:
+            last[0][...] = acc[...].astype(jnp.bfloat16)
+        else:
+            for lo in range(0, rows, STRIP):
+                here = pl.ds(lo, STRIP)
+                last[0][here, :] = (unit_rows(acc[here, :])[0] * gain_final[...]).astype(jnp.bfloat16)
+            last[1][...] = dot_nn(last[0][...], wo[...]).astype(jnp.bfloat16)
         for idx in range(KEPT_COUNT):
             store(idx).wait()
 
@@ -945,7 +954,7 @@
     ]
 
 
-def run_forward(only, x, gain_attn, gain_mlp, counts, weights, kept):
+def run_forward(only, x, gain_attn, gain_mlp, counts, gain_final, out_weight, weights, kept):
     wq, wp, wu, wd = weights
     rows, width = x.shape
     units = wd.shape[0]
@@ -953,13 +962,16 @@
     shapes = kept_shapes(rows, width, units)
     low = jnp.bfloat16
     given = 0 if kept is None else KEPT_COUNT
-    in_specs = [IN_VMEM] * 3 + [IN_SMEM] + [ANYWHERE] * (4 + given)
+    in_specs = [IN_VMEM] * 3 + [IN_SMEM] + [IN_VMEM] * 2 + [ANYWHERE] * (4 + given)
+    extra = [jax.ShapeDtypeStruct((rows, width), low)]
+    if only == 1:
+        extra.append(jax.ShapeDtypeStruct((rows, out_weight.shape[1]), low))
     return pl.pallas_call(
         functools.partial(forward_kernel, only, tile, given),
-        out_shape=shapes,
+        out_shape=shapes + extra,
         in_specs=in_specs,
-        out_specs=[ANYWHERE] * KEPT_COUNT,
-        input_output_aliases={8 + idx: idx for idx in range(given)},
+        out_specs=[ANYWHERE] * KEPT_COUNT + [IN_VMEM] * len(extra),
+        input_output_aliases={10 + idx: idx for idx in range(given)},
         scratch_shapes=[pltpu.VMEM(w.shape, w.dtype) for w in weights]
         + [pltpu.VMEM(s.shape, s.dtype) for s in shapes]
         + [
@@ -971,7 +983,7 @@
             pltpu.SemaphoreType.DMA((KEPT_COUNT,)),
         ],
         compiler_params=pltpu.CompilerParams(vmem_limit_bytes=56 << 20),
-    )(x, gain_attn, gain_mlp, counts, wq, wp, wu, wd, *(kept or ()))
+    )(x, gain_attn, gain_mlp, counts, gain_final, out_weight, wq, wp, wu, wd, *(kept or ()))
 
 
 GRAD_COUNT = 6
@@ -1001,12 +1013,14 @@
 
 
 def backward_kernel(only, tile, given, *refs):
-    grad, gain_attn, gain_mlp, counts, x_in, qkv_in, lse_in, mid_in, pre_in, wq, wp, wu, wd = refs[:13]
-    rest = refs[13 + given :]
+    grad_in, gain_attn, gain_mlp, counts, gain_final, wo, out_in = refs[:7]
+    x_in, qkv_in, lse_in, mid_in, pre_in, wq, wp, wu, wd = refs[7:16]
+    rest = refs[16 + given :]
     outs = rest[:GRAD_COUNT]
     qv, pv, uv, dv = rest[GRAD_COUNT : GRAD_COUNT + 4]
     made = rest[GRAD_COUNT + 4 : 2 * GRAD_COUNT + 4]
-    x, qkv, lse, mid, pre, gm, gmid, gatt, wsem, ksem, osem = rest[2 * GRAD_COUNT + 4 :]
+    x, qkv, lse, mid, pre, gm, gmid, gatt, gtop, wsem, ksem, osem = rest[2 * GRAD_COUNT + 4 :]
+    grad = gtop if only == 1 else grad_in
     gy, gpre, gz, gqkv, gx, gains = made
     rows, width = gm.shape
     units = dv.shape[0]
@@ -1028,18 +1042,30 @@
                 ((pre_in, pre), (mid_in, mid), (qkv_in, qkv), (lse_in, lse), (x_in, x))
             )
         ]
+        if only == 1:
+            kept.append(pltpu.make_async_copy(out_in, gtop, ksem.at[5]))
+            kept[5].start()
         kept[0].start()
         for lo in range(0, units, tile):
             load(wd.at[pl.ds(lo, tile)], dv.at[pl.ds(lo, tile)])
             load(wu.at[:, pl.ds(lo, tile)], uv.at[:, pl.ds(lo, tile)])
-        for copy in kept[1:]:
+        for copy in kept[1:5]:
             copy.start()
         load(wp, pv)
         load(wq, qv)
         loads = iter(loads)
+        gains[...] = jnp.zeros_like(gains)
+        if only == 1:
+            for copy in kept[5:]:
+                copy.wait()
+            gmid[...] = dot_nt(grad_in[...], wo[...])
+            for lo in range(0, rows, STRIP):
+                here = pl.ds(lo, STRIP)
+                step, gain = norm_pull(gtop[here, :], gain_final[...], gmid[here, :])
+                gtop[here, :] = step
+                gains[2:3, :] += gain
         gy[...] = grad[...].astype(jnp.bfloat16)
         store(0).start()
-        gains[...] = jnp.zeros_like(gains)
         kept[0].wait()
         gm[...] = jnp.zeros_like(gm)
         for lo in range(0, units, tile):
@@ -1106,22 +1132,22 @@
     pl.when(lax.axis_index("section") == only)(run)
 
 
-def run_backward(only, grad, gain_attn, gain_mlp, counts, kept, weights, made):
+def run_backward(only, grad, gain_attn, gain_mlp, counts, gain_final, out_weight, kept, weights, made):
     wq, wp, wu, wd = weights
-    x, _, qkv, lse, _, mid, _, pre, _, _ = kept
+    x, _, qkv, lse, _, mid, _, pre, _, out = kept
     rows, width = x.shape
     units = wd.shape[0]
     tile = 512
     shapes = grad_shapes(rows, width, units)
     low, f32 = jnp.bfloat16, jnp.float32
     given = 0 if made is None else GRAD_COUNT
-    in_specs = [IN_VMEM] * 3 + [IN_SMEM] + [ANYWHERE] * (9 + given)
+    in_specs = [IN_VMEM] * 3 + [IN_SMEM] + [IN_VMEM] * 2 + [ANYWHERE] * (10 + given)
     return pl.pallas_call(
         functools.partial(backward_kernel, only, tile, given),
         out_shape=shapes,
         in_specs=in_specs,
         out_specs=[ANYWHERE] * GRAD_COUNT,
-        input_output_aliases={13 + idx: idx for idx in range(given)},
+        input_output_aliases={16 + idx: idx for idx in range(given)},
         scratch_shapes=[pltpu.VMEM(w.shape, w.dtype) for w in weights]
         + [pltpu.VMEM(s.shape, s.dtype) for s in shapes]
         + [pltpu.VMEM(s.shape, s.dtype) for s in (x, qkv, lse, mid, pre)]
@@ -1129,15 +1155,18 @@
             pltpu.VMEM((rows, width), f32),
             pltpu.VMEM((rows, width), f32),
             pltpu.VMEM((rows, width), low),
+            pltpu.VMEM((rows, width), f32),
             pltpu.SemaphoreType.DMA((2 + 2 * units // tile,)),
-            pltpu.SemaphoreType.DMA((5,)),
+            pltpu.SemaphoreType.DMA((6,)),
             pltpu.SemaphoreType.DMA((GRAD_COUNT,)),
         ],
         compiler_params=pltpu.CompilerParams(vmem_limit_bytes=56 << 20),
-    )(grad, gain_attn, gain_mlp, counts, x, qkv, lse, mid, pre, wq, wp, wu, wd, *(made or ()))
-
-
-def vocabulary_kernel(only, tile, proj, ids, scale, table, gproj_out, loss_out, gtable, *scratch):
+    )(
+        grad, gain_attn, gain_mlp, counts, gain_final, out_weight, out, x, qkv, lse, mid, pre, wq, wp, wu, wd, *(made or ())
+    )
+
+
+def vocabulary_kernel(tile, proj, ids, scale, table, gproj_out, loss_out, gtable, *scratch):
     tv, gt, pall, gp, gsend, gin, stat, stats, whole, tsem, gsem, psem, prem, ssem, srem, qsem, qrem = scratch
     rows = proj.shape[0]
     vocab = tv.shape[0]
@@ -1145,25 +1174,43 @@
     sec = lax.axis_index("section")
     grp = lax.axis_index("group")
     pos = lax.axis_index("dp")
-    peers = [(sec, grp, lax.rem(pos + k, 4)) for k in (1, 2, 3)]
-    places = [lax.rem(pos + k, 4) for k in (1, 2, 3)]
-
-    def run():
+    places = [lax.rem(pos + k, 4) for k in range(4)]
+    peers = [(sec, grp, place) for place in places[1:]]
+    across = [(1 - sec, grp, place) for place in places]
+    barrier = pltpu.get_barrier_semaphore()
+
+    def hand(k):
+        return remote(proj, pall.at[pos], psem.at[k], prem.at[k], across[k])
+
+    def back(k):
+        return remote(gsend.at[places[k]], gin.at[k], qsem.at[k], qrem.at[k], across[k])
+
+    def greet(devices):
+        for device in devices:
+            pl.semaphore_signal(barrier, inc=1, device_id=device, device_id_type=MESH)
+
+    def give():
+        greet(across)
+        pl.semaphore_wait(barrier, 4)
+        for k in (2, 1, 3, 0):
+            hand(k).start()
+        for k in range(4):
+            back(k).wait_recv()
+        summed = gin[0].astype(jnp.float32)
+        for k in (1, 2, 3):
+            summed = summed + gin[k].astype(jnp.float32)
+        gproj_out[...] = summed.astype(jnp.bfloat16)
+        for k in range(4):
+            hand(k).wait_send()
+
+    def score():
         load = pltpu.make_async_copy(table, tv, tsem)
         load.start()
-        barrier = pltpu.get_barrier_semaphore()
-        for device in peers:
-            pl.semaphore_signal(barrier, inc=1, device_id=device, device_id_type=MESH)
-        pall[pos] = proj[...]
-        pl.semaphore_wait(barrier, 3)
-        first = [
-            remote(pall.at[pos], pall.at[pos], psem.at[k], prem.at[k], peers[k]) for k in range(3)
-        ]
-        for copy in first:
-            copy.start()
+        greet(across + peers)
+        pl.semaphore_wait(barrier, 7)
         load.wait()
-        for copy in first:
-            copy.wait()
+        for k in range(4):
+            hand(k).wait_recv()
         line_rows = pall[...].reshape(4 * rows, pall.shape[2])
 
         def logits_of(at):
@@ -1194,6 +1241,7 @@
         for copy in second:
             copy.start()
         stats[pos] = stat[...]
+        gp[...] = jnp.zeros_like(gp)
         for copy in second:
             copy.wait()
         top = stats[0, 0:1, :]
@@ -1207,7 +1255,6 @@
         log_total = top + jnp.log(total)
         whole[...] = jnp.where(scale[...] > 0, log_total - picked, 0.0)
         loss_out[...] = whole[:, pl.ds(pl.multiple_of(pos * rows, 128), rows)]
-        gp[...] = jnp.zeros_like(gp)
 
         def pull(at, carry):
             here = rows_at(at * tile, tile)
@@ -1218,33 +1265,24 @@
             return carry
 
         lax.fori_loop(0, count, pull, 0)
+        gsend[...] = gp[...].astype(jnp.bfloat16).reshape(gsend.shape)
+        for k in (2, 1, 3, 0):
+            back(k).start()
         keep = pltpu.make_async_copy(gt, gtable, gsem)
         keep.start()
-        gsend[...] = gp[...].astype(jnp.bfloat16).reshape(gsend.shape)
-        third = [
-            remote(gsend.at[places[k]], gin.at[k], qsem.at[k], qrem.at[k], peers[k])
-            for k in range(3)
-        ]
-        for copy in third:
-            copy.start()
-        summed = gp[rows_at(pos * rows, rows), :]
-        for k in range(3):
-            third[k].wait_recv()
-            summed = summed + gin[k].astype(jnp.float32)
-        gproj_out[...] = summed.astype(jnp.bfloat16)
-        for copy in third:
-            copy.wait_send()
+        for k in range(4):
+            back(k).wait_send()
         keep.wait()
 
-    pl.when(sec == only)(run)
-
-
-def run_vocabulary(only, proj, ids, scale, table, collective_id):
+    pl.when(sec == 0)(score)
+    pl.when(sec == 1)(give)
+
+
+def run_vocabulary(proj, ids, scale, table, collective_id):
     rows, emb = proj.shape
-    vocab = table.shape[0]
     low, f32, dma = jnp.bfloat16, jnp.float32, pltpu.SemaphoreType.DMA
     return pl.pallas_call(
-        functools.partial(vocabulary_kernel, only, 512),
+        functools.partial(vocabulary_kernel, 1024),
         out_shape=[
             jax.ShapeDtypeStruct((rows, emb), low),
             jax.ShapeDtypeStruct((1, rows), f32),
@@ -1258,18 +1296,46 @@
             pltpu.VMEM((4, rows, emb), low),
             pltpu.VMEM((4 * rows, emb), f32),
             pltpu.VMEM((4, rows, emb), low),
-            pltpu.VMEM((3, rows, emb), low),
+            pltpu.VMEM((4, rows, emb), low),
             pltpu.VMEM((8, 4 * rows), f32),
             pltpu.VMEM((4, 8, 4 * rows), f32),
             pltpu.VMEM((1, 4 * rows), f32),
             dma,
             dma,
-        ]
-        + [dma((3,))] * 6,
+            dma((4,)),
+            dma((4,)),
+            dma((3,)),
+            dma((3,)),
+            dma((4,)),
+            dma((4,)),
+        ],
         compiler_params=pltpu.CompilerParams(
             collective_id=collective_id, has_side_effects=True, vmem_limit_bytes=60 << 20
         ),
     )(proj, ids, scale, table)
+
+
+def widen_kernel(count, *refs):
+    for src, dst in zip(refs[:count], refs[count:]):
+        dst[...] = src[...].astype(jnp.float32)
+
+
+def widen(arrays):
+    steps = 8
+
+    def spec(x):
+        return pl.BlockSpec((x.shape[0] // steps, x.shape[1]), lambda at: (at, 0))
+
+    size = sum(x.size for x in arrays)
+    return pl.pallas_call(
+        functools.partial(widen_kernel, len(arrays)),
+        grid=(steps,),
+        out_shape=[jax.ShapeDtypeStruct(x.shape, jnp.float32) for x in arrays],
+        in_specs=[spec(x) for x in arrays],
+        out_specs=[spec(x) for x in arrays],
+        cost_estimate=pl.CostEstimate(flops=size, bytes_accessed=6 * size, transcendentals=0),
+        compiler_params=pltpu.CompilerParams(vmem_limit_bytes=60 << 20),
+    )(*arrays)
 
 
 def strip_of(rows, columns):
@@ -1293,8 +1359,8 @@
     lax.fori_loop(0, rows // strip, body, 0)
 
 
-def reduce_kernel(plan, spots, only, extras, pace, refs_of, *refs):
-    body = functools.partial(reduce_body, plan, spots, extras, pace, refs_of(refs))
+def reduce_kernel(plan, only, extras, pace, refs_of, *refs):
+    body = functools.partial(reduce_body, plan, extras, pace, refs_of(refs))
     if only is None:
         body()
     else:
@@ -1310,7 +1376,7 @@
     return kept
 
 
-def reduce_body(plan, spots, extras, pace, named):
+def reduce_body(plan, extras, pace, named):
     arrays, outs = named["arrays"], named["outs"]
     own, got1, got2, got3, got4, land = (
         named[k] for k in ("own", "got1", "got2", "got3", "got4", "land")
@@ -1409,31 +1475,11 @@
             if (r >> bit) & 1:
                 swap(p, stage + 1, kept[p][stage + 1].index(r ^ (1 << bit))).start()
 
-    pending = {}
-
-    def write_out(p, who, term):
-        rings = named["rings"][spots[p]]
-        turn = pending.setdefault(spots[p], [])
-        slot = len(turn) % 2
-        if len(turn) >= 2:
-            turn[-2].wait()
-        ring = rings.at[slot]
-
-        def store(here, total):
-            rings[slot, here, :] = total
-
-        add_rows(store, term, sub_of(p), columns_of(p))
+    def write_out(p, who, at):
         start = who * (rows_of(p) // 4) + plan[p][2] * sub_of(p)
-        copy = pltpu.make_async_copy(
-            ring, outs[plan[p][0]].at[rows_at(start, sub_of(p))], named["ring_sem"].at[spots[p], slot]
+        return pltpu.make_async_copy(
+            land[p].at[who], outs[plan[p][0]].at[rows_at(start, sub_of(p))], named["out_sem"].at[p, at]
         )
-        copy.start()
-        turn.append(copy)
-
-    def drain():
-        for turn in pending.values():
-            for copy in turn[-2:]:
-                copy.wait()
 
     def spread(p, way):
         if way < 2:
@@ -1473,14 +1519,14 @@
 
     def write_near(p):
         if spreads:
-            for who in (grp, grp ^ 1, grp ^ 2):
-                write_out(p, who, [lambda here, who=who: land[p][who, here, :]])
+            for at, who in enumerate((grp, grp ^ 1, grp ^ 2)):
+                write_out(p, who, at).start()
 
     def write_far(p):
         if spreads:
             spread(p, 2).wait_recv()
             spread(p, 3).wait_recv()
-            write_out(p, grp ^ 3, [lambda here: land[p][grp ^ 3, here, :]])
+            write_out(p, grp ^ 3, 3).start()
 
     if with_gains:
         gain_in, gain_got, sg, rg, gain_sem = named["gain_scratch"]
@@ -1619,9 +1665,10 @@
             total = total + gain_got[j]
         named["gain_out"][...] = total
     on_first(look_end)
-    drain()
     for p in range(count):
         if spreads:
+            for at, who in enumerate((grp, grp ^ 1, grp ^ 2, grp ^ 3)):
+                write_out(p, who, at).wait()
             for way in range(4):
                 spread(p, way).wait_send()
         else:
@@ -1639,16 +1686,13 @@
     extras = ("spread",) * spread + ("gains",) * (gains is not None) + ("looked",) * (look is not None)
     count = len(plan)
     inputs = list(arrays)
-    kind = f32 if spread else low
     lines = 4 if len(plan[0][1]) == 4 else 1
     share = lines if spread else 4 * lines
-    outs = [jax.ShapeDtypeStruct((x.shape[0] // share, x.shape[1]), kind) for x in arrays]
+    outs = [jax.ShapeDtypeStruct((x.shape[0] // share, x.shape[1]), low) for x in arrays]
     out_specs = [ANYWHERE] * len(arrays)
     in_specs = [ANYWHERE] * len(arrays)
     names = ["own", "got1", "got2", "got3", "got4", "land"]
     scratch = {name: [] for name in names}
-    ring_shapes = []
-    spots = []
     for src, _, _, chunks in plan:
         rows, columns = arrays[src].shape[0] // lines, arrays[src].shape[1]
         sub = rows // 4 // chunks
@@ -1656,14 +1700,11 @@
         for name, blocks in zip(names, held + (4 if spread else 1,)):
             shape = (blocks, sub, columns) if blocks else (8, 128)
             scratch[name].append(pltpu.VMEM(shape, low))
-        if (sub, columns) not in ring_shapes:
-            ring_shapes.append((sub, columns))
-        spots.append(ring_shapes.index((sub, columns)))
     flat = [item for name in names for item in scratch[name]]
     sems = [dma((count, 4, 8))] * 2 + [dma((count, 8))] + [dma((count, 4))] * 2 + [dma((count,))]
     tail = []
     if spread:
-        tail += [pltpu.VMEM((2,) + shape, f32) for shape in ring_shapes] + [dma((len(ring_shapes), 2))]
+        tail += [dma((count, 4))]
     if gains is not None:
         inputs.append(gains)
         in_specs.append(ANYWHERE)
@@ -1715,8 +1756,7 @@
             named[name] = take(count)
         named["sems"] = take(6)
         if spread:
-            named["rings"] = take(len(ring_shapes))
-            named["ring_sem"] = take(1)[0]
+            named["out_sem"] = take(1)[0]
         if gains is not None:
             named["gain_scratch"] = take(5)
         if look is not None:
@@ -1724,7 +1764,7 @@
         return named
 
     return pl.pallas_call(
-        functools.partial(reduce_kernel, plan, tuple(spots), only, extras, pace, refs_of),
+        functools.partial(reduce_kernel, plan, only, extras, pace, refs_of),
         out_shape=outs,
         in_specs=in_specs,
         out_specs=out_specs,
@@ -1733,7 +1773,6 @@
             collective_id=collective_id, has_side_effects=True, vmem_limit_bytes=60 << 20
         ),
     )(*inputs)
-
 
 def nothing_like(run):
     return jax.tree.map(lambda a: jnp.zeros(a.shape, a.dtype), jax.eval_shape(run))
@@ -1821,6 +1860,7 @@
     weights = (qkv_weight, proj_weight, up_weight, down_weight)
     gain_attn = gain_attn[None]
     gain_mlp = gain_mlp[None]
+    final_gain = final_gain[None]
     loss_scale = LOSS_GAIN / math.sqrt(rows * lax.axis_size(("group", "dp")))
 
     def look_up():
@@ -1844,34 +1884,34 @@
         return mixed_in, product(mixed_in, in_weight)
 
     mixed_in, x_first = only_on(first_section, front)
-    kept = run_forward(0, x_first, gain_attn, gain_mlp, lengths, weights, None)
-    out_first = kept[9].astype(jnp.bfloat16)
+    *kept, out_first = run_forward(
+        0, x_first, gain_attn, gain_mlp, lengths, final_gain, out_weight, weights, None
+    )
     x_second = passed_along(out_first, "section", 1)
-    kept = run_forward(1, x_second, gain_attn, gain_mlp, lengths, weights, kept)
-    final_in = normed(kept[9], final_gain).astype(jnp.bfloat16)
-    projected = product(final_in, out_weight).astype(jnp.bfloat16)
-    projected = passed_along(projected, "section", -1)
+    *kept, final_in, projected = run_forward(
+        1, x_second, gain_attn, gain_mlp, lengths, final_gain, out_weight, weights, kept
+    )
     line_parts = line_ids.reshape(4, 8, 128)
     line_tokens = line_parts[:, : rows // 128].reshape(1, -1)
     line_counts = line_parts[:, rows // 128, :seqs].reshape(-1, 1)
     line_valid = jnp.arange(length, dtype=jnp.int32)[None, :] < line_counts
     line_scale = jnp.where(line_valid.reshape(1, -1), loss_scale, 0.0)
-    grad_proj_a, entropy, table_g = run_vocabulary(
-        0, projected, line_tokens, line_scale, embed_table, 2
-    )
-    grad_proj = passed_along(grad_proj_a, "section", 1)
+    grad_proj, entropy, table_g = run_vocabulary(projected, line_tokens, line_scale, embed_table, 2)
     (table_fin,) = reduce_all(
-        (after(table_g, grad_proj),),
+        (table_g,),
         TABLE_PLAN,
         0,
         3,
         TABLE_PACE,
         spread=False,
     )
-    grad_top, gain_final = norm_back(kept[9], final_gain, product_nt(grad_proj, out_weight))
-    made = run_backward(1, grad_top, gain_attn, gain_mlp, lengths, kept, weights, None)
+    made = run_backward(
+        1, grad_proj, gain_attn, gain_mlp, lengths, final_gain, out_weight, kept, weights, None
+    )
     grad_first = passed_along(after(made[4], table_fin), "section", -1)
-    made = run_backward(0, grad_first, gain_attn, gain_mlp, lengths, kept, weights, made)
+    made = run_backward(
+        0, grad_first, gain_attn, gain_mlp, lengths, final_gain, out_weight, kept, weights, made
+    )
     shape = in_weight.shape
 
     def front_edge():
@@ -1884,9 +1924,7 @@
         return edge, jnp.zeros((rows, emb), jnp.bfloat16)
 
     edge_g, looked_grad = lax.cond(first_section, front_edge, back_edge)
-    gain_rows = made[5] + jnp.concatenate(
-        [jnp.zeros((2, width)), gain_final[None], jnp.zeros((5, width))], 0
-    )
+    gain_rows = made[5]
     gain_rows = gain_rows.reshape(8, 4, width // 4).transpose(1, 0, 2)
 
     def grads_of(rows_at_once, grads):
@@ -1917,6 +1955,7 @@
         high = jnp.where(first_section, theirs[at], mine[at])
         return low, high
 
+    up_r, down_r, proj_r, qkv_r = widen((up_r, down_r, proj_r, qkv_r))
     table_out = pair_of(0)[0].astype(jnp.float32)
     in_r, out_r = pair_of(1)
     final_r = pair_of(2)[1][2]
@@ -1924,7 +1963,7 @@
     return (
         token_loss,
         table_out,
-        in_r,
+        in_r.astype(jnp.float32),
         gain_r[0][None],
         qkv_r[None],
         proj_r[None],
@@ -1932,7 +1971,7 @@
         up_r[None],
         down_r[None],
         final_r,
-        out_r.reshape(-1, emb),
+        out_r.astype(jnp.float32).reshape(-1, emb),
     )
 
 

time: 597 us -> 570 us (0.955)
  waiting for transfers between devices: 25.2 us -> 9.69 us
  Pallas kernels: 454 us -> 466 us
  local copies, waits for them, and re-layouts: 18.1 us -> 7.64 us
  other arithmetic: 20.3 us -> 10.9 us
    pallas_call x3 -> x4, Pallas kernels: 294 us -> 313 us  [the longest x2 253 us: reduce_all(): pl.pallas_call(functools.partial(reduce_kernel, plan, only, extras, pace,...]
    ppermute x4 -> x2, waiting for transfers between devices: 22.2 us -> 9.68 us  [passed_along(): return lax.ppermute(x, axis, pairs)]
    unnamed x50 -> x32, local copies, waits for them, and re-layouts: 12.1 us -> 1.67 us
    pallas_call x2, Pallas kernels: 36.8 us -> 27.4 us  [run_backward(): pl.pallas_call(functools.partial(backward_kernel, only, tile, given), out...]
    ppermute x4 -> x2, starting transfers between devices: 45 us -> 42.3 us  [passed_along(): return lax.ppermute(x, axis, pairs)]
    dot_general x7 -> x6, matrix products: 22.2 us -> 22 us  [product(): return jnp.dot(left_side, right_side, preferred_element_type=jnp.float32)]
  transfers between devices with their start and end apart: 8 -> 6, of which waited for: 5 -> 2; matrix products, arithmetic and copies ran while one was open for 1% -> 1% of each run, Pallas kernels for 0% -> 2%
where the time goes in v9:
time: 570 us; the launch traced here: 562 us
  Pallas kernels  466 us (82%)
  starting transfers between devices  43.5 us (8%)
  matrix products  23.6 us (4%)
  other arithmetic  10.9 us (2%)
  waiting for transfers between devices  9.69 us (2%)
  local copies, waits for them, and re-layouts  7.64 us (1%)
    pallas_call x2, Pallas kernels, reduce_all(): pl.pallas_call(functools.partial(reduce_kernel, plan, only, extras, pace,...  253 us
    pallas_call x1, Pallas kernels, gather_all(): pl.pallas_call(functools.partial(gather_kernel, count, first_order, last_...  93.3 us
    pallas_call x1, Pallas kernels, run_vocabulary(): pl.pallas_call(functools.partial(vocabulary_kernel, 1024), out_shape=[jax...  52 us
    ppermute x2, starting transfers between devices, passed_along(): return lax.ppermute(x, axis, pairs)  42.3 us
    pallas_call x2, Pallas kernels, run_backward(): pl.pallas_call(functools.partial(backward_kernel, only, tile, given), out...  27.4 us
    dot_general x6, matrix products, product(): return jnp.dot(left_side, right_side, preferred_element_type=jnp.float32)  22 us
    pallas_call x2, Pallas kernels, run_forward(): pl.pallas_call(functools.partial(forward_kernel, only, tile, given), out_...  21.3 us
  transfers between devices with their start and end apart: 6, of which 2 were waited for; matrix products, arithmetic and copies ran while one was open for 1% of the time, Pallas kernels for 2%

profile of v9, /device:TPU:0, one launch (start us, length us, event | category | flops | bytes accessed | tf_op | source)
XLA Modules:
  0.0 562.3 jit_solution(14575219925427596202)
XLA Ops:
  0.7 0.7 pad_bitcast_fusion
  1.3 0.1 pad.3.clone
  1.4 0.7 broadcast_in_dim.42
  2.0 0.7 add_rsqrt_fusion
  2.7 0.1 pad.7.clone
  2.8 1.3 add_add_fusion.refs_7_
  4.1 1.4 maximum_maximum_fusion.refs_6_
  5.5 93.3 %shard_map.222 = (bf16[1024,3072]{1,0:T(8,128)(2,1)}, bf16[1024,1024]{1,0:T(8,128)(2,1)}, bf16[1024,4096]{1,0:T(8,128)(2,1)}, bf16[4096,1024]{1,0:T(8,128)(2,1)}...) custom-call(bf16[256,3072]{1,0:T(8,128)(2,1)} %bitcast.56, ...), custom_call_target="tpu_custom_call" | custom-call | tf_op jit(solution)/shard_map/pallas_call | solution.py:712
  98.9 1.5 fusion.5
  100.3 0.0 copy-done.8
  100.3 2.9 conditional.3
  100.3 2.9 fusion.2
  103.2 10.4 %shard_map.223 = (bf16[4,256,256]{2,1,0:T(8,128)(2,1)}, s32[4,32,128]{2,1,0:T(8,128)}) custom-call(bf16[4,256,256]{2,1,0:T(8,128)(2,1)S(1)} %get-tuple-element.209.rows_ref, s32[32,128]{1,0:T(8,128)S(1)} %get-tuple-element.124.ids_ref), custom_call_target="tpu_custom_call" | custom-call | tf_op jit(solution)/shard_map/pallas_call | solution.py:768
  113.6 0.1 broadcast_in_dim.46
  113.7 0.0 copy-done.13
  113.7 3.4 conditional.4
  113.7 1.1 convert_reduce_fusion
  114.8 0.1 broadcast_bitcast_fusion
  114.9 0.8 multiply_convert_fusion
  115.7 1.4 fusion.6
  117.1 18.7 %shard_map.224 = (f32[256,1024]{1,0:T(8,128)}, bf16[1024,256]{1,0:T(8,128)(2,1)}, bf16[256,3072]{1,0:T(8,128)(2,1)}, f32[16,1,256]{2,1,0:T(1,128)}, bf16[1024,25...) custom-call(f32[256,1024]{1,0:T(8,128)S(1)} %get-tuple-element.127.r, ...), custom_call_target="tpu_custom_call" | custom-call | tf_op jit(solution)/shard_map/pallas_call | solution.py:969
  135.9 41.0 %collective-permute-start = (bf16[256,1024]{1,0:T(8,128)(2,1)}, bf16[256,1024]{1,0:T(8,128)(2,1)S(1)}, u32[]{:S(2)}, u32[]{:S(2)}) collective-permute-start(bf16[256,1024]{1,0:T(8,128)(2,1)} %get-tuple-element.134), channel_id=1, source_target_pairs={{0,16},{1,17},{2,18},{3,19},{4,20},{5,21},{6,22},{7,23},{8,24},{9,... | collective-permute-start | bytes 1572872 | tf_op jit(solution)/shard_map/ppermute | solution.py:28
  176.9 0.6 slice.43
  177.5 0.1 lt.25
  177.6 0.7 fusion.4
  178.3 0.3 collective-permute-done.refs_0_
  178.6 0.8 copy-done.11
  179.4 2.6 shard_map.225
  182.0 52.0 %shard_map.226 = (bf16[256,256]{1,0:T(8,128)(2,1)S(1)}, f32[1,256]{1,0:T(1,128)}, bf16[4096,256]{1,0:T(8,128)(2,1)}) custom-call(bf16[256,256]{1,0:T(8,128)(2,1)} %get-tuple-element.145.proj, s32[1,1024]{1,0:T(1,128)} %bitcast.75, f32[1,1024]{1,0:T(1,128)} %bitcast.76, bf16[4096,256]{1,0:T(8,128)(2,1)S(1)} %copy-done.8), custom_call_target="tpu_custom_call" | custom-call | tf_op jit(solution)/shard_map/pallas_call | solution.py:1284
  234.0 18.5 %shard_map.228.refs_8_ = bf16[1024,256]{1,0:T(8,128)(2,1)} custom-call(bf16[4096,256]{1,0:T(8,128)(2,1)} %get-tuple-element.156.refs_0_), custom_call_target="tpu_custom_call" | custom-call | tf_op jit(solution)/shard_map/pallas_call | solution.py:1766
  252.5 1.8 shard_map.227
  254.3 1.3 collective-permute-start.1
  255.6 1.4 slice.45
  257.1 9.3 %collective-permute-done.1.refs_0_ = bf16[256,1024]{1,0:T(8,128)(2,1)S(1)} collective-permute-done((bf16[256,1024]{1,0:T(8,128)(2,1)S(1)}, bf16[256,1024]{1,0:T(8,128)(2,1)S(1)}, u32[]{:S(2)}, u32[]{:S(2)}) %collective-permute-start.1) | collective-permute-done | bytes 524320 | tf_op jit(solution)/shard_map/ppermute | solution.py:28
  266.4 0.8 copy-done.12
  267.2 25.6 %shard_map.229 = (bf16[256,1024]{1,0:T(8,128)(2,1)}, bf16[256,4096]{1,0:T(8,128)(2,1)}, bf16[256,1024]{1,0:T(8,128)(2,1)}, bf16[256,3072]{1,0:T(8,128)(2,1)}, bf...) custom-call(bf16[256,1024]{1,0:T(8,128)(2,1)} %copy-done.12, ...), custom_call_target="tpu_custom_call", output_to_operand_aliasing={{0}: (16, {}), {1}: (17, {}), {2}: (18, {}), {3}: (19, {}),... | custom-call | tf_op jit(solution)/shard_map/pallas_call | solution.py:1145
  292.8 0.0 copy-done.9
  292.8 0.0 copy-start.5
  292.9 0.0 copy-start.6
  292.9 1.6 conditional.5
  292.9 0.3 fusion.3
  293.2 1.2 convolution_convert_fusion.1
  294.5 0.0 copy-start.1
  294.5 2.0 convolution_convert_fusion.5.refs_3_
  296.6 5.6 %convolution_convert_fusion.3.refs_0_ = bf16[1024,4096]{1,0:T(8,128)(2,1)} fusion(bf16[1024,256]{1,0:T(8,128)(2,1)S(1)} %copy-done.7, bf16[256,4096]{1,0:T(8,128)(2,1)S(1)} %copy-done.1), kind=kOutput, calls=%fused_computation.13 | convolution fusion | flops 2151677952 | bytes 11010048 | tf_op jit(solution)/shard_map/dot_general | solution.py:32
  302.2 0.0 copy-done.2
  302.2 4.4 convolution_convert_fusion.4.refs_4_
  306.7 0.0 copy-done
  306.7 5.6 convolution_convert_fusion.2.refs_1_
  312.3 234.1 %shard_map.230 = (bf16[256,4096]{1,0:T(8,128)(2,1)}, bf16[1024,1024]{1,0:T(8,128)(2,1)}, bf16[64,1024]{1,0:T(8,128)(2,1)}, bf16[256,1024]{1,0:T(8,128)(2,1)}, bf...) custom-call(bf16[1024,4096]{1,0:T(8,128)(2,1)} %convolution_convert_fusion.3.refs_0_, ...), custom_call_target="tpu_custom_call" | custom-call | tf_op jit(solution)/shard_map/pallas_call | solution.py:1766
  546.4 0.1 collective-permute-start.3
  546.5 0.5 collective-permute-start.5
  547.0 0.1 collective-permute-start.2
  547.1 0.4 collective-permute-start.4
  547.6 8.7 %shard_map.231 = (f32[256,4096]{1,0:T(8,128)}, f32[1024,1024]{1,0:T(8,128)}, f32[256,1024]{1,0:T(8,128)}, f32[256,3072]{1,0:T(8,128)}) custom-call(bf16[256,4096]{1,0:T(8,128)(2,1)} %get-tuple-element.181.refs_0_, bf16[1024,1024]{1,0:T(8,128)(2,1)} %get-tuple-element.182.refs_1_, bf16[256,1024]{1,0:T(8,128)(2,1)} %get-tuple-element.183.refs_2_, ...), custom_call_target="tpu_custom_call" | custom-call | flops 3145728 | bytes 18874368 | tf_op jit(solution)/shard_map/pallas_call | solution.py:1330
  556.3 0.0 collective-permute-done.2
  556.3 0.5 broadcast_select_fusion.1
  556.8 0.0 collective-permute-done.5
  556.8 1.4 broadcast_select_fusion
  558.2 0.0 collective-permute-done.4
  558.2 0.7 select_convert_fusion.1
  558.9 0.8 reshape.106
  559.7 0.0 collective-permute-done.3
  559.7 2.3 select_convert_fusion
  (27 shorter events, 0.1 us)
Async XLA Ops:
  5.5 94.8 %copy-start.8 = (bf16[4096,256]{1,0:T(8,128)(2,1)S(1)}, bf16[4096,256]{1,0:T(8,128)(2,1)}, u32[]{:S(2)}) copy-start(bf16[4096,256]{1,0:T(8,128)(2,1)} %table.1) | copy-start | bytes 6291460
  100.3 13.4 %copy-start.13 = (bf16[256,256]{1,0:T(8,128)(2,1)S(1)}, bf16[256,256]{1,0:T(8,128)(2,1)}, u32[]{:S(2)}) copy-start(bf16[256,256]{1,0:T(8,128)(2,1)} %param.23) | copy-start | bytes 393220
  135.9 42.7 %collective-permute-start = (bf16[256,1024]{1,0:T(8,128)(2,1)}, bf16[256,1024]{1,0:T(8,128)(2,1)S(1)}, u32[]{:S(2)}, u32[]{:S(2)}) collective-permute-start(bf16[256,1024]{1,0:T(8,128)(2,1)} %get-tuple-element.134), channel_id=1, source_target_pairs={{0,16},{1,17},{2,18},{3,19},{4,20},{5,21},{6,22},{7,23},{8,24},{9,... | collective-permute-start | bytes 1572872 | tf_op jit(solution)/shard_map/ppermute | solution.py:28
  178.6 0.8 copy-start.11
  254.3 12.1 %collective-permute-start.1 = (bf16[256,1024]{1,0:T(8,128)(2,1)S(1)}, bf16[256,1024]{1,0:T(8,128)(2,1)S(1)}, u32[]{:S(2)}, u32[]{:S(2)}) collective-permute-start(bf16[256,1024]{1,0:T(8,128)(2,1)S(1)} %get-tuple-element.157.refs_20_), channel_id=1, source_target_pairs={{16,0},{17,1},{18,2},{19,3},{20,4},{21,5},{22,6},{23,7},{24,8},{25... | collective-permute-start | bytes 1572872 | tf_op jit(solution)/shard_map/ppermute | solution.py:28
  266.4 0.8 copy-start.12
  267.2 25.6 %copy-start.9 = (bf16[256,1024]{1,0:T(8,128)(2,1)S(1)}, bf16[256,1024]{1,0:T(8,128)(2,1)}, u32[]{:S(2)}) copy-start(bf16[256,1024]{1,0:T(8,128)(2,1)} %get-tuple-element.126) | copy-start | bytes 1572868
  292.8 1.6 copy-start.5
  292.9 1.6 copy-start.6
  294.5 2.1 copy-start.1
  294.5 2.1 copy-start.7
  296.6 5.6 %copy-start.2 = (bf16[256,3072]{1,0:T(8,128)(2,1)S(1)}, bf16[256,3072]{1,0:T(8,128)(2,1)}, u32[]{:S(2)}) copy-start(bf16[256,3072]{1,0:T(8,128)(2,1)} %get-tuple-element.173) | copy-start | bytes 4718596
  296.6 5.6 %copy-start.3 = (bf16[1024,256]{1,0:T(8,128)(2,1)S(1)}, bf16[1024,256]{1,0:T(8,128)(2,1)}, u32[]{:S(2)}) copy-start(bf16[1024,256]{1,0:T(8,128)(2,1)} %get-tuple-element.172) | copy-start | bytes 1572868
  302.2 4.5 copy-start
  302.2 4.5 copy-start.4
  312.3 234.7 %copy-start.15 = (f32[1,256]{1,0:T(1,128)S(1)}, f32[1,256]{1,0:T(1,128)}, u32[]{:S(2)}) copy-start(f32[1,256]{1,0:T(1,128)} %get-tuple-element.178) | copy-start | bytes 3076
  546.4 13.3 %collective-permute-start.3 = (bf16[4096,256]{1,0:T(8,128)(2,1)}, bf16[4096,256]{1,0:T(8,128)(2,1)}, u32[]{:S(2)}, u32[]{:S(2)}) collective-permute-start(bf16[4096,256]{1,0:T(8,128)(2,1)} %get-tuple-element.179), channel_id=1, source_target_pairs={{0,16},{16,0},{1,17},{17,1},{2,18},{18,2},{3,19},{19,3},{4,20},{20... | collective-permute-start | bytes 6291464 | tf_op jit(solution)/shard_map/ppermute | solution.py:1951
  546.5 10.3 %collective-permute-start.5 = (f32[8,256]{1,0:T(8,128)}, f32[8,256]{1,0:T(8,128)S(1)}, u32[]{:S(2)}, u32[]{:S(2)}) collective-permute-start(f32[8,256]{1,0:T(8,128)} %get-tuple-element.177), channel_id=1, source_target_pairs={{0,16},{16,0},{1,17},{17,1},{2,18},{18,2},{3,19},{19,3},{4,20},{20... | collective-permute-start | bytes 24584 | tf_op jit(solution)/shard_map/ppermute | solution.py:1951
  547.0 9.3 %collective-permute-start.2 = (bf16[256]{0:T(256)(128)(2,1)S(1)}, bf16[256]{0:T(256)(128)(2,1)S(1)}, u32[]{:S(2)}, u32[]{:S(2)}) collective-permute-start(bf16[256]{0:T(256)(128)(2,1)S(1)} %convert_reduce_fusion.1), channel_id=1, source_target_pairs={{0,16},{16,0},{1,17},{17,1},{2,18},{18,2},{3,19},{19,3},{4,20},{20... | collective-permute-start | bytes 1544 | tf_op jit(solution)/shard_map/ppermute | solution.py:1951
  547.1 11.1 %collective-permute-start.4 = (bf16[64,1024]{1,0:T(8,128)(2,1)}, bf16[64,1024]{1,0:T(8,128)(2,1)S(1)}, u32[]{:S(2)}, u32[]{:S(2)}) collective-permute-start(bf16[64,1024]{1,0:T(8,128)(2,1)} %get-tuple-element.180), channel_id=1, source_target_pairs={{0,16},{16,0},{1,17},{17,1},{2,18},{18,2},{3,19},{19,3},{4,20},{20... | collective-permute-start | bytes 393224 | tf_op jit(solution)/shard_map/ppermute | solution.py:1951
  547.6 10.6 %copy-start.14 = (bf16[64,1024]{1,0:T(8,128)(2,1)S(1)}, bf16[64,1024]{1,0:T(8,128)(2,1)}, u32[]{:S(2)}) copy-start(bf16[64,1024]{1,0:T(8,128)(2,1)} %get-tuple-element.180) | copy-start | bytes 393220
  547.6 12.2 %copy-start.10 = (bf16[4096,256]{1,0:T(8,128)(2,1)S(1)}, bf16[4096,256]{1,0:T(8,128)(2,1)}, u32[]{:S(2)}) copy-start(bf16[4096,256]{1,0:T(8,128)(2,1)} %get-tuple-element.179) | copy-start | bytes 6291460

commit v10 on v9

--- a/solution.py
+++ b/solution.py
@@ -1377,7 +1377,8 @@
 
 
 def reduce_body(plan, extras, pace, named):
-    arrays, outs = named["arrays"], named["outs"]
+    arrays, outs, shapes = named["arrays"], named["outs"], named["shapes"]
+    lefts, rights, made = named["lefts"], named["rights"], named["made"]
     own, got1, got2, got3, got4, land = (
         named[k] for k in ("own", "got1", "got2", "got3", "got4", "land")
     )
@@ -1412,19 +1413,53 @@
     pl.semaphore_wait(barrier, len(peers))
 
     def rows_of(p):
-        return arrays[plan[p][0]].shape[0] // (len(kept[p][0]) // 2)
+        return shapes[plan[p][0]][0] // (len(kept[p][0]) // 2)
 
     def columns_of(p):
-        return arrays[plan[p][0]].shape[1]
+        return shapes[plan[p][0]][1]
 
     def sub_of(p):
         return rows_of(p) // 4 // plan[p][3]
 
-    def block(p, r):
+    def block_rows(p, r):
         who = grp ^ (r & 3)
         line = pos ^ (r >> 2) if len(plan[p][1]) == 4 else 0
         start = line * rows_of(p) + who * (rows_of(p) // 4) + plan[p][2] * sub_of(p)
-        return arrays[plan[p][0]].at[rows_at(start, sub_of(p))]
+        return rows_at(start, sub_of(p))
+
+    def block(p, r):
+        return arrays[plan[p][0]].at[block_rows(p, r)]
+
+    def is_product(p):
+        return plan[p][0] in lefts
+
+    def load_factors(src):
+        hbm_left, left, hbm_right, right = lefts[src] + rights[src]
+        sem = named["factor_sem"]
+        return (
+            pltpu.make_async_copy(hbm_left, left, sem.at[src, 0]),
+            pltpu.make_async_copy(hbm_right, right, sem.at[src, 1]),
+        )
+
+    ready = []
+
+    def multiply(p, blocks, store):
+        src = plan[p][0]
+        left, right = lefts[src][1], rights[src][1]
+        if src not in ready:
+            for copy in load_factors(src):
+                copy.wait()
+            ready.append(src)
+        rows = jnp.concatenate([left[block_rows(p, r), :] for r in blocks], 0)
+        wide = min(columns_of(p), 1024)
+
+        def body(at, carry):
+            cols = pl.ds(pl.multiple_of(at * wide, 128), wide)
+            total = dot_nn(rows, right[:, cols])
+            store(cols, total.reshape(len(blocks), sub_of(p), wide))
+            return carry
+
+        lax.fori_loop(0, columns_of(p) // wide, body, 0)
 
     def spot(p, r):
         return kept[p][0].index(r)
@@ -1432,7 +1467,10 @@
     def swap(p, stage, at):
         bit = plan[p][1][stage]
         r = kept[p][stage][at] | (1 << bit)
-        src = block(p, r) if stage == 0 else own[p].at[spot(p, r)]
+        if stage:
+            src = own[p].at[spot(p, r)]
+        else:
+            src = made[p].at[at] if is_product(p) else block(p, r)
         return remote(
             src, got[stage][p].at[at], ssem.at[p, stage, at], rsem.at[p, stage, at], swaps[bit]
         )
@@ -1448,11 +1486,33 @@
         return sorted(places, key=lambda at: 1 - ((kept[p][stage][at] >> bit) & 1))
 
     def begin(p):
+        if is_product(p):
+
+            def store(cols, total):
+                made[p][:, :, cols] = total.astype(jnp.bfloat16)
+
+            multiply(p, [r | (1 << plan[p][1][0]) for r in kept[p][0]], store)
         for at in order_of(p, 0):
             swap(p, 0, at).start()
-            load_own(p, at).start()
+            if not is_product(p):
+                load_own(p, at).start()
 
     def advance(p, stage):
+        if stage == 0 and is_product(p):
+            for at in order_of(p, 0):
+                swap(p, 0, at).wait_recv()
+
+            def store_sum(cols, total):
+                total = total + got1[p][:, :, cols].astype(jnp.float32)
+                got1[p][:, :, cols] = total.astype(jnp.bfloat16)
+
+            multiply(p, kept[p][0], store_sum)
+            bit = plan[p][1][1]
+            for at in order_of(p, 0):
+                r = kept[p][0][at]
+                if (r >> bit) & 1:
+                    swap(p, 1, kept[p][1].index(r ^ (1 << bit))).start()
+            return
         for at in order_of(p, stage):
             r = kept[p][stage][at]
             place = spot(p, r)
@@ -1637,6 +1697,12 @@
         look_begin = look_middle = look_sum = look_pass = look_end = None
 
     ahead, lag, lag_end = pace
+    for piece in plan:
+        if piece[0] in lefts and piece[0] not in ready:
+            ready.append(piece[0])
+            for copy in load_factors(piece[0]):
+                copy.start()
+    ready.clear()
     on_first(look_begin)
     for p in range(min(ahead, count)):
         begin(p)
@@ -1685,16 +1751,20 @@
     low, f32, dma = jnp.bfloat16, jnp.float32, pltpu.SemaphoreType.DMA
     extras = ("spread",) * spread + ("gains",) * (gains is not None) + ("looked",) * (look is not None)
     count = len(plan)
-    inputs = list(arrays)
+    factors = {src: x for src, x in enumerate(arrays) if isinstance(x, tuple)}
+    plain = [x for x in arrays if not isinstance(x, tuple)]
+    flat_factors = [part for x in factors.values() for part in x]
+    inputs = plain + flat_factors
+    sizes = [(x[0].shape[0], x[1].shape[1]) if isinstance(x, tuple) else x.shape for x in arrays]
     lines = 4 if len(plan[0][1]) == 4 else 1
     share = lines if spread else 4 * lines
-    outs = [jax.ShapeDtypeStruct((x.shape[0] // share, x.shape[1]), low) for x in arrays]
+    outs = [jax.ShapeDtypeStruct((rows // share, columns), low) for rows, columns in sizes]
     out_specs = [ANYWHERE] * len(arrays)
-    in_specs = [ANYWHERE] * len(arrays)
+    in_specs = [ANYWHERE] * len(inputs)
     names = ["own", "got1", "got2", "got3", "got4", "land"]
     scratch = {name: [] for name in names}
     for src, _, _, chunks in plan:
-        rows, columns = arrays[src].shape[0] // lines, arrays[src].shape[1]
+        rows, columns = sizes[src][0] // lines, sizes[src][1]
         sub = rows // 4 // chunks
         held = (8, 8, 4, 2, 1) if lines == 4 else (2, 2, 1, 0, 0)
         for name, blocks in zip(names, held + (4 if spread else 1,)):
@@ -1703,6 +1773,8 @@
     flat = [item for name in names for item in scratch[name]]
     sems = [dma((count, 4, 8))] * 2 + [dma((count, 8))] + [dma((count, 4))] * 2 + [dma((count,))]
     tail = []
+    if factors:
+        tail += [pltpu.VMEM(x.shape, low) for x in flat_factors] + [dma((len(arrays), 2))]
     if spread:
         tail += [dma((count, 4))]
     if gains is not None:
@@ -1742,7 +1814,9 @@
             at += n
             return list(refs[at - n : at])
 
-        named = {"arrays": take(len(arrays))}
+        plain_refs = iter(take(len(plain)))
+        named = {"shapes": sizes, "arrays": [None if src in factors else next(plain_refs) for src in range(len(arrays))]}
+        pair_refs = take(len(flat_factors))
         if gains is not None:
             named["gains"] = take(1)[0]
         if look is not None:
@@ -1755,6 +1829,17 @@
         for name in names:
             named[name] = take(count)
         named["sems"] = take(6)
+        pair_bufs = take(len(flat_factors))
+        named["lefts"], named["rights"], named["made"] = {}, {}, {}
+        for nth, src in enumerate(factors):
+            named["lefts"][src] = (pair_refs[2 * nth], pair_bufs[2 * nth])
+            named["rights"][src] = (pair_refs[2 * nth + 1], pair_bufs[2 * nth + 1])
+        if factors:
+            named["factor_sem"] = take(1)[0]
+        for p in range(count):
+            if plan[p][0] in factors:
+                named["made"][p] = named["own"][p]
+                named["own"][p] = named["got1"][p]
         if spread:
             named["out_sem"] = take(1)[0]
         if gains is not None:
@@ -1774,6 +1859,7 @@
         ),
     )(*inputs)
 
+
 def nothing_like(run):
     return jax.tree.map(lambda a: jnp.zeros(a.shape, a.dtype), jax.eval_shape(run))
 
@@ -1790,8 +1876,8 @@
 LAYER_PLAN = (
     tuple((0, ORDERS[chunk], chunk, 4) for chunk in range(4))
     + tuple((1, ORDERS[chunk], chunk, 4) for chunk in range(4))
-    + tuple((4, ORDERS[chunk], chunk, 4) for chunk in range(4))
-    + ((3, Y_FIRST, 0, 2), (3, Z_THEN_X, 1, 2), (2, X_FIRST, 0, 1))
+    + ((4, X_FIRST, 0, 4), (4, Y_FIRST, 1, 4), (4, X_FIRST, 2, 4), (4, Z_THEN_Y, 3, 4))
+    + ((3, X_FIRST, 0, 2), (3, Y_FIRST, 1, 2), (2, X_FIRST, 0, 1))
 )
 TABLE_PLAN = tuple((0, ((0, 1), (1, 0))[chunk % 2], chunk, 4) for chunk in range(4))
 LAYER_PACE = (8, 4, 2)
@@ -1927,15 +2013,12 @@
     gain_rows = made[5]
     gain_rows = gain_rows.reshape(8, 4, width // 4).transpose(1, 0, 2)
 
-    def grads_of(rows_at_once, grads):
-        return product(rows_at_once, grads).astype(jnp.bfloat16)
-
     order = (
-        grads_of(kept[6], made[1]),
-        grads_of(kept[8], made[0]),
+        (kept[6], made[1]),
+        (kept[8], made[0]),
         edge_g,
-        grads_of(kept[4], made[2]),
-        grads_of(kept[1], made[3]),
+        (kept[4], made[2]),
+        (kept[1], made[3]),
     )
     up_r, down_r, edge_r, proj_r, qkv_r, gain_r, table_r = reduce_all(
         order,

time: 570 us -> 564 us (0.989)
  matrix products: 23.6 us -> 5.83 us
  Pallas kernels: 466 us -> 477 us
    dot_general x6 -> x2, matrix products: 22 us -> 4.27 us  [product(): return jnp.dot(left_side, right_side, preferred_element_type=jnp.float32)]
    pallas_call x2, Pallas kernels: 253 us -> 264 us  [reduce_all(): pl.pallas_call(functools.partial(reduce_kernel, plan, only, extras, pace,...]
where the time goes in v10:
time: 564 us; the launch traced here: 556 us
  Pallas kernels  477 us (85%)
  starting transfers between devices  43.5 us (8%)
  other arithmetic  10.9 us (2%)
  waiting for transfers between devices  9.64 us (2%)
  local copies, waits for them, and re-layouts  7.6 us (1%)
  matrix products  5.83 us (1%)
    pallas_call x2, Pallas kernels, reduce_all(): pl.pallas_call(functools.partial(reduce_kernel, plan, only, extras, pace,...  264 us
    pallas_call x1, Pallas kernels, gather_all(): pl.pallas_call(functools.partial(gather_kernel, count, first_order, last_...  93.3 us
    pallas_call x1, Pallas kernels, run_vocabulary(): pl.pallas_call(functools.partial(vocabulary_kernel, 1024), out_shape=[jax...  52.1 us
    ppermute x2, starting transfers between devices, passed_along(): return lax.ppermute(x, axis, pairs)  42.3 us
    pallas_call x2, Pallas kernels, run_backward(): pl.pallas_call(functools.partial(backward_kernel, only, tile, given), out...  27.4 us
    pallas_call x2, Pallas kernels, run_forward(): pl.pallas_call(functools.partial(forward_kernel, only, tile, given), out_...  21.4 us
  transfers between devices with their start and end apart: 6, of which 2 were waited for; matrix products, arithmetic and copies ran while one was open for 1% of the time, Pallas kernels for 2%

profile of v10, /device:TPU:0, one launch (start us, length us, event | category | flops | bytes accessed | tf_op | source)
XLA Modules:
  0.0 555.8 jit_solution(12491759740614790916)
XLA Ops:
  0.7 0.7 pad_bitcast_fusion
  1.3 0.1 pad.3.clone
  1.4 0.7 broadcast_in_dim.42
  2.0 0.7 add_rsqrt_fusion
  2.7 0.1 pad.7.clone
  2.8 1.3 add_add_fusion.refs_7_
  4.1 1.4 maximum_maximum_fusion.refs_6_
  5.5 0.0 copy-start
  5.5 93.3 %shard_map.222 = (bf16[1024,3072]{1,0:T(8,128)(2,1)}, bf16[1024,1024]{1,0:T(8,128)(2,1)}, bf16[1024,4096]{1,0:T(8,128)(2,1)}, bf16[4096,1024]{1,0:T(8,128)(2,1)}...) custom-call(bf16[256,3072]{1,0:T(8,128)(2,1)} %bitcast.48, ...), custom_call_target="tpu_custom_call" | custom-call | tf_op jit(solution)/shard_map/pallas_call | solution.py:712
  98.9 1.5 fusion.5
  100.3 0.0 copy-done
  100.3 0.0 copy-start.5
  100.3 2.9 conditional.3
  100.4 2.9 fusion.2
  103.2 10.5 %shard_map.223 = (bf16[4,256,256]{2,1,0:T(8,128)(2,1)}, s32[4,32,128]{2,1,0:T(8,128)}) custom-call(bf16[4,256,256]{2,1,0:T(8,128)(2,1)S(1)} %get-tuple-element.209.rows_ref, s32[32,128]{1,0:T(8,128)S(1)} %get-tuple-element.124.ids_ref), custom_call_target="tpu_custom_call" | custom-call | tf_op jit(solution)/shard_map/pallas_call | solution.py:768
  113.7 0.1 broadcast_in_dim.46
  113.8 0.0 copy-done.5
  113.8 3.4 conditional.4
  113.8 1.1 convert_reduce_fusion
  114.9 0.1 broadcast_bitcast_fusion
  115.0 0.8 multiply_convert_fusion
  115.8 1.4 fusion.6
  117.2 18.7 %shard_map.224 = (f32[256,1024]{1,0:T(8,128)}, bf16[1024,256]{1,0:T(8,128)(2,1)}, bf16[256,3072]{1,0:T(8,128)(2,1)}, f32[16,1,256]{2,1,0:T(1,128)}, bf16[1024,25...) custom-call(f32[256,1024]{1,0:T(8,128)S(1)} %get-tuple-element.127.r, ...), custom_call_target="tpu_custom_call" | custom-call | tf_op jit(solution)/shard_map/pallas_call | solution.py:969
  136.0 41.0 %collective-permute-start = (bf16[256,1024]{1,0:T(8,128)(2,1)}, bf16[256,1024]{1,0:T(8,128)(2,1)S(1)}, u32[]{:S(2)}, u32[]{:S(2)}) collective-permute-start(bf16[256,1024]{1,0:T(8,128)(2,1)} %get-tuple-element.134), channel_id=1, source_target_pairs={{0,16},{1,17},{2,18},{3,19},{4,20},{5,21},{6,22},{7,23},{8,24},{9,... | collective-permute-start | bytes 1572872 | tf_op jit(solution)/shard_map/ppermute | solution.py:28
  177.0 0.6 slice.43
  177.6 0.1 lt.25
  177.7 0.7 fusion.4
  178.4 0.3 collective-permute-done.refs_0_
  178.7 0.0 copy-start.3
  178.7 0.8 copy-done.3
  179.5 2.6 shard_map.225
  182.2 52.1 %shard_map.226 = (bf16[256,256]{1,0:T(8,128)(2,1)S(1)}, f32[1,256]{1,0:T(1,128)}, bf16[4096,256]{1,0:T(8,128)(2,1)}) custom-call(bf16[256,256]{1,0:T(8,128)(2,1)} %get-tuple-element.145.proj, s32[1,1024]{1,0:T(1,128)} %bitcast.67, f32[1,1024]{1,0:T(1,128)} %bitcast.68, bf16[4096,256]{1,0:T(8,128)(2,1)S(1)} %copy-done), custom_call_target="tpu_custom_call" | custom-call | tf_op jit(solution)/shard_map/pallas_call | solution.py:1284
  234.2 18.6 %shard_map.228.refs_12_ = bf16[1024,256]{1,0:T(8,128)(2,1)} custom-call(bf16[4096,256]{1,0:T(8,128)(2,1)} %get-tuple-element.157.refs_0_), custom_call_target="tpu_custom_call" | custom-call | tf_op jit(solution)/shard_map/pallas_call | solution.py:1851
  252.8 1.8 shard_map.227
  254.6 1.3 collective-permute-start.1
  255.9 1.4 slice.45
  257.3 9.3 %collective-permute-done.1.refs_0_ = bf16[256,1024]{1,0:T(8,128)(2,1)S(1)} collective-permute-done((bf16[256,1024]{1,0:T(8,128)(2,1)S(1)}, bf16[256,1024]{1,0:T(8,128)(2,1)S(1)}, u32[]{:S(2)}, u32[]{:S(2)}) %collective-permute-start.1) | collective-permute-done | bytes 524320 | tf_op jit(solution)/shard_map/ppermute | solution.py:28
  266.6 0.0 copy-start.4
  266.6 0.8 copy-done.4
  267.4 0.0 copy-start.1
  267.4 25.6 %shard_map.229 = (bf16[256,1024]{1,0:T(8,128)(2,1)}, bf16[256,4096]{1,0:T(8,128)(2,1)}, bf16[256,1024]{1,0:T(8,128)(2,1)}, bf16[256,3072]{1,0:T(8,128)(2,1)}, bf...) custom-call(bf16[256,1024]{1,0:T(8,128)(2,1)} %copy-done.4, ...), custom_call_target="tpu_custom_call", output_to_operand_aliasing={{0}: (16, {}), {1}: (17, {}), {2}: (18, {}), {3}: (19, {}),... | custom-call | tf_op jit(solution)/shard_map/pallas_call | solution.py:1145
  293.0 0.0 copy-done.1
  293.0 1.6 conditional.5
  293.1 0.3 fusion.3
  293.4 1.2 convolution_convert_fusion.1
  294.6 0.0 copy-start.7
  294.7 245.3 %shard_map.230 = (bf16[256,4096]{1,0:T(8,128)(2,1)}, bf16[1024,1024]{1,0:T(8,128)(2,1)}, bf16[64,1024]{1,0:T(8,128)(2,1)}, bf16[256,1024]{1,0:T(8,128)(2,1)}, bf...) custom-call(bf16[256,1024]{1,0:T(8,128)(2,1)S(1)} %get-tuple-element.165.refs_0_, ...), custom_call_target="tpu_custom_call" | custom-call | tf_op jit(solution)/shard_map/pallas_call | solution.py:1851
  540.0 0.1 collective-permute-start.3
  540.1 0.5 collective-permute-start.5
  540.6 0.0 copy-done.7
  540.6 0.1 collective-permute-start.2
  540.7 0.4 collective-permute-start.4
  541.2 8.7 %shard_map.231 = (f32[256,4096]{1,0:T(8,128)}, f32[1024,1024]{1,0:T(8,128)}, f32[256,1024]{1,0:T(8,128)}, f32[256,3072]{1,0:T(8,128)}) custom-call(bf16[256,4096]{1,0:T(8,128)(2,1)} %get-tuple-element.181.refs_0_, bf16[1024,1024]{1,0:T(8,128)(2,1)} %get-tuple-element.182.refs_1_, bf16[256,1024]{1,0:T(8,128)(2,1)} %get-tuple-element.183.refs_2_, ...), custom_call_target="tpu_custom_call" | custom-call | flops 3145728 | bytes 18874368 | tf_op jit(solution)/shard_map/pallas_call | solution.py:1330
  549.9 0.0 collective-permute-done.2
  549.9 0.5 broadcast_select_fusion.1
  550.4 0.0 collective-permute-done.5
  550.4 1.4 broadcast_select_fusion
  551.8 0.0 collective-permute-done.4
  551.8 0.0 copy-done.6
  551.8 0.7 select_convert_fusion.1
  552.5 0.8 reshape.106
  553.3 0.0 collective-permute-done.3
  553.3 0.0 copy-done.2
  553.3 2.3 select_convert_fusion
  (7 shorter events, 0.0 us)
Async XLA Ops:
  5.5 94.8 %copy-start = (bf16[4096,256]{1,0:T(8,128)(2,1)S(1)}, bf16[4096,256]{1,0:T(8,128)(2,1)}, u32[]{:S(2)}) copy-start(bf16[4096,256]{1,0:T(8,128)(2,1)} %table.1) | copy-start | bytes 6291460
  100.3 13.4 %copy-start.5 = (bf16[256,256]{1,0:T(8,128)(2,1)S(1)}, bf16[256,256]{1,0:T(8,128)(2,1)}, u32[]{:S(2)}) copy-start(bf16[256,256]{1,0:T(8,128)(2,1)} %param.23) | copy-start | bytes 393220
  136.0 42.7 %collective-permute-start = (bf16[256,1024]{1,0:T(8,128)(2,1)}, bf16[256,1024]{1,0:T(8,128)(2,1)S(1)}, u32[]{:S(2)}, u32[]{:S(2)}) collective-permute-start(bf16[256,1024]{1,0:T(8,128)(2,1)} %get-tuple-element.134), channel_id=1, source_target_pairs={{0,16},{1,17},{2,18},{3,19},{4,20},{5,21},{6,22},{7,23},{8,24},{9,... | collective-permute-start | bytes 1572872 | tf_op jit(solution)/shard_map/ppermute | solution.py:28
  178.7 0.8 copy-start.3
  254.6 12.0 %collective-permute-start.1 = (bf16[256,1024]{1,0:T(8,128)(2,1)S(1)}, bf16[256,1024]{1,0:T(8,128)(2,1)S(1)}, u32[]{:S(2)}, u32[]{:S(2)}) collective-permute-start(bf16[256,1024]{1,0:T(8,128)(2,1)S(1)} %get-tuple-element.158.refs_20_), channel_id=1, source_target_pairs={{16,0},{17,1},{18,2},{19,3},{20,4},{21,5},{22,6},{23,7},{24,8},{25... | collective-permute-start | bytes 1572872 | tf_op jit(solution)/shard_map/ppermute | solution.py:28
  266.6 0.8 copy-start.4
  267.4 25.6 %copy-start.1 = (bf16[256,1024]{1,0:T(8,128)(2,1)S(1)}, bf16[256,1024]{1,0:T(8,128)(2,1)}, u32[]{:S(2)}) copy-start(bf16[256,1024]{1,0:T(8,128)(2,1)} %get-tuple-element.126) | copy-start | bytes 1572868
  294.6 245.9 %copy-start.7 = (f32[1,256]{1,0:T(1,128)S(1)}, f32[1,256]{1,0:T(1,128)}, u32[]{:S(2)}) copy-start(f32[1,256]{1,0:T(1,128)} %get-tuple-element.178) | copy-start | bytes 3076
  540.0 13.3 %collective-permute-start.3 = (bf16[4096,256]{1,0:T(8,128)(2,1)}, bf16[4096,256]{1,0:T(8,128)(2,1)}, u32[]{:S(2)}, u32[]{:S(2)}) collective-permute-start(bf16[4096,256]{1,0:T(8,128)(2,1)} %get-tuple-element.179), channel_id=1, source_target_pairs={{0,16},{16,0},{1,17},{17,1},{2,18},{18,2},{3,19},{19,3},{4,20},{20... | collective-permute-start | bytes 6291464 | tf_op jit(solution)/shard_map/ppermute | solution.py:2034
  540.1 10.3 %collective-permute-start.5 = (f32[8,256]{1,0:T(8,128)}, f32[8,256]{1,0:T(8,128)S(1)}, u32[]{:S(2)}, u32[]{:S(2)}) collective-permute-start(f32[8,256]{1,0:T(8,128)} %get-tuple-element.177), channel_id=1, source_target_pairs={{0,16},{16,0},{1,17},{17,1},{2,18},{18,2},{3,19},{19,3},{4,20},{20... | collective-permute-start | bytes 24584 | tf_op jit(solution)/shard_map/ppermute | solution.py:2034
  540.6 9.3 %collective-permute-start.2 = (bf16[256]{0:T(256)(128)(2,1)S(1)}, bf16[256]{0:T(256)(128)(2,1)S(1)}, u32[]{:S(2)}, u32[]{:S(2)}) collective-permute-start(bf16[256]{0:T(256)(128)(2,1)S(1)} %convert_reduce_fusion.1), channel_id=1, source_target_pairs={{0,16},{16,0},{1,17},{17,1},{2,18},{18,2},{3,19},{19,3},{4,20},{20... | collective-permute-start | bytes 1544 | tf_op jit(solution)/shard_map/ppermute | solution.py:2034
  540.7 11.1 %collective-permute-start.4 = (bf16[64,1024]{1,0:T(8,128)(2,1)}, bf16[64,1024]{1,0:T(8,128)(2,1)S(1)}, u32[]{:S(2)}, u32[]{:S(2)}) collective-permute-start(bf16[64,1024]{1,0:T(8,128)(2,1)} %get-tuple-element.180), channel_id=1, source_target_pairs={{0,16},{16,0},{1,17},{17,1},{2,18},{18,2},{3,19},{19,3},{4,20},{20... | collective-permute-start | bytes 393224 | tf_op jit(solution)/shard_map/ppermute | solution.py:2034
  541.2 10.6 %copy-start.6 = (bf16[64,1024]{1,0:T(8,128)(2,1)S(1)}, bf16[64,1024]{1,0:T(8,128)(2,1)}, u32[]{:S(2)}) copy-start(bf16[64,1024]{1,0:T(8,128)(2,1)} %get-tuple-element.180) | copy-start | bytes 393220
  541.2 12.2 %copy-start.2 = (bf16[4096,256]{1,0:T(8,128)(2,1)S(1)}, bf16[4096,256]{1,0:T(8,128)(2,1)}, u32[]{:S(2)}) copy-start(bf16[4096,256]{1,0:T(8,128)(2,1)} %get-tuple-element.179) | copy-start | bytes 6291460

commit v11 on v10

--- a/solution.py
+++ b/solution.py
@@ -962,7 +962,7 @@
     shapes = kept_shapes(rows, width, units)
     low = jnp.bfloat16
     given = 0 if kept is None else KEPT_COUNT
-    in_specs = [IN_VMEM] * 3 + [IN_SMEM] + [IN_VMEM] * 2 + [ANYWHERE] * (4 + given)
+    in_specs = [IN_VMEM] * 3 + [IN_SMEM] + [IN_VMEM, IN_VMEM if only == 1 else ANYWHERE] + [ANYWHERE] * (4 + given)
     extra = [jax.ShapeDtypeStruct((rows, width), low)]
     if only == 1:
         extra.append(jax.ShapeDtypeStruct((rows, out_weight.shape[1]), low))
@@ -1141,7 +1141,7 @@
     shapes = grad_shapes(rows, width, units)
     low, f32 = jnp.bfloat16, jnp.float32
     given = 0 if made is None else GRAD_COUNT
-    in_specs = [IN_VMEM] * 3 + [IN_SMEM] + [IN_VMEM] * 2 + [ANYWHERE] * (10 + given)
+    in_specs = [IN_VMEM] * 3 + [IN_SMEM] + [IN_VMEM, IN_VMEM if only == 1 else ANYWHERE] + [ANYWHERE] * (10 + given)
     return pl.pallas_call(
         functools.partial(backward_kernel, only, tile, given),
         out_shape=shapes,
@@ -1876,11 +1876,11 @@
 LAYER_PLAN = (
     tuple((0, ORDERS[chunk], chunk, 4) for chunk in range(4))
     + tuple((1, ORDERS[chunk], chunk, 4) for chunk in range(4))
-    + ((4, X_FIRST, 0, 4), (4, Y_FIRST, 1, 4), (4, X_FIRST, 2, 4), (4, Z_THEN_Y, 3, 4))
-    + ((3, X_FIRST, 0, 2), (3, Y_FIRST, 1, 2), (2, X_FIRST, 0, 1))
+    + tuple((4, ORDERS[chunk], chunk, 4) for chunk in range(4))
+    + ((3, Y_FIRST, 0, 2), (3, Z_THEN_X, 1, 2), (2, X_FIRST, 0, 1))
 )
 TABLE_PLAN = tuple((0, ((0, 1), (1, 0))[chunk % 2], chunk, 4) for chunk in range(4))
-LAYER_PACE = (8, 4, 2)
+LAYER_PACE = (8, 5, 4)
 TABLE_PACE = (4, 2, 1)
 
 

time: 564 us -> 554 us (0.982)
  Pallas kernels: 477 us -> 467 us
    pallas_call x2, Pallas kernels: 264 us -> 254 us  [reduce_all(): pl.pallas_call(functools.partial(reduce_kernel, plan, only, extras, pace,...]
where the time goes in v11:
time: 554 us; the launch traced here: 545 us
  Pallas kernels  467 us (84%)
  starting transfers between devices  43.4 us (8%)
  other arithmetic  10.9 us (2%)
  waiting for transfers between devices  9.65 us (2%)
  local copies, waits for them, and re-layouts  7.6 us (1%)
  matrix products  5.83 us (1%)
    pallas_call x2, Pallas kernels, reduce_all(): pl.pallas_call(functools.partial(reduce_kernel, plan, only, extras, pace,...  254 us
    pallas_call x1, Pallas kernels, gather_all(): pl.pallas_call(functools.partial(gather_kernel, count, first_order, last_...  93.3 us
    pallas_call x1, Pallas kernels, run_vocabulary(): pl.pallas_call(functools.partial(vocabulary_kernel, 1024), out_shape=[jax...  52.1 us
    ppermute x2, starting transfers between devices, passed_along(): return lax.ppermute(x, axis, pairs)  42.3 us
    pallas_call x2, Pallas kernels, run_backward(): pl.pallas_call(functools.partial(backward_kernel, only, tile, given), out...  27.2 us
    pallas_call x2, Pallas kernels, run_forward(): pl.pallas_call(functools.partial(forward_kernel, only, tile, given), out_...  21.2 us
  transfers between devices with their start and end apart: 6, of which 2 were waited for; matrix products, arithmetic and copies ran while one was open for 1% of the time, Pallas kernels for 2%

profile of v11, /device:TPU:0, one launch (start us, length us, event | category | flops | bytes accessed | tf_op | source)
XLA Modules:
  0.0 545.4 jit_solution(3010515356583400505)
XLA Ops:
  0.7 0.7 pad_bitcast_fusion
  1.3 0.1 pad.3.clone
  1.4 0.7 broadcast_in_dim.42
  2.0 0.7 add_rsqrt_fusion
  2.7 0.1 pad.7.clone
  2.8 1.3 add_add_fusion.refs_7_
  4.1 1.4 maximum_maximum_fusion.refs_6_
  5.5 0.0 copy-start
  5.5 93.3 %shard_map.222 = (bf16[1024,3072]{1,0:T(8,128)(2,1)}, bf16[1024,1024]{1,0:T(8,128)(2,1)}, bf16[1024,4096]{1,0:T(8,128)(2,1)}, bf16[4096,1024]{1,0:T(8,128)(2,1)}...) custom-call(bf16[256,3072]{1,0:T(8,128)(2,1)} %bitcast.48, ...), custom_call_target="tpu_custom_call" | custom-call | tf_op jit(solution)/shard_map/pallas_call | solution.py:712
  98.9 1.5 fusion.5
  100.3 0.0 copy-done
  100.3 0.0 copy-start.5
  100.3 2.9 conditional.3
  100.4 2.9 fusion.2
  103.2 10.5 %shard_map.223 = (bf16[4,256,256]{2,1,0:T(8,128)(2,1)}, s32[4,32,128]{2,1,0:T(8,128)}) custom-call(bf16[4,256,256]{2,1,0:T(8,128)(2,1)S(1)} %get-tuple-element.209.rows_ref, s32[32,128]{1,0:T(8,128)S(1)} %get-tuple-element.124.ids_ref), custom_call_target="tpu_custom_call" | custom-call | tf_op jit(solution)/shard_map/pallas_call | solution.py:768
  113.7 0.1 broadcast_in_dim.46
  113.8 0.0 copy-done.5
  113.8 3.4 conditional.4
  113.8 1.1 convert_reduce_fusion
  114.9 0.1 broadcast_bitcast_fusion
  115.0 0.8 multiply_convert_fusion
  115.8 1.4 fusion.6
  117.2 18.5 %shard_map.224 = (f32[256,1024]{1,0:T(8,128)}, bf16[1024,256]{1,0:T(8,128)(2,1)}, bf16[256,3072]{1,0:T(8,128)(2,1)}, f32[16,1,256]{2,1,0:T(1,128)}, bf16[1024,25...) custom-call(f32[256,1024]{1,0:T(8,128)S(1)} %get-tuple-element.127.r, ...), custom_call_target="tpu_custom_call" | custom-call | tf_op jit(solution)/shard_map/pallas_call | solution.py:969
  135.7 41.0 %collective-permute-start = (bf16[256,1024]{1,0:T(8,128)(2,1)}, bf16[256,1024]{1,0:T(8,128)(2,1)S(1)}, u32[]{:S(2)}, u32[]{:S(2)}) collective-permute-start(bf16[256,1024]{1,0:T(8,128)(2,1)} %get-tuple-element.134), channel_id=1, source_target_pairs={{0,16},{1,17},{2,18},{3,19},{4,20},{5,21},{6,22},{7,23},{8,24},{9,... | collective-permute-start | bytes 1572872 | tf_op jit(solution)/shard_map/ppermute | solution.py:28
  176.7 0.6 slice.43
  177.3 0.1 lt.25
  177.4 0.7 fusion.4
  178.1 0.3 collective-permute-done.refs_0_
  178.4 0.0 copy-start.3
  178.4 0.8 copy-done.3
  179.2 2.6 shard_map.225
  181.9 52.1 %shard_map.226 = (bf16[256,256]{1,0:T(8,128)(2,1)S(1)}, f32[1,256]{1,0:T(1,128)}, bf16[4096,256]{1,0:T(8,128)(2,1)}) custom-call(bf16[256,256]{1,0:T(8,128)(2,1)} %get-tuple-element.145.proj, s32[1,1024]{1,0:T(1,128)} %bitcast.67, f32[1,1024]{1,0:T(1,128)} %bitcast.68, bf16[4096,256]{1,0:T(8,128)(2,1)S(1)} %copy-done), custom_call_target="tpu_custom_call" | custom-call | tf_op jit(solution)/shard_map/pallas_call | solution.py:1284
  234.0 18.6 %shard_map.228.refs_12_ = bf16[1024,256]{1,0:T(8,128)(2,1)} custom-call(bf16[4096,256]{1,0:T(8,128)(2,1)} %get-tuple-element.157.refs_0_), custom_call_target="tpu_custom_call" | custom-call | tf_op jit(solution)/shard_map/pallas_call | solution.py:1851
  252.5 1.8 shard_map.227
  254.3 1.3 collective-permute-start.1
  255.6 1.4 slice.45
  257.0 9.3 %collective-permute-done.1.refs_0_ = bf16[256,1024]{1,0:T(8,128)(2,1)S(1)} collective-permute-done((bf16[256,1024]{1,0:T(8,128)(2,1)S(1)}, bf16[256,1024]{1,0:T(8,128)(2,1)S(1)}, u32[]{:S(2)}, u32[]{:S(2)}) %collective-permute-start.1) | collective-permute-done | bytes 524320 | tf_op jit(solution)/shard_map/ppermute | solution.py:28
  266.3 0.0 copy-start.4
  266.3 0.8 copy-done.4
  267.2 0.0 copy-start.1
  267.2 25.4 %shard_map.229 = (bf16[256,1024]{1,0:T(8,128)(2,1)}, bf16[256,4096]{1,0:T(8,128)(2,1)}, bf16[256,1024]{1,0:T(8,128)(2,1)}, bf16[256,3072]{1,0:T(8,128)(2,1)}, bf...) custom-call(bf16[256,1024]{1,0:T(8,128)(2,1)} %copy-done.4, ...), custom_call_target="tpu_custom_call", output_to_operand_aliasing={{0}: (16, {}), {1}: (17, {}), {2}: (18, {}), {3}: (19, {}),... | custom-call | tf_op jit(solution)/shard_map/pallas_call | solution.py:1145
  292.6 0.0 copy-done.1
  292.6 1.6 conditional.5
  292.6 0.3 fusion.3
  293.0 1.2 convolution_convert_fusion.1
  294.2 0.0 copy-start.7
  294.2 235.3 %shard_map.230 = (bf16[256,4096]{1,0:T(8,128)(2,1)}, bf16[1024,1024]{1,0:T(8,128)(2,1)}, bf16[64,1024]{1,0:T(8,128)(2,1)}, bf16[256,1024]{1,0:T(8,128)(2,1)}, bf...) custom-call(bf16[256,1024]{1,0:T(8,128)(2,1)S(1)} %get-tuple-element.165.refs_0_, ...), custom_call_target="tpu_custom_call" | custom-call | tf_op jit(solution)/shard_map/pallas_call | solution.py:1851
  529.6 0.1 collective-permute-start.3
  529.6 0.5 collective-permute-start.5
  530.1 0.0 copy-done.7
  530.2 0.1 collective-permute-start.2
  530.3 0.4 collective-permute-start.4
  530.7 8.7 %shard_map.231 = (f32[256,4096]{1,0:T(8,128)}, f32[1024,1024]{1,0:T(8,128)}, f32[256,1024]{1,0:T(8,128)}, f32[256,3072]{1,0:T(8,128)}) custom-call(bf16[256,4096]{1,0:T(8,128)(2,1)} %get-tuple-element.181.refs_0_, bf16[1024,1024]{1,0:T(8,128)(2,1)} %get-tuple-element.182.refs_1_, bf16[256,1024]{1,0:T(8,128)(2,1)} %get-tuple-element.183.refs_2_, ...), custom_call_target="tpu_custom_call" | custom-call | flops 3145728 | bytes 18874368 | tf_op jit(solution)/shard_map/pallas_call | solution.py:1330
  539.4 0.0 collective-permute-done.2
  539.4 0.5 broadcast_select_fusion.1
  540.0 0.0 collective-permute-done.5
  540.0 1.4 broadcast_select_fusion
  541.3 0.0 collective-permute-done.4
  541.3 0.0 copy-done.6
  541.4 0.7 select_convert_fusion.1
  542.1 0.8 reshape.106
  542.9 0.0 collective-permute-done.3
  542.9 0.0 copy-done.2
  542.9 2.3 select_convert_fusion
  (7 shorter events, 0.0 us)
Async XLA Ops:
  5.5 94.8 %copy-start = (bf16[4096,256]{1,0:T(8,128)(2,1)S(1)}, bf16[4096,256]{1,0:T(8,128)(2,1)}, u32[]{:S(2)}) copy-start(bf16[4096,256]{1,0:T(8,128)(2,1)} %table.1) | copy-start | bytes 6291460
  100.3 13.4 %copy-start.5 = (bf16[256,256]{1,0:T(8,128)(2,1)S(1)}, bf16[256,256]{1,0:T(8,128)(2,1)}, u32[]{:S(2)}) copy-start(bf16[256,256]{1,0:T(8,128)(2,1)} %param.23) | copy-start | bytes 393220
  135.7 42.7 %collective-permute-start = (bf16[256,1024]{1,0:T(8,128)(2,1)}, bf16[256,1024]{1,0:T(8,128)(2,1)S(1)}, u32[]{:S(2)}, u32[]{:S(2)}) collective-permute-start(bf16[256,1024]{1,0:T(8,128)(2,1)} %get-tuple-element.134), channel_id=1, source_target_pairs={{0,16},{1,17},{2,18},{3,19},{4,20},{5,21},{6,22},{7,23},{8,24},{9,... | collective-permute-start | bytes 1572872 | tf_op jit(solution)/shard_map/ppermute | solution.py:28
  178.4 0.8 copy-start.3
  254.3 12.0 %collective-permute-start.1 = (bf16[256,1024]{1,0:T(8,128)(2,1)S(1)}, bf16[256,1024]{1,0:T(8,128)(2,1)S(1)}, u32[]{:S(2)}, u32[]{:S(2)}) collective-permute-start(bf16[256,1024]{1,0:T(8,128)(2,1)S(1)} %get-tuple-element.158.refs_20_), channel_id=1, source_target_pairs={{16,0},{17,1},{18,2},{19,3},{20,4},{21,5},{22,6},{23,7},{24,8},{25... | collective-permute-start | bytes 1572872 | tf_op jit(solution)/shard_map/ppermute | solution.py:28
  266.3 0.8 copy-start.4
  267.2 25.4 %copy-start.1 = (bf16[256,1024]{1,0:T(8,128)(2,1)S(1)}, bf16[256,1024]{1,0:T(8,128)(2,1)}, u32[]{:S(2)}) copy-start(bf16[256,1024]{1,0:T(8,128)(2,1)} %get-tuple-element.126) | copy-start | bytes 1572868
  294.2 235.9 %copy-start.7 = (f32[1,256]{1,0:T(1,128)S(1)}, f32[1,256]{1,0:T(1,128)}, u32[]{:S(2)}) copy-start(f32[1,256]{1,0:T(1,128)} %get-tuple-element.178) | copy-start | bytes 3076
  529.6 13.3 %collective-permute-start.3 = (bf16[4096,256]{1,0:T(8,128)(2,1)}, bf16[4096,256]{1,0:T(8,128)(2,1)}, u32[]{:S(2)}, u32[]{:S(2)}) collective-permute-start(bf16[4096,256]{1,0:T(8,128)(2,1)} %get-tuple-element.179), channel_id=1, source_target_pairs={{0,16},{16,0},{1,17},{17,1},{2,18},{18,2},{3,19},{19,3},{4,20},{20... | collective-permute-start | bytes 6291464 | tf_op jit(solution)/shard_map/ppermute | solution.py:2034
  529.6 10.3 %collective-permute-start.5 = (f32[8,256]{1,0:T(8,128)}, f32[8,256]{1,0:T(8,128)S(1)}, u32[]{:S(2)}, u32[]{:S(2)}) collective-permute-start(f32[8,256]{1,0:T(8,128)} %get-tuple-element.177), channel_id=1, source_target_pairs={{0,16},{16,0},{1,17},{17,1},{2,18},{18,2},{3,19},{19,3},{4,20},{20... | collective-permute-start | bytes 24584 | tf_op jit(solution)/shard_map/ppermute | solution.py:2034
  530.2 9.3 %collective-permute-start.2 = (bf16[256]{0:T(256)(128)(2,1)S(1)}, bf16[256]{0:T(256)(128)(2,1)S(1)}, u32[]{:S(2)}, u32[]{:S(2)}) collective-permute-start(bf16[256]{0:T(256)(128)(2,1)S(1)} %convert_reduce_fusion.1), channel_id=1, source_target_pairs={{0,16},{16,0},{1,17},{17,1},{2,18},{18,2},{3,19},{19,3},{4,20},{20... | collective-permute-start | bytes 1544 | tf_op jit(solution)/shard_map/ppermute | solution.py:2034
  530.3 11.1 %collective-permute-start.4 = (bf16[64,1024]{1,0:T(8,128)(2,1)}, bf16[64,1024]{1,0:T(8,128)(2,1)S(1)}, u32[]{:S(2)}, u32[]{:S(2)}) collective-permute-start(bf16[64,1024]{1,0:T(8,128)(2,1)} %get-tuple-element.180), channel_id=1, source_target_pairs={{0,16},{16,0},{1,17},{17,1},{2,18},{18,2},{3,19},{19,3},{4,20},{20... | collective-permute-start | bytes 393224 | tf_op jit(solution)/shard_map/ppermute | solution.py:2034
  530.7 10.6 %copy-start.6 = (bf16[64,1024]{1,0:T(8,128)(2,1)S(1)}, bf16[64,1024]{1,0:T(8,128)(2,1)}, u32[]{:S(2)}) copy-start(bf16[64,1024]{1,0:T(8,128)(2,1)} %get-tuple-element.180) | copy-start | bytes 393220
  530.7 12.2 %copy-start.2 = (bf16[4096,256]{1,0:T(8,128)(2,1)S(1)}, bf16[4096,256]{1,0:T(8,128)(2,1)}, u32[]{:S(2)}) copy-start(bf16[4096,256]{1,0:T(8,128)(2,1)} %get-tuple-element.179) | copy-start | bytes 6291460

commit v12 on v11

--- a/solution.py
+++ b/solution.py
@@ -1880,7 +1880,7 @@
     + ((3, Y_FIRST, 0, 2), (3, Z_THEN_X, 1, 2), (2, X_FIRST, 0, 1))
 )
 TABLE_PLAN = tuple((0, ((0, 1), (1, 0))[chunk % 2], chunk, 4) for chunk in range(4))
-LAYER_PACE = (8, 5, 4)
+LAYER_PACE = (6, 5, 6)
 TABLE_PACE = (4, 2, 1)
 
 

time: 554 us -> 556 us (level)
  no operation moved by 1% of the time
where the time goes in v12:
time: 556 us; the launch traced here: 547 us
  Pallas kernels  469 us (84%)
  starting transfers between devices  43.4 us (8%)
  other arithmetic  10.9 us (2%)
  waiting for transfers between devices  9.65 us (2%)
  local copies, waits for them, and re-layouts  7.6 us (1%)
  matrix products  5.83 us (1%)
    pallas_call x2, Pallas kernels, reduce_all(): pl.pallas_call(functools.partial(reduce_kernel, plan, only, extras, pace,...  256 us
    pallas_call x1, Pallas kernels, gather_all(): pl.pallas_call(functools.partial(gather_kernel, count, first_order, last_...  93.3 us
    pallas_call x1, Pallas kernels, run_vocabulary(): pl.pallas_call(functools.partial(vocabulary_kernel, 1024), out_shape=[jax...  52.1 us
    ppermute x2, starting transfers between devices, passed_along(): return lax.ppermute(x, axis, pairs)  42.3 us
    pallas_call x2, Pallas kernels, run_backward(): pl.pallas_call(functools.partial(backward_kernel, only, tile, given), out...  27.2 us
    pallas_call x2, Pallas kernels, run_forward(): pl.pallas_call(functools.partial(forward_kernel, only, tile, given), out_...  21.2 us
  transfers between devices with their start and end apart: 6, of which 2 were waited for; matrix products, arithmetic and copies ran while one was open for 1% of the time, Pallas kernels for 2%

profile of v12, /device:TPU:0, one launch (start us, length us, event | category | flops | bytes accessed | tf_op | source)
XLA Modules:
  0.0 547.5 jit_solution(4157931500126798128)
XLA Ops:
  0.7 0.7 pad_bitcast_fusion
  1.3 0.1 pad.3.clone
  1.4 0.7 broadcast_in_dim.42
  2.0 0.7 add_rsqrt_fusion
  2.7 0.1 pad.7.clone
  2.8 1.3 add_add_fusion.refs_7_
  4.1 1.4 maximum_maximum_fusion.refs_6_
  5.5 0.0 copy-start
  5.5 93.3 %shard_map.222 = (bf16[1024,3072]{1,0:T(8,128)(2,1)}, bf16[1024,1024]{1,0:T(8,128)(2,1)}, bf16[1024,4096]{1,0:T(8,128)(2,1)}, bf16[4096,1024]{1,0:T(8,128)(2,1)}...) custom-call(bf16[256,3072]{1,0:T(8,128)(2,1)} %bitcast.48, ...), custom_call_target="tpu_custom_call" | custom-call | tf_op jit(solution)/shard_map/pallas_call | solution.py:712
  98.9 1.5 fusion.5
  100.3 0.0 copy-done
  100.3 0.0 copy-start.5
  100.3 2.9 conditional.3
  100.4 2.9 fusion.2
  103.2 10.5 %shard_map.223 = (bf16[4,256,256]{2,1,0:T(8,128)(2,1)}, s32[4,32,128]{2,1,0:T(8,128)}) custom-call(bf16[4,256,256]{2,1,0:T(8,128)(2,1)S(1)} %get-tuple-element.209.rows_ref, s32[32,128]{1,0:T(8,128)S(1)} %get-tuple-element.124.ids_ref), custom_call_target="tpu_custom_call" | custom-call | tf_op jit(solution)/shard_map/pallas_call | solution.py:768
  113.7 0.1 broadcast_in_dim.46
  113.8 0.0 copy-done.5
  113.8 3.4 conditional.4
  113.8 1.1 convert_reduce_fusion
  114.9 0.1 broadcast_bitcast_fusion
  115.0 0.8 multiply_convert_fusion
  115.8 1.4 fusion.6
  117.2 18.5 %shard_map.224 = (f32[256,1024]{1,0:T(8,128)}, bf16[1024,256]{1,0:T(8,128)(2,1)}, bf16[256,3072]{1,0:T(8,128)(2,1)}, f32[16,1,256]{2,1,0:T(1,128)}, bf16[1024,25...) custom-call(f32[256,1024]{1,0:T(8,128)S(1)} %get-tuple-element.127.r, ...), custom_call_target="tpu_custom_call" | custom-call | tf_op jit(solution)/shard_map/pallas_call | solution.py:969
  135.7 41.0 %collective-permute-start = (bf16[256,1024]{1,0:T(8,128)(2,1)}, bf16[256,1024]{1,0:T(8,128)(2,1)S(1)}, u32[]{:S(2)}, u32[]{:S(2)}) collective-permute-start(bf16[256,1024]{1,0:T(8,128)(2,1)} %get-tuple-element.134), channel_id=1, source_target_pairs={{0,16},{1,17},{2,18},{3,19},{4,20},{5,21},{6,22},{7,23},{8,24},{9,... | collective-permute-start | bytes 1572872 | tf_op jit(solution)/shard_map/ppermute | solution.py:28
  176.7 0.6 slice.43
  177.3 0.1 lt.25
  177.4 0.7 fusion.4
  178.1 0.3 collective-permute-done.refs_0_
  178.4 0.0 copy-start.3
  178.4 0.8 copy-done.3
  179.2 2.6 shard_map.225
  181.9 52.1 %shard_map.226 = (bf16[256,256]{1,0:T(8,128)(2,1)S(1)}, f32[1,256]{1,0:T(1,128)}, bf16[4096,256]{1,0:T(8,128)(2,1)}) custom-call(bf16[256,256]{1,0:T(8,128)(2,1)} %get-tuple-element.145.proj, s32[1,1024]{1,0:T(1,128)} %bitcast.67, f32[1,1024]{1,0:T(1,128)} %bitcast.68, bf16[4096,256]{1,0:T(8,128)(2,1)S(1)} %copy-done), custom_call_target="tpu_custom_call" | custom-call | tf_op jit(solution)/shard_map/pallas_call | solution.py:1284
  234.0 18.6 %shard_map.228.refs_12_ = bf16[1024,256]{1,0:T(8,128)(2,1)} custom-call(bf16[4096,256]{1,0:T(8,128)(2,1)} %get-tuple-element.157.refs_0_), custom_call_target="tpu_custom_call" | custom-call | tf_op jit(solution)/shard_map/pallas_call | solution.py:1851
  252.5 1.8 shard_map.227
  254.3 1.3 collective-permute-start.1
  255.6 1.4 slice.45
  257.0 9.3 %collective-permute-done.1.refs_0_ = bf16[256,1024]{1,0:T(8,128)(2,1)S(1)} collective-permute-done((bf16[256,1024]{1,0:T(8,128)(2,1)S(1)}, bf16[256,1024]{1,0:T(8,128)(2,1)S(1)}, u32[]{:S(2)}, u32[]{:S(2)}) %collective-permute-start.1) | collective-permute-done | bytes 524320 | tf_op jit(solution)/shard_map/ppermute | solution.py:28
  266.3 0.0 copy-start.4
  266.3 0.8 copy-done.4
  267.2 0.0 copy-start.1
  267.2 25.4 %shard_map.229 = (bf16[256,1024]{1,0:T(8,128)(2,1)}, bf16[256,4096]{1,0:T(8,128)(2,1)}, bf16[256,1024]{1,0:T(8,128)(2,1)}, bf16[256,3072]{1,0:T(8,128)(2,1)}, bf...) custom-call(bf16[256,1024]{1,0:T(8,128)(2,1)} %copy-done.4, ...), custom_call_target="tpu_custom_call", output_to_operand_aliasing={{0}: (16, {}), {1}: (17, {}), {2}: (18, {}), {3}: (19, {}),... | custom-call | tf_op jit(solution)/shard_map/pallas_call | solution.py:1145
  292.6 0.0 copy-done.1
  292.6 1.6 conditional.5
  292.6 0.3 fusion.3
  293.0 1.2 convolution_convert_fusion.1
  294.2 0.0 copy-start.7
  294.2 237.4 %shard_map.230 = (bf16[256,4096]{1,0:T(8,128)(2,1)}, bf16[1024,1024]{1,0:T(8,128)(2,1)}, bf16[64,1024]{1,0:T(8,128)(2,1)}, bf16[256,1024]{1,0:T(8,128)(2,1)}, bf...) custom-call(bf16[256,1024]{1,0:T(8,128)(2,1)S(1)} %get-tuple-element.165.refs_0_, ...), custom_call_target="tpu_custom_call" | custom-call | tf_op jit(solution)/shard_map/pallas_call | solution.py:1851
  531.7 0.1 collective-permute-start.3
  531.7 0.5 collective-permute-start.5
  532.2 0.0 copy-done.7
  532.3 0.1 collective-permute-start.2
  532.4 0.4 collective-permute-start.4
  532.8 8.7 %shard_map.231 = (f32[256,4096]{1,0:T(8,128)}, f32[1024,1024]{1,0:T(8,128)}, f32[256,1024]{1,0:T(8,128)}, f32[256,3072]{1,0:T(8,128)}) custom-call(bf16[256,4096]{1,0:T(8,128)(2,1)} %get-tuple-element.181.refs_0_, bf16[1024,1024]{1,0:T(8,128)(2,1)} %get-tuple-element.182.refs_1_, bf16[256,1024]{1,0:T(8,128)(2,1)} %get-tuple-element.183.refs_2_, ...), custom_call_target="tpu_custom_call" | custom-call | flops 3145728 | bytes 18874368 | tf_op jit(solution)/shard_map/pallas_call | solution.py:1330
  541.5 0.0 collective-permute-done.2
  541.5 0.5 broadcast_select_fusion.1
  542.1 0.0 collective-permute-done.5
  542.1 1.4 broadcast_select_fusion
  543.4 0.0 collective-permute-done.4
  543.4 0.0 copy-done.6
  543.5 0.7 select_convert_fusion.1
  544.2 0.8 reshape.106
  545.0 0.0 collective-permute-done.3
  545.0 0.0 copy-done.2
  545.0 2.3 select_convert_fusion
  (7 shorter events, 0.0 us)
Async XLA Ops:
  5.5 94.8 %copy-start = (bf16[4096,256]{1,0:T(8,128)(2,1)S(1)}, bf16[4096,256]{1,0:T(8,128)(2,1)}, u32[]{:S(2)}) copy-start(bf16[4096,256]{1,0:T(8,128)(2,1)} %table.1) | copy-start | bytes 6291460
  100.3 13.4 %copy-start.5 = (bf16[256,256]{1,0:T(8,128)(2,1)S(1)}, bf16[256,256]{1,0:T(8,128)(2,1)}, u32[]{:S(2)}) copy-start(bf16[256,256]{1,0:T(8,128)(2,1)} %param.23) | copy-start | bytes 393220
  135.7 42.7 %collective-permute-start = (bf16[256,1024]{1,0:T(8,128)(2,1)}, bf16[256,1024]{1,0:T(8,128)(2,1)S(1)}, u32[]{:S(2)}, u32[]{:S(2)}) collective-permute-start(bf16[256,1024]{1,0:T(8,128)(2,1)} %get-tuple-element.134), channel_id=1, source_target_pairs={{0,16},{1,17},{2,18},{3,19},{4,20},{5,21},{6,22},{7,23},{8,24},{9,... | collective-permute-start | bytes 1572872 | tf_op jit(solution)/shard_map/ppermute | solution.py:28
  178.4 0.8 copy-start.3
  254.3 12.0 %collective-permute-start.1 = (bf16[256,1024]{1,0:T(8,128)(2,1)S(1)}, bf16[256,1024]{1,0:T(8,128)(2,1)S(1)}, u32[]{:S(2)}, u32[]{:S(2)}) collective-permute-start(bf16[256,1024]{1,0:T(8,128)(2,1)S(1)} %get-tuple-element.158.refs_20_), channel_id=1, source_target_pairs={{16,0},{17,1},{18,2},{19,3},{20,4},{21,5},{22,6},{23,7},{24,8},{25... | collective-permute-start | bytes 1572872 | tf_op jit(solution)/shard_map/ppermute | solution.py:28
  266.3 0.8 copy-start.4
  267.2 25.4 %copy-start.1 = (bf16[256,1024]{1,0:T(8,128)(2,1)S(1)}, bf16[256,1024]{1,0:T(8,128)(2,1)}, u32[]{:S(2)}) copy-start(bf16[256,1024]{1,0:T(8,128)(2,1)} %get-tuple-element.126) | copy-start | bytes 1572868
  294.2 238.0 %copy-start.7 = (f32[1,256]{1,0:T(1,128)S(1)}, f32[1,256]{1,0:T(1,128)}, u32[]{:S(2)}) copy-start(f32[1,256]{1,0:T(1,128)} %get-tuple-element.178) | copy-start | bytes 3076
  531.7 13.3 %collective-permute-start.3 = (bf16[4096,256]{1,0:T(8,128)(2,1)}, bf16[4096,256]{1,0:T(8,128)(2,1)}, u32[]{:S(2)}, u32[]{:S(2)}) collective-permute-start(bf16[4096,256]{1,0:T(8,128)(2,1)} %get-tuple-element.179), channel_id=1, source_target_pairs={{0,16},{16,0},{1,17},{17,1},{2,18},{18,2},{3,19},{19,3},{4,20},{20... | collective-permute-start | bytes 6291464 | tf_op jit(solution)/shard_map/ppermute | solution.py:2034
  531.7 10.3 %collective-permute-start.5 = (f32[8,256]{1,0:T(8,128)}, f32[8,256]{1,0:T(8,128)S(1)}, u32[]{:S(2)}, u32[]{:S(2)}) collective-permute-start(f32[8,256]{1,0:T(8,128)} %get-tuple-element.177), channel_id=1, source_target_pairs={{0,16},{16,0},{1,17},{17,1},{2,18},{18,2},{3,19},{19,3},{4,20},{20... | collective-permute-start | bytes 24584 | tf_op jit(solution)/shard_map/ppermute | solution.py:2034
  532.3 9.3 %collective-permute-start.2 = (bf16[256]{0:T(256)(128)(2,1)S(1)}, bf16[256]{0:T(256)(128)(2,1)S(1)}, u32[]{:S(2)}, u32[]{:S(2)}) collective-permute-start(bf16[256]{0:T(256)(128)(2,1)S(1)} %convert_reduce_fusion.1), channel_id=1, source_target_pairs={{0,16},{16,0},{1,17},{17,1},{2,18},{18,2},{3,19},{19,3},{4,20},{20... | collective-permute-start | bytes 1544 | tf_op jit(solution)/shard_map/ppermute | solution.py:2034
  532.4 11.1 %collective-permute-start.4 = (bf16[64,1024]{1,0:T(8,128)(2,1)}, bf16[64,1024]{1,0:T(8,128)(2,1)S(1)}, u32[]{:S(2)}, u32[]{:S(2)}) collective-permute-start(bf16[64,1024]{1,0:T(8,128)(2,1)} %get-tuple-element.180), channel_id=1, source_target_pairs={{0,16},{16,0},{1,17},{17,1},{2,18},{18,2},{3,19},{19,3},{4,20},{20... | collective-permute-start | bytes 393224 | tf_op jit(solution)/shard_map/ppermute | solution.py:2034
  532.8 10.6 %copy-start.6 = (bf16[64,1024]{1,0:T(8,128)(2,1)S(1)}, bf16[64,1024]{1,0:T(8,128)(2,1)}, u32[]{:S(2)}) copy-start(bf16[64,1024]{1,0:T(8,128)(2,1)} %get-tuple-element.180) | copy-start | bytes 393220
  532.8 12.2 %copy-start.2 = (bf16[4096,256]{1,0:T(8,128)(2,1)S(1)}, bf16[4096,256]{1,0:T(8,128)(2,1)}, u32[]{:S(2)}) copy-start(bf16[4096,256]{1,0:T(8,128)(2,1)} %get-tuple-element.179) | copy-start | bytes 6291460
